TPU v7x, 32 devices: a whole 2x2x4 slice. The times are simulated.
32 devices in a mesh: blk: 8 (over z, x), head: 4 (over y, core).
Axes of the slice: x: 2, y: 2, z: 4, core: 2. Of those that a mesh axis runs over, the one named last changes fastest.
Arguments:
- tokens: bfloat16 [16384, 1536], P(('blk', 'head')), may hold values from -6 to 6
- segment: int32 [16384], P('blk'), may hold values from 0 to 15, never falling along the last dimension, each value on 1 to 2000 neighbouring positions
- norm1_gain: float32 [1536], P(('blk', 'head')), may hold values from 0.5 to 1.5
- w_query: float32 [1536, 1536], P(('blk', 'head')), may hold values from -0.15625 to 0.15625
- w_key: float32 [1536, 1536], P(('blk', 'head')), may hold values from -0.15625 to 0.15625
- w_value: float32 [1536, 1536], P(('blk', 'head')), may hold values from -0.15625 to 0.15625
- w_gate_out: float32 [1536, 1536], P(('blk', 'head')), may hold values from -0.15625 to 0.15625
- w_forget: float32 [1536, 24], P(('blk', 'head')), may hold values from -0.15625 to 0.15625
- forget_bias: float32 [24], replicated, may hold values from 3 to 10
- w_output: float32 [1536, 1536], P(('blk', 'head')), may hold values from -1.75 to 1.75
- norm2_gain: float32 [1536], P(('blk', 'head')), may hold values from 0.5 to 1.5
- w_gate: float32 [1536, 4096], P(('blk', 'head')), may hold values from -0.15625 to 0.15625
- w_up: float32 [1536, 4096], P(('blk', 'head')), may hold values from -0.15625 to 0.15625
- w_down: float32 [1536, 4096], P(('blk', 'head')), may hold values from -0.09375 to 0.09375
- cotangent: bfloat16 [16384, 1536], P(('blk', 'head')), may hold values from -6 to 6
Outputs:
- tokens_out: bfloat16 [16384, 1536], P(('blk', 'head'))
- tokens_grad: float32 [16384, 1536], P(('blk', 'head'))
- norm1_gain_grad: float32 [1536], P(('blk', 'head'))
- w_query_grad: float32 [1536, 1536], P(('blk', 'head'))
- w_key_grad: float32 [1536, 1536], P(('blk', 'head'))
- w_value_grad: float32 [1536, 1536], P(('blk', 'head'))
- w_gate_out_grad: float32 [1536, 1536], P(('blk', 'head'))
- w_forget_grad: float32 [1536, 24], P(('blk', 'head'))
- forget_bias_grad: float32 [24], replicated
- w_output_grad: float32 [1536, 1536], P(('blk', 'head'))
- norm2_gain_grad: float32 [1536], P(('blk', 'head'))
- w_gate_grad: float32 [1536, 4096], P(('blk', 'head'))
- w_up_grad: float32 [1536, 4096], P(('blk', 'head'))
- w_down_grad: float32 [1536, 4096], P(('blk', 'head'))
Inputs may be any that keep to these rules, and one draw needn't show every extreme that they name: `segment`: segment numbers never fall along the tokens and every number occurs; a document has 1 to 2000 tokens and one has exactly 2000.
All inputs are finite; a program needn't handle non-finite values.
Results may differ from a plain program's by a relative error of at most 0.014.
The roundings to bfloat16 on the way count: a program that leaves them out, or rounds other values in their place, can miss the bound.
Values may be sent and summed in bfloat16 or wider, within the bound.
A program may use at most 384 MiB of HBM per device.

v0:
```python
import functools

import jax
import jax.numpy as jnp
from jax import lax
from jax.experimental import pallas as pl
from jax.experimental.pallas import tpu as pltpu
from jax.sharding import PartitionSpec as P

epsilon = 1e-06
LANES = 128
Q_TILE = 512
K_TILE = 256
FAR = -1e30
NT = (((1,), (1,)), ((), ()))
NN = (((1,), (0,)), ((), ()))
bf16 = jnp.bfloat16
f32 = jnp.float32


def dot(a, b, dims=NN, **kw):
    return lax.dot_general(a, b, dims, preferred_element_type=f32, **kw)


def passed_along(array, axis, by):
    peers = lax.axis_size(axis)
    pairs = [(i, i + by) for i in range(peers) if 0 <= i + by < peers]
    return lax.ppermute(array, axis, pairs)


def split3(value):
    high = value.astype(bf16)
    rest = value - high.astype(f32)
    mid = rest.astype(bf16)
    low = (rest - mid.astype(f32)).astype(bf16)
    return high, mid, low


def running(value_of, steps, rows, upper):
    place = lax.broadcasted_iota(jnp.int32, (rows, rows), 0)
    other = lax.broadcasted_iota(jnp.int32, (rows, rows), 1)
    tri = jnp.where((other >= place) if upper else (other <= place), 1.0, 0.0).astype(bf16)
    outs = [None] * steps
    carry = jnp.zeros((1, LANES), f32)
    order = range(steps - 1, -1, -1) if upper else range(steps)
    for n in order:
        block = value_of(n)
        total = sum(dot(tri, part) for part in split3(block)) + carry
        outs[n] = total
        carry = total[0:1] if upper else total[rows - 1 : rows]
    return outs, carry


def decay_kernel(local_heads, logf_ref, own_ref, halo_ref):
    rows = 256
    steps = logf_ref.shape[0] // rows
    lane = lax.broadcasted_iota(jnp.int32, (rows, LANES), 1)

    def value_of(n):
        return jnp.where(lane < local_heads, logf_ref[n * rows : (n + 1) * rows, :], 0.0)

    sums, total = running(value_of, steps, rows, False)
    one = jnp.where(lane == 3 * local_heads, 1.0, 0.0)

    def terms(value):
        high, mid, low = split3(value)
        return (
            high.astype(f32)
            + pltpu.roll(mid.astype(f32), local_heads, 1)
            + pltpu.roll(low.astype(f32), 2 * local_heads, 1)
            + one
        ).astype(bf16)

    for n in range(steps):
        own_ref[n * rows : (n + 1) * rows, :] = terms(sums[n])
        halo_ref[n * rows : (n + 1) * rows, :] = terms(sums[n] - total)


def decay_terms(logf, local_heads):
    shape = jax.ShapeDtypeStruct(logf.shape, bf16)
    return pl.pallas_call(
        functools.partial(decay_kernel, local_heads),
        out_shape=(shape, shape),
        name="decay_terms",
    )(logf)


def decay_back_kernel(own_ref, halo_ref, out_ref):
    rows = 256
    steps = own_ref.shape[0] // rows
    own, _ = running(lambda n: own_ref[n * rows : (n + 1) * rows, :], steps, rows, True)
    halo, _ = running(lambda n: halo_ref[n * rows : (n + 1) * rows, :], steps, rows, False)
    for n in range(steps):
        part = slice(n * rows, (n + 1) * rows)
        out_ref[part, :] = own[n] + (halo[n] - halo_ref[part, :])


def decay_back(own, halo):
    return pl.pallas_call(
        decay_back_kernel,
        out_shape=jax.ShapeDtypeStruct(own.shape, f32),
        name="decay_back",
    )(own, halo)


def placing(pair, local_heads, for_query):
    row = lax.broadcasted_iota(jnp.int32, (LANES, LANES), 0)
    col = lax.broadcasted_iota(jnp.int32, (LANES, LANES), 1)
    head = jnp.where(col < 64, 2 * pair + 1, 2 * pair)
    spot = jnp.where(col < 64, col, col - 64)
    term = jnp.where(for_query, spot, spot - 3)
    is_term = (term >= 0) & (term < 3) & (row == term * local_heads + head)
    ones = jnp.where(for_query, spot - 3, spot)
    is_one = (ones >= 0) & (ones < 3) & (row == 3 * local_heads)
    sign = 1.0 if for_query else -1.0
    return (jnp.where(is_term, sign, 0.0) + jnp.where(is_one, 1.0, 0.0)).astype(bf16)


def allowed_pairs(first_key, query_tile, rows, begin_row):
    shape = (K_TILE, Q_TILE)
    key_place = first_key + lax.broadcasted_iota(jnp.int32, shape, 0)
    query_place = rows + query_tile * Q_TILE + lax.broadcasted_iota(jnp.int32, shape, 1)
    return (key_place >= begin_row) & (key_place <= query_place)


def key_range(ranges_ref, query_tile, rows, own):
    count = rows // K_TILE
    base = count if own else 0
    first = jnp.clip(ranges_ref[0, query_tile] - base, 0, count)
    full = jnp.clip(ranges_ref[1, query_tile] - base, first, count)
    return first, full


def key_loops(ranges_ref, query_tile, rows, own, step, carry):
    first, full = key_range(ranges_ref, query_tile, rows, own)
    inside = query_tile * (Q_TILE // K_TILE) if own else rows // K_TILE
    full = jnp.minimum(full, inside)
    carry = lax.fori_loop(first, full, functools.partial(step, True), carry)
    carry = lax.fori_loop(full, inside, functools.partial(step, False), carry)
    if own:
        carry = lax.fori_loop(
            inside, inside + Q_TILE // K_TILE, functools.partial(step, True), carry
        )
    return carry


def tile_of(number, size):
    return pl.ds(pl.multiple_of(number * size, size), size)


def fill_keys(pair, local_heads, first, key_ref, terms_ref, keys):
    place = placing(pair, local_heads, False)
    lane = lax.broadcasted_iota(jnp.int32, (K_TILE, LANES), 1)

    def fill(n, carry):
        here = tile_of(n, K_TILE)
        extra = dot(terms_ref[here, :], place).astype(bf16)
        key = key_ref[here, :]
        keys[0][here, :] = jnp.where(lane < 64, key, extra)
        keys[1][here, :] = jnp.where(lane < 64, extra, key)
        return carry

    lax.fori_loop(first, key_ref.shape[0] // K_TILE, fill, 0)


def query_tiles(q_ref, terms_ref, place, here, scaling):
    lane = lax.broadcasted_iota(jnp.int32, (Q_TILE, LANES), 1)
    extra = dot(terms_ref[here, :], place).astype(bf16)
    query = (q_ref[here, :].astype(f32) * scaling).astype(bf16)
    return jnp.where(lane < 64, query, extra), jnp.where(lane < 64, extra, query)


def attend_kernel(local_heads, own, ranges_ref, q_ref, k_ref, v_ref, t_query_ref, t_key_ref,
                  begin_ref, *refs):
    if own:
        acc_out_ref, state_out_ref, key0, key1, values, acc0, acc1 = refs
    else:
        acc_in_ref, state_in_ref, o_ref, lse_ref, key0, key1, values, acc0, acc1 = refs
    pair = pl.program_id(0)
    rows = q_ref.shape[0]
    base = rows if own else 0
    keys, accs = (key0, key1), (acc0, acc1)
    first, _ = key_range(ranges_ref, 0, rows, own)
    fill_keys(pair, local_heads, first, k_ref, t_key_ref, keys)

    def turn(n, carry):
        values[:, tile_of(n, K_TILE)] = v_ref[tile_of(n, K_TILE), :].T
        return carry

    lax.fori_loop(first, rows // K_TILE, turn, 0)
    place = placing(pair, local_heads, True)

    def query_loop(tile, carry):
        here = tile_of(tile, Q_TILE)
        queries = query_tiles(q_ref, t_query_ref, place, here, 64**-0.5)
        begin_row = begin_ref[0:1, here]
        if own:
            low = jnp.full((1, Q_TILE), FAR, f32)
            zero = jnp.zeros((1, Q_TILE), f32)
            state = (low, zero, low, zero)
            for acc in accs:
                acc[...] = jnp.zeros_like(acc)
        else:
            state = tuple(state_in_ref[n : n + 1, here] for n in range(4))
            for h in range(2):
                accs[h][...] = acc_in_ref[64 * h : 64 * (h + 1), here]

        def step(masked, number, state):
            there = tile_of(number, K_TILE)
            fresh = []
            if masked:
                allowed = allowed_pairs(base + number * K_TILE, tile, rows, begin_row)
            for h in range(2):
                largest, total = state[2 * h], state[2 * h + 1]
                scores = dot(keys[h][there, :], queries[h], NT)
                if masked:
                    scores = jnp.where(allowed, scores, FAR)
                now = jnp.maximum(largest, jnp.max(scores, axis=0, keepdims=True))
                fade = jnp.exp(largest - now)
                weights = jnp.exp(scores - now)
                total = total * fade + jnp.sum(weights, axis=0, keepdims=True)
                accs[h][...] = accs[h][...] * fade + dot(
                    values[64 * h : 64 * (h + 1), there], weights.astype(bf16)
                )
                fresh += [now, total]
            return tuple(fresh)

        state = key_loops(ranges_ref, tile, rows, own, step, state)
        if own:
            for h in range(2):
                acc_out_ref[64 * h : 64 * (h + 1), here] = accs[h][...]
            for n in range(4):
                state_out_ref[n : n + 1, here] = state[n]
        else:
            mixed = jnp.concatenate(
                [accs[h][...] * (1.0 / state[2 * h + 1]) for h in range(2)], axis=0
            )
            o_ref[here, :] = mixed.T.astype(bf16)
            for h in range(2):
                lse_ref[h : h + 1, here] = state[2 * h] + jnp.log(state[2 * h + 1])
        return carry

    lax.fori_loop(0, rows // Q_TILE, query_loop, 0)


def lane_block(rows, offset):
    return pl.BlockSpec((rows, LANES), lambda p, *_: (0, offset + p))


def fixed(shape):
    return pl.BlockSpec(shape, lambda p, *_: (0, 0))


def pair_block(height, rows):
    return pl.BlockSpec((height, rows), lambda p, *_: (p, 0))


def attend(own, ranges, query, key_value, terms, key_terms, begins, local_heads, so_far=()):
    rows = query.shape[0]
    pairs = local_heads // 2
    running_specs = [pair_block(LANES, rows), pair_block(8, rows)]
    running_shape = (
        jax.ShapeDtypeStruct((LANES * pairs, rows), f32),
        jax.ShapeDtypeStruct((8 * pairs, rows), f32),
    )
    final_specs = [lane_block(rows, 0), pair_block(8, rows)]
    final_shape = (
        jax.ShapeDtypeStruct((rows, pairs * LANES), bf16),
        jax.ShapeDtypeStruct((8 * pairs, rows), f32),
    )
    return pl.pallas_call(
        functools.partial(attend_kernel, local_heads, own),
        grid_spec=pltpu.PrefetchScalarGridSpec(
            num_scalar_prefetch=1,
            grid=(pairs,),
            in_specs=[
                lane_block(rows, 0),
                lane_block(rows, 0),
                lane_block(rows, pairs),
                fixed((rows, LANES)),
                fixed((rows, LANES)),
                fixed((8, rows)),
            ]
            + ([] if own else running_specs),
            out_specs=running_specs if own else final_specs,
            scratch_shapes=[
                pltpu.VMEM((rows, LANES), bf16),
                pltpu.VMEM((rows, LANES), bf16),
                pltpu.VMEM((LANES, rows), bf16),
                pltpu.VMEM((64, Q_TILE), f32),
                pltpu.VMEM((64, Q_TILE), f32),
            ],
        ),
        out_shape=running_shape if own else final_shape,
        cost_estimate=pl.CostEstimate(
            flops=40_000_000_000 if own else 10_000_000_000,
            transcendentals=20_000_000,
            bytes_accessed=12_000_000,
        ),
        name="attend_own" if own else "attend_prev",
    )(ranges, query, key_value, key_value, terms, key_terms, begins, *so_far)


def attend_back_kernel(local_heads, own, ranges_ref, q_ref, k_ref, v_ref, t_query_ref, t_key_ref,
                       begin_ref, grad_ref, o_ref, lse_ref, *refs):
    if own:
        dq_in_ref, decay_in_ref, dq_ref, dk_ref, dv_ref, decay_ref = refs[:6]
    else:
        dq_ref, row_decay_ref, dkv_ref, decay_ref = refs[:4]
        dk_ref, dv_ref = dkv_ref.at[0], dkv_ref.at[1]
    key0, key1, key_t0, key_t1, dk0, dk1, dv, dq0, dq1 = refs[-9:]
    pair = pl.program_id(0)
    rows = q_ref.shape[0]
    base = rows if own else 0
    keys, keys_t, dks, dqs = (key0, key1), (key_t0, key_t1), (dk0, dk1), (dq0, dq1)
    first, _ = key_range(ranges_ref, 0, rows, own)
    fill_keys(pair, local_heads, first, k_ref, t_key_ref, keys)

    def turn(n, carry):
        here = tile_of(n, K_TILE)
        for h in range(2):
            keys_t[h][:, here] = keys[h][here, :].T
        return carry

    lax.fori_loop(first, rows // K_TILE, turn, 0)
    for ref in (dk0, dk1, dv):
        ref[...] = jnp.zeros_like(ref)
    place = placing(pair, local_heads, True)
    lane = lax.broadcasted_iota(jnp.int32, (Q_TILE, LANES), 1)
    pick_row = lax.broadcasted_iota(jnp.int32, (8, LANES), 0)
    pick_lane = lax.broadcasted_iota(jnp.int32, (8, LANES), 1)
    pick = jnp.where((pick_lane // 64) == pick_row, 1.0, 0.0)
    sums_ref = decay_ref if own else row_decay_ref

    @pl.when(pair == 0)
    def _():
        if own:
            decay_ref[...] = decay_in_ref[...]
        else:
            decay_ref[...] = jnp.zeros_like(decay_ref)
            row_decay_ref[...] = jnp.zeros_like(row_decay_ref)

    def query_tile(tile):
        here = tile_of(tile, Q_TILE)
        queries = query_tiles(q_ref, t_query_ref, place, here, 64**-0.5)
        begin_row = begin_ref[0:1, here]
        grad = grad_ref[here, :]
        nothing = jnp.zeros_like(grad)
        grads = (jnp.where(lane < 64, grad, nothing), jnp.where(lane < 64, nothing, grad))
        product = grad.astype(f32) * o_ref[here, :].astype(f32)
        inner = dot(pick, product, NT, precision=lax.Precision.HIGHEST)
        for dq in dqs:
            dq[...] = jnp.zeros_like(dq)

        def step(masked, number, state):
            there = tile_of(number, K_TILE)
            if masked:
                allowed = allowed_pairs(base + number * K_TILE, tile, rows, begin_row)
            value = v_ref[there, :]
            value_part = 0.0
            for h in range(2):
                scores = dot(keys[h][there, :], queries[h], NT)
                prob = jnp.exp(scores - lse_ref[h : h + 1, here])
                if masked:
                    prob = jnp.where(allowed, prob, 0.0)
                grad_prob = dot(value, grads[h], NT)
                grad_score = (prob * (grad_prob - inner[h : h + 1, :])).astype(bf16)
                value_part = value_part + dot(prob.astype(bf16), grads[h])
                dks[h][there, :] += dot(grad_score, queries[h])
                dqs[h][...] += dot(keys_t[h][:, there], grad_score)
            dv[there, :] += value_part
            return state

        key_loops(ranges_ref, tile, rows, own, step, 0)
        turned = [dq[...].T for dq in dqs]
        dq_tile = jnp.where(lane < 64, turned[0], turned[1]) * 64**-0.5
        if own:
            dq_tile = dq_tile + dq_in_ref[here, :]
        dq_ref[here, :] = dq_tile.astype(dq_ref.dtype)
        sums = sums_ref[here, :]
        sums = sums + jnp.where(lane == 2 * pair, turned[0][:, 64:65], 0.0)
        sums = sums + jnp.where(lane == 2 * pair + 1, turned[1][:, 0:1], 0.0)
        sums_ref[here, :] = sums

    def query_loop(tile, carry):
        if own:
            query_tile(tile)
        else:
            reaches = key_range(ranges_ref, tile, rows, own)[0] < rows // K_TILE
            pl.when(reaches)(lambda: query_tile(tile))

            @pl.when(jnp.logical_not(reaches))
            def _():
                dq_ref[tile_of(tile, Q_TILE), :] = jnp.zeros((Q_TILE, LANES), dq_ref.dtype)

        return carry

    lax.fori_loop(0, rows // Q_TILE, query_loop, 0)
    sign = -1.0 if own else 1.0

    def finish(n, carry):
        here = tile_of(n, Q_TILE)
        left, right = dk0[here, :], dk1[here, :]
        dk_ref[here, :] = jnp.where(lane < 64, left, right).astype(dk_ref.dtype)
        dv_ref[here, :] = dv[here, :].astype(dv_ref.dtype)
        decay = decay_ref[here, :]
        decay = decay + jnp.where(lane == 2 * pair, sign * left[:, 67:68], 0.0)
        decay = decay + jnp.where(lane == 2 * pair + 1, sign * right[:, 3:4], 0.0)
        decay_ref[here, :] = decay
        return carry

    lax.fori_loop(0, rows // Q_TILE, finish, 0)


def attend_back(
    own, ranges, query, key_value, terms, key_terms, begins, grad, mixed, lse, local_heads,
    so_far=(),
):
    rows = query.shape[0]
    pairs = local_heads // 2
    wide = jax.ShapeDtypeStruct((rows, pairs * LANES), f32)
    sums = jax.ShapeDtypeStruct((rows, LANES), f32)
    if own:
        out_specs = [lane_block(rows, 0)] * 3 + [fixed((rows, LANES))]
        out_shape = (jax.ShapeDtypeStruct(wide.shape, bf16), wide, wide, sums)
    else:
        both = pl.BlockSpec((2, rows, LANES), lambda p, *_: (0, 0, p))
        out_specs = [lane_block(rows, 0), fixed((rows, LANES)), both, fixed((rows, LANES))]
        out_shape = (
            wide, sums, jax.ShapeDtypeStruct((2, rows, pairs * LANES), bf16), sums,
        )
    return pl.pallas_call(
        functools.partial(attend_back_kernel, local_heads, own),
        grid_spec=pltpu.PrefetchScalarGridSpec(
            num_scalar_prefetch=1,
            grid=(pairs,),
            in_specs=[
                lane_block(rows, 0),
                lane_block(rows, 0),
                lane_block(rows, pairs),
                fixed((rows, LANES)),
                fixed((rows, LANES)),
                fixed((8, rows)),
                lane_block(rows, 0),
                lane_block(rows, 0),
                pair_block(8, rows),
            ]
            + ([lane_block(rows, 0), fixed((rows, LANES))] if own else []),
            out_specs=out_specs,
            scratch_shapes=[
                pltpu.VMEM((rows, LANES), bf16),
                pltpu.VMEM((rows, LANES), bf16),
                pltpu.VMEM((LANES, rows), bf16),
                pltpu.VMEM((LANES, rows), bf16),
                pltpu.VMEM((rows, LANES), f32),
                pltpu.VMEM((rows, LANES), f32),
                pltpu.VMEM((rows, LANES), f32),
                pltpu.VMEM((LANES, Q_TILE), f32),
                pltpu.VMEM((LANES, Q_TILE), f32),
            ],
        ),
        out_shape=out_shape,
        cost_estimate=pl.CostEstimate(
            flops=80_000_000_000 if own else 15_000_000_000,
            transcendentals=20_000_000,
            bytes_accessed=25_000_000,
        ),
        name="attend_back_own" if own else "attend_back_prev",
    )(
        ranges, query, key_value, key_value, terms, key_terms, begins, grad, mixed, lse, *so_far
    )


PIECES = 4


def partners():
    me = lax.axis_index("head")
    near = me + 1 - 2 * (me % 2)
    far = (me + 2) % 4
    cross = (near + 2) % 4
    return me, near, far, cross


def signal(other):
    pl.semaphore_signal(
        pltpu.get_barrier_semaphore(), inc=1, device_id=other, device_id_type=pl.DeviceIdType.MESH
    )


def greet(others):
    for other in others:
        signal(other)
    pl.semaphore_wait(pltpu.get_barrier_semaphore(), len(others))


def remote(source, target, send, receive, other):
    return pltpu.make_async_remote_copy(
        src_ref=source,
        dst_ref=target,
        send_sem=send,
        recv_sem=receive,
        device_id=other,
        device_id_type=pl.DeviceIdType.MESH,
    )


def on_head(index):
    return {"head": index}


def on_blk(index):
    return {"blk": index}


def rows_of(ref, shard, piece, size):
    span = size // PIECES
    start = pl.multiple_of(shard * size + piece * span, span)
    return ref.at[pl.ds(start, span), :]


def spread_piece(source, all_ref, size, sems, piece):
    me, near, far, _ = partners()
    far_send, far_recv, near_send, near_recv, _, _, own = sems
    place = rows_of(all_ref, me, piece, size)
    copies = (
        remote(source, place, far_send.at[piece], far_recv.at[piece], on_head(far)),
        remote(source, place, near_send.at[piece], near_recv.at[piece], on_head(near)),
        pltpu.make_async_copy(source, place, own.at[piece]),
    )
    for copy in copies:
        copy.start()
    return copies


def hand_on(all_ref, size, sems, sent):
    me, near, far, cross = partners()
    far_send, far_recv, near_send, near_recv, on_send, on_recv, own = sems
    passed = []
    for piece in range(PIECES):
        there = rows_of(all_ref, far, piece, size)
        remote(there, there, far_send.at[piece], far_recv.at[piece], on_head(far)).wait_recv()
        copy = remote(there, there, on_send.at[piece], on_recv.at[piece], on_head(near))
        copy.start()
        passed.append(copy)

    def finish():
        for piece in range(PIECES):
            to_far, to_near, local = sent[piece]
            to_far.wait_send()
            to_near.wait_send()
            local.wait()
            passed[piece].wait_send()
            there = rows_of(all_ref, near, piece, size)
            remote(there, there, near_send.at[piece], near_recv.at[piece], on_head(near)).wait_recv()
            there = rows_of(all_ref, cross, piece, size)
            remote(there, there, on_send.at[piece], on_recv.at[piece], on_head(near)).wait_recv()

    return finish


def gather_sems():
    return [pltpu.SemaphoreType.DMA((PIECES,)) for _ in range(7)]


def blk_peers():
    here = lax.axis_index("blk")
    half = lax.axis_size("blk") // 2
    low, high = here % 2, here // 2
    partner = here + 1 - 2 * low
    after = [((high + t) % half) * 2 + low for t in range(half)]
    before = [((high + half - t) % half) * 2 + low for t in range(half)]
    return here, partner, after, before


def gather_first_kernel(pack_ref, tokens_ref, cotangent_ref, pack_all, tokens_all, cotangent_all,
                        *sems):
    (swap_send, swap_recv, swap_own, line_send, line_recv, pair_send, pair_recv) = sems[:7]
    token_sems, cotangent_sems = sems[7:14], sems[14:21]
    me, near, far, cross = partners()
    here, partner, after, before = blk_peers()
    steps = len(after)
    greet(
        [on_head(near), on_head(far), on_head(cross), on_blk(partner)]
        + [on_blk(peer) for peer in after[1:]]
    )
    swaps = [pltpu.make_async_copy(pack_ref.at[me], pack_all.at[here, me], swap_own)]
    for kind, other in enumerate((near, far, cross)):
        swaps.append(
            remote(
                pack_ref.at[other],
                pack_all.at[here, me],
                swap_send.at[kind],
                swap_recv.at[kind],
                on_head(other),
            )
        )
    for swap in swaps:
        swap.start()
    size = tokens_ref.shape[0]
    span = size // PIECES

    def spread_all(ref, all_ref, some):
        return [
            spread_piece(ref.at[pl.ds(piece * span, span), :], all_ref, size, some, piece)
            for piece in range(PIECES)
        ]

    tokens_sent = spread_all(tokens_ref, tokens_all, token_sems)
    sources = (me, near, far, cross)
    waiting = []
    for kind, source in enumerate(sources):
        block = pack_all.at[here, source]
        if kind == 0:
            swaps[0].wait()
        else:
            remote(
                block, block, swap_send.at[kind - 1], swap_recv.at[kind - 1], on_head(source)
            ).wait_recv()
        for t in range(steps):
            if t == 0:
                copy = remote(
                    block, block, pair_send.at[kind, 0], pair_recv.at[kind, 0], on_blk(partner)
                )
            else:
                copy = remote(
                    block, block, line_send.at[kind, t], line_recv.at[kind, t], on_blk(after[t])
                )
            copy.start()
            waiting.append(copy)
    cotangent_sent = spread_all(cotangent_ref, cotangent_all, cotangent_sems)
    finish_tokens = finish_cotangent = None
    for t in range(1, steps):
        for kind, source in enumerate(sources):
            block = pack_all.at[before[t], source]
            remote(
                block, block, line_send.at[kind, t], line_recv.at[kind, t], on_blk(after[t])
            ).wait_recv()
            copy = remote(
                block, block, pair_send.at[kind, t], pair_recv.at[kind, t], on_blk(partner)
            )
            copy.start()
            waiting.append(copy)
        if t == min(2, steps - 1):
            finish_tokens = hand_on(tokens_all, size, token_sems, tokens_sent)
    finish_cotangent = hand_on(cotangent_all, size, cotangent_sems, cotangent_sent)
    for swap in swaps[1:]:
        swap.wait_send()
    for copy in waiting:
        copy.wait_send()
    for t in range(steps):
        for kind, source in enumerate(sources):
            block = pack_all.at[before[t] + partner - here, source]
            remote(
                block, block, pair_send.at[kind, t], pair_recv.at[kind, t], on_blk(partner)
            ).wait_recv()
    finish_tokens()
    finish_cotangent()


def gather_first(pack, tokens, cotangent, number):
    groups, share, columns = pack.shape
    peers = lax.axis_size("blk")
    rows, width = tokens.shape
    whole = jax.ShapeDtypeStruct((groups * rows, width), bf16)
    vmem, anywhere = pl.BlockSpec(memory_space=pltpu.VMEM), pl.BlockSpec(memory_space=pl.ANY)
    all_pack, all_tokens, all_cotangent = pl.pallas_call(
        gather_first_kernel,
        in_specs=[vmem] * 3,
        out_specs=[anywhere] * 3,
        out_shape=[jax.ShapeDtypeStruct((peers, groups, share, columns), bf16), whole, whole],
        scratch_shapes=[
            pltpu.SemaphoreType.DMA((3,)),
            pltpu.SemaphoreType.DMA((3,)),
            pltpu.SemaphoreType.DMA,
        ]
        + [pltpu.SemaphoreType.DMA((4, peers // 2)) for _ in range(4)]
        + gather_sems()
        + gather_sems(),
        compiler_params=pltpu.CompilerParams(collective_id=number, has_side_effects=True),
        cost_estimate=pl.CostEstimate(
            flops=70_000_000_000, transcendentals=0, bytes_accessed=30_000_000
        ),
        name="gather_first",
    )(pack, tokens, cotangent)
    return all_pack.reshape(peers * groups * share, columns), all_tokens, all_cotangent


class Sum:
    def __init__(self, part_ref, buffers, sems, size):
        self.part_ref, self.size, self.span = part_ref, size, size // PIECES
        self.near_buf, self.turn_buf, self.far_buf = buffers
        self.near_send, self.near_recv, self.far_send, self.far_recv = sems
        self.near_copies, self.far_copies = [], []

    def piece(self, n):
        return slice(n * self.span, (n + 1) * self.span)

    def start(self):
        me, near, far, cross = partners()
        for which, shard in ((0, cross), (1, near)):
            for n in range(PIECES):
                copy = remote(
                    rows_of(self.part_ref, shard, n, self.size),
                    self.near_buf.at[which, pl.ds(n * self.span, self.span), :],
                    self.near_send.at[which, n],
                    self.near_recv.at[which, n],
                    on_head(near),
                )
                copy.start()
                self.near_copies.append(copy)

    def turn(self):
        me, near, far, cross = partners()
        for n in range(PIECES):
            here = self.piece(n)
            self.near_copies[n].wait_recv()
            self.turn_buf[here, :] = (
                rows_of(self.part_ref, far, n, self.size)[...].astype(f32)
                + self.near_buf[0, here, :].astype(f32)
            ).astype(bf16)
            copy = remote(
                self.turn_buf.at[pl.ds(n * self.span, self.span), :],
                self.far_buf.at[pl.ds(n * self.span, self.span), :],
                self.far_send.at[n],
                self.far_recv.at[n],
                on_head(far),
            )
            copy.start()
            self.far_copies.append(copy)

    def total(self, n):
        me = lax.axis_index("head")
        self.near_copies[PIECES + n].wait_recv()
        self.far_copies[n].wait_recv()
        here = self.piece(n)
        return (
            rows_of(self.part_ref, me, n, self.size)[...].astype(f32)
            + self.near_buf[1, here, :].astype(f32)
            + self.far_buf[here, :].astype(f32)
        )

    def finish(self):
        for copy in self.near_copies + self.far_copies:
            copy.wait_send()


def sum_buffers(size, width):
    return [
        pltpu.VMEM((2, size, width), bf16),
        pltpu.VMEM((size, width), bf16),
        pltpu.VMEM((size, width), bf16),
    ]


def sum_sems():
    return [
        pltpu.SemaphoreType.DMA((2, PIECES)),
        pltpu.SemaphoreType.DMA((2, PIECES)),
        pltpu.SemaphoreType.DMA((PIECES,)),
        pltpu.SemaphoreType.DMA((PIECES,)),
    ]


def exchange_kernel(local, extras, *refs):
    part_ref, extra_refs = refs[0], refs[1 : 1 + extras]
    out_ref, all_ref, near_buf, turn_buf, far_buf, payload = refs[1 + extras : 7 + extras]
    sems = refs[7 + extras :]
    size = out_ref.shape[0]
    _, near, far, _ = partners()
    greet([on_head(near), on_head(far)])
    shares = Sum(part_ref, (near_buf, turn_buf, far_buf), sems[:4], size)
    shares.start()
    shares.turn()
    sent = []
    for piece in range(PIECES):
        here = shares.piece(piece)
        result, share = local(shares.total(piece), here, *extra_refs)
        out_ref[here, :] = result.astype(out_ref.dtype)
        payload[here, :] = share.astype(bf16)
        source = payload.at[pl.ds(piece * shares.span, shares.span), :]
        sent.append(spread_piece(source, all_ref, size, sems[4:], piece))
    hand_on(all_ref, size, sems[4:], sent)()
    shares.finish()


def exchange(local, part, extras, number, name):
    rows, width = part.shape
    size = rows // 4
    vmem = pl.BlockSpec(memory_space=pltpu.VMEM)
    return pl.pallas_call(
        functools.partial(exchange_kernel, local, len(extras)),
        in_specs=[vmem] * (1 + len(extras)),
        out_specs=[vmem, pl.BlockSpec(memory_space=pl.ANY)],
        out_shape=[
            jax.ShapeDtypeStruct((size, width), f32),
            jax.ShapeDtypeStruct((rows, width), bf16),
        ],
        scratch_shapes=sum_buffers(size, width)
        + [pltpu.VMEM((size, width), bf16)]
        + sum_sems()
        + gather_sems(),
        compiler_params=pltpu.CompilerParams(collective_id=number, has_side_effects=True),
        cost_estimate=pl.CostEstimate(
            flops=70_000_000_000, transcendentals=0, bytes_accessed=16_000_000
        ),
        name=name,
    )(part, *extras)


def finish_last_kernel(grad_ref, first_ref, down_ref, grad_middle_ref, tokens_ref, gain_ref,
                       middle_ref, weights_ref, tokens_grad_ref, result_ref, pair_buf, turn_buf,
                       line_buf, row_buf, near1, turn1, far1, near2, turn2, far2, *sems):
    pair_send, pair_recv, line_send, line_recv, swap_send, swap_recv = sems[:6]
    me, near, far, cross = partners()
    here, partner, after, before = blk_peers()
    steps = len(after)
    groups = grad_ref.shape[1]
    greet(
        [on_head(near), on_head(far), on_head(cross), on_blk(partner)]
        + [on_blk(peer) for peer in after[1:]]
    )
    size = result_ref.shape[0]
    first = Sum(first_ref, (near1, turn1, far1), sems[6:10], size)
    down = Sum(down_ref, (near2, turn2, far2), sems[10:14], size)
    first.start()
    order = list(range(1, steps)) + [0]
    pair_copies = {}
    for t in order:
        copy = remote(
            grad_ref.at[after[t] + partner - here],
            pair_buf.at[t],
            pair_send.at[t],
            pair_recv.at[t],
            on_blk(partner),
        )
        copy.start()
        pair_copies[t] = copy
    first.turn()
    down.start()
    down.turn()
    line_copies = {}

    def pass_on(t):
        pair_copies[t].wait_recv()

        def add(group, carry):
            turn_buf[t, group] = (
                grad_ref[after[t], group].astype(f32) + pair_buf[t, group].astype(f32)
            ).astype(bf16)
            return carry

        lax.fori_loop(0, groups, add, 0)
        copy = remote(
            turn_buf.at[t], line_buf.at[t], line_send.at[t], line_recv.at[t], on_blk(after[t])
        )
        copy.start()
        line_copies[t] = copy

    def put(shares, local, out_ref, extra_refs):
        for piece in range(PIECES):
            rows = shares.piece(piece)
            value, _ = local(shares.total(piece), rows, *extra_refs)
            out_ref[rows, :] = value.astype(out_ref.dtype)

    for t in range(1, steps):
        pass_on(t)
        if t == min(2, steps - 1):
            put(first, after_first, tokens_grad_ref, (grad_middle_ref, tokens_ref, gain_ref))
    pair_copies[0].wait_recv()
    for t in range(1, steps):
        line_copies[t].wait_recv()

    def add_all(group, carry):
        total = grad_ref[here, group].astype(f32) + pair_buf[0, group].astype(f32)
        for t in range(1, steps):
            total = total + line_buf[t, group].astype(f32)
        row_buf[group] = total.astype(bf16)
        return carry

    lax.fori_loop(0, groups, add_all, 0)
    swaps = []
    for kind, other in enumerate((near, far, cross)):
        copy = remote(
            row_buf.at[other],
            weights_ref.at[me],
            swap_send.at[kind],
            swap_recv.at[kind],
            on_head(other),
        )
        copy.start()
        swaps.append(copy)
    weights_ref[me] = row_buf[me]
    put(down, after_down, result_ref, (middle_ref,))
    for kind, other in enumerate((near, far, cross)):
        block = weights_ref.at[other]
        remote(block, block, swap_send.at[kind], swap_recv.at[kind], on_head(other)).wait_recv()
        swaps[kind].wait_send()
    for copy in list(pair_copies.values()) + list(line_copies.values()):
        copy.wait_send()
    first.finish()
    down.finish()


def finish_last(grad, groups, part_first, part_down, grad_middle, tokens, gain, middle, number):
    peers = lax.axis_size("blk")
    all_rows, columns = grad.shape
    share = all_rows // (peers * groups)
    rows, width = tokens.shape
    vmem = pl.BlockSpec(memory_space=pltpu.VMEM)
    half = peers // 2
    return pl.pallas_call(
        finish_last_kernel,
        in_specs=[vmem] * 7,
        out_specs=[vmem] * 3,
        out_shape=[
            jax.ShapeDtypeStruct((groups, share, columns), bf16),
            jax.ShapeDtypeStruct((rows, width), f32),
            jax.ShapeDtypeStruct((rows, width), bf16),
        ],
        scratch_shapes=[pltpu.VMEM((half, groups, share, columns), bf16) for _ in range(3)]
        + [pltpu.VMEM((groups, share, columns), bf16)]
        + sum_buffers(rows, width)
        + sum_buffers(rows, width)
        + [pltpu.SemaphoreType.DMA((half,)) for _ in range(4)]
        + [pltpu.SemaphoreType.DMA((3,)) for _ in range(2)]
        + sum_sems()
        + sum_sems(),
        compiler_params=pltpu.CompilerParams(
            collective_id=number, has_side_effects=True, vmem_limit_bytes=60 << 20
        ),
        cost_estimate=pl.CostEstimate(
            flops=80_000_000_000, transcendentals=0, bytes_accessed=40_000_000
        ),
        name="finish_last",
    )(
        grad.reshape(peers, groups, share, columns), part_first, part_down, grad_middle, tokens,
        gain, middle,
    )


def inverse_rms(value):
    return lax.rsqrt(jnp.mean(value * value, axis=1, keepdims=True) + epsilon)


def through_norm(grad, value):
    factor = inverse_rms(value)
    normed = value * factor
    return factor * (grad - normed * jnp.mean(grad * normed, axis=1, keepdims=True))


def after_attention(total, here, tokens_ref, gain_ref):
    middle = tokens_ref[here, :].astype(f32) + total
    return middle, middle * inverse_rms(middle) * gain_ref[0:1, :]


def after_hidden(total, here, cotangent_ref, middle_ref, gain_ref):
    grad = cotangent_ref[here, :].astype(f32) + through_norm(
        total * gain_ref[0:1, :], middle_ref[here, :]
    )
    return grad, grad


def after_first(total, here, grad_ref, tokens_ref, gain_ref):
    grad = grad_ref[here, :] + through_norm(
        total * gain_ref[0:1, :], tokens_ref[here, :].astype(f32)
    )
    return grad, None


def after_down(total, here, middle_ref):
    return middle_ref[here, :] + total, None


def over_tokens(operand, other_side):
    return lax.dot_general(
        operand, other_side, (((0,), (0,)), ((), ())), preferred_element_type=f32
    )


def sent_columns(pieces, groups):
    packed = jnp.concatenate(
        [piece.reshape(piece.shape[0], groups, -1) for piece in pieces], axis=2
    )
    mine = lax.all_to_all(packed, "head", split_axis=1, concat_axis=0, tiled=True)
    return mine.reshape(mine.shape[0], mine.shape[2])


def all_rows(mine):
    return lax.all_gather(mine, "blk", axis=0, tiled=True)


def row_sums(grad):
    return lax.psum_scatter(grad, "blk", scatter_dimension=0, tiled=True)


def own_rows(summed, groups):
    rows, columns = summed.shape
    parts = lax.all_to_all(
        summed.reshape(groups, rows // groups, columns), "head", split_axis=0, concat_axis=0
    )
    return jnp.swapaxes(parts, 0, 1).astype(f32)


def body(
    tokens,
    segment,
    norm1_gain,
    w_query,
    w_key,
    w_value,
    w_gate_out,
    w_forget,
    forget_bias,
    w_output,
    norm2_gain,
    w_gate,
    w_up,
    w_down,
    cotangent,
):
    token_rows, model_width = tokens.shape
    groups = lax.axis_size("head")
    head_count = forget_bias.shape[0]
    local_heads = head_count // groups
    local_width = model_width // groups
    hidden_width = w_gate.shape[1] // groups
    rows = token_rows * groups
    share = w_query.shape[0]
    group = lax.axis_index("head")

    low = lambda array: array.astype(bf16)
    spread = lambda gain: jnp.broadcast_to(low(gain)[:, None, None], (share, groups, 1))
    forget_low = low(w_forget).reshape(share, groups, local_heads)
    rest = LANES - local_heads - 2
    small = jnp.concatenate(
        [forget_low, spread(norm1_gain), spread(norm2_gain), jnp.zeros((share, groups, rest), bf16)],
        axis=2,
    )
    pack = jnp.concatenate(
        [
            low(piece).reshape(share, groups, -1)
            for piece in (w_key, w_value, small, w_query, w_gate_out, w_output)
        ],
        axis=2,
    )
    first, tokens_all, cotangent_all = gather_first(
        jnp.swapaxes(pack, 0, 1), tokens, cotangent, 0
    )
    kv_width = 2 * local_width + LANES
    output_weight = first[:, kv_width + 2 * local_width :]

    segment_plus = segment + 1
    earlier_segment = passed_along(segment_plus, "blk", 1)
    window = jnp.concatenate([earlier_segment, segment_plus])
    begins = jnp.sum(
        (window[:, None] < segment_plus[None, :]).astype(jnp.int32), axis=0
    )
    tiles = begins.reshape(rows // Q_TILE, Q_TILE)
    ranges = jnp.stack([tiles[:, 0] // K_TILE, (tiles[:, -1] + K_TILE - 1) // K_TILE])
    begins = jnp.broadcast_to(begins[None, :], (8, rows))

    def gain_rows(column):
        gain = first[:, 2 * local_width + local_heads + column].astype(f32)
        return jnp.broadcast_to(gain[None, :], (8, model_width))

    gain1, gain2 = gain_rows(0), gain_rows(1)
    wide_all = tokens_all.astype(f32)
    input1 = (wide_all * inverse_rms(wide_all) * gain1[0:1]).astype(bf16)
    key_value = dot(input1, first[:, : 2 * local_width]).astype(bf16)
    earlier_kv = passed_along(key_value, "blk", 1)
    bias = lax.dynamic_slice_in_dim(forget_bias, group * local_heads, local_heads, 0)
    bias = jnp.pad(bias, (0, LANES - local_heads))
    forget = dot(input1, first[:, 2 * local_width : kv_width]) + bias[None, :]
    forget = forget.astype(bf16).astype(f32)
    terms, halo_terms = decay_terms(jax.nn.log_sigmoid(forget), local_heads)
    earlier_terms = passed_along(halo_terms, "blk", 1)
    query = dot(input1, first[:, kv_width : kv_width + local_width]).astype(bf16)
    gate_raw = dot(
        input1, first[:, kv_width + local_width : kv_width + 2 * local_width]
    )

    so_far = attend(True, ranges, query, key_value, terms, terms, begins, local_heads)
    mine = sent_columns([low(w_gate), low(w_up), low(w_down)], groups)
    mine, earlier_kv, so_far = lax.optimization_barrier((mine, earlier_kv, so_far))
    second = all_rows(mine)
    attended, lse = attend(
        False, ranges, query, earlier_kv, terms, earlier_terms, begins, local_heads, so_far
    )
    opened = jax.nn.sigmoid(gate_raw)
    attended_wide = attended.astype(f32)
    gated = (opened * attended_wide).astype(bf16)
    branch = dot(gated, output_weight, NT).astype(bf16)
    middle, input2 = exchange(after_attention, branch, [tokens, gain2], 1, "exchange_middle")
    gate_act = dot(input2, second[:, :hidden_width])
    up_act = dot(input2, second[:, hidden_width : 2 * hidden_width])
    opening = jax.nn.sigmoid(gate_act)
    hidden = (gate_act * opening * up_act).astype(bf16)
    down = dot(hidden, second[:, 2 * hidden_width :], NT).astype(bf16)
    grad_hidden = dot(cotangent_all, second[:, 2 * hidden_width :])
    grad_gate_act = (grad_hidden * up_act * opening * (1.0 + gate_act * (1.0 - opening))).astype(
        bf16
    )
    grad_up_act = (grad_hidden * gate_act * opening).astype(bf16)
    grad_act = jnp.concatenate([grad_gate_act, grad_up_act], axis=1)
    grad_input2 = dot(grad_act, second[:, : 2 * hidden_width], NT).astype(bf16)
    second_grad = jnp.concatenate(
        [over_tokens(input2, grad_act).astype(bf16), over_tokens(cotangent_all, hidden).astype(bf16)],
        axis=1,
    )
    second_grad, grad_input2 = lax.optimization_barrier((second_grad, grad_input2))
    second_part = row_sums(second_grad)
    grad_middle, grad_branch = exchange(
        after_hidden, grad_input2, [cotangent, middle, gain2], 2, "exchange_hidden"
    )

    grad_gated = dot(grad_branch, output_weight)
    grad_attended = (grad_gated * opened).astype(bf16)
    grad_gate_pre = (grad_gated * attended_wide * opened * (1.0 - opened)).astype(bf16)
    dq_prev, rows_prev, dkv_prev, decay_prev = attend_back(
        False, ranges, query, earlier_kv, terms, earlier_terms, begins, grad_attended, attended,
        lse, local_heads,
    )
    dkv_later = passed_along(dkv_prev, "blk", -1)
    decay_later = passed_along(decay_prev[:, :8], "blk", -1)
    decay_later = jnp.pad(decay_later, ((0, 0), (0, LANES - 8)))
    dq, dk_own, dv_own, decay_own = attend_back(
        True, ranges, query, key_value, terms, terms, begins, grad_attended, attended,
        lse, local_heads, (dq_prev, rows_prev),
    )
    dk = (dk_own + dkv_later[0].astype(f32)).astype(bf16)
    dv = (dv_own + dkv_later[1].astype(f32)).astype(bf16)
    logf_grad = decay_back(decay_own, decay_later)
    forget_grad = jnp.where(
        jnp.arange(LANES)[None, :] < local_heads, logf_grad * jax.nn.sigmoid(-forget), 0.0
    ).astype(bf16)
    grads = jnp.concatenate([dk, dv, forget_grad, dq], axis=1)
    first_grad = over_tokens(input1, grads)
    bias_part = jnp.sum(forget_grad.astype(f32), axis=0)
    row = jnp.arange(model_width)[:, None] % share
    column = jnp.arange(3 * local_width + LANES)[None, :]
    spread_bias = jnp.sum(
        jnp.where(row == jnp.arange(LANES)[None, :], bias_part[None, :], 0.0), axis=1, keepdims=True
    )
    first_grad = jnp.where(column == 2 * local_width + local_heads, spread_bias, first_grad)
    first_grad = jnp.concatenate(
        [
            first_grad.astype(bf16),
            over_tokens(input1, grad_gate_pre).astype(bf16),
            over_tokens(grad_branch, gated).astype(bf16),
        ],
        axis=1,
    )
    grad_input1 = (
        dot(grads, first[:, : kv_width + local_width], NT)
        + dot(
            grad_gate_pre, first[:, kv_width + local_width : kv_width + 2 * local_width], NT
        )
    ).astype(bf16)
    first_sum, tokens_grad, result = finish_last(
        first_grad, groups, grad_input1, down, grad_middle, tokens, gain1, middle, 3
    )
    first_sum = jnp.swapaxes(first_sum, 0, 1).astype(f32)
    second_sum = own_rows(second_part, groups)

    def columns(array, start, width):
        return array[:, :, start : start + width].reshape(share, groups * width)

    key_sum, value_sum = (columns(first_sum, n * local_width, local_width) for n in range(2))
    forget_sum = columns(first_sum, 2 * local_width, local_heads)
    bias_total = first_sum[:local_heads, :, 2 * local_width + local_heads].T.reshape(head_count)
    query_sum, gate_out_sum, output_total = (
        columns(first_sum, kv_width + n * local_width, local_width) for n in range(3)
    )
    gate_sum, up_sum, down_sum = (
        columns(second_sum, n * hidden_width, hidden_width) for n in range(3)
    )

    def along(weight, grad):
        return jnp.sum(low(weight).astype(f32) * grad, axis=1)

    gain1_total = (
        along(w_query, query_sum)
        + along(w_key, key_sum)
        + along(w_value, value_sum)
        + along(w_gate_out, gate_out_sum)
        + along(w_forget, forget_sum)
    ) / low(norm1_gain).astype(f32)
    gain2_total = (along(w_gate, gate_sum) + along(w_up, up_sum)) / low(norm2_gain).astype(f32)
    return (
        result,
        tokens_grad,
        gain1_total,
        query_sum,
        key_sum,
        value_sum,
        gate_out_sum,
        forget_sum,
        bias_total,
        output_total,
        gain2_total,
        gate_sum,
        up_sum,
        down_sum,
    )


def solution(mesh):
    both = ("blk", "head")
    matrix, vector = P(both, None), P(both)
    return jax.shard_map(
        body,
        mesh=mesh,
        in_specs=(
            matrix, P("blk"), vector, matrix, matrix, matrix, matrix, matrix, P(), matrix, vector,
            matrix, matrix, matrix, matrix,
        ),
        out_specs=(
            matrix, matrix, vector, matrix, matrix, matrix, matrix, matrix, P(), matrix, vector,
            matrix, matrix, matrix,
        ),
        check_vma=False,
    )
```

profile of v0, /device:TPU:0, one launch (start us, length us, event | category | flops | bytes accessed | tf_op | source)
XLA Modules:
  0.0 913.3 jit_solution(5348872099380157858)
XLA Ops:
  7.9 4.8 collective-permute-start
  21.2 95.7 %gather_first.1 = (bf16[8,4,48,2048]{3,2,1,0:T(8,128)(2,1)}, bf16[2048,1536]{1,0:T(8,128)(2,1)}, bf16[2048,1536]{1,0:T(8,128)(2,1)}) custom-call(bf16[4,48,2048]{2,1,0:T(8,128)(2,1)} %bitcast.123, bf16[512,1536]{1,0:T(8,128)(2,1)} %tokens_ref.3, bf16[512,1536]{1,0:T(8,128)(2,1)} %refs_1_.3), custom_call_target="tpu_custom_call" | custom-call | flops 70000001024 | bytes 30000000 | tf_op jit(solution)/shard_map/gather_first/pallas_call | solution.py:667
  124.8 10.1 %convolution_convert_fusion.5.k_ref.v_ref = bf16[2048,768]{1,0:T(8,128)(2,1)} fusion(bf16[2048,1536]{1,0:T(8,128)(2,1)S(1)} %fusion.2, bf16[1536,2048]{1,0:T(8,128)(2,1)} %bitcast.125), kind=kOutput, calls=%fused_computation.27 | convolution fusion | flops 4833411072 | bytes 11796480 | tf_op jit(solution)/shard_map/dot_general | solution.py:22
  146.1 7.7 convolution_convert_fusion.8.q_ref
  153.8 6.2 fusion.24
  168.4 45.4 %attend_own.1 = (f32[384,2048]{1,0:T(8,128)}, f32[24,2048]{1,0:T(8,128)}) custom-call(s32[2,4]{1,0:T(2,128)} %pad_add_fusion.1.ranges_ref, bf16[2048,384]{1,0:T(8,128)(2,1)} %convolution_convert_fusion.8.q_ref, bf16[2048,768]{1,0:T(8,128)(2,1)} %convolution_convert_fusion.5.k_ref.v_ref, bf16[2048,768]{1,0:T(8,128)(2,1)} %convolution_convert_fusion.5.k_ref.v_ref, ...), custom_call_target="tpu_custom_call" | custom-call | flops 40000000000 | bytes 12000000 | tf_op jit(solution)/shard_map/attend_own/pallas_call | solution.py:271
  214.9 8.3 collective-permute-start.2
  223.2 8.5 add_divide_fusion.1
  235.4 8.5 attend_prev.1
  243.8 9.2 %convolution_convert_fusion.1.refs_0_ = bf16[2048,1536]{1,0:T(8,128)(2,1)} fusion(bf16[1536,2048]{1,0:T(8,128)(2,1)} %bitcast.129, f32[2048,384]{1,0:T(8,128)} %add_divide_fusion.1, bf16[2048,384]{1,0:T(8,128)(2,1)} %get-tuple-element.53.o_ref), kind=kOutput, calls=%fused_computation.16 | convolution fusion | flops 2421424128 | bytes 12189696 | tf_op jit(solution)/shard_map/dot_general | solution.py:22
  253.6 79.4 %exchange_middle.1 = (f32[512,1536]{1,0:T(8,128)}, bf16[2048,1536]{1,0:T(8,128)(2,1)}) custom-call(bf16[2048,1536]{1,0:T(8,128)(2,1)} %convolution_convert_fusion.1.refs_0_, bf16[512,1536]{1,0:T(8,128)(2,1)} %tokens_ref.3, f32[8,1536]{1,0:T(8,128)} %broadcast_in_dim.50.refs_2_.refs_3_), custom_call_target="tpu_custom_call" | custom-call | flops 70000001024 | bytes 16000000 | tf_op jit(solution)/shard_map/exchange_middle/pallas_call | solution.py:791
  333.0 48.0 %all-gather.2.cloned.1.call-done = bf16[1536,3072]{1,0:T(8,128)(2,1)} async-done(((bf16[192,3072]{1,0:T(8,128)(2,1)}), bf16[1536,3072]{1,0:T(8,128)(2,1)}) %all-gather.2.cloned.1.call-update) | async-done | bytes 9437200 | tf_op jit(solution)/shard_map/all_gather | solution.py:990
  381.0 11.8 %fusion.13 = f32[2048,1024]{0,1:T(8,128)} fusion(bf16[2048,1536]{1,0:T(8,128)(2,1)} %get-tuple-element.54, bf16[1536,3072]{1,0:T(8,128)(2,1)} %all-gather.2.cloned.1.call-done), kind=kOutput, calls=%fused_computation.34 | convolution fusion | flops 6442450944 | bytes 17825792 | tf_op jit(solution)/shard_map/dot_general | solution.py:22
  392.9 12.0 %fusion.18 = f32[2048,1024]{0,1:T(8,128)} fusion(bf16[2048,1536]{1,0:T(8,128)(2,1)} %get-tuple-element.55, bf16[1536,3072]{1,0:T(8,128)(2,1)} %all-gather.2.cloned.1.call-done), kind=kOutput, calls=%fused_computation.47 | convolution fusion | flops 6442450944 | bytes 17825792 | tf_op jit(solution)/shard_map/dot_general | solution.py:22
  404.9 19.8 %multiply_convert_fusion.2 = (bf16[2048,1024]{0,1:T(8,128)(2,1)}, bf16[2048,1024]{0,1:T(8,128)(2,1)}, bf16[2048,1024]{0,1:T(8,128)(2,1)}) fusion(f32[2048,1024]{0,1:T(8,128)} %fusion.18, f32[2048,1024]{0,1:T(8,128)} %fusion.13, bf16[2048,1536]{1,0:T(8,128)(2,1)} %get-tuple-element.54, bf16[1536,3072]{1,0:T(8,128)(2,1)} %all-gather.2.cloned.1.call-done), kind=kOutput, calls=%fused_computation.12 | convolution fusion | flops 6476005376 | bytes 38797312 | tf_op jit(solution)/shard_map/dot_general | solution.py:22
  424.7 10.4 %convolution_convert_fusion.4 = bf16[1536,1024]{1,0:T(8,128)(2,1)S(1)} fusion(bf16[2048,1536]{1,0:T(8,128)(2,1)} %get-tuple-element.55, bf16[2048,1024]{0,1:T(8,128)(2,1)} %get-tuple-element.80), kind=kOutput, calls=%fused_computation.26 | convolution fusion | flops 6444023808 | bytes 13631488 | tf_op jit(solution)/shard_map/dot_general | solution.py:976
  435.2 16.6 %convolution_convert_fusion.3 = bf16[1536,2048]{1,0:T(8,128)(2,1)S(1)} fusion(bf16[2048,1536]{1,0:T(8,128)(2,1)} %get-tuple-element.54, bf16[2048,1024]{0,1:T(8,128)(2,1)} %get-tuple-element.79, bf16[2048,1024]{0,1:T(8,128)(2,1)S(1)} %copy-done.37), kind=kOutput, calls=%fused_computation.18 | convolution fusion | flops 12904824832 | bytes 20971520 | tf_op jit(solution)/shard_map/dot_general | solution.py:976
  451.8 4.7 pad_maximum_fusion
  456.4 19.8 %convolution_convert_fusion.2.refs_0_ = bf16[2048,1536]{1,0:T(8,128)(2,1)} fusion(bf16[1536,3072]{1,0:T(8,128)(2,1)} %all-gather.2.cloned.1.call-done, bf16[2048,1024]{0,1:T(8,128)(2,1)} %get-tuple-element.79, bf16[2048,1024]{0,1:T(8,128)(2,1)} %get-tuple-element.78), kind=kOutput, calls=%fused_computation.17 | convolution fusion | flops 12904824832 | bytes 20971520 | tf_op jit(solution)/shard_map/dot_general | solution.py:22
  476.3 80.3 %exchange_hidden.1 = (f32[512,1536]{1,0:T(8,128)}, bf16[2048,1536]{1,0:T(8,128)(2,1)}) custom-call(bf16[2048,1536]{1,0:T(8,128)(2,1)} %convolution_convert_fusion.2.refs_0_, bf16[512,1536]{1,0:T(8,128)(2,1)} %refs_1_.3, f32[512,1536]{1,0:T(8,128)} %get-tuple-element.58.refs_2_.middle_ref, f32[8,1536]{1,0:T(8,128)} %broadcast_in_dim.50.refs_2_.refs_3_), custom_call_target="tpu_custom_call" | custom-call | flops 70000001024 | bytes 16000000 | tf_op jit(solution)/shard_map/exchange_hidden/pallas_call | solution.py:791
  556.6 9.0 multiply_convert_fusion.3
  565.6 11.0 %attend_back_prev.1 = (f32[2048,384]{1,0:T(8,128)}, f32[2048,128]{1,0:T(8,128)}, bf16[2,2048,384]{2,1,0:T(8,128)(2,1)}, f32[2048,128]{1,0:T(8,128)}) custom-call(s32[2,4]{1,0:T(2,128)} %pad_add_fusion.1.ranges_ref, bf16[2048,384]{1,0:T(8,128)(2,1)} %convolution_convert_fusion.8.q_ref, bf16[2048,768]{1,0:T(8,128)(2,1)} %collective-permute-done.1.k_ref.v_ref, ...), custom_call_target="tpu_custom_call" | custom-call | flops 15000000512 | bytes 25000000 | tf_op jit(solution)/shard_map/attend_back_prev/pallas_call | solution.py:432
  580.8 62.2 %attend_back_own.1 = (bf16[2048,384]{1,0:T(8,128)(2,1)}, f32[2048,384]{1,0:T(8,128)}, f32[2048,384]{1,0:T(8,128)}, f32[2048,128]{1,0:T(8,128)}) custom-call(s32[2,4]{1,0:T(2,128)} %pad_add_fusion.1.ranges_ref, bf16[2048,384]{1,0:T(8,128)(2,1)} %convolution_convert_fusion.8.q_ref, bf16[2048,768]{1,0:T(8,128)(2,1)} %convolution_convert_fusion.5.k_ref.v_ref, ...), custom_call_target="tpu_custom_call" | custom-call | flops 80000000000 | bytes 25000000 | tf_op jit(solution)/shard_map/attend_back_own/pallas_call | solution.py:432
  643.0 6.9 convolution_convert_fusion.6
  650.0 10.9 %convolution_convert_fusion.down_ref = bf16[2048,1536]{1,0:T(8,128)(2,1)} fusion(bf16[2048,1024]{0,1:T(8,128)(2,1)S(1)} %copy-done.36, bf16[1536,3072]{1,0:T(8,128)(2,1)} %all-gather.2.cloned.1.call-done), kind=kOutput, calls=%fused_computation.15 | convolution fusion | flops 6445596672 | bytes 13631488 | tf_op jit(solution)/shard_map/dot_general | solution.py:22
  664.6 18.5 %collective-permute-done.3 = f32[2048,8]{0,1:T(8,128)S(1)} collective-permute-done((f32[2048,8]{0,1:T(8,128)S(1)}, f32[2048,8]{0,1:T(8,128)S(1)}, u32[]{:S(2)}, u32[]{:S(2)}) %collective-permute-start.3) | collective-permute-done | bytes 65568 | tf_op jit(solution)/shard_map/ppermute | solution.py:28
  696.9 9.9 %fusion.3 = bf16[1536,1280]{0,1:T(8,128)(2,1)S(1)} fusion(bf16[2048,1536]{1,0:T(8,128)(2,1)S(1)} %bitcast.105, bf16[1536]{0:T(1024)(128)(2,1)S(1)} %select_reduce_fusion, pred[1280]{0:T(1024)(128)(4,1)S(1)} %copy-done.28, bf16[2048,384]{1,0:T(8,128)(2,1)S(1)} %copy-done.38, bf16[2048,128]{1,0:T(8,128)(2,1)S(1)} %get-tuple-element.77, ...), kind=kOutput, calls=%fused_computation.14 | convolution fusion | flops 8076001280 | bytes 15470848 | tf_op jit(solution)/shard_map/dot_general | solution.py:976
  709.9 9.1 copy.107
  719.1 11.8 %fusion.5 = f32[2048,1536]{1,0:T(8,128)S(1)} fusion(bf16[1536,2048]{1,0:T(8,128)(2,1)} %bitcast.131, bf16[2048,384]{1,0:T(8,128)(2,1)} %get-tuple-element.68, bf16[2048,128]{1,0:T(8,128)(2,1)} %copy-done.22, bf16[2048,384]{1,0:T(8,128)(2,1)S(1)} %copy-done.13, bf16[2048,384]{1,0:T(8,128)(2,1)S(1)} %copy-done.11), kind=kOutput, calls=%fused_computation.22 | convolution fusion | flops 8074035200 | bytes 21757952 | tf_op jit(solution)/shard_map/dot_general | solution.py:22
  730.9 6.6 add_convert_fusion.first_ref
  738.2 140.1 %finish_last.1 = (bf16[4,48,2048]{2,1,0:T(8,128)(2,1)}, f32[512,1536]{1,0:T(8,128)}, bf16[512,1536]{1,0:T(8,128)(2,1)}) custom-call(bf16[8,4,48,2048]{3,2,1,0:T(8,128)(2,1)} %bitcast.106, bf16[2048,1536]{1,0:T(8,128)(2,1)} %add_convert_fusion.first_ref, bf16[2048,1536]{1,0:T(8,128)(2,1)} %convolution_convert_fusion.down_ref, ...), custom_call_target="tpu_custom_call" | custom-call | flops 80000000000 | bytes 40000000 | tf_op jit(solution)/shard_map/finish_last/pallas_call | solution.py:912
  894.9 5.2 all-to-all-done.1
  (189 shorter events, 89.3 us)
Async XLA Ops:
  7.9 155.8 %collective-permute-start = (s32[2048]{0:T(1024)S(1)}, s32[2048]{0:T(1024)S(1)}, u32[]{:S(2)}, u32[]{:S(2)}) collective-permute-start(s32[2048]{0:T(1024)S(1)} %broadcast_add_fusion), channel_id=1, source_target_pairs={{0,4},{4,8},{8,12},{12,16},{16,20},{20,24},{24,28},{1,5},{5,9},{9,... | collective-permute-start | bytes 24584 | tf_op jit(solution)/shard_map/ppermute | solution.py:28
  124.7 10.1 %copy-start.1 = (bf16[2048,1536]{1,0:T(8,128)(2,1)}, bf16[2048,1536]{1,0:T(8,128)(2,1)S(1)}, u32[]{:S(2)}) copy-start(bf16[2048,1536]{1,0:T(8,128)(2,1)S(1)} %fusion.2) | copy-start | bytes 18874372
  124.7 14.6 %copy-start.6 = (f32[48,4096]{1,0:T(8,128)S(1)}, f32[48,4096]{1,0:T(8,128)}, u32[]{:S(2)}) copy-start(f32[48,4096]{1,0:T(8,128)} %param.26) | copy-start | bytes 2359300
  124.7 14.9 %copy-start.4 = (f32[48,4096]{1,0:T(8,128)S(1)}, f32[48,4096]{1,0:T(8,128)}, u32[]{:S(2)}) copy-start(f32[48,4096]{1,0:T(8,128)} %param.27) | copy-start | bytes 2359300
  124.8 15.2 %copy-start.21 = (f32[48,4096]{1,0:T(8,128)S(1)}, f32[48,4096]{1,0:T(8,128)}, u32[]{:S(2)}) copy-start(f32[48,4096]{1,0:T(8,128)} %param.28) | copy-start | bytes 2359300
  134.8 79.0 %collective-permute-start.1 = (bf16[2048,768]{1,0:T(8,128)(2,1)}, bf16[2048,768]{1,0:T(8,128)(2,1)}, u32[]{:S(2)}, u32[]{:S(2)}) collective-permute-start(bf16[2048,768]{1,0:T(8,128)(2,1)} %convolution_convert_fusion.5.k_ref.v_ref), channel_id=1, source_target_pairs={{0,4},{4,8},{8,12},{12,16},{16,20},{20,24},{24,28},{1,5},{5,9},{9,... | collective-permute-start | bytes 9437192 | tf_op jit(solution)/shard_map/ppermute | solution.py:28
  142.2 71.5 %all-to-all-start = ((bf16[48,4,3072]{2,0,1:T(8,128)(2,1)}), bf16[48,4,3072]{2,0,1:T(8,128)(2,1)S(1)}, u32[]{:S(2)}, u32[]{:S(2)}) async-start(bf16[48,4,3072]{2,0,1:T(8,128)(2,1)} %copy.102), calls=%async_computation | async-start | bytes 2359296 | tf_op jit(solution)/shard_map/all_to_all | solution.py:985
  145.8 235.2 %all-gather.2.cloned.1.call-start = ((), (), s32[]{:S(2)}) async-start(), calls=%async_computation.3 | async-start | bytes 10616832 | tf_op jit(solution)/shard_map/all_gather | solution.py:990
  168.4 46.5 %copy-start.33 = (bf16[2048,128]{1,0:T(8,128)(2,1)S(1)}, bf16[2048,128]{1,0:T(8,128)(2,1)}, u32[]{:S(2)}) copy-start(bf16[2048,128]{1,0:T(8,128)(2,1)} %get-tuple-element.50) | copy-start | bytes 1572868
  214.9 665.7 %reduce-scatter.2.cloned.1.call-start = ((), (), s32[]{:S(2)}) async-start(), calls=%async_computation.4 | async-start | bytes 10616832 | tf_op jit(solution)/shard_map/reduce_scatter | solution.py:994
  214.9 19.6 %collective-permute-start.2 = (bf16[2048,128]{1,0:T(8,128)(2,1)S(1)}, bf16[2048,128]{1,0:T(8,128)(2,1)S(1)}, u32[]{:S(2)}, u32[]{:S(2)}) collective-permute-start(bf16[2048,128]{1,0:T(8,128)(2,1)S(1)} %copy-done.33), channel_id=1, source_target_pairs={{0,4},{4,8},{8,12},{12,16},{16,20},{20,24},{24,28},{1,5},{5,9},{9,... | collective-permute-start | bytes 1572872 | tf_op jit(solution)/shard_map/ppermute | solution.py:28
  424.7 10.5 %copy-start.37 = (bf16[2048,1024]{0,1:T(8,128)(2,1)S(1)}, bf16[2048,1024]{0,1:T(8,128)(2,1)}, u32[]{:S(2)}) copy-start(bf16[2048,1024]{0,1:T(8,128)(2,1)} %get-tuple-element.78) | copy-start | bytes 12582916
  476.3 80.3 %copy-start.35 = (bf16[2048,384]{1,0:T(8,128)(2,1)S(1)}, bf16[2048,384]{1,0:T(8,128)(2,1)}, u32[]{:S(2)}) copy-start(bf16[2048,384]{1,0:T(8,128)(2,1)} %get-tuple-element.53.o_ref) | copy-start | bytes 4718596
  565.6 95.3 %copy-start.15 = (bf16[2048,384]{1,0:T(8,128)(2,1)}, bf16[2048,384]{1,0:T(8,128)(2,1)S(1)}, u32[]{:S(2)}) copy-start(bf16[2048,384]{1,0:T(8,128)(2,1)S(1)} %get-tuple-element.82) | copy-start | bytes 4718596
  576.6 114.8 %collective-permute-start.4 = (bf16[2,2048,384]{2,1,0:T(8,128)(2,1)}, bf16[2,2048,384]{2,1,0:T(8,128)(2,1)}, u32[]{:S(2)}, u32[]{:S(2)}) collective-permute-start(bf16[2,2048,384]{2,1,0:T(8,128)(2,1)} %get-tuple-element.66), channel_id=1, source_target_pairs={{4,0},{8,4},{12,8},{16,12},{20,16},{24,20},{28,24},{5,1},{9,5},{13... | collective-permute-start | bytes 9437192 | tf_op jit(solution)/shard_map/ppermute | solution.py:28
  579.5 103.7 %collective-permute-start.3 = (f32[2048,8]{0,1:T(8,128)S(1)}, f32[2048,8]{0,1:T(8,128)S(1)}, u32[]{:S(2)}, u32[]{:S(2)}) collective-permute-start(f32[2048,8]{0,1:T(8,128)S(1)} %copy.105), channel_id=1, source_target_pairs={{4,0},{8,4},{12,8},{16,12},{20,16},{24,20},{28,24},{5,1},{9,5},{13... | collective-permute-start | bytes 196616 | tf_op jit(solution)/shard_map/ppermute | solution.py:28
  643.0 17.9 %slice-start = ((s8[6291456]{0:T(1024)(128)(4,1)}), s8[4194304]{0:T(1024)(128)(4,1)S(1)}, s32[]{:S(2)}) async-start(s8[6291456]{0:T(1024)(128)(4,1)} %bitcast.102), calls=%async_computation.5 | async-start | bytes 8388608
  650.0 11.0 %slice-start.1 = ((s8[6291456]{0:T(1024)(128)(4,1)}), s8[2097152]{0:T(1024)(128)(4,1)S(1)}, s32[]{:S(2)}) async-start(s8[6291456]{0:T(1024)(128)(4,1)} %bitcast.102), calls=%async_computation.6 | async-start | bytes 4194304
  664.6 24.4 %copy-start.29 = (pred[128]{0:T(512)(128)(4,1)S(1)}, pred[128]{0:T(512)(128)(4,1)}, u32[]{:S(2)}) copy-start(pred[128]{0:T(512)(128)(4,1)} %iota_compare_fusion.2) | copy-start | bytes 388
  664.6 26.3 %copy-start.27 = (s32[1536]{0:T(1024)S(1)}, s32[1536]{0:T(1024)}, u32[]{:S(2)}) copy-start(s32[1536]{0:T(1024)} %add_select_fusion) | copy-start | bytes 18436
  684.6 11.5 %slice-start.2 = ((s8[6291456]{0:T(1024)(128)(4,1)}), s8[2097152]{0:T(1024)(128)(4,1)S(1)}, s32[]{:S(2)}) async-start(s8[6291456]{0:T(1024)(128)(4,1)} %bitcast.104), calls=%async_computation.7 | async-start | bytes 4194304
  696.0 10.8 %copy-start.10 = (bf16[2048,384]{1,0:T(8,128)(2,1)}, bf16[2048,384]{1,0:T(8,128)(2,1)S(1)}, u32[]{:S(2)}) copy-start(bf16[2048,384]{1,0:T(8,128)(2,1)S(1)} %get-tuple-element.85) | copy-start | bytes 4718596
  696.0 10.8 %copy-start.12 = (bf16[2048,384]{1,0:T(8,128)(2,1)}, bf16[2048,384]{1,0:T(8,128)(2,1)S(1)}, u32[]{:S(2)}) copy-start(bf16[2048,384]{1,0:T(8,128)(2,1)S(1)} %get-tuple-element.86) | copy-start | bytes 4718596
  696.9 10.0 %copy-start.17 = (bf16[1536,384]{0,1:T(8,128)(2,1)S(1)}, bf16[1536,384]{0,1:T(8,128)(2,1)}, u32[]{:S(2)}) copy-start(bf16[1536,384]{0,1:T(8,128)(2,1)} %convolution_convert_fusion.7) | copy-start | bytes 3538948
  709.9 9.1 %copy-start.13 = (bf16[2048,384]{1,0:T(8,128)(2,1)S(1)}, bf16[2048,384]{1,0:T(8,128)(2,1)}, u32[]{:S(2)}) copy-start(bf16[2048,384]{1,0:T(8,128)(2,1)} %copy-done.12) | copy-start | bytes 4718596
  719.1 11.8 %copy-start.16 = (bf16[2048,384]{1,0:T(8,128)(2,1)S(1)}, bf16[2048,384]{1,0:T(8,128)(2,1)}, u32[]{:S(2)}) copy-start(bf16[2048,384]{1,0:T(8,128)(2,1)} %copy-done.15) | copy-start | bytes 4718596
  878.3 11.4 %copy-start.26 = (f32[48,24]{0,1:T(8,128)S(1)}, f32[48,24]{0,1:T(8,128)}, u32[]{:S(2)}) copy-start(f32[48,24]{0,1:T(8,128)} %param.22) | copy-start | bytes 13828
  879.6 14.7 %copy-start.30 = (f32[48]{0:T(128)S(1)}, f32[48]{0:T(128)}, u32[]{:S(2)}) copy-start(f32[48]{0:T(128)} %param.17) | copy-start | bytes 580
  880.6 19.5 %all-to-all-start.1 = ((bf16[4,48,3072]{2,1,0:T(8,128)(2,1)}), bf16[4,48,3072]{2,1,0:T(8,128)(2,1)S(1)}, u32[]{:S(2)}, u32[]{:S(2)}) async-start(bf16[4,48,3072]{2,1,0:T(8,128)(2,1)} %bitcast.112), calls=%async_computation.2 | async-start | bytes 2359296 | tf_op jit(solution)/shard_map/all_to_all | solution.py:999
  885.3 15.4 %copy-start.18 = (f32[4,6,8,384]{3,2,0,1:T(8,128)}, f32[4,6,8,384]{3,2,0,1:T(8,128)S(1)}, u32[]{:S(2)}) copy-start(f32[4,6,8,384]{3,2,0,1:T(8,128)S(1)} %copy.128) | copy-start | bytes 884740
  886.4 14.3 %copy-start.19 = (f32[4,6,8,384]{3,2,0,1:T(8,128)}, f32[4,6,8,384]{3,2,0,1:T(8,128)S(1)}, u32[]{:S(2)}) copy-start(f32[4,6,8,384]{3,2,0,1:T(8,128)S(1)} %copy.127) | copy-start | bytes 884740
  888.4 12.3 %copy-start.25 = (f32[48,24]{0,1:T(8,128)}, f32[48,24]{0,1:T(8,128)S(1)}, u32[]{:S(2)}) copy-start(f32[48,24]{0,1:T(8,128)S(1)} %reshape.310) | copy-start | bytes 13828
  (20 other events, 93.6 us)
Sparse Core Ops, SparseCore 0:
  215.0 165.9 all-gather.1
  476.4 188.5 reduce-scatter.1
where the time goes:
time: 929 us; the launch traced here: 913 us
  Pallas kernels  531 us (57%)
  matrix products  191 us (21%)
  waiting for transfers between devices  72.8 us (8%)
  other arithmetic  42.1 us (5%)
  local copies, waits for them, and re-layouts  33.8 us (4%)
  starting transfers between devices  27.6 us (3%)
  between operations  15.4 us (2%)
    pallas_call x2, Pallas kernels, exchange(): pl.pallas_call(functools.partial(exchange_kernel, local, len(extras)), in...  160 us
    dot_general x13, matrix products, dot(): return lax.dot_general(a, b, dims, preferred_element_type=f32, **kw)  143 us
    pallas_call x1, Pallas kernels, finish_last(): pl.pallas_call(finish_last_kernel, in_specs=[vmem] * 7, out_specs=[vmem]...  140 us
    pallas_call x1, Pallas kernels, gather_first(): pl.pallas_call(gather_first_kernel, in_specs=[vmem] * 3, out_specs=[anywh...  95.7 us
    pallas_call x2, Pallas kernels, attend_back(): pl.pallas_call(functools.partial(attend_back_kernel, local_heads, own), g...  73.3 us
    pallas_call x2, Pallas kernels, attend(): pl.pallas_call(functools.partial(attend_kernel, local_heads, own), grid_s...  53.9 us
    all_gather x1, waiting for transfers between devices, all_rows(): return lax.all_gather(mine, 'blk', axis=0, tiled=True)  48 us
    dot_general x5, matrix products, over_tokens(): lax.dot_general(operand, other_side, (((0,), (0,)), ((), ())), preferred_...  47.6 us
  transfers between devices with their start and end apart: 9, of which 4 were waited for; matrix products, arithmetic and copies ran while one was open for 18% of the time, Pallas kernels for 58%

commit v1 on v0

--- a/solution.py
+++ b/solution.py
@@ -10,7 +10,7 @@
 epsilon = 1e-06
 LANES = 128
 Q_TILE = 512
-K_TILE = 256
+K_TILE = 512
 FAR = -1e30
 NT = (((1,), (1,)), ((), ()))
 NN = (((1,), (0,)), ((), ()))
@@ -255,6 +255,10 @@
     return pl.BlockSpec((height, rows), lambda p, *_: (p, 0))
 
 
+def terms_block(own, rows, pairs):
+    return pl.BlockSpec((rows, LANES), lambda p, *_: (0, 0 if own else 2 * pairs))
+
+
 def attend(own, ranges, query, key_value, terms, key_terms, begins, local_heads, so_far=()):
     rows = query.shape[0]
     pairs = local_heads // 2
@@ -278,7 +282,7 @@
                 lane_block(rows, 0),
                 lane_block(rows, pairs),
                 fixed((rows, LANES)),
-                fixed((rows, LANES)),
+                terms_block(own, rows, pairs),
                 fixed((8, rows)),
             ]
             + ([] if own else running_specs),
@@ -439,7 +443,7 @@
                 lane_block(rows, 0),
                 lane_block(rows, pairs),
                 fixed((rows, LANES)),
-                fixed((rows, LANES)),
+                terms_block(own, rows, pairs),
                 fixed((8, rows)),
                 lane_block(rows, 0),
                 lane_block(rows, 0),
@@ -569,21 +573,102 @@
     low, high = here % 2, here // 2
     partner = here + 1 - 2 * low
     after = [((high + t) % half) * 2 + low for t in range(half)]
-    before = [((high + half - t) % half) * 2 + low for t in range(half)]
-    return here, partner, after, before
+    return here, partner, after
+
+
+class Line:
+    def __init__(self, block_of, kinds, sems):
+        self.block_of, self.kinds = block_of, kinds
+        self.pair_send, self.pair_recv, self.up_send, self.up_recv, self.down_send, self.down_recv = sems
+        here = lax.axis_index("blk")
+        self.half = lax.axis_size("blk") // 2
+        self.low, self.high = here % 2, here // 2
+        self.partner = here + 1 - 2 * self.low
+        self.has_up, self.has_down = self.high < self.half - 1, self.high > 0
+
+    def greet(self, others):
+        greet_sum = len(others) + 1
+        for other in others + [on_blk(self.partner)]:
+            signal(other)
+        pl.when(self.has_up)(lambda: signal(on_blk(self.at(self.high + 1))))
+        pl.when(self.has_down)(lambda: signal(on_blk(self.at(self.high - 1))))
+        ends = (self.high == 0).astype(jnp.int32) + (self.high == self.half - 1).astype(jnp.int32)
+        pl.semaphore_wait(pltpu.get_barrier_semaphore(), greet_sum + 2 - ends)
+
+    def at(self, high):
+        return high * 2 + self.low
+
+    def pair_copy(self, kind, high, low):
+        block = self.block_of(kind, high * 2 + low)
+        return remote(
+            block, block, self.pair_send.at[kind, high], self.pair_recv.at[kind, high],
+            on_blk(self.partner),
+        )
+
+    def up_copy(self, kind, high):
+        block = self.block_of(kind, self.at(high))
+        return remote(
+            block, block, self.up_send.at[kind, high], self.up_recv.at[kind, high],
+            on_blk(self.at(jnp.minimum(self.high + 1, self.half - 1))),
+        )
+
+    def down_copy(self, kind, high):
+        block = self.block_of(kind, self.at(high))
+        return remote(
+            block, block, self.down_send.at[kind, high], self.down_recv.at[kind, high],
+            on_blk(self.at(jnp.maximum(self.high - 1, 0))),
+        )
+
+    def launch(self, kind):
+        self.pair_copy(kind, self.high, self.low).start()
+        pl.when(self.has_up)(lambda: self.up_copy(kind, self.high).start())
+        pl.when(self.has_down)(lambda: self.down_copy(kind, self.high).start())
+
+    def step(self, t):
+        for kind in range(self.kinds):
+            below, above = self.high - t, self.high + t
+
+            @pl.when(below >= 0)
+            def _():
+                self.up_copy(kind, below).wait_recv()
+                self.pair_copy(kind, below, self.low).start()
+                pl.when(self.has_up)(lambda: self.up_copy(kind, below).start())
+
+            @pl.when(above < self.half)
+            def _():
+                self.down_copy(kind, above).wait_recv()
+                self.pair_copy(kind, above, self.low).start()
+                pl.when(self.has_down)(lambda: self.down_copy(kind, above).start())
+
+    def finish(self):
+        for kind in range(self.kinds):
+
+            def wait(high, carry):
+                self.pair_copy(kind, high, self.low).wait_send()
+                self.pair_copy(kind, high, 1 - self.low).wait_recv()
+
+                @pl.when((high <= self.high) & self.has_up)
+                def _():
+                    self.up_copy(kind, high).wait_send()
+
+                @pl.when((high >= self.high) & self.has_down)
+                def _():
+                    self.down_copy(kind, high).wait_send()
+
+                return carry
+
+            lax.fori_loop(0, self.half, wait, 0)
 
 
 def gather_first_kernel(pack_ref, tokens_ref, cotangent_ref, pack_all, tokens_all, cotangent_all,
                         *sems):
-    (swap_send, swap_recv, swap_own, line_send, line_recv, pair_send, pair_recv) = sems[:7]
-    token_sems, cotangent_sems = sems[7:14], sems[14:21]
+    swap_send, swap_recv, swap_own = sems[:3]
+    token_sems, cotangent_sems = sems[9:16], sems[16:23]
     me, near, far, cross = partners()
-    here, partner, after, before = blk_peers()
-    steps = len(after)
-    greet(
-        [on_head(near), on_head(far), on_head(cross), on_blk(partner)]
-        + [on_blk(peer) for peer in after[1:]]
-    )
+    sources = (me, near, far, cross)
+    line = Line(lambda kind, blk: pack_all.at[blk, sources[kind]], 4, sems[3:9])
+    here = lax.axis_index("blk")
+    line.greet([on_head(near), on_head(far), on_head(cross)])
     swaps = [pltpu.make_async_copy(pack_ref.at[me], pack_all.at[here, me], swap_own)]
     for kind, other in enumerate((near, far, cross)):
         swaps.append(
@@ -607,53 +692,22 @@
         ]
 
     tokens_sent = spread_all(tokens_ref, tokens_all, token_sems)
-    sources = (me, near, far, cross)
-    waiting = []
-    for kind, source in enumerate(sources):
+    swaps[0].wait()
+    line.launch(0)
+    for kind, source in enumerate((near, far, cross)):
         block = pack_all.at[here, source]
-        if kind == 0:
-            swaps[0].wait()
-        else:
-            remote(
-                block, block, swap_send.at[kind - 1], swap_recv.at[kind - 1], on_head(source)
-            ).wait_recv()
-        for t in range(steps):
-            if t == 0:
-                copy = remote(
-                    block, block, pair_send.at[kind, 0], pair_recv.at[kind, 0], on_blk(partner)
-                )
-            else:
-                copy = remote(
-                    block, block, line_send.at[kind, t], line_recv.at[kind, t], on_blk(after[t])
-                )
-            copy.start()
-            waiting.append(copy)
+        remote(
+            block, block, swap_send.at[kind], swap_recv.at[kind], on_head(source)
+        ).wait_recv()
+        line.launch(kind + 1)
     cotangent_sent = spread_all(cotangent_ref, cotangent_all, cotangent_sems)
-    finish_tokens = finish_cotangent = None
-    for t in range(1, steps):
-        for kind, source in enumerate(sources):
-            block = pack_all.at[before[t], source]
-            remote(
-                block, block, line_send.at[kind, t], line_recv.at[kind, t], on_blk(after[t])
-            ).wait_recv()
-            copy = remote(
-                block, block, pair_send.at[kind, t], pair_recv.at[kind, t], on_blk(partner)
-            )
-            copy.start()
-            waiting.append(copy)
-        if t == min(2, steps - 1):
-            finish_tokens = hand_on(tokens_all, size, token_sems, tokens_sent)
+    for t in range(1, line.half):
+        line.step(t)
+    finish_tokens = hand_on(tokens_all, size, token_sems, tokens_sent)
     finish_cotangent = hand_on(cotangent_all, size, cotangent_sems, cotangent_sent)
     for swap in swaps[1:]:
         swap.wait_send()
-    for copy in waiting:
-        copy.wait_send()
-    for t in range(steps):
-        for kind, source in enumerate(sources):
-            block = pack_all.at[before[t] + partner - here, source]
-            remote(
-                block, block, pair_send.at[kind, t], pair_recv.at[kind, t], on_blk(partner)
-            ).wait_recv()
+    line.finish()
     finish_tokens()
     finish_cotangent()
 
@@ -674,7 +728,7 @@
             pltpu.SemaphoreType.DMA((3,)),
             pltpu.SemaphoreType.DMA,
         ]
-        + [pltpu.SemaphoreType.DMA((4, peers // 2)) for _ in range(4)]
+        + [pltpu.SemaphoreType.DMA((4, peers // 2)) for _ in range(6)]
         + gather_sems()
         + gather_sems(),
         compiler_params=pltpu.CompilerParams(collective_id=number, has_side_effects=True),
@@ -808,54 +862,61 @@
     )(part, *extras)
 
 
-def finish_last_kernel(grad_ref, first_ref, down_ref, grad_middle_ref, tokens_ref, gain_ref,
-                       middle_ref, weights_ref, tokens_grad_ref, result_ref, pair_buf, turn_buf,
-                       line_buf, row_buf, near1, turn1, far1, near2, turn2, far2, *sems):
-    pair_send, pair_recv, line_send, line_recv, swap_send, swap_recv = sems[:6]
+def finish_last_kernel(grad_ref, output_grad_ref, first_ref, down_ref, grad_middle_ref, tokens_ref,
+                       gain_ref, middle_ref, weights_ref, output_ref, tokens_grad_ref, result_ref,
+                       *refs):
+    buffers, (near1, turn1, far1, near2, turn2, far2) = refs[:8], refs[8:14]
+    sems = refs[14:]
     me, near, far, cross = partners()
-    here, partner, after, before = blk_peers()
+    here, partner, after = blk_peers()
     steps = len(after)
-    groups = grad_ref.shape[1]
     greet(
         [on_head(near), on_head(far), on_head(cross), on_blk(partner)]
         + [on_blk(peer) for peer in after[1:]]
     )
     size = result_ref.shape[0]
-    first = Sum(first_ref, (near1, turn1, far1), sems[6:10], size)
-    down = Sum(down_ref, (near2, turn2, far2), sems[10:14], size)
+    first = Sum(first_ref, (near1, turn1, far1), sems[12:16], size)
+    down = Sum(down_ref, (near2, turn2, far2), sems[16:20], size)
+    sums = (
+        (grad_ref, weights_ref, buffers[:4], sems[:6]),
+        (output_grad_ref, output_ref, buffers[4:], sems[6:12]),
+    )
     first.start()
-    order = list(range(1, steps)) + [0]
-    pair_copies = {}
-    for t in order:
-        copy = remote(
-            grad_ref.at[after[t] + partner - here],
-            pair_buf.at[t],
-            pair_send.at[t],
-            pair_recv.at[t],
-            on_blk(partner),
-        )
-        copy.start()
-        pair_copies[t] = copy
+    sent = []
+    for t in list(range(1, steps)) + [0]:
+        for ref, _, (pair_buf, _, _, _), (pair_send, pair_recv, *_) in sums:
+            copy = remote(
+                ref.at[after[t] + partner - here],
+                pair_buf.at[t],
+                pair_send.at[t],
+                pair_recv.at[t],
+                on_blk(partner),
+            )
+            copy.start()
+            sent.append(copy)
     first.turn()
     down.start()
     down.turn()
-    line_copies = {}
-
-    def pass_on(t):
-        pair_copies[t].wait_recv()
-
-        def add(group, carry):
-            turn_buf[t, group] = (
-                grad_ref[after[t], group].astype(f32) + pair_buf[t, group].astype(f32)
-            ).astype(bf16)
-            return carry
-
-        lax.fori_loop(0, groups, add, 0)
-        copy = remote(
-            turn_buf.at[t], line_buf.at[t], line_send.at[t], line_recv.at[t], on_blk(after[t])
-        )
-        copy.start()
-        line_copies[t] = copy
+    lines = []
+    for t in range(1, steps):
+        for ref, _, (pair_buf, turn_buf, line_buf, _), some in sums:
+            pair_send, pair_recv, line_send, line_recv = some[:4]
+            remote(
+                pair_buf.at[t], pair_buf.at[t], pair_send.at[t], pair_recv.at[t], on_blk(partner)
+            ).wait_recv()
+
+            def add(group, carry):
+                turn_buf[t, group] = (
+                    ref[after[t], group].astype(f32) + pair_buf[t, group].astype(f32)
+                ).astype(bf16)
+                return carry
+
+            lax.fori_loop(0, ref.shape[1], add, 0)
+            copy = remote(
+                turn_buf.at[t], line_buf.at[t], line_send.at[t], line_recv.at[t], on_blk(after[t])
+            )
+            copy.start()
+            lines.append(copy)
 
     def put(shares, local, out_ref, extra_refs):
         for piece in range(PIECES):
@@ -863,67 +924,84 @@
             value, _ = local(shares.total(piece), rows, *extra_refs)
             out_ref[rows, :] = value.astype(out_ref.dtype)
 
-    for t in range(1, steps):
-        pass_on(t)
-        if t == min(2, steps - 1):
-            put(first, after_first, tokens_grad_ref, (grad_middle_ref, tokens_ref, gain_ref))
-    pair_copies[0].wait_recv()
-    for t in range(1, steps):
-        line_copies[t].wait_recv()
-
-    def add_all(group, carry):
-        total = grad_ref[here, group].astype(f32) + pair_buf[0, group].astype(f32)
+    put(first, after_first, tokens_grad_ref, (grad_middle_ref, tokens_ref, gain_ref))
+    swaps = []
+    for ref, out_ref, (pair_buf, _, line_buf, row_buf), some in sums:
+        pair_send, pair_recv, line_send, line_recv, swap_send, swap_recv = some
+        remote(
+            pair_buf.at[0], pair_buf.at[0], pair_send.at[0], pair_recv.at[0], on_blk(partner)
+        ).wait_recv()
         for t in range(1, steps):
-            total = total + line_buf[t, group].astype(f32)
-        row_buf[group] = total.astype(bf16)
-        return carry
-
-    lax.fori_loop(0, groups, add_all, 0)
-    swaps = []
-    for kind, other in enumerate((near, far, cross)):
-        copy = remote(
-            row_buf.at[other],
-            weights_ref.at[me],
-            swap_send.at[kind],
-            swap_recv.at[kind],
-            on_head(other),
-        )
-        copy.start()
-        swaps.append(copy)
-    weights_ref[me] = row_buf[me]
+            remote(
+                line_buf.at[t], line_buf.at[t], line_send.at[t], line_recv.at[t], on_blk(after[t])
+            ).wait_recv()
+
+        def add_all(group, carry):
+            total = ref[here, group].astype(f32) + pair_buf[0, group].astype(f32)
+            for t in range(1, steps):
+                total = total + line_buf[t, group].astype(f32)
+            row_buf[group] = total.astype(bf16)
+            return carry
+
+        lax.fori_loop(0, ref.shape[1], add_all, 0)
+        for kind, other in enumerate((near, far, cross)):
+            copy = remote(
+                row_buf.at[other],
+                out_ref.at[me],
+                swap_send.at[kind],
+                swap_recv.at[kind],
+                on_head(other),
+            )
+            copy.start()
+            swaps.append(copy)
+        out_ref[me] = row_buf[me]
     put(down, after_down, result_ref, (middle_ref,))
-    for kind, other in enumerate((near, far, cross)):
-        block = weights_ref.at[other]
-        remote(block, block, swap_send.at[kind], swap_recv.at[kind], on_head(other)).wait_recv()
-        swaps[kind].wait_send()
-    for copy in list(pair_copies.values()) + list(line_copies.values()):
+    for _, out_ref, _, some in sums:
+        for kind, other in enumerate((near, far, cross)):
+            block = out_ref.at[other]
+            remote(
+                block, block, some[4].at[kind], some[5].at[kind], on_head(other)
+            ).wait_recv()
+    for copy in sent + lines + swaps:
         copy.wait_send()
     first.finish()
     down.finish()
 
 
-def finish_last(grad, groups, part_first, part_down, grad_middle, tokens, gain, middle, number):
+def finish_last(grad, output_grad, groups, part_first, part_down, grad_middle, tokens, gain, middle,
+                number):
     peers = lax.axis_size("blk")
-    all_rows, columns = grad.shape
-    share = all_rows // (peers * groups)
+    share = grad.shape[0] // (peers * groups)
     rows, width = tokens.shape
     vmem = pl.BlockSpec(memory_space=pltpu.VMEM)
     half = peers // 2
+    widths = (grad.shape[1], output_grad.shape[1])
+
+    def blocks(columns):
+        return [pltpu.VMEM((half, groups, share, columns), bf16) for _ in range(3)] + [
+            pltpu.VMEM((groups, share, columns), bf16)
+        ]
+
+    swap_sems = [pltpu.SemaphoreType.DMA((half,)) for _ in range(4)] + [
+        pltpu.SemaphoreType.DMA((3,)) for _ in range(2)
+    ]
     return pl.pallas_call(
         finish_last_kernel,
-        in_specs=[vmem] * 7,
-        out_specs=[vmem] * 3,
+        in_specs=[vmem] * 8,
+        out_specs=[vmem] * 4,
         out_shape=[
-            jax.ShapeDtypeStruct((groups, share, columns), bf16),
+            jax.ShapeDtypeStruct((groups, share, columns), bf16) for columns in widths
+        ]
+        + [
             jax.ShapeDtypeStruct((rows, width), f32),
             jax.ShapeDtypeStruct((rows, width), bf16),
         ],
-        scratch_shapes=[pltpu.VMEM((half, groups, share, columns), bf16) for _ in range(3)]
-        + [pltpu.VMEM((groups, share, columns), bf16)]
+        scratch_shapes=blocks(widths[0])
+        + blocks(widths[1])
         + sum_buffers(rows, width)
         + sum_buffers(rows, width)
-        + [pltpu.SemaphoreType.DMA((half,)) for _ in range(4)]
-        + [pltpu.SemaphoreType.DMA((3,)) for _ in range(2)]
+        + swap_sems
+        + swap_sems
         + sum_sems()
         + sum_sems(),
         compiler_params=pltpu.CompilerParams(
@@ -934,8 +1012,9 @@
         ),
         name="finish_last",
     )(
-        grad.reshape(peers, groups, share, columns), part_first, part_down, grad_middle, tokens,
-        gain, middle,
+        grad.reshape(peers, groups, share, widths[0]),
+        output_grad.reshape(peers, groups, share, widths[1]),
+        part_first, part_down, grad_middle, tokens, gain, middle,
     )
 
 
@@ -970,6 +1049,101 @@
 
 def after_down(total, here, middle_ref):
     return middle_ref[here, :] + total, None
+
+
+FEED_TILE = 256
+FEED_COLUMNS = 512
+
+
+def feed_kernel(input_ref, cotangent_ref, weight_ref, down_ref, grad_input_ref, grad_ref, total,
+                down_sum, input_sum, turned):
+    step = pl.program_id(0)
+    width = input_ref.shape[1]
+    hidden_width = weight_ref.shape[1] // 3
+    inputs, cotangent = input_ref[...], cotangent_ref[...]
+    turned[0] = inputs.T
+    turned[1] = cotangent.T
+
+    def columns(which, n):
+        return pl.ds(pl.multiple_of(which * hidden_width + n * FEED_COLUMNS, FEED_COLUMNS), FEED_COLUMNS)
+
+    def chunk(n, carry):
+        gate_at, up_at, down_at = columns(0, n), columns(1, n), columns(2, n)
+        gate = dot(inputs, weight_ref[:, gate_at])
+        up = dot(inputs, weight_ref[:, up_at])
+        grad_hidden = dot(cotangent, weight_ref[:, down_at])
+        opening = jax.nn.sigmoid(gate)
+        active = gate * opening
+        hidden = (active * up).astype(bf16)
+        grad_gate = (grad_hidden * up * opening * (1.0 + gate * (1.0 - opening))).astype(bf16)
+        grad_up = (grad_hidden * active).astype(bf16)
+        down = dot(hidden, weight_ref[:, down_at], NT)
+        back = dot(grad_gate, weight_ref[:, gate_at], NT) + dot(grad_up, weight_ref[:, up_at], NT)
+
+        @pl.when(n == 0)
+        def _():
+            down_sum[...] = down
+            input_sum[...] = back
+
+        @pl.when(n > 0)
+        def _():
+            down_sum[...] += down
+            input_sum[...] += back
+
+        for at, side, grad in ((gate_at, 0, grad_gate), (up_at, 0, grad_up), (down_at, 1, hidden)):
+
+            @pl.when(step == 0)
+            def _():
+                total[:, at] = dot(turned[side], grad)
+
+            @pl.when(step > 0)
+            def _():
+                total[:, at] += dot(turned[side], grad)
+
+        return carry
+
+    lax.fori_loop(0, hidden_width // FEED_COLUMNS, chunk, 0)
+    down_ref[...] = down_sum[...].astype(bf16)
+    grad_input_ref[...] = input_sum[...].astype(bf16)
+
+    @pl.when(step == pl.num_programs(0) - 1)
+    def _():
+        def store(n, carry):
+            at = pl.ds(pl.multiple_of(n * 128, 128), 128)
+            grad_ref[at, :] = total[at, :].astype(bf16)
+            return carry
+
+        lax.fori_loop(0, width // 128, store, 0)
+
+
+def feed(inputs, cotangent, weight):
+    rows, width = inputs.shape
+    columns = weight.shape[1]
+    tile = pl.BlockSpec((FEED_TILE, width), lambda n: (n, 0))
+    whole = pl.BlockSpec((width, columns), lambda n: (0, 0), pipeline_mode=pl.Buffered(1))
+    return pl.pallas_call(
+        feed_kernel,
+        grid=(rows // FEED_TILE,),
+        in_specs=[tile, tile, whole],
+        out_specs=[tile, tile, whole],
+        out_shape=[
+            jax.ShapeDtypeStruct((rows, width), bf16),
+            jax.ShapeDtypeStruct((rows, width), bf16),
+            jax.ShapeDtypeStruct((width, columns), bf16),
+        ],
+        scratch_shapes=[
+            pltpu.VMEM((width, columns), f32),
+            pltpu.VMEM((FEED_TILE, width), f32),
+            pltpu.VMEM((FEED_TILE, width), f32),
+            pltpu.VMEM((2, width, FEED_TILE), bf16),
+        ],
+        compiler_params=pltpu.CompilerParams(vmem_limit_bytes=60 << 20),
+        cost_estimate=pl.CostEstimate(
+            flops=6 * rows * width * columns, transcendentals=rows * columns // 3,
+            bytes_accessed=45_000_000,
+        ),
+        name="feed",
+    )(inputs, cotangent, weight)
 
 
 def over_tokens(operand, other_side):
@@ -1066,15 +1240,16 @@
 
     gain1, gain2 = gain_rows(0), gain_rows(1)
     wide_all = tokens_all.astype(f32)
-    input1 = (wide_all * inverse_rms(wide_all) * gain1[0:1]).astype(bf16)
+    input1 = lax.optimization_barrier(
+        (wide_all * inverse_rms(wide_all) * gain1[0:1]).astype(bf16)
+    )
     key_value = dot(input1, first[:, : 2 * local_width]).astype(bf16)
-    earlier_kv = passed_along(key_value, "blk", 1)
     bias = lax.dynamic_slice_in_dim(forget_bias, group * local_heads, local_heads, 0)
     bias = jnp.pad(bias, (0, LANES - local_heads))
     forget = dot(input1, first[:, 2 * local_width : kv_width]) + bias[None, :]
     forget = forget.astype(bf16).astype(f32)
     terms, halo_terms = decay_terms(jax.nn.log_sigmoid(forget), local_heads)
-    earlier_terms = passed_along(halo_terms, "blk", 1)
+    earlier_kv = passed_along(jnp.concatenate([key_value, halo_terms], axis=1), "blk", 1)
     query = dot(input1, first[:, kv_width : kv_width + local_width]).astype(bf16)
     gate_raw = dot(
         input1, first[:, kv_width + local_width : kv_width + 2 * local_width]
@@ -1085,30 +1260,14 @@
     mine, earlier_kv, so_far = lax.optimization_barrier((mine, earlier_kv, so_far))
     second = all_rows(mine)
     attended, lse = attend(
-        False, ranges, query, earlier_kv, terms, earlier_terms, begins, local_heads, so_far
+        False, ranges, query, earlier_kv, terms, earlier_kv, begins, local_heads, so_far
     )
     opened = jax.nn.sigmoid(gate_raw)
     attended_wide = attended.astype(f32)
     gated = (opened * attended_wide).astype(bf16)
     branch = dot(gated, output_weight, NT).astype(bf16)
     middle, input2 = exchange(after_attention, branch, [tokens, gain2], 1, "exchange_middle")
-    gate_act = dot(input2, second[:, :hidden_width])
-    up_act = dot(input2, second[:, hidden_width : 2 * hidden_width])
-    opening = jax.nn.sigmoid(gate_act)
-    hidden = (gate_act * opening * up_act).astype(bf16)
-    down = dot(hidden, second[:, 2 * hidden_width :], NT).astype(bf16)
-    grad_hidden = dot(cotangent_all, second[:, 2 * hidden_width :])
-    grad_gate_act = (grad_hidden * up_act * opening * (1.0 + gate_act * (1.0 - opening))).astype(
-        bf16
-    )
-    grad_up_act = (grad_hidden * gate_act * opening).astype(bf16)
-    grad_act = jnp.concatenate([grad_gate_act, grad_up_act], axis=1)
-    grad_input2 = dot(grad_act, second[:, : 2 * hidden_width], NT).astype(bf16)
-    second_grad = jnp.concatenate(
-        [over_tokens(input2, grad_act).astype(bf16), over_tokens(cotangent_all, hidden).astype(bf16)],
-        axis=1,
-    )
-    second_grad, grad_input2 = lax.optimization_barrier((second_grad, grad_input2))
+    down, grad_input2, second_grad = feed(input2, cotangent_all, second)
     second_part = row_sums(second_grad)
     grad_middle, grad_branch = exchange(
         after_hidden, grad_input2, [cotangent, middle, gain2], 2, "exchange_hidden"
@@ -1118,7 +1277,7 @@
     grad_attended = (grad_gated * opened).astype(bf16)
     grad_gate_pre = (grad_gated * attended_wide * opened * (1.0 - opened)).astype(bf16)
     dq_prev, rows_prev, dkv_prev, decay_prev = attend_back(
-        False, ranges, query, earlier_kv, terms, earlier_terms, begins, grad_attended, attended,
+        False, ranges, query, earlier_kv, terms, earlier_kv, begins, grad_attended, attended,
         lse, local_heads,
     )
     dkv_later = passed_along(dkv_prev, "blk", -1)
@@ -1134,34 +1293,26 @@
     forget_grad = jnp.where(
         jnp.arange(LANES)[None, :] < local_heads, logf_grad * jax.nn.sigmoid(-forget), 0.0
     ).astype(bf16)
-    grads = jnp.concatenate([dk, dv, forget_grad, dq], axis=1)
+    grads = jnp.concatenate([dk, dv, forget_grad, dq, grad_gate_pre], axis=1)
     first_grad = over_tokens(input1, grads)
     bias_part = jnp.sum(forget_grad.astype(f32), axis=0)
     row = jnp.arange(model_width)[:, None] % share
-    column = jnp.arange(3 * local_width + LANES)[None, :]
+    column = jnp.arange(kv_width + 2 * local_width)[None, :]
     spread_bias = jnp.sum(
         jnp.where(row == jnp.arange(LANES)[None, :], bias_part[None, :], 0.0), axis=1, keepdims=True
     )
-    first_grad = jnp.where(column == 2 * local_width + local_heads, spread_bias, first_grad)
-    first_grad = jnp.concatenate(
-        [
-            first_grad.astype(bf16),
-            over_tokens(input1, grad_gate_pre).astype(bf16),
-            over_tokens(grad_branch, gated).astype(bf16),
-        ],
-        axis=1,
-    )
-    grad_input1 = (
-        dot(grads, first[:, : kv_width + local_width], NT)
-        + dot(
-            grad_gate_pre, first[:, kv_width + local_width : kv_width + 2 * local_width], NT
-        )
+    first_grad = jnp.where(
+        column == 2 * local_width + local_heads, spread_bias, first_grad
     ).astype(bf16)
-    first_sum, tokens_grad, result = finish_last(
-        first_grad, groups, grad_input1, down, grad_middle, tokens, gain1, middle, 3
+    output_grad = over_tokens(grad_branch, gated).astype(bf16)
+    grad_input1 = dot(grads, first[:, : kv_width + 2 * local_width], NT).astype(bf16)
+    second_sum = own_rows(second_part, groups)
+    grad_input1, second_sum = lax.optimization_barrier((grad_input1, second_sum))
+    first_sum, output_sum, tokens_grad, result = finish_last(
+        first_grad, output_grad, groups, grad_input1, down, grad_middle, tokens, gain1, middle, 3
     )
     first_sum = jnp.swapaxes(first_sum, 0, 1).astype(f32)
-    second_sum = own_rows(second_part, groups)
+    output_sum = jnp.swapaxes(output_sum, 0, 1).astype(f32)
 
     def columns(array, start, width):
         return array[:, :, start : start + width].reshape(share, groups * width)
@@ -1169,9 +1320,10 @@
     key_sum, value_sum = (columns(first_sum, n * local_width, local_width) for n in range(2))
     forget_sum = columns(first_sum, 2 * local_width, local_heads)
     bias_total = first_sum[:local_heads, :, 2 * local_width + local_heads].T.reshape(head_count)
-    query_sum, gate_out_sum, output_total = (
-        columns(first_sum, kv_width + n * local_width, local_width) for n in range(3)
-    )
+    query_sum, gate_out_sum = (
+        columns(first_sum, kv_width + n * local_width, local_width) for n in range(2)
+    )
+    output_total = columns(output_sum, 0, local_width)
     gate_sum, up_sum, down_sum = (
         columns(second_sum, n * hidden_width, hidden_width) for n in range(3)
     )

time: 929 us -> 861 us (0.927)
  matrix products: 191 us -> 83.1 us
  Pallas kernels: 531 us -> 596 us
    dot_general x13 -> x7, matrix products: 143 us -> 61.4 us  [dot(): return lax.dot_general(a, b, dims, preferred_element_type=f32, **kw)]
    pallas_call x1 -> x2, Pallas kernels: 140 us -> 221 us  [the longest x1 131 us: finish_last(): pl.pallas_call(finish_last_kernel, in_specs=[vmem] * 8, out_specs=[vmem]...]
    dot_general x5 -> x2, matrix products: 47.6 us -> 21.7 us  [over_tokens(): lax.dot_general(operand, other_side, (((0,), (0,)), ((), ())), preferred_...]
    ppermute x5 -> x4, waiting for transfers between devices: 19.5 us -> 40.3 us  [passed_along(): return lax.ppermute(array, axis, pairs)]
    all_gather x1, waiting for transfers between devices: 48 us -> 34.6 us  [all_rows(): return lax.all_gather(mine, 'blk', axis=0, tiled=True)]
    pallas_call x1, Pallas kernels: 95.7 us -> 84.4 us  [gather_first(): pl.pallas_call(gather_first_kernel, in_specs=[vmem] * 3, out_specs=[anywh...]
    concatenate x2 -> x0, local copies, waits for them, and re-layouts: 10.5 us -> none  [the longest x1 9.12 us: body(): jnp.concatenate([first_grad.astype(bf16), over_tokens(input1, grad_gate_p...]
    ppermute x5 -> x4, starting transfers between devices: 20.2 us -> 12.6 us  [passed_along(): return lax.ppermute(array, axis, pairs)]
  transfers between devices with their start and end apart: 9 -> 8, of which waited for: 4 -> 3; matrix products, arithmetic and copies ran while one was open for 18% -> 15% of each run, Pallas kernels for 58% -> 44%
where the time goes in v1:
time: 861 us; the launch traced here: 851 us
  Pallas kernels  596 us (69%)
  matrix products  83.1 us (10%)
  waiting for transfers between devices  74.9 us (9%)
  other arithmetic  37 us (4%)
  local copies, waits for them, and re-layouts  24.7 us (3%)
  starting transfers between devices  20.4 us (2%)
  between operations  15.2 us (2%)
    pallas_call x2, Pallas kernels, exchange(): pl.pallas_call(functools.partial(exchange_kernel, local, len(extras)), in...  160 us
    pallas_call x1, Pallas kernels, finish_last(): pl.pallas_call(finish_last_kernel, in_specs=[vmem] * 8, out_specs=[vmem]...  131 us
    pallas_call x1, Pallas kernels, feed(): pl.pallas_call(feed_kernel, grid=(rows // FEED_TILE,), in_specs=[tile, ti...  90.3 us
    pallas_call x1, Pallas kernels, gather_first(): pl.pallas_call(gather_first_kernel, in_specs=[vmem] * 3, out_specs=[anywh...  84.4 us
    pallas_call x2, Pallas kernels, attend_back(): pl.pallas_call(functools.partial(attend_back_kernel, local_heads, own), g...  72.5 us
    dot_general x7, matrix products, dot(): return lax.dot_general(a, b, dims, preferred_element_type=f32, **kw)  61.4 us
    pallas_call x2, Pallas kernels, attend(): pl.pallas_call(functools.partial(attend_kernel, local_heads, own), grid_s...  50 us
    ppermute x4, waiting for transfers between devices, passed_along(): return lax.ppermute(array, axis, pairs)  40.3 us
  transfers between devices with their start and end apart: 8, of which 3 were waited for; matrix products, arithmetic and copies ran while one was open for 15% of the time, Pallas kernels for 44%

profile of v1, /device:TPU:0, one launch (start us, length us, event | category | flops | bytes accessed | tf_op | source)
XLA Modules:
  0.0 851.5 jit_solution(5896931625254915174)
XLA Ops:
  7.9 4.8 collective-permute-start
  21.2 84.4 %gather_first.1 = (bf16[8,4,48,2048]{3,2,1,0:T(8,128)(2,1)}, bf16[2048,1536]{1,0:T(8,128)(2,1)}, bf16[2048,1536]{1,0:T(8,128)(2,1)}) custom-call(bf16[4,48,2048]{2,1,0:T(8,128)(2,1)} %bitcast.128, bf16[512,1536]{1,0:T(8,128)(2,1)} %tokens_ref.3, bf16[512,1536]{1,0:T(8,128)(2,1)} %refs_1_.3), custom_call_target="tpu_custom_call" | custom-call | flops 70000001024 | bytes 30000000 | tf_op jit(solution)/shard_map/gather_first/pallas_call | solution.py:721
  107.3 4.2 fusion
  111.9 4.1 fusion.2
  116.0 7.8 convolution_convert_fusion.2.k_ref.v_ref
  124.6 6.4 fusion.18
  131.0 3.7 decay_terms.1
  134.7 3.3 pad_maximum_fusion
  138.0 5.2 collective-permute-start.1
  144.6 3.5 all-to-all-start
  148.4 7.7 convolution_convert_fusion.4.q_ref
  156.0 3.3 convert_reduce_fusion
  160.8 40.5 %attend_own.1 = (f32[384,2048]{1,0:T(8,128)}, f32[24,2048]{1,0:T(8,128)}) custom-call(s32[2,4]{1,0:T(2,128)} %pad_add_fusion.1.ranges_ref, bf16[2048,384]{1,0:T(8,128)(2,1)} %convolution_convert_fusion.4.q_ref, bf16[2048,768]{1,0:T(8,128)(2,1)} %copy-done.3, bf16[2048,768]{1,0:T(8,128)(2,1)} %copy-done.3, ...), custom_call_target="tpu_custom_call" | custom-call | flops 40000000000 | bytes 12000000 | tf_op jit(solution)/shard_map/attend_own/pallas_call | solution.py:275
  201.3 19.6 %collective-permute-done.1.k_ref.v_ref.t_key_ref = bf16[2048,896]{1,0:T(8,128)(2,1)} collective-permute-done((bf16[2048,896]{1,0:T(8,128)(2,1)}, bf16[2048,896]{1,0:T(8,128)(2,1)}, u32[]{:S(2)}, u32[]{:S(2)}) %collective-permute-start.1) | collective-permute-done | bytes 3670048 | tf_op jit(solution)/shard_map/ppermute | solution.py:28
  223.1 6.1 add_divide_fusion
  229.2 9.5 %attend_prev.1 = (bf16[2048,384]{1,0:T(8,128)(2,1)}, f32[24,2048]{1,0:T(8,128)}) custom-call(s32[2,4]{1,0:T(2,128)} %pad_add_fusion.1.ranges_ref, bf16[2048,384]{1,0:T(8,128)(2,1)} %convolution_convert_fusion.4.q_ref, bf16[2048,896]{1,0:T(8,128)(2,1)} %collective-permute-done.1.k_ref.v_ref.t_key_ref, ...), custom_call_target="tpu_custom_call" | custom-call | flops 10000000000 | bytes 12000000 | tf_op jit(solution)/shard_map/attend_prev/pallas_call | solution.py:275
  238.8 7.9 convolution_convert_fusion.refs_0_
  247.3 79.3 %exchange_middle.1 = (f32[512,1536]{1,0:T(8,128)}, bf16[2048,1536]{1,0:T(8,128)(2,1)}) custom-call(bf16[2048,1536]{1,0:T(8,128)(2,1)} %convolution_convert_fusion.refs_0_, bf16[512,1536]{1,0:T(8,128)(2,1)} %tokens_ref.3, f32[8,1536]{1,0:T(8,128)} %broadcast_in_dim.50.refs_2_.refs_3_), custom_call_target="tpu_custom_call" | custom-call | flops 70000001024 | bytes 16000000 | tf_op jit(solution)/shard_map/exchange_middle/pallas_call | solution.py:845
  326.5 34.6 %all-gather.2.cloned.1.call-done.weight_ref = bf16[1536,3072]{1,0:T(8,128)(2,1)} async-done(((bf16[192,3072]{1,0:T(8,128)(2,1)}), bf16[1536,3072]{1,0:T(8,128)(2,1)}) %all-gather.2.cloned.1.call-update) | async-done | bytes 9437200 | tf_op jit(solution)/shard_map/all_gather | solution.py:1164
  361.1 90.3 %feed.1 = (bf16[2048,1536]{1,0:T(8,128)(2,1)}, bf16[2048,1536]{1,0:T(8,128)(2,1)}, bf16[1536,3072]{1,0:T(8,128)(2,1)}) custom-call(bf16[2048,1536]{1,0:T(8,128)(2,1)} %get-tuple-element.58.input_ref, bf16[2048,1536]{1,0:T(8,128)(2,1)} %get-tuple-element.59.cotangent_ref, bf16[1536,3072]{1,0:T(8,128)(2,1)} %all-gather.2.cloned.1.call-done.weight_ref), custom_call_target="tpu_custom_call" | custom-call | flops 57982058496 | bytes 45000000 | tf_op jit(solution)/shard_map/feed/pallas_call | solution.py:1124
  451.4 80.4 %exchange_hidden.1 = (f32[512,1536]{1,0:T(8,128)}, bf16[2048,1536]{1,0:T(8,128)(2,1)}) custom-call(bf16[2048,1536]{1,0:T(8,128)(2,1)} %get-tuple-element.61.refs_0_, bf16[512,1536]{1,0:T(8,128)(2,1)} %refs_1_.3, f32[512,1536]{1,0:T(8,128)} %get-tuple-element.62.refs_2_.middle_ref, f32[8,1536]{1,0:T(8,128)} %broadcast_in_dim.50.refs_2_.refs_3_), custom_call_target="tpu_custom_call" | custom-call | flops 70000001024 | bytes 16000000 | tf_op jit(solution)/shard_map/exchange_hidden/pallas_call | solution.py:845
  531.8 8.7 %multiply_convert_fusion = (bf16[2048,384]{1,0:T(8,128)(2,1)}, f32[2048,384]{1,0:T(8,128)}) fusion(f32[2048,384]{1,0:T(8,128)S(1)} %copy-done.15, bf16[2048,1536]{1,0:T(8,128)(2,1)} %get-tuple-element.63, bf16[1536,2048]{1,0:T(8,128)(2,1)} %bitcast.142), kind=kOutput, calls=%fused_computation.22 | convolution fusion | flops 2417491968 | bytes 15335424 | tf_op jit(solution)/shard_map/dot_general | solution.py:22
  540.5 11.2 %attend_back_prev.1 = (f32[2048,384]{1,0:T(8,128)}, f32[2048,128]{1,0:T(8,128)}, bf16[2,2048,384]{2,1,0:T(8,128)(2,1)}, f32[2048,128]{1,0:T(8,128)}) custom-call(s32[2,4]{1,0:T(2,128)} %pad_add_fusion.1.ranges_ref, bf16[2048,384]{1,0:T(8,128)(2,1)} %convolution_convert_fusion.4.q_ref, bf16[2048,896]{1,0:T(8,128)(2,1)} %collective-permute-done.1.k_ref.v_ref.t_key_ref, ...), custom_call_target="tpu_custom_call" | custom-call | flops 15000000512 | bytes 25000000 | tf_op jit(solution)/shard_map/attend_back_prev/pallas_call | solution.py:436
  555.8 61.3 %attend_back_own.1 = (bf16[2048,384]{1,0:T(8,128)(2,1)}, f32[2048,384]{1,0:T(8,128)}, f32[2048,384]{1,0:T(8,128)}, f32[2048,128]{1,0:T(8,128)}) custom-call(s32[2,4]{1,0:T(2,128)} %pad_add_fusion.1.ranges_ref, bf16[2048,384]{1,0:T(8,128)(2,1)} %convolution_convert_fusion.4.q_ref, bf16[2048,768]{1,0:T(8,128)(2,1)} %copy-done.3, bf16[2048,768]{1,0:T(8,128)(2,1)} %copy-done.3, ...), custom_call_target="tpu_custom_call" | custom-call | flops 80000000000 | bytes 25000000 | tf_op jit(solution)/shard_map/attend_back_own/pallas_call | solution.py:436
  617.1 7.8 convolution_convert_fusion.3
  626.3 4.5 decay_back.1
  633.2 20.7 %collective-permute-done.3 = bf16[2,2048,384]{2,1,0:T(8,128)(2,1)} collective-permute-done((bf16[2,2048,384]{2,1,0:T(8,128)(2,1)}, bf16[2,2048,384]{2,1,0:T(8,128)(2,1)}, u32[]{:S(2)}, u32[]{:S(2)}) %collective-permute-start.3) | collective-permute-done | bytes 3145760 | tf_op jit(solution)/shard_map/ppermute | solution.py:28
  661.5 2.8 copy-done.29
  664.4 14.0 %select_convert_fusion = bf16[1536,1664]{1,0:T(8,128)(2,1)} fusion(bf16[2048,1536]{1,0:T(8,128)(2,1)S(1)} %bitcast.107, bf16[2048,1664]{1,0:T(8,128)(2,1)S(1)} %fusion.15, bf16[1536]{0:T(1024)(128)(2,1)S(1)} %select_reduce_fusion, pred[1664]{0:T(1024)(128)(4,1)S(1)} %copy-done.36), kind=kOutput, calls=%fused_computation.6 | convolution fusion | flops 10471538688 | bytes 18223744 | tf_op jit(solution)/shard_map/dot_general | solution.py:1150
  678.3 3.8 all-to-all-start.1
  682.1 16.9 %convolution_convert_fusion.1.first_ref = bf16[2048,1536]{1,0:T(8,128)(2,1)} fusion(bf16[2048,1664]{1,0:T(8,128)(2,1)} %copy-done.29, bf16[1536,2048]{1,0:T(8,128)(2,1)} %bitcast.143), kind=kOutput, calls=%fused_computation.8 | convolution fusion | flops 10472128512 | bytes 18219008 | tf_op jit(solution)/shard_map/dot_general | solution.py:22
  700.3 131.1 %finish_last.1 = (bf16[4,48,1664]{2,1,0:T(8,128)(2,1)}, bf16[4,48,384]{2,1,0:T(8,128)(2,1)}, f32[512,1536]{1,0:T(8,128)}, bf16[512,1536]{1,0:T(8,128)(2,1)}) custom-call(bf16[8,4,48,1664]{3,2,1,0:T(8,128)(2,1)} %bitcast.145, bf16[8,4,48,384]{3,2,1,0:T(8,128)(2,1)} %bitcast.146, bf16[2048,1536]{1,0:T(8,128)(2,1)} %convolution_convert_fusion.1.first_ref, ...), custom_call_target="tpu_custom_call" | custom-call | flops 80000000000 | bytes 40000000 | tf_op jit(solution)/shard_map/finish_last/pallas_call | solution.py:988
  (178 shorter events, 47.0 us)
Async XLA Ops:
  7.9 148.2 %collective-permute-start = (s32[2048]{0:T(1024)S(1)}, s32[2048]{0:T(1024)S(1)}, u32[]{:S(2)}, u32[]{:S(2)}) collective-permute-start(s32[2048]{0:T(1024)S(1)} %broadcast_add_fusion), channel_id=1, source_target_pairs={{0,4},{4,8},{8,12},{12,16},{16,20},{20,24},{24,28},{1,5},{5,9},{9,... | collective-permute-start | bytes 24584 | tf_op jit(solution)/shard_map/ppermute | solution.py:28
  107.2 4.3 copy-start.31
  107.3 4.6 copy-start
  123.8 10.9 %copy-start.3 = (bf16[2048,768]{1,0:T(8,128)(2,1)}, bf16[2048,768]{1,0:T(8,128)(2,1)S(1)}, u32[]{:S(2)}) copy-start(bf16[2048,768]{1,0:T(8,128)(2,1)S(1)} %convolution_convert_fusion.2.k_ref.v_ref) | copy-start | bytes 9437188
  134.7 8.5 %copy-start.8 = (f32[48,4096]{1,0:T(8,128)S(1)}, f32[48,4096]{1,0:T(8,128)}, u32[]{:S(2)}) copy-start(f32[48,4096]{1,0:T(8,128)} %param.27) | copy-start | bytes 2359300
  134.7 8.6 %copy-start.28 = (f32[48,4096]{1,0:T(8,128)S(1)}, f32[48,4096]{1,0:T(8,128)}, u32[]{:S(2)}) copy-start(f32[48,4096]{1,0:T(8,128)} %param.28) | copy-start | bytes 2359300
  134.7 8.6 %copy-start.10 = (f32[48,4096]{1,0:T(8,128)S(1)}, f32[48,4096]{1,0:T(8,128)}, u32[]{:S(2)}) copy-start(f32[48,4096]{1,0:T(8,128)} %param.26) | copy-start | bytes 2359300
  138.0 82.9 %collective-permute-start.1 = (bf16[2048,896]{1,0:T(8,128)(2,1)}, bf16[2048,896]{1,0:T(8,128)(2,1)}, u32[]{:S(2)}, u32[]{:S(2)}) collective-permute-start(bf16[2048,896]{1,0:T(8,128)(2,1)} %pad_maximum_fusion), channel_id=1, source_target_pairs={{0,4},{4,8},{8,12},{12,16},{16,20},{20,24},{24,28},{1,5},{5,9},{9,... | collective-permute-start | bytes 11010056 | tf_op jit(solution)/shard_map/ppermute | solution.py:28
  144.6 56.7 %all-to-all-start = ((bf16[48,4,3072]{2,0,1:T(8,128)(2,1)}), bf16[48,4,3072]{2,0,1:T(8,128)(2,1)S(1)}, u32[]{:S(2)}, u32[]{:S(2)}) async-start(bf16[48,4,3072]{2,0,1:T(8,128)(2,1)} %pad_maximum_fusion.1), calls=%async_computation | async-start | bytes 2359296 | tf_op jit(solution)/shard_map/all_to_all | solution.py:1159
  148.2 212.9 %all-gather.2.cloned.1.call-start = ((), (), s32[]{:S(2)}) async-start(), calls=%async_computation.3 | async-start | bytes 10616832 | tf_op jit(solution)/shard_map/all_gather | solution.py:1164
  201.3 19.6 %copy-start.2 = (bf16[48,4,3072]{2,0,1:T(8,128)(2,1)}, bf16[48,4,3072]{2,0,1:T(8,128)(2,1)S(1)}, u32[]{:S(2)}) copy-start(bf16[48,4,3072]{2,0,1:T(8,128)(2,1)S(1)} %all-to-all-done) | copy-start | bytes 3538948
  220.9 457.4 %reduce-scatter.2.cloned.1.call-start = ((), (), s32[]{:S(2)}) async-start(), calls=%async_computation.4 | async-start | bytes 10616832 | tf_op jit(solution)/shard_map/reduce_scatter | solution.py:1168
  229.2 9.5 %copy-start.14 = (f32[2048,384]{1,0:T(8,128)}, f32[2048,384]{1,0:T(8,128)S(1)}, u32[]{:S(2)}) copy-start(f32[2048,384]{1,0:T(8,128)S(1)} %add_divide_fusion) | copy-start | bytes 9437188
  451.4 80.4 %copy-start.15 = (f32[2048,384]{1,0:T(8,128)S(1)}, f32[2048,384]{1,0:T(8,128)}, u32[]{:S(2)}) copy-start(f32[2048,384]{1,0:T(8,128)} %copy-done.14) | copy-start | bytes 9437188
  553.2 71.7 %collective-permute-start.2 = (f32[2048,8]{0,1:T(8,128)S(1)}, f32[2048,8]{0,1:T(8,128)S(1)}, u32[]{:S(2)}, u32[]{:S(2)}) collective-permute-start(f32[2048,8]{0,1:T(8,128)S(1)} %copy.127), channel_id=1, source_target_pairs={{4,0},{8,4},{12,8},{16,12},{20,16},{24,20},{28,24},{5,1},{9,5},{13... | collective-permute-start | bytes 196616 | tf_op jit(solution)/shard_map/ppermute | solution.py:28
  554.5 99.4 %collective-permute-start.3 = (bf16[2,2048,384]{2,1,0:T(8,128)(2,1)}, bf16[2,2048,384]{2,1,0:T(8,128)(2,1)}, u32[]{:S(2)}, u32[]{:S(2)}) collective-permute-start(bf16[2,2048,384]{2,1,0:T(8,128)(2,1)} %get-tuple-element.70), channel_id=1, source_target_pairs={{4,0},{8,4},{12,8},{16,12},{20,16},{24,20},{28,24},{5,1},{9,5},{13... | collective-permute-start | bytes 9437192 | tf_op jit(solution)/shard_map/ppermute | solution.py:28
  624.9 5.9 copy-start.37
  626.3 6.4 copy-start.35
  626.3 27.6 %copy-start.7 = (f32[2048,384]{1,0:T(8,128)S(1)}, f32[2048,384]{1,0:T(8,128)}, u32[]{:S(2)}) copy-start(f32[2048,384]{1,0:T(8,128)} %get-tuple-element.69) | copy-start | bytes 9437188
  653.9 4.7 copy-start.19
  653.9 5.0 copy-start.18
  656.3 8.1 slice-start
  658.6 5.7 slice-start.1
  660.8 3.6 copy-start.36
  678.3 20.7 %all-to-all-start.1 = ((bf16[4,48,3072]{2,1,0:T(8,128)(2,1)}), bf16[4,48,3072]{2,1,0:T(8,128)(2,1)S(1)}, u32[]{:S(2)}, u32[]{:S(2)}) async-start(bf16[4,48,3072]{2,1,0:T(8,128)(2,1)} %bitcast.117), calls=%async_computation.2 | async-start | bytes 2359296 | tf_op jit(solution)/shard_map/all_to_all | solution.py:1173
  835.6 3.2 copy-start.24
  835.8 3.6 copy-start.38
  835.9 6.7 copy-start.25
  836.0 6.5 copy-start.26
  836.2 6.3 copy-start.27
  836.5 7.7 copy-start.33
  837.1 5.4 copy-start.5
  (19 other events, 33.9 us)
Sparse Core Ops, SparseCore 0:
  221.0 139.9 all-gather.1
  451.5 173.1 reduce-scatter.1

commit v2 on v1

--- a/solution.py
+++ b/solution.py
@@ -51,38 +51,68 @@
     return outs, carry
 
 
-def decay_kernel(local_heads, logf_ref, own_ref, halo_ref):
-    rows = 256
-    steps = logf_ref.shape[0] // rows
+PROJECT_TILE = 256
+
+
+def project_kernel(local_heads, tokens_ref, gain_ref, weight_ref, bias_ref, input_ref, out_ref,
+                   forget_ref, carry_ref):
+    rows = tokens_ref.shape[0]
+    wide = weight_ref.shape[1] - LANES
+
+    @pl.when(pl.program_id(0) == 0)
+    def _():
+        carry_ref[...] = jnp.zeros_like(carry_ref)
+
+    tokens = tokens_ref[...].astype(f32)
+    input1 = (tokens * inverse_rms(tokens) * gain_ref[0:1, :]).astype(bf16)
+    input_ref[...] = input1
+    raw = dot(input1, weight_ref[...])
+    out_ref[:, :wide] = raw[:, :wide].astype(bf16)
+    forget = (raw[:, wide:] + bias_ref[0:1, :]).astype(bf16).astype(f32)
+    forget_ref[...] = forget
     lane = lax.broadcasted_iota(jnp.int32, (rows, LANES), 1)
-
-    def value_of(n):
-        return jnp.where(lane < local_heads, logf_ref[n * rows : (n + 1) * rows, :], 0.0)
-
-    sums, total = running(value_of, steps, rows, False)
-    one = jnp.where(lane == 3 * local_heads, 1.0, 0.0)
-
-    def terms(value):
-        high, mid, low = split3(value)
-        return (
-            high.astype(f32)
-            + pltpu.roll(mid.astype(f32), local_heads, 1)
-            + pltpu.roll(low.astype(f32), 2 * local_heads, 1)
-            + one
-        ).astype(bf16)
-
-    for n in range(steps):
-        own_ref[n * rows : (n + 1) * rows, :] = terms(sums[n])
-        halo_ref[n * rows : (n + 1) * rows, :] = terms(sums[n] - total)
-
-
-def decay_terms(logf, local_heads):
-    shape = jax.ShapeDtypeStruct(logf.shape, bf16)
+    logf = jnp.minimum(forget, 0.0) - jnp.log1p(jnp.exp(-jnp.abs(forget)))
+    logf = jnp.where(lane < local_heads, logf, 0.0)
+    place = lax.broadcasted_iota(jnp.int32, (rows, rows), 0)
+    other = lax.broadcasted_iota(jnp.int32, (rows, rows), 1)
+    tri = jnp.where(other <= place, 1.0, 0.0).astype(bf16)
+    sums = sum(dot(tri, part) for part in split3(logf)) + carry_ref[0:1, :]
+    carry_ref[0:1, :] = sums[rows - 1 : rows, :]
+    high, mid, low = split3(sums)
+    out_ref[:, wide:] = (
+        high.astype(f32)
+        + pltpu.roll(mid.astype(f32), local_heads, 1)
+        + pltpu.roll(low.astype(f32), 2 * local_heads, 1)
+        + jnp.where(lane == 3 * local_heads, 1.0, 0.0)
+    ).astype(bf16)
+
+
+def project(tokens, gain, weight, bias, wide, local_heads):
+    rows, width = tokens.shape
+
+    def tile(columns):
+        return pl.BlockSpec((PROJECT_TILE, columns), lambda n: (n, 0))
+
+    def whole(*shape):
+        return pl.BlockSpec(shape, lambda n: (0, 0))
+
     return pl.pallas_call(
-        functools.partial(decay_kernel, local_heads),
-        out_shape=(shape, shape),
-        name="decay_terms",
-    )(logf)
+        functools.partial(project_kernel, local_heads),
+        grid=(rows // PROJECT_TILE,),
+        in_specs=[tile(width), whole(8, width), whole(width, wide + LANES), whole(8, LANES)],
+        out_specs=[tile(width), tile(wide + LANES), tile(LANES)],
+        out_shape=[
+            jax.ShapeDtypeStruct((rows, width), bf16),
+            jax.ShapeDtypeStruct((rows, wide + LANES), bf16),
+            jax.ShapeDtypeStruct((rows, LANES), f32),
+        ],
+        scratch_shapes=[pltpu.VMEM((8, LANES), f32)],
+        cost_estimate=pl.CostEstimate(
+            flops=2 * rows * width * (wide + LANES), transcendentals=rows * LANES,
+            bytes_accessed=20_000_000,
+        ),
+        name="project",
+    )(tokens, gain, weight, bias)
 
 
 def decay_back_kernel(own_ref, halo_ref, out_ref):
@@ -103,16 +133,22 @@
     )(own, halo)
 
 
-def placing(pair, local_heads, for_query):
+QUERY, KEY, TOTAL = range(3)
+
+
+def placing(pair, local_heads, role):
     row = lax.broadcasted_iota(jnp.int32, (LANES, LANES), 0)
     col = lax.broadcasted_iota(jnp.int32, (LANES, LANES), 1)
     head = jnp.where(col < 64, 2 * pair + 1, 2 * pair)
     spot = jnp.where(col < 64, col, col - 64)
-    term = jnp.where(for_query, spot, spot - 3)
+    term = spot - 3 * role
     is_term = (term >= 0) & (term < 3) & (row == term * local_heads + head)
-    ones = jnp.where(for_query, spot - 3, spot)
-    is_one = (ones >= 0) & (ones < 3) & (row == 3 * local_heads)
-    sign = 1.0 if for_query else -1.0
+    if role == QUERY:
+        ones = (spot >= 3) & (spot < 9)
+    else:
+        ones = (spot < 3) & (role == KEY)
+    is_one = ones & (row == 3 * local_heads)
+    sign = -1.0 if role == KEY else 1.0
     return (jnp.where(is_term, sign, 0.0) + jnp.where(is_one, 1.0, 0.0)).astype(bf16)
 
 
@@ -148,19 +184,24 @@
     return pl.ds(pl.multiple_of(number * size, size), size)
 
 
-def fill_keys(pair, local_heads, first, key_ref, terms_ref, keys):
-    place = placing(pair, local_heads, False)
+def fill_keys(pair, local_heads, own, first, key_ref, terms_ref, keys):
+    place = placing(pair, local_heads, KEY)
     lane = lax.broadcasted_iota(jnp.int32, (K_TILE, LANES), 1)
+    rows = key_ref.shape[0]
+    total = 0.0
+    if not own:
+        last = dot(terms_ref[rows - 16 : rows, :], placing(pair, local_heads, TOTAL))
+        total = last[15:16, :]
 
     def fill(n, carry):
         here = tile_of(n, K_TILE)
-        extra = dot(terms_ref[here, :], place).astype(bf16)
+        extra = (dot(terms_ref[here, :], place) + total).astype(bf16)
         key = key_ref[here, :]
         keys[0][here, :] = jnp.where(lane < 64, key, extra)
         keys[1][here, :] = jnp.where(lane < 64, extra, key)
         return carry
 
-    lax.fori_loop(first, key_ref.shape[0] // K_TILE, fill, 0)
+    lax.fori_loop(first, rows // K_TILE, fill, 0)
 
 
 def query_tiles(q_ref, terms_ref, place, here, scaling):
@@ -181,14 +222,14 @@
     base = rows if own else 0
     keys, accs = (key0, key1), (acc0, acc1)
     first, _ = key_range(ranges_ref, 0, rows, own)
-    fill_keys(pair, local_heads, first, k_ref, t_key_ref, keys)
+    fill_keys(pair, local_heads, own, first, k_ref, t_key_ref, keys)
 
     def turn(n, carry):
         values[:, tile_of(n, K_TILE)] = v_ref[tile_of(n, K_TILE), :].T
         return carry
 
     lax.fori_loop(first, rows // K_TILE, turn, 0)
-    place = placing(pair, local_heads, True)
+    place = placing(pair, local_heads, QUERY)
 
     def query_loop(tile, carry):
         here = tile_of(tile, Q_TILE)
@@ -255,11 +296,11 @@
     return pl.BlockSpec((height, rows), lambda p, *_: (p, 0))
 
 
-def terms_block(own, rows, pairs):
-    return pl.BlockSpec((rows, LANES), lambda p, *_: (0, 0 if own else 2 * pairs))
-
-
-def attend(own, ranges, query, key_value, terms, key_terms, begins, local_heads, so_far=()):
+def terms_block(rows, pairs):
+    return pl.BlockSpec((rows, LANES), lambda p, *_: (0, 2 * pairs))
+
+
+def attend(own, ranges, query, key_value, own_terms, begins, local_heads, so_far=()):
     rows = query.shape[0]
     pairs = local_heads // 2
     running_specs = [pair_block(LANES, rows), pair_block(8, rows)]
@@ -281,8 +322,8 @@
                 lane_block(rows, 0),
                 lane_block(rows, 0),
                 lane_block(rows, pairs),
-                fixed((rows, LANES)),
-                terms_block(own, rows, pairs),
+                terms_block(rows, pairs),
+                terms_block(rows, pairs),
                 fixed((8, rows)),
             ]
             + ([] if own else running_specs),
@@ -302,7 +343,7 @@
             bytes_accessed=12_000_000,
         ),
         name="attend_own" if own else "attend_prev",
-    )(ranges, query, key_value, key_value, terms, key_terms, begins, *so_far)
+    )(ranges, query, key_value, key_value, own_terms, key_value, begins, *so_far)
 
 
 def attend_back_kernel(local_heads, own, ranges_ref, q_ref, k_ref, v_ref, t_query_ref, t_key_ref,
@@ -318,7 +359,7 @@
     base = rows if own else 0
     keys, keys_t, dks, dqs = (key0, key1), (key_t0, key_t1), (dk0, dk1), (dq0, dq1)
     first, _ = key_range(ranges_ref, 0, rows, own)
-    fill_keys(pair, local_heads, first, k_ref, t_key_ref, keys)
+    fill_keys(pair, local_heads, own, first, k_ref, t_key_ref, keys)
 
     def turn(n, carry):
         here = tile_of(n, K_TILE)
@@ -329,7 +370,7 @@
     lax.fori_loop(first, rows // K_TILE, turn, 0)
     for ref in (dk0, dk1, dv):
         ref[...] = jnp.zeros_like(ref)
-    place = placing(pair, local_heads, True)
+    place = placing(pair, local_heads, QUERY)
     lane = lax.broadcasted_iota(jnp.int32, (Q_TILE, LANES), 1)
     pick_row = lax.broadcasted_iota(jnp.int32, (8, LANES), 0)
     pick_lane = lax.broadcasted_iota(jnp.int32, (8, LANES), 1)
@@ -417,7 +458,7 @@
 
 
 def attend_back(
-    own, ranges, query, key_value, terms, key_terms, begins, grad, mixed, lse, local_heads,
+    own, ranges, query, key_value, own_terms, begins, grad, mixed, lse, local_heads,
     so_far=(),
 ):
     rows = query.shape[0]
@@ -442,8 +483,8 @@
                 lane_block(rows, 0),
                 lane_block(rows, 0),
                 lane_block(rows, pairs),
-                fixed((rows, LANES)),
-                terms_block(own, rows, pairs),
+                terms_block(rows, pairs),
+                terms_block(rows, pairs),
                 fixed((8, rows)),
                 lane_block(rows, 0),
                 lane_block(rows, 0),
@@ -471,7 +512,7 @@
         ),
         name="attend_back_own" if own else "attend_back_prev",
     )(
-        ranges, query, key_value, key_value, terms, key_terms, begins, grad, mixed, lse, *so_far
+        ranges, query, key_value, key_value, own_terms, key_value, begins, grad, mixed, lse, *so_far
     )
 
 
@@ -517,34 +558,50 @@
     return {"blk": index}
 
 
-def rows_of(ref, shard, piece, size):
+def piece_at(ref, slot, piece, size):
     span = size // PIECES
-    start = pl.multiple_of(shard * size + piece * span, span)
-    return ref.at[pl.ds(start, span), :]
-
-
-def spread_piece(source, all_ref, size, sems, piece):
+    return ref.at[pl.ds(pl.multiple_of(slot * size + piece * span, span), span), :]
+
+
+class Slots:
+    def __init__(self, by_device):
+        me, near, far, cross = partners()
+        if by_device:
+            self.own = self.sent_near = self.sent_far = me
+            self.near, self.far, self.cross = near, far, cross
+            self.passed = far
+        else:
+            self.own, self.sent_near, self.sent_far = 3, 2, 1
+            self.near, self.far, self.cross = 2, 1, 0
+            self.passed = 0
+
+
+def spread_piece(source, all_ref, size, sems, piece, slots):
     me, near, far, _ = partners()
     far_send, far_recv, near_send, near_recv, _, _, own = sems
-    place = rows_of(all_ref, me, piece, size)
     copies = (
-        remote(source, place, far_send.at[piece], far_recv.at[piece], on_head(far)),
-        remote(source, place, near_send.at[piece], near_recv.at[piece], on_head(near)),
-        pltpu.make_async_copy(source, place, own.at[piece]),
+        remote(source, piece_at(all_ref, slots.sent_far, piece, size), far_send.at[piece],
+               far_recv.at[piece], on_head(far)),
+        remote(source, piece_at(all_ref, slots.sent_near, piece, size), near_send.at[piece],
+               near_recv.at[piece], on_head(near)),
+        pltpu.make_async_copy(source, piece_at(all_ref, slots.own, piece, size), own.at[piece]),
     )
     for copy in copies:
         copy.start()
     return copies
 
 
-def hand_on(all_ref, size, sems, sent):
+def hand_on(all_ref, size, sems, sent, slots):
     me, near, far, cross = partners()
     far_send, far_recv, near_send, near_recv, on_send, on_recv, own = sems
     passed = []
     for piece in range(PIECES):
-        there = rows_of(all_ref, far, piece, size)
+        there = piece_at(all_ref, slots.far, piece, size)
         remote(there, there, far_send.at[piece], far_recv.at[piece], on_head(far)).wait_recv()
-        copy = remote(there, there, on_send.at[piece], on_recv.at[piece], on_head(near))
+        copy = remote(
+            there, piece_at(all_ref, slots.passed, piece, size), on_send.at[piece],
+            on_recv.at[piece], on_head(near),
+        )
         copy.start()
         passed.append(copy)
 
@@ -555,9 +612,9 @@
             to_near.wait_send()
             local.wait()
             passed[piece].wait_send()
-            there = rows_of(all_ref, near, piece, size)
+            there = piece_at(all_ref, slots.near, piece, size)
             remote(there, there, near_send.at[piece], near_recv.at[piece], on_head(near)).wait_recv()
-            there = rows_of(all_ref, cross, piece, size)
+            there = piece_at(all_ref, slots.cross, piece, size)
             remote(there, there, on_send.at[piece], on_recv.at[piece], on_head(near)).wait_recv()
 
     return finish
@@ -685,13 +742,14 @@
     size = tokens_ref.shape[0]
     span = size // PIECES
 
-    def spread_all(ref, all_ref, some):
+    def spread_all(ref, all_ref, some, slots):
         return [
-            spread_piece(ref.at[pl.ds(piece * span, span), :], all_ref, size, some, piece)
+            spread_piece(ref.at[pl.ds(piece * span, span), :], all_ref, size, some, piece, slots)
             for piece in range(PIECES)
         ]
 
-    tokens_sent = spread_all(tokens_ref, tokens_all, token_sems)
+    by_device, crossing = Slots(True), Slots(False)
+    tokens_sent = spread_all(tokens_ref, tokens_all, token_sems, by_device)
     swaps[0].wait()
     line.launch(0)
     for kind, source in enumerate((near, far, cross)):
@@ -700,11 +758,11 @@
             block, block, swap_send.at[kind], swap_recv.at[kind], on_head(source)
         ).wait_recv()
         line.launch(kind + 1)
-    cotangent_sent = spread_all(cotangent_ref, cotangent_all, cotangent_sems)
+    cotangent_sent = spread_all(cotangent_ref, cotangent_all, cotangent_sems, crossing)
     for t in range(1, line.half):
         line.step(t)
-    finish_tokens = hand_on(tokens_all, size, token_sems, tokens_sent)
-    finish_cotangent = hand_on(cotangent_all, size, cotangent_sems, cotangent_sent)
+    finish_tokens = hand_on(tokens_all, size, token_sems, tokens_sent, by_device)
+    finish_cotangent = hand_on(cotangent_all, size, cotangent_sems, cotangent_sent, crossing)
     for swap in swaps[1:]:
         swap.wait_send()
     line.finish()
@@ -741,8 +799,9 @@
 
 
 class Sum:
-    def __init__(self, part_ref, buffers, sems, size):
+    def __init__(self, part_ref, buffers, sems, size, by_device):
         self.part_ref, self.size, self.span = part_ref, size, size // PIECES
+        self.slots = Slots(by_device)
         self.near_buf, self.turn_buf, self.far_buf = buffers
         self.near_send, self.near_recv, self.far_send, self.far_recv = sems
         self.near_copies, self.far_copies = [], []
@@ -752,10 +811,10 @@
 
     def start(self):
         me, near, far, cross = partners()
-        for which, shard in ((0, cross), (1, near)):
+        for which, shard in ((0, self.slots.cross), (1, self.slots.near)):
             for n in range(PIECES):
                 copy = remote(
-                    rows_of(self.part_ref, shard, n, self.size),
+                    piece_at(self.part_ref, shard, n, self.size),
                     self.near_buf.at[which, pl.ds(n * self.span, self.span), :],
                     self.near_send.at[which, n],
                     self.near_recv.at[which, n],
@@ -770,7 +829,7 @@
             here = self.piece(n)
             self.near_copies[n].wait_recv()
             self.turn_buf[here, :] = (
-                rows_of(self.part_ref, far, n, self.size)[...].astype(f32)
+                piece_at(self.part_ref, self.slots.far, n, self.size)[...].astype(f32)
                 + self.near_buf[0, here, :].astype(f32)
             ).astype(bf16)
             copy = remote(
@@ -784,12 +843,11 @@
             self.far_copies.append(copy)
 
     def total(self, n):
-        me = lax.axis_index("head")
         self.near_copies[PIECES + n].wait_recv()
         self.far_copies[n].wait_recv()
         here = self.piece(n)
         return (
-            rows_of(self.part_ref, me, n, self.size)[...].astype(f32)
+            piece_at(self.part_ref, self.slots.own, n, self.size)[...].astype(f32)
             + self.near_buf[1, here, :].astype(f32)
             + self.far_buf[here, :].astype(f32)
         )
@@ -816,47 +874,53 @@
     ]
 
 
-def exchange_kernel(local, extras, *refs):
+def exchange_kernel(local, extras, summed, *refs):
     part_ref, extra_refs = refs[0], refs[1 : 1 + extras]
-    out_ref, all_ref, near_buf, turn_buf, far_buf, payload = refs[1 + extras : 7 + extras]
-    sems = refs[7 + extras :]
+    out_ref, all_ref, payload = refs[1 + extras : 4 + extras]
+    sems = refs[4 + extras :]
     size = out_ref.shape[0]
+    span = size // PIECES
     _, near, far, _ = partners()
     greet([on_head(near), on_head(far)])
-    shares = Sum(part_ref, (near_buf, turn_buf, far_buf), sems[:4], size)
-    shares.start()
-    shares.turn()
+    slots = Slots(summed)
+    if not summed:
+        shares = Sum(part_ref, sems[7:10], sems[10:], size, True)
+        shares.start()
+        shares.turn()
     sent = []
     for piece in range(PIECES):
-        here = shares.piece(piece)
-        result, share = local(shares.total(piece), here, *extra_refs)
+        here = slice(piece * span, (piece + 1) * span)
+        total = part_ref[here, :] if summed else shares.total(piece)
+        result, share = local(total, here, *extra_refs)
         out_ref[here, :] = result.astype(out_ref.dtype)
         payload[here, :] = share.astype(bf16)
-        source = payload.at[pl.ds(piece * shares.span, shares.span), :]
-        sent.append(spread_piece(source, all_ref, size, sems[4:], piece))
-    hand_on(all_ref, size, sems[4:], sent)()
-    shares.finish()
-
-
-def exchange(local, part, extras, number, name):
+        source = payload.at[pl.ds(piece * span, span), :]
+        sent.append(spread_piece(source, all_ref, size, sems[:7], piece, slots))
+    hand_on(all_ref, size, sems[:7], sent, slots)()
+    if not summed:
+        shares.finish()
+
+
+def exchange(local, part, extras, summed, number, name):
     rows, width = part.shape
-    size = rows // 4
+    size = rows if summed else rows // 4
     vmem = pl.BlockSpec(memory_space=pltpu.VMEM)
     return pl.pallas_call(
-        functools.partial(exchange_kernel, local, len(extras)),
+        functools.partial(exchange_kernel, local, len(extras), summed),
         in_specs=[vmem] * (1 + len(extras)),
         out_specs=[vmem, pl.BlockSpec(memory_space=pl.ANY)],
         out_shape=[
             jax.ShapeDtypeStruct((size, width), f32),
-            jax.ShapeDtypeStruct((rows, width), bf16),
+            jax.ShapeDtypeStruct((4 * size, width), bf16),
         ],
-        scratch_shapes=sum_buffers(size, width)
-        + [pltpu.VMEM((size, width), bf16)]
-        + sum_sems()
-        + gather_sems(),
+        scratch_shapes=[pltpu.VMEM((size, width), bf16)]
+        + gather_sems()
+        + ([] if summed else sum_buffers(size, width) + sum_sems()),
         compiler_params=pltpu.CompilerParams(collective_id=number, has_side_effects=True),
         cost_estimate=pl.CostEstimate(
-            flops=70_000_000_000, transcendentals=0, bytes_accessed=16_000_000
+            flops=40_000_000_000 if summed else 70_000_000_000,
+            transcendentals=0,
+            bytes_accessed=16_000_000,
         ),
         name=name,
     )(part, *extras)
@@ -875,8 +939,8 @@
         + [on_blk(peer) for peer in after[1:]]
     )
     size = result_ref.shape[0]
-    first = Sum(first_ref, (near1, turn1, far1), sems[12:16], size)
-    down = Sum(down_ref, (near2, turn2, far2), sems[16:20], size)
+    first = Sum(first_ref, (near1, turn1, far1), sems[12:16], size, True)
+    down = Sum(down_ref, (near2, turn2, far2), sems[16:20], size, False)
     sums = (
         (grad_ref, weights_ref, buffers[:4], sems[:6]),
         (output_grad_ref, output_ref, buffers[4:], sems[6:12]),
@@ -1055,20 +1119,43 @@
 FEED_COLUMNS = 512
 
 
-def feed_kernel(input_ref, cotangent_ref, weight_ref, down_ref, grad_input_ref, grad_ref, total,
-                down_sum, input_sum, turned):
+def feed_kernel(input_ref, cotangent_ref, weight_ref, down_ref, grad_ref, total_ref, acts, turned0,
+                turned1, stage, near_buf, far_buf, near_send, near_recv, far_send, far_recv):
     step = pl.program_id(0)
-    width = input_ref.shape[1]
     hidden_width = weight_ref.shape[1] // 3
-    inputs, cotangent = input_ref[...], cotangent_ref[...]
-    turned[0] = inputs.T
-    turned[1] = cotangent.T
-
-    def columns(which, n):
-        return pl.ds(pl.multiple_of(which * hidden_width + n * FEED_COLUMNS, FEED_COLUMNS), FEED_COLUMNS)
-
-    def chunk(n, carry):
-        gate_at, up_at, down_at = columns(0, n), columns(1, n), columns(2, n)
+    size = total_ref.shape[0]
+    per = size // FEED_TILE
+    tiles = 4 * per
+    _, near, far, _ = partners()
+
+    @pl.when(step == 0)
+    def _():
+        greet([on_head(near), on_head(far)])
+
+    def to_near(which, piece):
+        return remote(
+            stage.at[which * per + piece],
+            near_buf.at[which, piece],
+            near_send.at[which, piece],
+            near_recv.at[which, piece],
+            on_head(near),
+        )
+
+    def to_far(piece):
+        return remote(
+            near_buf.at[0, piece], far_buf.at[piece], far_send.at[piece], far_recv.at[piece],
+            on_head(far),
+        )
+
+    @pl.when(step < tiles)
+    def _():
+        here = tile_of(step, FEED_TILE)
+        inputs, cotangent = input_ref[...], cotangent_ref[...]
+        turned0[:, here] = inputs.T
+        turned1[:, here] = cotangent.T
+        gate_at, up_at, down_at = (
+            slice(n * hidden_width, (n + 1) * hidden_width) for n in range(3)
+        )
         gate = dot(inputs, weight_ref[:, gate_at])
         up = dot(inputs, weight_ref[:, up_at])
         grad_hidden = dot(cotangent, weight_ref[:, down_at])
@@ -1077,67 +1164,95 @@
         hidden = (active * up).astype(bf16)
         grad_gate = (grad_hidden * up * opening * (1.0 + gate * (1.0 - opening))).astype(bf16)
         grad_up = (grad_hidden * active).astype(bf16)
-        down = dot(hidden, weight_ref[:, down_at], NT)
-        back = dot(grad_gate, weight_ref[:, gate_at], NT) + dot(grad_up, weight_ref[:, up_at], NT)
-
-        @pl.when(n == 0)
+        acts[here, gate_at] = grad_gate
+        acts[here, up_at] = grad_up
+        acts[here, down_at] = hidden
+        down_ref[...] = dot(hidden, weight_ref[:, down_at], NT).astype(bf16)
+        back = dot(grad_gate, weight_ref[:, gate_at], NT) + dot(
+            grad_up, weight_ref[:, up_at], NT
+        )
+        for piece in range(per):
+            for which, first in ((0, 0), (1, 2 * per)):
+
+                @pl.when(step == first + piece)
+                def _():
+                    stage[which * per + piece] = back.astype(bf16)
+                    to_near(which, piece).start()
+
+            @pl.when(step == per + piece)
+            def _():
+                to_near(0, piece).wait_recv()
+                near_buf[0, piece] = (back + near_buf[0, piece].astype(f32)).astype(bf16)
+                to_far(piece).start()
+
+            @pl.when(step == 3 * per + piece)
+            def _():
+                total_ref[piece * FEED_TILE : (piece + 1) * FEED_TILE, :] = back
+
+    @pl.when(step >= tiles)
+    def _():
+        at = tile_of(step - tiles, FEED_COLUMNS)
+        from_input = (step - tiles) * FEED_COLUMNS < 2 * hidden_width
+
+        @pl.when(from_input)
         def _():
-            down_sum[...] = down
-            input_sum[...] = back
-
-        @pl.when(n > 0)
+            grad_ref[...] = dot(turned0[...], acts[:, at]).astype(bf16)
+
+        @pl.when(jnp.logical_not(from_input))
         def _():
-            down_sum[...] += down
-            input_sum[...] += back
-
-        for at, side, grad in ((gate_at, 0, grad_gate), (up_at, 0, grad_up), (down_at, 1, hidden)):
-
-            @pl.when(step == 0)
-            def _():
-                total[:, at] = dot(turned[side], grad)
-
-            @pl.when(step > 0)
-            def _():
-                total[:, at] += dot(turned[side], grad)
-
-        return carry
-
-    lax.fori_loop(0, hidden_width // FEED_COLUMNS, chunk, 0)
-    down_ref[...] = down_sum[...].astype(bf16)
-    grad_input_ref[...] = input_sum[...].astype(bf16)
+            grad_ref[...] = dot(turned1[...], acts[:, at]).astype(bf16)
 
     @pl.when(step == pl.num_programs(0) - 1)
     def _():
-        def store(n, carry):
-            at = pl.ds(pl.multiple_of(n * 128, 128), 128)
-            grad_ref[at, :] = total[at, :].astype(bf16)
-            return carry
-
-        lax.fori_loop(0, width // 128, store, 0)
-
-
-def feed(inputs, cotangent, weight):
+        for piece in range(per):
+            here = slice(piece * FEED_TILE, (piece + 1) * FEED_TILE)
+            to_near(1, piece).wait_recv()
+            to_far(piece).wait_recv()
+            total_ref[here, :] += near_buf[1, piece].astype(f32) + far_buf[piece].astype(f32)
+            to_near(0, piece).wait_send()
+            to_near(1, piece).wait_send()
+            to_far(piece).wait_send()
+
+
+def feed(inputs, cotangent, weight, number):
     rows, width = inputs.shape
     columns = weight.shape[1]
-    tile = pl.BlockSpec((FEED_TILE, width), lambda n: (n, 0))
-    whole = pl.BlockSpec((width, columns), lambda n: (0, 0), pipeline_mode=pl.Buffered(1))
+    size = rows // 4
+    tiles, per = rows // FEED_TILE, size // FEED_TILE
+    tile = pl.BlockSpec((FEED_TILE, width), lambda n: (jnp.minimum(n, tiles - 1), 0))
+
+    def whole(shape):
+        return pl.BlockSpec(shape, lambda n: (0, 0), pipeline_mode=pl.Buffered(1))
+
     return pl.pallas_call(
         feed_kernel,
-        grid=(rows // FEED_TILE,),
-        in_specs=[tile, tile, whole],
-        out_specs=[tile, tile, whole],
+        grid=(tiles + columns // FEED_COLUMNS,),
+        in_specs=[tile, tile, whole((width, columns))],
+        out_specs=[
+            tile,
+            pl.BlockSpec((width, FEED_COLUMNS), lambda n: (0, jnp.maximum(n - tiles, 0))),
+            whole((size, width)),
+        ],
         out_shape=[
             jax.ShapeDtypeStruct((rows, width), bf16),
-            jax.ShapeDtypeStruct((rows, width), bf16),
             jax.ShapeDtypeStruct((width, columns), bf16),
+            jax.ShapeDtypeStruct((size, width), f32),
         ],
         scratch_shapes=[
-            pltpu.VMEM((width, columns), f32),
-            pltpu.VMEM((FEED_TILE, width), f32),
-            pltpu.VMEM((FEED_TILE, width), f32),
-            pltpu.VMEM((2, width, FEED_TILE), bf16),
+            pltpu.VMEM((rows, columns), bf16),
+            pltpu.VMEM((width, rows), bf16),
+            pltpu.VMEM((width, rows), bf16),
+            pltpu.VMEM((2 * per, FEED_TILE, width), bf16),
+            pltpu.VMEM((2, per, FEED_TILE, width), bf16),
+            pltpu.VMEM((per, FEED_TILE, width), bf16),
+            pltpu.SemaphoreType.DMA((2, per)),
+            pltpu.SemaphoreType.DMA((2, per)),
+            pltpu.SemaphoreType.DMA((per,)),
+            pltpu.SemaphoreType.DMA((per,)),
         ],
-        compiler_params=pltpu.CompilerParams(vmem_limit_bytes=60 << 20),
+        compiler_params=pltpu.CompilerParams(
+            collective_id=number, has_side_effects=True, vmem_limit_bytes=63 << 20
+        ),
         cost_estimate=pl.CostEstimate(
             flops=6 * rows * width * columns, transcendentals=rows * columns // 3,
             bytes_accessed=45_000_000,
@@ -1239,52 +1354,49 @@
         return jnp.broadcast_to(gain[None, :], (8, model_width))
 
     gain1, gain2 = gain_rows(0), gain_rows(1)
-    wide_all = tokens_all.astype(f32)
-    input1 = lax.optimization_barrier(
-        (wide_all * inverse_rms(wide_all) * gain1[0:1]).astype(bf16)
-    )
-    key_value = dot(input1, first[:, : 2 * local_width]).astype(bf16)
     bias = lax.dynamic_slice_in_dim(forget_bias, group * local_heads, local_heads, 0)
-    bias = jnp.pad(bias, (0, LANES - local_heads))
-    forget = dot(input1, first[:, 2 * local_width : kv_width]) + bias[None, :]
-    forget = forget.astype(bf16).astype(f32)
-    terms, halo_terms = decay_terms(jax.nn.log_sigmoid(forget), local_heads)
-    earlier_kv = passed_along(jnp.concatenate([key_value, halo_terms], axis=1), "blk", 1)
+    bias = jnp.broadcast_to(jnp.pad(bias, (0, LANES - local_heads))[None, :], (8, LANES))
+    input1, key_value, forget = project(
+        tokens_all, gain1, first, bias, 2 * local_width, local_heads
+    )
+    earlier_kv = passed_along(key_value, "blk", 1)
     query = dot(input1, first[:, kv_width : kv_width + local_width]).astype(bf16)
     gate_raw = dot(
         input1, first[:, kv_width + local_width : kv_width + 2 * local_width]
     )
 
-    so_far = attend(True, ranges, query, key_value, terms, terms, begins, local_heads)
+    so_far = attend(True, ranges, query, key_value, key_value, begins, local_heads)
     mine = sent_columns([low(w_gate), low(w_up), low(w_down)], groups)
     mine, earlier_kv, so_far = lax.optimization_barrier((mine, earlier_kv, so_far))
     second = all_rows(mine)
     attended, lse = attend(
-        False, ranges, query, earlier_kv, terms, earlier_kv, begins, local_heads, so_far
+        False, ranges, query, earlier_kv, key_value, begins, local_heads, so_far
     )
     opened = jax.nn.sigmoid(gate_raw)
     attended_wide = attended.astype(f32)
     gated = (opened * attended_wide).astype(bf16)
     branch = dot(gated, output_weight, NT).astype(bf16)
-    middle, input2 = exchange(after_attention, branch, [tokens, gain2], 1, "exchange_middle")
-    down, grad_input2, second_grad = feed(input2, cotangent_all, second)
+    middle, input2 = exchange(
+        after_attention, branch, [tokens, gain2], False, 1, "exchange_middle"
+    )
+    down, second_grad, grad_input2 = feed(input2, cotangent_all, second, 4)
     second_part = row_sums(second_grad)
     grad_middle, grad_branch = exchange(
-        after_hidden, grad_input2, [cotangent, middle, gain2], 2, "exchange_hidden"
+        after_hidden, grad_input2, [cotangent, middle, gain2], True, 2, "exchange_hidden"
     )
 
     grad_gated = dot(grad_branch, output_weight)
     grad_attended = (grad_gated * opened).astype(bf16)
     grad_gate_pre = (grad_gated * attended_wide * opened * (1.0 - opened)).astype(bf16)
     dq_prev, rows_prev, dkv_prev, decay_prev = attend_back(
-        False, ranges, query, earlier_kv, terms, earlier_kv, begins, grad_attended, attended,
+        False, ranges, query, earlier_kv, key_value, begins, grad_attended, attended,
         lse, local_heads,
     )
     dkv_later = passed_along(dkv_prev, "blk", -1)
     decay_later = passed_along(decay_prev[:, :8], "blk", -1)
     decay_later = jnp.pad(decay_later, ((0, 0), (0, LANES - 8)))
     dq, dk_own, dv_own, decay_own = attend_back(
-        True, ranges, query, key_value, terms, terms, begins, grad_attended, attended,
+        True, ranges, query, key_value, key_value, begins, grad_attended, attended,
         lse, local_heads, (dq_prev, rows_prev),
     )
     dk = (dk_own + dkv_later[0].astype(f32)).astype(bf16)

time: 861 us -> 813 us (0.944)
  Pallas kernels: 596 us -> 536 us
  waiting for transfers between devices: 74.9 us -> 118 us
  matrix products: 83.1 us -> 70.9 us
  other arithmetic: 37 us -> 25.4 us
    pallas_call x4, Pallas kernels: 254 us -> 213 us  [the longest x2 122 us: exchange(): pl.pallas_call(functools.partial(exchange_kernel, local, len(extras), sum...]
    reduce_scatter x1, waiting for transfers between devices: 0.01 us -> 28.7 us  [row_sums(): return lax.psum_scatter(grad, 'blk', scatter_dimension=0, tiled=True)]
    pallas_call x1, Pallas kernels: 131 us -> 104 us  [finish_last(): pl.pallas_call(finish_last_kernel, in_specs=[vmem] * 8, out_specs=[vmem]...]
    ppermute x4, waiting for transfers between devices: 40.3 us -> 54.9 us  [passed_along(): return lax.ppermute(array, axis, pairs)]
    dot_general x7 -> x5, matrix products: 61.4 us -> 47.6 us  [dot(): return lax.dot_general(a, b, dims, preferred_element_type=f32, **kw)]
    pallas_call x1, Pallas kernels: 84.4 us -> 93.1 us  [gather_first(): pl.pallas_call(gather_first_kernel, in_specs=[vmem] * 3, out_specs=[anywh...]
  transfers between devices with their start and end apart: 8 -> 8, of which waited for: 3 -> 4; matrix products, arithmetic and copies ran while one was open for 15% -> 12% of each run, Pallas kernels for 44% -> 44%
where the time goes in v2:
time: 813 us; the launch traced here: 807 us
  Pallas kernels  536 us (66%)
  waiting for transfers between devices  118 us (15%)
  matrix products  70.9 us (9%)
  other arithmetic  25.4 us (3%)
  local copies, waits for them, and re-layouts  21.3 us (3%)
  starting transfers between devices  20.5 us (3%)
  between operations  15.2 us (2%)
    pallas_call x2, Pallas kernels, exchange(): pl.pallas_call(functools.partial(exchange_kernel, local, len(extras), sum...  122 us
    pallas_call x1, Pallas kernels, finish_last(): pl.pallas_call(finish_last_kernel, in_specs=[vmem] * 8, out_specs=[vmem]...  104 us
    pallas_call x1, Pallas kernels, gather_first(): pl.pallas_call(gather_first_kernel, in_specs=[vmem] * 3, out_specs=[anywh...  93.1 us
    pallas_call x1, Pallas kernels, feed(): pl.pallas_call(feed_kernel, grid=(tiles + columns // FEED_COLUMNS,), in_s...  75 us
    pallas_call x2, Pallas kernels, attend_back(): pl.pallas_call(functools.partial(attend_back_kernel, local_heads, own), g...  71.9 us
    ppermute x4, waiting for transfers between devices, passed_along(): return lax.ppermute(array, axis, pairs)  54.9 us
    pallas_call x2, Pallas kernels, attend(): pl.pallas_call(functools.partial(attend_kernel, local_heads, own), grid_s...  50 us
    dot_general x5, matrix products, dot(): return lax.dot_general(a, b, dims, preferred_element_type=f32, **kw)  47.6 us
  transfers between devices with their start and end apart: 8, of which 4 were waited for; matrix products, arithmetic and copies ran while one was open for 12% of the time, Pallas kernels for 44%

profile of v2, /device:TPU:0, one launch (start us, length us, event | category | flops | bytes accessed | tf_op | source)
XLA Modules:
  0.0 807.0 jit_solution(8417328859276255679)
XLA Ops:
  8.0 4.8 collective-permute-start
  16.5 3.5 all-to-all-start
  21.9 93.1 %gather_first.1 = (bf16[8,4,48,2048]{3,2,1,0:T(8,128)(2,1)}, bf16[2048,1536]{1,0:T(8,128)(2,1)}, bf16[2048,1536]{1,0:T(8,128)(2,1)}) custom-call(bf16[4,48,2048]{2,1,0:T(8,128)(2,1)} %bitcast.124, bf16[512,1536]{1,0:T(8,128)(2,1)} %tokens_ref.3, bf16[512,1536]{1,0:T(8,128)(2,1)} %refs_1_.3), custom_call_target="tpu_custom_call" | custom-call | flops 70000001024 | bytes 30000000 | tf_op jit(solution)/shard_map/gather_first/pallas_call | solution.py:779
  115.0 1.7 convert_reduce_fusion.2
  118.0 15.7 %project.1 = (bf16[2048,1536]{1,0:T(8,128)(2,1)}, bf16[2048,896]{1,0:T(8,128)(2,1)}, f32[2048,128]{1,0:T(8,128)}) custom-call(bf16[2048,1536]{1,0:T(8,128)(2,1)} %get-tuple-element.49.tokens_ref, f32[8,1536]{1,0:T(8,128)} %broadcast_in_dim.53.gain_ref, bf16[1536,2048]{1,0:T(8,128)(2,1)} %bitcast.133, f32[8,128]{1,0:T(8,128)} %broadcast_in_dim.54.bias_ref), custom_call_target="tpu_custom_call" | custom-call | flops 5637144576 | bytes 20000000 | tf_op jit(solution)/shard_map/project/pallas_call | solution.py:99
  133.7 5.5 collective-permute-start.1
  139.2 7.7 convolution_convert_fusion.3.q_ref
  146.8 3.3 convert_reduce_fusion
  151.6 40.2 %attend_own.1 = (f32[384,2048]{1,0:T(8,128)}, f32[24,2048]{1,0:T(8,128)}) custom-call(s32[2,4]{1,0:T(2,128)} %pad_add_fusion.1.ranges_ref, bf16[2048,384]{1,0:T(8,128)(2,1)} %convolution_convert_fusion.3.q_ref, bf16[2048,896]{1,0:T(8,128)(2,1)} %get-tuple-element.52.k_ref.v_ref.t_query_ref.t_key_ref, ...), custom_call_target="tpu_custom_call" | custom-call | flops 40000000000 | bytes 12000000 | tf_op jit(solution)/shard_map/attend_own/pallas_call | solution.py:316
  191.8 24.7 %collective-permute-done.1.k_ref.v_ref.t_key_ref = bf16[2048,896]{1,0:T(8,128)(2,1)} collective-permute-done((bf16[2048,896]{1,0:T(8,128)(2,1)}, bf16[2048,896]{1,0:T(8,128)(2,1)}, u32[]{:S(2)}, u32[]{:S(2)}) %collective-permute-start.1) | collective-permute-done | bytes 3670048 | tf_op jit(solution)/shard_map/ppermute | solution.py:28
  218.6 6.1 add_divide_fusion
  224.7 9.8 %attend_prev.1 = (bf16[2048,384]{1,0:T(8,128)(2,1)}, f32[24,2048]{1,0:T(8,128)}) custom-call(s32[2,4]{1,0:T(2,128)} %pad_add_fusion.1.ranges_ref, bf16[2048,384]{1,0:T(8,128)(2,1)} %convolution_convert_fusion.3.q_ref, bf16[2048,896]{1,0:T(8,128)(2,1)} %collective-permute-done.1.k_ref.v_ref.t_key_ref, ...), custom_call_target="tpu_custom_call" | custom-call | flops 10000000000 | bytes 12000000 | tf_op jit(solution)/shard_map/attend_prev/pallas_call | solution.py:316
  234.5 7.9 convolution_convert_fusion.refs_0_
  243.1 78.7 %exchange_middle.1 = (f32[512,1536]{1,0:T(8,128)}, bf16[2048,1536]{1,0:T(8,128)(2,1)}) custom-call(bf16[2048,1536]{1,0:T(8,128)(2,1)} %convolution_convert_fusion.refs_0_, bf16[512,1536]{1,0:T(8,128)(2,1)} %tokens_ref.3, f32[8,1536]{1,0:T(8,128)} %broadcast_in_dim.95.refs_2_.refs_3_), custom_call_target="tpu_custom_call" | custom-call | flops 70000001024 | bytes 16000000 | tf_op jit(solution)/shard_map/exchange_middle/pallas_call | solution.py:908
  321.8 34.2 %all-gather.2.cloned.1.call-done.weight_ref = bf16[1536,3072]{1,0:T(8,128)(2,1)} async-done(((bf16[192,3072]{1,0:T(8,128)(2,1)}), bf16[1536,3072]{1,0:T(8,128)(2,1)}) %all-gather.2.cloned.1.call-update) | async-done | bytes 9437200 | tf_op jit(solution)/shard_map/all_gather | solution.py:1279
  356.0 75.0 %feed.1 = (bf16[2048,1536]{1,0:T(8,128)(2,1)}, bf16[1536,3072]{1,0:T(8,128)(2,1)}, f32[512,1536]{1,0:T(8,128)}) custom-call(bf16[2048,1536]{1,0:T(8,128)(2,1)} %get-tuple-element.59.input_ref, bf16[2048,1536]{1,0:T(8,128)(2,1)} %get-tuple-element.60.cotangent_ref, bf16[1536,3072]{1,0:T(8,128)(2,1)} %all-gather.2.cloned.1.call-done.weight_ref), custom_call_target="tpu_custom_call" | custom-call | flops 57982058496 | bytes 45000000 | tf_op jit(solution)/shard_map/feed/pallas_call | solution.py:1227
  431.0 43.2 %exchange_hidden.1 = (f32[512,1536]{1,0:T(8,128)}, bf16[2048,1536]{1,0:T(8,128)(2,1)}) custom-call(f32[512,1536]{1,0:T(8,128)} %get-tuple-element.62.refs_0_, bf16[512,1536]{1,0:T(8,128)(2,1)} %refs_1_.3, f32[512,1536]{1,0:T(8,128)} %get-tuple-element.63.refs_2_.middle_ref, f32[8,1536]{1,0:T(8,128)} %broadcast_in_dim.95.refs_2_.refs_3_), custom_call_target="tpu_custom_call" | custom-call | flops 40000000000 | bytes 16000000 | tf_op jit(solution)/shard_map/exchange_hidden/pallas_call | solution.py:908
  474.2 9.0 %multiply_convert_fusion = (bf16[2048,384]{1,0:T(8,128)(2,1)}, f32[2048,384]{1,0:T(8,128)}) fusion(f32[2048,384]{1,0:T(8,128)S(1)} %copy-done.10, bf16[2048,1536]{1,0:T(8,128)(2,1)} %get-tuple-element.64, bf16[1536,2048]{1,0:T(8,128)(2,1)} %bitcast.137), kind=kOutput, calls=%fused_computation.15 | convolution fusion | flops 2417491968 | bytes 15335424 | tf_op jit(solution)/shard_map/dot_general | solution.py:22
  483.2 11.1 %attend_back_prev.1 = (f32[2048,384]{1,0:T(8,128)}, f32[2048,128]{1,0:T(8,128)}, bf16[2,2048,384]{2,1,0:T(8,128)(2,1)}, f32[2048,128]{1,0:T(8,128)}) custom-call(s32[2,4]{1,0:T(2,128)} %pad_add_fusion.1.ranges_ref, bf16[2048,384]{1,0:T(8,128)(2,1)} %convolution_convert_fusion.3.q_ref, bf16[2048,896]{1,0:T(8,128)(2,1)} %collective-permute-done.1.k_ref.v_ref.t_key_ref, ...), custom_call_target="tpu_custom_call" | custom-call | flops 15000000512 | bytes 25000000 | tf_op jit(solution)/shard_map/attend_back_prev/pallas_call | solution.py:477
  498.5 60.7 %attend_back_own.1 = (bf16[2048,384]{1,0:T(8,128)(2,1)}, f32[2048,384]{1,0:T(8,128)}, f32[2048,384]{1,0:T(8,128)}, f32[2048,128]{1,0:T(8,128)}) custom-call(s32[2,4]{1,0:T(2,128)} %pad_add_fusion.1.ranges_ref, bf16[2048,384]{1,0:T(8,128)(2,1)} %convolution_convert_fusion.3.q_ref, bf16[2048,896]{1,0:T(8,128)(2,1)} %get-tuple-element.52.k_ref.v_ref.t_query_ref.t_key_ref, ...), custom_call_target="tpu_custom_call" | custom-call | flops 80000000000 | bytes 25000000 | tf_op jit(solution)/shard_map/attend_back_own/pallas_call | solution.py:477
  559.2 7.8 convolution_convert_fusion.2
  568.4 4.5 decay_back.1
  572.9 1.9 convert_reduce_fusion.1
  575.2 30.1 %collective-permute-done.3 = bf16[2,2048,384]{2,1,0:T(8,128)(2,1)} collective-permute-done((bf16[2,2048,384]{2,1,0:T(8,128)(2,1)}, bf16[2,2048,384]{2,1,0:T(8,128)(2,1)}, u32[]{:S(2)}, u32[]{:S(2)}) %collective-permute-start.3) | collective-permute-done | bytes 3145760 | tf_op jit(solution)/shard_map/ppermute | solution.py:28
  605.4 1.9 fusion.7
  607.7 2.2 fusion.8
  613.0 2.7 copy-done.26
  615.7 15.5 %select_convert_fusion = bf16[1536,1664]{1,0:T(8,128)(2,1)} fusion(bf16[2048,1536]{1,0:T(8,128)(2,1)} %get-tuple-element.51, bf16[2048,1664]{1,0:T(8,128)(2,1)S(1)} %fusion.9, bf16[1536]{0:T(1024)(128)(2,1)S(1)} %select_reduce_fusion, pred[1664]{0:T(1024)(128)(4,1)S(1)} %copy-done.31), kind=kOutput, calls=%fused_computation.1 | convolution fusion | flops 10471538688 | bytes 18223744 | tf_op jit(solution)/shard_map/dot_general | solution.py:1265
  631.3 28.7 %reduce-scatter.2.cloned.1.call-done = bf16[192,3072]{1,0:T(8,128)(2,1)} async-done(((bf16[1536,3072]{1,0:T(8,128)(2,1)}), bf16[192,3072]{1,0:T(8,128)(2,1)}) %reduce-scatter.2.cloned.1.call-update) | async-done | bytes 1179664 | tf_op jit(solution)/shard_map/reduce_scatter | solution.py:1283
  660.0 3.8 all-to-all-start.1
  663.8 16.9 %convolution_convert_fusion.1.first_ref = bf16[2048,1536]{1,0:T(8,128)(2,1)} fusion(bf16[2048,1664]{1,0:T(8,128)(2,1)} %copy-done.26, bf16[1536,2048]{1,0:T(8,128)(2,1)} %bitcast.138), kind=kOutput, calls=%fused_computation.3 | convolution fusion | flops 10472128512 | bytes 18219008 | tf_op jit(solution)/shard_map/dot_general | solution.py:22
  681.0 103.8 %finish_last.1 = (bf16[4,48,1664]{2,1,0:T(8,128)(2,1)}, bf16[4,48,384]{2,1,0:T(8,128)(2,1)}, f32[512,1536]{1,0:T(8,128)}, bf16[512,1536]{1,0:T(8,128)(2,1)}) custom-call(bf16[8,4,48,1664]{3,2,1,0:T(8,128)(2,1)} %bitcast.140, bf16[8,4,48,384]{3,2,1,0:T(8,128)(2,1)} %bitcast.141, bf16[2048,1536]{1,0:T(8,128)(2,1)} %convolution_convert_fusion.1.first_ref, ...), custom_call_target="tpu_custom_call" | custom-call | flops 80000000000 | bytes 40000000 | tf_op jit(solution)/shard_map/finish_last/pallas_call | solution.py:1052
  (159 shorter events, 36.0 us)
Async XLA Ops:
  7.2 8.0 copy-start.4
  8.0 138.9 %collective-permute-start = (s32[2048]{0:T(1024)S(1)}, s32[2048]{0:T(1024)S(1)}, u32[]{:S(2)}, u32[]{:S(2)}) collective-permute-start(s32[2048]{0:T(1024)S(1)} %broadcast_add_fusion), channel_id=1, source_target_pairs={{0,4},{4,8},{8,12},{12,16},{16,20},{20,24},{24,28},{1,5},{5,9},{9,... | collective-permute-start | bytes 24584 | tf_op jit(solution)/shard_map/ppermute | solution.py:28
  15.3 4.9 copy-start.33
  15.3 4.9 copy-start.35
  15.3 4.9 copy-start.29
  15.3 5.0 copy-start.27
  15.3 5.0 copy-start.20
  15.4 5.0 copy-start.16
  15.4 5.0 copy-start.18
  15.4 5.1 copy-start.17
  16.5 175.3 %all-to-all-start = ((bf16[48,4,3072]{2,0,1:T(8,128)(2,1)}), bf16[48,4,3072]{2,0,1:T(8,128)(2,1)S(1)}, u32[]{:S(2)}, u32[]{:S(2)}) async-start(bf16[48,4,3072]{2,0,1:T(8,128)(2,1)} %pad_maximum_fusion), calls=%async_computation | async-start | bytes 2359296 | tf_op jit(solution)/shard_map/all_to_all | solution.py:1274
  20.1 336.0 %all-gather.2.cloned.1.call-start = ((), (), s32[]{:S(2)}) async-start(), calls=%async_computation.3 | async-start | bytes 10616832 | tf_op jit(solution)/shard_map/all_gather | solution.py:1279
  21.9 94.8 %copy-start.37 = (f32[24]{0:T(128)S(1)}, f32[24]{0:T(128)}, u32[]{:S(2)}) copy-start(f32[24]{0:T(128)} %param.23) | copy-start | bytes 292
  133.7 82.9 %collective-permute-start.1 = (bf16[2048,896]{1,0:T(8,128)(2,1)}, bf16[2048,896]{1,0:T(8,128)(2,1)}, u32[]{:S(2)}, u32[]{:S(2)}) collective-permute-start(bf16[2048,896]{1,0:T(8,128)(2,1)} %get-tuple-element.52.k_ref.v_ref.t_query_ref.t_key_ref), channel_id=1, source_target_pairs={{0,4},{4,8},{8,12},{12,16},{16,20},{20,24},{24,28},{1,5},{5,9},{9,... | collective-permute-start | bytes 11010056 | tf_op jit(solution)/shard_map/ppermute | solution.py:28
  191.8 24.7 %copy-start = (bf16[48,4,3072]{2,0,1:T(8,128)(2,1)}, bf16[48,4,3072]{2,0,1:T(8,128)(2,1)S(1)}, u32[]{:S(2)}) copy-start(bf16[48,4,3072]{2,0,1:T(8,128)(2,1)S(1)} %all-to-all-done) | copy-start | bytes 3538948
  216.6 443.4 %reduce-scatter.2.cloned.1.call-start = ((), (), s32[]{:S(2)}) async-start(), calls=%async_computation.4 | async-start | bytes 10616832 | tf_op jit(solution)/shard_map/reduce_scatter | solution.py:1283
  224.7 9.8 %copy-start.9 = (f32[2048,384]{1,0:T(8,128)}, f32[2048,384]{1,0:T(8,128)S(1)}, u32[]{:S(2)}) copy-start(f32[2048,384]{1,0:T(8,128)S(1)} %add_divide_fusion) | copy-start | bytes 9437188
  431.0 43.2 %copy-start.10 = (f32[2048,384]{1,0:T(8,128)S(1)}, f32[2048,384]{1,0:T(8,128)}, u32[]{:S(2)}) copy-start(f32[2048,384]{1,0:T(8,128)} %copy-done.9) | copy-start | bytes 9437188
  495.9 71.1 %collective-permute-start.2 = (f32[2048,8]{0,1:T(8,128)S(1)}, f32[2048,8]{0,1:T(8,128)S(1)}, u32[]{:S(2)}, u32[]{:S(2)}) collective-permute-start(f32[2048,8]{0,1:T(8,128)S(1)} %copy.114), channel_id=1, source_target_pairs={{4,0},{8,4},{12,8},{16,12},{20,16},{24,20},{28,24},{5,1},{9,5},{13... | collective-permute-start | bytes 196616 | tf_op jit(solution)/shard_map/ppermute | solution.py:28
  497.2 108.2 %collective-permute-start.3 = (bf16[2,2048,384]{2,1,0:T(8,128)(2,1)}, bf16[2,2048,384]{2,1,0:T(8,128)(2,1)}, u32[]{:S(2)}, u32[]{:S(2)}) collective-permute-start(bf16[2,2048,384]{2,1,0:T(8,128)(2,1)} %get-tuple-element.72), channel_id=1, source_target_pairs={{4,0},{8,4},{12,8},{16,12},{20,16},{24,20},{28,24},{5,1},{9,5},{13... | collective-permute-start | bytes 9437192 | tf_op jit(solution)/shard_map/ppermute | solution.py:28
  567.0 5.9 copy-start.32
  568.4 6.3 copy-start.30
  568.4 37.0 %copy-start.3 = (f32[2048,384]{1,0:T(8,128)S(1)}, f32[2048,384]{1,0:T(8,128)}, u32[]{:S(2)}) copy-start(f32[2048,384]{1,0:T(8,128)} %get-tuple-element.71) | copy-start | bytes 9437188
  607.7 3.3 copy-start.13
  612.2 3.5 copy-start.31
  660.0 20.7 %all-to-all-start.1 = ((bf16[4,48,3072]{2,1,0:T(8,128)(2,1)}), bf16[4,48,3072]{2,1,0:T(8,128)(2,1)S(1)}, u32[]{:S(2)}, u32[]{:S(2)}) async-start(bf16[4,48,3072]{2,1,0:T(8,128)(2,1)} %bitcast.113), calls=%async_computation.2 | async-start | bytes 2359296 | tf_op jit(solution)/shard_map/all_to_all | solution.py:1288
  789.9 3.4 copy-start.19
  789.9 3.5 copy-start.21
  789.9 3.9 copy-start.22
  794.9 3.1 copy-start.7
  795.2 2.9 copy-start.1
  795.2 4.5 copy-start.8
  (14 other events, 25.7 us)
Sparse Core Ops, SparseCore 0:
  216.7 139.2 all-gather.1
  431.1 228.8 reduce-scatter.1

commit v3 on v2

--- a/solution.py
+++ b/solution.py
@@ -52,10 +52,11 @@
 
 
 PROJECT_TILE = 256
+TERM_ROWS = 32
 
 
 def project_kernel(local_heads, tokens_ref, gain_ref, weight_ref, bias_ref, input_ref, out_ref,
-                   forget_ref, carry_ref):
+                   terms_ref, turned_ref, forget_ref, carry_ref):
     rows = tokens_ref.shape[0]
     wide = weight_ref.shape[1] - LANES
 
@@ -67,7 +68,7 @@
     input1 = (tokens * inverse_rms(tokens) * gain_ref[0:1, :]).astype(bf16)
     input_ref[...] = input1
     raw = dot(input1, weight_ref[...])
-    out_ref[:, :wide] = raw[:, :wide].astype(bf16)
+    out_ref[...] = raw[:, :wide].astype(bf16)
     forget = (raw[:, wide:] + bias_ref[0:1, :]).astype(bf16).astype(f32)
     forget_ref[...] = forget
     lane = lax.broadcasted_iota(jnp.int32, (rows, LANES), 1)
@@ -79,12 +80,14 @@
     sums = sum(dot(tri, part) for part in split3(logf)) + carry_ref[0:1, :]
     carry_ref[0:1, :] = sums[rows - 1 : rows, :]
     high, mid, low = split3(sums)
-    out_ref[:, wide:] = (
+    terms = (
         high.astype(f32)
         + pltpu.roll(mid.astype(f32), local_heads, 1)
         + pltpu.roll(low.astype(f32), 2 * local_heads, 1)
         + jnp.where(lane == 3 * local_heads, 1.0, 0.0)
     ).astype(bf16)
+    terms_ref[...] = terms
+    turned_ref[...] = terms.T[0:TERM_ROWS, :]
 
 
 def project(tokens, gain, weight, bias, wide, local_heads):
@@ -100,10 +103,18 @@
         functools.partial(project_kernel, local_heads),
         grid=(rows // PROJECT_TILE,),
         in_specs=[tile(width), whole(8, width), whole(width, wide + LANES), whole(8, LANES)],
-        out_specs=[tile(width), tile(wide + LANES), tile(LANES)],
+        out_specs=[
+            tile(width),
+            tile(wide),
+            tile(LANES),
+            pl.BlockSpec((TERM_ROWS, PROJECT_TILE), lambda n: (0, n)),
+            tile(LANES),
+        ],
         out_shape=[
             jax.ShapeDtypeStruct((rows, width), bf16),
-            jax.ShapeDtypeStruct((rows, wide + LANES), bf16),
+            jax.ShapeDtypeStruct((rows, wide), bf16),
+            jax.ShapeDtypeStruct((rows, LANES), bf16),
+            jax.ShapeDtypeStruct((TERM_ROWS, rows), bf16),
             jax.ShapeDtypeStruct((rows, LANES), f32),
         ],
         scratch_shapes=[pltpu.VMEM((8, LANES), f32)],
@@ -188,14 +199,17 @@
     place = placing(pair, local_heads, KEY)
     lane = lax.broadcasted_iota(jnp.int32, (K_TILE, LANES), 1)
     rows = key_ref.shape[0]
-    total = 0.0
     if not own:
-        last = dot(terms_ref[rows - 16 : rows, :], placing(pair, local_heads, TOTAL))
-        total = last[15:16, :]
+        last = terms_ref[:, rows - LANES : rows].T
+        total = dot(last, placing(pair, local_heads, TOTAL)[0:TERM_ROWS, :])[LANES - 1 : LANES, :]
 
     def fill(n, carry):
         here = tile_of(n, K_TILE)
-        extra = (dot(terms_ref[here, :], place) + total).astype(bf16)
+        if own:
+            extra = dot(terms_ref[here, :], place).astype(bf16)
+        else:
+            extra = dot(terms_ref[:, here].T, place[0:TERM_ROWS, :])
+            extra = (extra + total).astype(bf16)
         key = key_ref[here, :]
         keys[0][here, :] = jnp.where(lane < 64, key, extra)
         keys[1][here, :] = jnp.where(lane < 64, extra, key)
@@ -296,11 +310,7 @@
     return pl.BlockSpec((height, rows), lambda p, *_: (p, 0))
 
 
-def terms_block(rows, pairs):
-    return pl.BlockSpec((rows, LANES), lambda p, *_: (0, 2 * pairs))
-
-
-def attend(own, ranges, query, key_value, own_terms, begins, local_heads, so_far=()):
+def attend(own, ranges, query, key_value, terms, key_terms, begins, local_heads, so_far=()):
     rows = query.shape[0]
     pairs = local_heads // 2
     running_specs = [pair_block(LANES, rows), pair_block(8, rows)]
@@ -322,8 +332,8 @@
                 lane_block(rows, 0),
                 lane_block(rows, 0),
                 lane_block(rows, pairs),
-                terms_block(rows, pairs),
-                terms_block(rows, pairs),
+                fixed((rows, LANES)),
+                fixed((rows, LANES) if own else (TERM_ROWS, rows)),
                 fixed((8, rows)),
             ]
             + ([] if own else running_specs),
@@ -343,7 +353,7 @@
             bytes_accessed=12_000_000,
         ),
         name="attend_own" if own else "attend_prev",
-    )(ranges, query, key_value, key_value, own_terms, key_value, begins, *so_far)
+    )(ranges, query, key_value, key_value, terms, key_terms, begins, *so_far)
 
 
 def attend_back_kernel(local_heads, own, ranges_ref, q_ref, k_ref, v_ref, t_query_ref, t_key_ref,
@@ -458,7 +468,7 @@
 
 
 def attend_back(
-    own, ranges, query, key_value, own_terms, begins, grad, mixed, lse, local_heads,
+    own, ranges, query, key_value, terms, key_terms, begins, grad, mixed, lse, local_heads,
     so_far=(),
 ):
     rows = query.shape[0]
@@ -483,8 +493,8 @@
                 lane_block(rows, 0),
                 lane_block(rows, 0),
                 lane_block(rows, pairs),
-                terms_block(rows, pairs),
-                terms_block(rows, pairs),
+                fixed((rows, LANES)),
+                fixed((rows, LANES) if own else (TERM_ROWS, rows)),
                 fixed((8, rows)),
                 lane_block(rows, 0),
                 lane_block(rows, 0),
@@ -512,7 +522,7 @@
         ),
         name="attend_back_own" if own else "attend_back_prev",
     )(
-        ranges, query, key_value, key_value, own_terms, key_value, begins, grad, mixed, lse, *so_far
+        ranges, query, key_value, key_value, terms, key_terms, begins, grad, mixed, lse, *so_far
     )
 
 
@@ -926,61 +936,86 @@
     )(part, *extras)
 
 
-def finish_last_kernel(grad_ref, output_grad_ref, first_ref, down_ref, grad_middle_ref, tokens_ref,
-                       gain_ref, middle_ref, weights_ref, output_ref, tokens_grad_ref, result_ref,
-                       *refs):
-    buffers, (near1, turn1, far1, near2, turn2, far2) = refs[:8], refs[8:14]
-    sems = refs[14:]
+def column_chunks(width):
+    count = max(width // 512, 1)
+    first = width - 512 * (count - 1)
+    return [(0, first)] + [(first + 512 * n, 512) for n in range(count - 1)]
+
+
+def finish_last_kernel(grad_ref, output_grad_ref, second_ref, first_ref, down_ref, grad_middle_ref,
+                       tokens_ref, gain_ref, middle_ref, weights_ref, output_ref, second_out_ref,
+                       tokens_grad_ref, result_ref, *refs):
+    buffers = (refs[0:3], refs[3:6])
+    first_buffers, down_buffers = refs[6:9], refs[9:12]
+    pair_send, pair_recv, line_send, line_recv, swap_send, swap_recv = refs[12:18]
+    first_sems, down_sems = refs[18:22], refs[22:26]
     me, near, far, cross = partners()
+    others = (near, far, cross)
     here, partner, after = blk_peers()
     steps = len(after)
     greet(
-        [on_head(near), on_head(far), on_head(cross), on_blk(partner)]
+        [on_head(other) for other in others]
+        + [on_blk(partner)]
         + [on_blk(peer) for peer in after[1:]]
     )
     size = result_ref.shape[0]
-    first = Sum(first_ref, (near1, turn1, far1), sems[12:16], size, True)
-    down = Sum(down_ref, (near2, turn2, far2), sems[16:20], size, False)
-    sums = (
-        (grad_ref, weights_ref, buffers[:4], sems[:6]),
-        (output_grad_ref, output_ref, buffers[4:], sems[6:12]),
-    )
+    first = Sum(first_ref, first_buffers, first_sems, size, True)
+    down = Sum(down_ref, down_buffers, down_sems, size, False)
+    chunks = []
+    for ref, out_ref, some in (
+        (grad_ref, weights_ref, buffers[0]), (output_grad_ref, output_ref, buffers[1])
+    ):
+        for start, wide in column_chunks(ref.shape[3]):
+            chunks.append((ref, out_ref, some, pl.ds(start, wide)))
+    groups = grad_ref.shape[1]
     first.start()
     sent = []
-    for t in list(range(1, steps)) + [0]:
-        for ref, _, (pair_buf, _, _, _), (pair_send, pair_recv, *_) in sums:
+    for c, (ref, _, (pair_buf, _, _), at) in enumerate(chunks):
+        for t in list(range(1, steps)) + [0]:
             copy = remote(
-                ref.at[after[t] + partner - here],
-                pair_buf.at[t],
-                pair_send.at[t],
-                pair_recv.at[t],
+                ref.at[after[t] + partner - here, :, :, at],
+                pair_buf.at[t, :, :, at],
+                pair_send.at[c, t],
+                pair_recv.at[c, t],
                 on_blk(partner),
             )
             copy.start()
             sent.append(copy)
     first.turn()
+
+    def swap(source_ref, out_ref, c):
+        for kind, other in enumerate(others):
+            copy = remote(
+                source_ref.at[other], out_ref.at[me], swap_send.at[c, kind],
+                swap_recv.at[c, kind], on_head(other),
+            )
+            copy.start()
+            sent.append(copy)
+
+    swap(second_ref, second_out_ref, len(chunks))
     down.start()
     down.turn()
-    lines = []
-    for t in range(1, steps):
-        for ref, _, (pair_buf, turn_buf, line_buf, _), some in sums:
-            pair_send, pair_recv, line_send, line_recv = some[:4]
+
+    def add_up(c):
+        ref, out_ref, (pair_buf, line_buf, row_buf), at = chunks[c]
+        block = pair_buf.at[0, :, :, at]
+        remote(block, block, pair_send.at[c, 0], pair_recv.at[c, 0], on_blk(partner)).wait_recv()
+        for t in range(1, steps):
+            block = line_buf.at[t, :, :, at]
             remote(
-                pair_buf.at[t], pair_buf.at[t], pair_send.at[t], pair_recv.at[t], on_blk(partner)
+                block, block, line_send.at[c, t], line_recv.at[c, t], on_blk(after[t])
             ).wait_recv()
 
-            def add(group, carry):
-                turn_buf[t, group] = (
-                    ref[after[t], group].astype(f32) + pair_buf[t, group].astype(f32)
-                ).astype(bf16)
-                return carry
-
-            lax.fori_loop(0, ref.shape[1], add, 0)
-            copy = remote(
-                turn_buf.at[t], line_buf.at[t], line_send.at[t], line_recv.at[t], on_blk(after[t])
-            )
-            copy.start()
-            lines.append(copy)
+        def add_all(group, carry):
+            total = ref[here, group, :, at].astype(f32) + pair_buf[0, group, :, at].astype(f32)
+            for t in range(1, steps):
+                total = total + line_buf[t, group, :, at].astype(f32)
+            row_buf[group, :, at] = total.astype(bf16)
+            return carry
+
+        lax.fori_loop(0, groups, add_all, 0)
+        out_ref[me, :, at] = row_buf[me, :, at]
+        swap(row_buf.at[:, :, at], out_ref.at[:, :, at], c)
 
     def put(shares, local, out_ref, extra_refs):
         for piece in range(PIECES):
@@ -988,73 +1023,72 @@
             value, _ = local(shares.total(piece), rows, *extra_refs)
             out_ref[rows, :] = value.astype(out_ref.dtype)
 
-    put(first, after_first, tokens_grad_ref, (grad_middle_ref, tokens_ref, gain_ref))
-    swaps = []
-    for ref, out_ref, (pair_buf, _, line_buf, row_buf), some in sums:
-        pair_send, pair_recv, line_send, line_recv, swap_send, swap_recv = some
-        remote(
-            pair_buf.at[0], pair_buf.at[0], pair_send.at[0], pair_recv.at[0], on_blk(partner)
-        ).wait_recv()
+    for c, (ref, _, (pair_buf, line_buf, _), at) in enumerate(chunks):
         for t in range(1, steps):
+            block = pair_buf.at[t, :, :, at]
             remote(
-                line_buf.at[t], line_buf.at[t], line_send.at[t], line_recv.at[t], on_blk(after[t])
+                block, block, pair_send.at[c, t], pair_recv.at[c, t], on_blk(partner)
             ).wait_recv()
 
-        def add_all(group, carry):
-            total = ref[here, group].astype(f32) + pair_buf[0, group].astype(f32)
-            for t in range(1, steps):
-                total = total + line_buf[t, group].astype(f32)
-            row_buf[group] = total.astype(bf16)
-            return carry
-
-        lax.fori_loop(0, ref.shape[1], add_all, 0)
-        for kind, other in enumerate((near, far, cross)):
+            def add(group, carry):
+                pair_buf[t, group, :, at] = (
+                    ref[after[t], group, :, at].astype(f32)
+                    + pair_buf[t, group, :, at].astype(f32)
+                ).astype(bf16)
+                return carry
+
+            lax.fori_loop(0, groups, add, 0)
             copy = remote(
-                row_buf.at[other],
-                out_ref.at[me],
-                swap_send.at[kind],
-                swap_recv.at[kind],
-                on_head(other),
+                block, line_buf.at[t, :, :, at], line_send.at[c, t], line_recv.at[c, t],
+                on_blk(after[t]),
             )
             copy.start()
-            swaps.append(copy)
-        out_ref[me] = row_buf[me]
+            sent.append(copy)
+        if c > 0:
+            add_up(c - 1)
+    put(first, after_first, tokens_grad_ref, (grad_middle_ref, tokens_ref, gain_ref))
+    add_up(len(chunks) - 1)
     put(down, after_down, result_ref, (middle_ref,))
-    for _, out_ref, _, some in sums:
-        for kind, other in enumerate((near, far, cross)):
+    second_out_ref[me] = second_ref[me]
+    for c in range(len(chunks) + 1):
+        if c < len(chunks):
+            _, out_ref, _, at = chunks[c]
+            out_ref = out_ref.at[:, :, at]
+        else:
+            out_ref = second_out_ref
+        for kind, other in enumerate(others):
             block = out_ref.at[other]
             remote(
-                block, block, some[4].at[kind], some[5].at[kind], on_head(other)
+                block, block, swap_send.at[c, kind], swap_recv.at[c, kind], on_head(other)
             ).wait_recv()
-    for copy in sent + lines + swaps:
+    for copy in sent:
         copy.wait_send()
     first.finish()
     down.finish()
 
 
-def finish_last(grad, output_grad, groups, part_first, part_down, grad_middle, tokens, gain, middle,
-                number):
+def finish_last(grad, output_grad, second, groups, part_first, part_down, grad_middle, tokens, gain,
+                middle, number):
     peers = lax.axis_size("blk")
     share = grad.shape[0] // (peers * groups)
     rows, width = tokens.shape
     vmem = pl.BlockSpec(memory_space=pltpu.VMEM)
     half = peers // 2
     widths = (grad.shape[1], output_grad.shape[1])
+    chunks = sum(len(column_chunks(width)) for width in widths)
 
     def blocks(columns):
-        return [pltpu.VMEM((half, groups, share, columns), bf16) for _ in range(3)] + [
+        return [pltpu.VMEM((half, groups, share, columns), bf16) for _ in range(2)] + [
             pltpu.VMEM((groups, share, columns), bf16)
         ]
 
-    swap_sems = [pltpu.SemaphoreType.DMA((half,)) for _ in range(4)] + [
-        pltpu.SemaphoreType.DMA((3,)) for _ in range(2)
-    ]
     return pl.pallas_call(
         finish_last_kernel,
-        in_specs=[vmem] * 8,
-        out_specs=[vmem] * 4,
+        in_specs=[vmem] * 9,
+        out_specs=[vmem] * 5,
         out_shape=[
-            jax.ShapeDtypeStruct((groups, share, columns), bf16) for columns in widths
+            jax.ShapeDtypeStruct((groups, share, columns), bf16)
+            for columns in widths + (second.shape[1],)
         ]
         + [
             jax.ShapeDtypeStruct((rows, width), f32),
@@ -1064,8 +1098,8 @@
         + blocks(widths[1])
         + sum_buffers(rows, width)
         + sum_buffers(rows, width)
-        + swap_sems
-        + swap_sems
+        + [pltpu.SemaphoreType.DMA((chunks, half)) for _ in range(4)]
+        + [pltpu.SemaphoreType.DMA((chunks + 1, 3)) for _ in range(2)]
         + sum_sems()
         + sum_sems(),
         compiler_params=pltpu.CompilerParams(
@@ -1078,6 +1112,7 @@
     )(
         grad.reshape(peers, groups, share, widths[0]),
         output_grad.reshape(peers, groups, share, widths[1]),
+        second.reshape(groups, share, second.shape[1]),
         part_first, part_down, grad_middle, tokens, gain, middle,
     )
 
@@ -1283,14 +1318,6 @@
     return lax.psum_scatter(grad, "blk", scatter_dimension=0, tiled=True)
 
 
-def own_rows(summed, groups):
-    rows, columns = summed.shape
-    parts = lax.all_to_all(
-        summed.reshape(groups, rows // groups, columns), "head", split_axis=0, concat_axis=0
-    )
-    return jnp.swapaxes(parts, 0, 1).astype(f32)
-
-
 def body(
     tokens,
     segment,
@@ -1356,21 +1383,25 @@
     gain1, gain2 = gain_rows(0), gain_rows(1)
     bias = lax.dynamic_slice_in_dim(forget_bias, group * local_heads, local_heads, 0)
     bias = jnp.broadcast_to(jnp.pad(bias, (0, LANES - local_heads))[None, :], (8, LANES))
-    input1, key_value, forget = project(
+    input1, key_value, terms, turned_terms, forget = project(
         tokens_all, gain1, first, bias, 2 * local_width, local_heads
     )
     earlier_kv = passed_along(key_value, "blk", 1)
+    earlier_terms = passed_along(turned_terms, "blk", 1)
     query = dot(input1, first[:, kv_width : kv_width + local_width]).astype(bf16)
     gate_raw = dot(
         input1, first[:, kv_width + local_width : kv_width + 2 * local_width]
     )
 
-    so_far = attend(True, ranges, query, key_value, key_value, begins, local_heads)
-    mine = sent_columns([low(w_gate), low(w_up), low(w_down)], groups)
-    mine, earlier_kv, so_far = lax.optimization_barrier((mine, earlier_kv, so_far))
+    so_far = attend(True, ranges, query, key_value, terms, terms, begins, local_heads)
+    later = lax.optimization_barrier((low(w_gate), low(w_up), low(w_down), key_value))
+    mine = sent_columns(later[:3], groups)
+    mine, earlier_kv, earlier_terms, so_far = lax.optimization_barrier(
+        (mine, earlier_kv, earlier_terms, so_far)
+    )
     second = all_rows(mine)
     attended, lse = attend(
-        False, ranges, query, earlier_kv, key_value, begins, local_heads, so_far
+        False, ranges, query, earlier_kv, terms, earlier_terms, begins, local_heads, so_far
     )
     opened = jax.nn.sigmoid(gate_raw)
     attended_wide = attended.astype(f32)
@@ -1389,14 +1420,14 @@
     grad_attended = (grad_gated * opened).astype(bf16)
     grad_gate_pre = (grad_gated * attended_wide * opened * (1.0 - opened)).astype(bf16)
     dq_prev, rows_prev, dkv_prev, decay_prev = attend_back(
-        False, ranges, query, earlier_kv, key_value, begins, grad_attended, attended,
+        False, ranges, query, earlier_kv, terms, earlier_terms, begins, grad_attended, attended,
         lse, local_heads,
     )
     dkv_later = passed_along(dkv_prev, "blk", -1)
     decay_later = passed_along(decay_prev[:, :8], "blk", -1)
     decay_later = jnp.pad(decay_later, ((0, 0), (0, LANES - 8)))
     dq, dk_own, dv_own, decay_own = attend_back(
-        True, ranges, query, key_value, key_value, begins, grad_attended, attended,
+        True, ranges, query, key_value, terms, terms, begins, grad_attended, attended,
         lse, local_heads, (dq_prev, rows_prev),
     )
     dk = (dk_own + dkv_later[0].astype(f32)).astype(bf16)
@@ -1418,13 +1449,13 @@
     ).astype(bf16)
     output_grad = over_tokens(grad_branch, gated).astype(bf16)
     grad_input1 = dot(grads, first[:, : kv_width + 2 * local_width], NT).astype(bf16)
-    second_sum = own_rows(second_part, groups)
-    grad_input1, second_sum = lax.optimization_barrier((grad_input1, second_sum))
-    first_sum, output_sum, tokens_grad, result = finish_last(
-        first_grad, output_grad, groups, grad_input1, down, grad_middle, tokens, gain1, middle, 3
-    )
-    first_sum = jnp.swapaxes(first_sum, 0, 1).astype(f32)
-    output_sum = jnp.swapaxes(output_sum, 0, 1).astype(f32)
+    first_sum, output_sum, second_sum, tokens_grad, result = finish_last(
+        first_grad, output_grad, second_part, groups, grad_input1, down, grad_middle, tokens,
+        gain1, middle, 3,
+    )
+    first_sum, output_sum, second_sum = (
+        jnp.swapaxes(array, 0, 1).astype(f32) for array in (first_sum, output_sum, second_sum)
+    )
 
     def columns(array, start, width):
         return array[:, :, start : start + width].reshape(share, groups * width)

time: 813 us -> 775 us (0.953)
  waiting for transfers between devices: 118 us -> 97.9 us
  Pallas kernels: 536 us -> 524 us
    reduce_scatter x1, waiting for transfers between devices: 28.7 us -> 17.4 us  [row_sums(): return lax.psum_scatter(grad, 'blk', scatter_dimension=0, tiled=True)]
    pallas_call x1, Pallas kernels: 93.1 us -> 84.4 us  [gather_first(): pl.pallas_call(gather_first_kernel, in_specs=[vmem] * 3, out_specs=[anywh...]
    ppermute x4 -> x5, waiting for transfers between devices: 54.9 us -> 46.3 us  [passed_along(): return lax.ppermute(array, axis, pairs)]
  transfers between devices with their start and end apart: 8 -> 8, of which waited for: 4 -> 4; matrix products, arithmetic and copies ran while one was open for 12% -> 13% of each run, Pallas kernels for 44% -> 44%
where the time goes in v3:
time: 775 us; the launch traced here: 771 us
  Pallas kernels  524 us (68%)
  waiting for transfers between devices  97.9 us (13%)
  matrix products  67.8 us (9%)
  other arithmetic  27.7 us (4%)
  starting transfers between devices  20 us (3%)
  local copies, waits for them, and re-layouts  18.5 us (2%)
  between operations  15.2 us (2%)
    pallas_call x2, Pallas kernels, exchange(): pl.pallas_call(functools.partial(exchange_kernel, local, len(extras), sum...  122 us
    pallas_call x1, Pallas kernels, finish_last(): pl.pallas_call(finish_last_kernel, in_specs=[vmem] * 9, out_specs=[vmem]...  107 us
    pallas_call x1, Pallas kernels, gather_first(): pl.pallas_call(gather_first_kernel, in_specs=[vmem] * 3, out_specs=[anywh...  84.4 us
    pallas_call x1, Pallas kernels, feed(): pl.pallas_call(feed_kernel, grid=(tiles + columns // FEED_COLUMNS,), in_s...  75 us
    pallas_call x2, Pallas kernels, attend_back(): pl.pallas_call(functools.partial(attend_back_kernel, local_heads, own), g...  67.7 us
    pallas_call x2, Pallas kernels, attend(): pl.pallas_call(functools.partial(attend_kernel, local_heads, own), grid_s...  46.6 us
    ppermute x5, waiting for transfers between devices, passed_along(): return lax.ppermute(array, axis, pairs)  46.3 us
    dot_general x5, matrix products, dot(): return lax.dot_general(a, b, dims, preferred_element_type=f32, **kw)  46.3 us
  transfers between devices with their start and end apart: 8, of which 4 were waited for; matrix products, arithmetic and copies ran while one was open for 13% of the time, Pallas kernels for 44%

profile of v3, /device:TPU:0, one launch (start us, length us, event | category | flops | bytes accessed | tf_op | source)
XLA Modules:
  0.0 771.3 jit_solution(5808658204828372446)
XLA Ops:
  7.9 4.8 collective-permute-start
  21.2 84.4 %gather_first.1 = (bf16[8,4,48,2048]{3,2,1,0:T(8,128)(2,1)}, bf16[2048,1536]{1,0:T(8,128)(2,1)}, bf16[2048,1536]{1,0:T(8,128)(2,1)}) custom-call(bf16[4,48,2048]{2,1,0:T(8,128)(2,1)} %bitcast.127, bf16[512,1536]{1,0:T(8,128)(2,1)} %tokens_ref.3, bf16[512,1536]{1,0:T(8,128)(2,1)} %refs_1_.3), custom_call_target="tpu_custom_call" | custom-call | flops 70000001024 | bytes 30000000 | tf_op jit(solution)/shard_map/gather_first/pallas_call | solution.py:789
  105.6 1.8 convert_reduce_fusion.2
  108.7 16.3 %project.1 = (bf16[2048,1536]{1,0:T(8,128)(2,1)}, bf16[2048,768]{1,0:T(8,128)(2,1)}, bf16[2048,128]{1,0:T(8,128)(2,1)}, bf16[32,2048]{1,0:T(8,128)(2,1)}, f32[2048,128]{1,0:T(8,128)}) custom-call(bf16[2048,1536]{1,0:T(8,128)(2,1)} %get-tuple-element.54.tokens_ref, f32[8,1536]{1,0:T(8,128)} %broadcast_in_dim.53.gain_ref, bf16[1536,2048]{1,0:T(8,128)(2,1)} %bitcast.136, ...), custom_call_target="tpu_custom_call" | custom-call | flops 5637144576 | bytes 20000000 | tf_op jit(solution)/shard_map/project/pallas_call | solution.py:102
  125.1 3.5 collective-permute-start.2
  128.5 5.0 collective-permute-start.1
  134.9 3.5 all-to-all-start
  138.7 7.7 convolution_convert_fusion.3.q_ref
  146.4 3.3 convert_reduce_fusion
  151.2 36.9 %attend_own.1 = (f32[384,2048]{1,0:T(8,128)}, f32[24,2048]{1,0:T(8,128)}) custom-call(s32[2,4]{1,0:T(2,128)} %pad_add_fusion.1.ranges_ref, bf16[2048,384]{1,0:T(8,128)(2,1)} %convolution_convert_fusion.3.q_ref, bf16[2048,768]{1,0:T(8,128)(2,1)} %get-tuple-element.57.k_ref.v_ref, bf16[2048,768]{1,0:T(8,128)(2,1)} %get-tuple-element.57.k_ref.v_ref, ...), custom_call_target="tpu_custom_call" | custom-call | flops 40000000000 | bytes 12000000 | tf_op jit(solution)/shard_map/attend_own/pallas_call | solution.py:326
  188.1 11.7 %collective-permute-done.1.k_ref.v_ref = bf16[2048,768]{1,0:T(8,128)(2,1)} collective-permute-done((bf16[2048,768]{1,0:T(8,128)(2,1)}, bf16[2048,768]{1,0:T(8,128)(2,1)}, u32[]{:S(2)}, u32[]{:S(2)}) %collective-permute-start.1) | collective-permute-done | bytes 3145760 | tf_op jit(solution)/shard_map/ppermute | solution.py:28
  201.9 6.1 add_divide_fusion
  208.0 9.7 %attend_prev.1 = (bf16[2048,384]{1,0:T(8,128)(2,1)}, f32[24,2048]{1,0:T(8,128)}) custom-call(s32[2,4]{1,0:T(2,128)} %pad_add_fusion.1.ranges_ref, bf16[2048,384]{1,0:T(8,128)(2,1)} %convolution_convert_fusion.3.q_ref, bf16[2048,768]{1,0:T(8,128)(2,1)} %collective-permute-done.1.k_ref.v_ref, bf16[2048,768]{1,0:T(8,128)(2,1)} %collective-permute-done.1.k_ref.v_ref, ...), custom_call_target="tpu_custom_call" | custom-call | flops 10000000000 | bytes 12000000 | tf_op jit(solution)/shard_map/attend_prev/pallas_call | solution.py:326
  217.7 8.0 %convolution_convert_fusion.refs_0_ = bf16[2048,1536]{1,0:T(8,128)(2,1)} fusion(bf16[1536,2048]{1,0:T(8,128)(2,1)} %bitcast.139, f32[2048,384]{1,0:T(8,128)S(1)} %add_divide_fusion, bf16[2048,384]{1,0:T(8,128)(2,1)} %get-tuple-element.69.o_ref), kind=kOutput, calls=%fused_computation.2 | convolution fusion | flops 2421424128 | bytes 12189696 | tf_op jit(solution)/shard_map/dot_general | solution.py:22
  226.3 79.3 %exchange_middle.1 = (f32[512,1536]{1,0:T(8,128)}, bf16[2048,1536]{1,0:T(8,128)(2,1)}) custom-call(bf16[2048,1536]{1,0:T(8,128)(2,1)} %convolution_convert_fusion.refs_0_, bf16[512,1536]{1,0:T(8,128)(2,1)} %tokens_ref.3, f32[8,1536]{1,0:T(8,128)} %broadcast_in_dim.95.refs_2_.refs_3_), custom_call_target="tpu_custom_call" | custom-call | flops 70000001024 | bytes 16000000 | tf_op jit(solution)/shard_map/exchange_middle/pallas_call | solution.py:918
  305.6 34.1 %all-gather.2.cloned.1.call-done.weight_ref = bf16[1536,3072]{1,0:T(8,128)(2,1)} async-done(((bf16[192,3072]{1,0:T(8,128)(2,1)}), bf16[1536,3072]{1,0:T(8,128)(2,1)}) %all-gather.2.cloned.1.call-update) | async-done | bytes 9437200 | tf_op jit(solution)/shard_map/all_gather | solution.py:1314
  339.7 75.0 %feed.1 = (bf16[2048,1536]{1,0:T(8,128)(2,1)}, bf16[1536,3072]{1,0:T(8,128)(2,1)}, f32[512,1536]{1,0:T(8,128)}) custom-call(bf16[2048,1536]{1,0:T(8,128)(2,1)} %get-tuple-element.70.input_ref, bf16[2048,1536]{1,0:T(8,128)(2,1)} %get-tuple-element.71.cotangent_ref, bf16[1536,3072]{1,0:T(8,128)(2,1)} %all-gather.2.cloned.1.call-done.weight_ref), custom_call_target="tpu_custom_call" | custom-call | flops 57982058496 | bytes 45000000 | tf_op jit(solution)/shard_map/feed/pallas_call | solution.py:1262
  414.8 43.1 %exchange_hidden.1 = (f32[512,1536]{1,0:T(8,128)}, bf16[2048,1536]{1,0:T(8,128)(2,1)}) custom-call(f32[512,1536]{1,0:T(8,128)} %get-tuple-element.73.refs_0_, bf16[512,1536]{1,0:T(8,128)(2,1)} %refs_1_.3, f32[512,1536]{1,0:T(8,128)} %get-tuple-element.74.refs_2_.middle_ref, f32[8,1536]{1,0:T(8,128)} %broadcast_in_dim.95.refs_2_.refs_3_), custom_call_target="tpu_custom_call" | custom-call | flops 40000000000 | bytes 16000000 | tf_op jit(solution)/shard_map/exchange_hidden/pallas_call | solution.py:918
  457.9 8.9 %multiply_convert_fusion = (bf16[2048,384]{1,0:T(8,128)(2,1)}, f32[2048,384]{1,0:T(8,128)}) fusion(f32[2048,384]{1,0:T(8,128)S(1)} %copy-done.11, bf16[2048,1536]{1,0:T(8,128)(2,1)} %get-tuple-element.75, bf16[1536,2048]{1,0:T(8,128)(2,1)} %bitcast.140), kind=kOutput, calls=%fused_computation.15 | convolution fusion | flops 2417491968 | bytes 15335424 | tf_op jit(solution)/shard_map/dot_general | solution.py:22
  466.8 10.9 %attend_back_prev.1 = (f32[2048,384]{1,0:T(8,128)}, f32[2048,128]{1,0:T(8,128)}, bf16[2,2048,384]{2,1,0:T(8,128)(2,1)}, f32[2048,128]{1,0:T(8,128)}) custom-call(s32[2,4]{1,0:T(2,128)} %pad_add_fusion.1.ranges_ref, bf16[2048,384]{1,0:T(8,128)(2,1)} %convolution_convert_fusion.3.q_ref, bf16[2048,768]{1,0:T(8,128)(2,1)} %collective-permute-done.1.k_ref.v_ref, ...), custom_call_target="tpu_custom_call" | custom-call | flops 15000000512 | bytes 25000000 | tf_op jit(solution)/shard_map/attend_back_prev/pallas_call | solution.py:487
  481.9 56.9 %attend_back_own.1 = (bf16[2048,384]{1,0:T(8,128)(2,1)}, f32[2048,384]{1,0:T(8,128)}, f32[2048,384]{1,0:T(8,128)}, f32[2048,128]{1,0:T(8,128)}) custom-call(s32[2,4]{1,0:T(2,128)} %pad_add_fusion.1.ranges_ref, bf16[2048,384]{1,0:T(8,128)(2,1)} %convolution_convert_fusion.3.q_ref, bf16[2048,768]{1,0:T(8,128)(2,1)} %get-tuple-element.57.k_ref.v_ref, ...), custom_call_target="tpu_custom_call" | custom-call | flops 80000000000 | bytes 25000000 | tf_op jit(solution)/shard_map/attend_back_own/pallas_call | solution.py:487
  538.7 7.7 convolution_convert_fusion.2
  547.8 4.5 decay_back.1
  552.3 1.9 convert_reduce_fusion.1
  554.7 34.6 %collective-permute-done.4 = bf16[2,2048,384]{2,1,0:T(8,128)(2,1)} collective-permute-done((bf16[2,2048,384]{2,1,0:T(8,128)(2,1)}, bf16[2,2048,384]{2,1,0:T(8,128)(2,1)}, u32[]{:S(2)}, u32[]{:S(2)}) %collective-permute-start.4) | collective-permute-done | bytes 3145760 | tf_op jit(solution)/shard_map/ppermute | solution.py:28
  589.3 1.9 fusion.7
  591.7 2.2 fusion.8
  596.9 15.6 %convolution_convert_fusion.1.first_ref = bf16[2048,1536]{1,0:T(8,128)(2,1)} fusion(bf16[2048,1664]{1,0:T(8,128)(2,1)S(1)} %fusion.9, bf16[1536,2048]{1,0:T(8,128)(2,1)} %bitcast.141), kind=kOutput, calls=%fused_computation.3 | convolution fusion | flops 10472128512 | bytes 18219008 | tf_op jit(solution)/shard_map/dot_general | solution.py:22
  612.5 13.8 %select_convert_fusion = bf16[1536,1664]{1,0:T(8,128)(2,1)} fusion(bf16[2048,1536]{1,0:T(8,128)(2,1)S(1)} %bitcast.147, bf16[2048,1664]{1,0:T(8,128)(2,1)S(1)} %fusion.9, bf16[1536]{0:T(1024)(128)(2,1)S(1)} %select_reduce_fusion, pred[1664]{0:T(1024)(128)(4,1)S(1)} %copy-done.29), kind=kOutput, calls=%fused_computation.1 | convolution fusion | flops 10471538688 | bytes 18223744 | tf_op jit(solution)/shard_map/dot_general | solution.py:1300
  626.3 17.4 %reduce-scatter.2.cloned.1.call-done = bf16[192,3072]{1,0:T(8,128)(2,1)} async-done(((bf16[1536,3072]{1,0:T(8,128)(2,1)}), bf16[192,3072]{1,0:T(8,128)(2,1)}) %reduce-scatter.2.cloned.1.call-update) | async-done | bytes 1179664 | tf_op jit(solution)/shard_map/reduce_scatter | solution.py:1318
  643.8 107.2 %finish_last.1 = (bf16[4,48,1664]{2,1,0:T(8,128)(2,1)}, bf16[4,48,384]{2,1,0:T(8,128)(2,1)}, bf16[4,48,3072]{2,1,0:T(8,128)(2,1)}, f32[512,1536]{1,0:T(8,128)}, bf16[512,1536]{1,0:T(8,128)(2,1)}) custom-call(bf16[8,4,48,1664]{3,2,1,0:T(8,128)(2,1)} %bitcast.144, bf16[8,4,48,384]{3,2,1,0:T(8,128)(2,1)} %bitcast.145, bf16[4,48,3072]{2,1,0:T(8,128)(2,1)} %bitcast.143, ...), custom_call_target="tpu_custom_call" | custom-call | flops 80000000000 | bytes 40000000 | tf_op jit(solution)/shard_map/finish_last/pallas_call | solution.py:1085
  762.3 1.7 copy.160
  (159 shorter events, 36.8 us)
Async XLA Ops:
  7.9 138.5 %collective-permute-start = (s32[2048]{0:T(1024)S(1)}, s32[2048]{0:T(1024)S(1)}, u32[]{:S(2)}, u32[]{:S(2)}) collective-permute-start(s32[2048]{0:T(1024)S(1)} %broadcast_add_fusion), channel_id=1, source_target_pairs={{0,4},{4,8},{8,12},{12,16},{16,20},{20,24},{24,28},{1,5},{5,9},{9,... | collective-permute-start | bytes 24584 | tf_op jit(solution)/shard_map/ppermute | solution.py:28
  21.2 86.2 %copy-start.34 = (f32[24]{0:T(128)S(1)}, f32[24]{0:T(128)}, u32[]{:S(2)}) copy-start(f32[24]{0:T(128)} %param.23) | copy-start | bytes 292
  108.7 24.9 %copy-start.26 = (f32[48,4096]{1,0:T(8,128)S(1)}, f32[48,4096]{1,0:T(8,128)}, u32[]{:S(2)}) copy-start(f32[48,4096]{1,0:T(8,128)} %param.28) | copy-start | bytes 2359300
  108.7 24.9 %copy-start.6 = (f32[48,4096]{1,0:T(8,128)S(1)}, f32[48,4096]{1,0:T(8,128)}, u32[]{:S(2)}) copy-start(f32[48,4096]{1,0:T(8,128)} %param.26) | copy-start | bytes 2359300
  108.7 25.0 %copy-start.4 = (f32[48,4096]{1,0:T(8,128)S(1)}, f32[48,4096]{1,0:T(8,128)}, u32[]{:S(2)}) copy-start(f32[48,4096]{1,0:T(8,128)} %param.27) | copy-start | bytes 2359300
  125.1 63.0 %collective-permute-start.2 = (bf16[32,2048]{1,0:T(8,128)(2,1)}, bf16[32,2048]{1,0:T(8,128)(2,1)S(1)}, u32[]{:S(2)}, u32[]{:S(2)}) collective-permute-start(bf16[32,2048]{1,0:T(8,128)(2,1)} %get-tuple-element.62), channel_id=1, source_target_pairs={{0,4},{4,8},{8,12},{12,16},{16,20},{20,24},{24,28},{1,5},{5,9},{9,... | collective-permute-start | bytes 393224 | tf_op jit(solution)/shard_map/ppermute | solution.py:28
  128.5 71.3 %collective-permute-start.1 = (bf16[2048,768]{1,0:T(8,128)(2,1)}, bf16[2048,768]{1,0:T(8,128)(2,1)}, u32[]{:S(2)}, u32[]{:S(2)}) collective-permute-start(bf16[2048,768]{1,0:T(8,128)(2,1)} %get-tuple-element.57.k_ref.v_ref), channel_id=1, source_target_pairs={{0,4},{4,8},{8,12},{12,16},{16,20},{20,24},{24,28},{1,5},{5,9},{9,... | collective-permute-start | bytes 9437192 | tf_op jit(solution)/shard_map/ppermute | solution.py:28
  134.9 53.2 %all-to-all-start = ((bf16[48,4,3072]{2,0,1:T(8,128)(2,1)}), bf16[48,4,3072]{2,0,1:T(8,128)(2,1)S(1)}, u32[]{:S(2)}, u32[]{:S(2)}) async-start(bf16[48,4,3072]{2,0,1:T(8,128)(2,1)} %pad_maximum_fusion), calls=%async_computation | async-start | bytes 2359296 | tf_op jit(solution)/shard_map/all_to_all | solution.py:1309
  138.5 201.2 %all-gather.2.cloned.1.call-start = ((), (), s32[]{:S(2)}) async-start(), calls=%async_computation.2 | async-start | bytes 10616832 | tf_op jit(solution)/shard_map/all_gather | solution.py:1314
  188.1 19.9 %copy-start.33 = (bf16[32,2048]{1,0:T(8,128)(2,1)}, bf16[32,2048]{1,0:T(8,128)(2,1)S(1)}, u32[]{:S(2)}) copy-start(bf16[32,2048]{1,0:T(8,128)(2,1)S(1)} %collective-permute-done.2.t_key_ref) | copy-start | bytes 393220
  188.1 11.7 %copy-start = (bf16[48,4,3072]{2,0,1:T(8,128)(2,1)}, bf16[48,4,3072]{2,0,1:T(8,128)(2,1)S(1)}, u32[]{:S(2)}) copy-start(bf16[48,4,3072]{2,0,1:T(8,128)(2,1)S(1)} %all-to-all-done) | copy-start | bytes 3538948
  199.9 443.9 %reduce-scatter.2.cloned.1.call-start = ((), (), s32[]{:S(2)}) async-start(), calls=%async_computation.3 | async-start | bytes 10616832 | tf_op jit(solution)/shard_map/reduce_scatter | solution.py:1318
  208.0 9.7 %copy-start.10 = (f32[2048,384]{1,0:T(8,128)}, f32[2048,384]{1,0:T(8,128)S(1)}, u32[]{:S(2)}) copy-start(f32[2048,384]{1,0:T(8,128)S(1)} %add_divide_fusion) | copy-start | bytes 9437188
  414.8 43.1 %copy-start.11 = (f32[2048,384]{1,0:T(8,128)S(1)}, f32[2048,384]{1,0:T(8,128)}, u32[]{:S(2)}) copy-start(f32[2048,384]{1,0:T(8,128)} %copy-done.10) | copy-start | bytes 9437188
  479.3 67.2 %collective-permute-start.3 = (f32[2048,8]{0,1:T(8,128)S(1)}, f32[2048,8]{0,1:T(8,128)S(1)}, u32[]{:S(2)}, u32[]{:S(2)}) collective-permute-start(f32[2048,8]{0,1:T(8,128)S(1)} %copy.111), channel_id=1, source_target_pairs={{4,0},{8,4},{12,8},{16,12},{20,16},{24,20},{28,24},{5,1},{9,5},{13... | collective-permute-start | bytes 196616 | tf_op jit(solution)/shard_map/ppermute | solution.py:28
  480.6 108.7 %collective-permute-start.4 = (bf16[2,2048,384]{2,1,0:T(8,128)(2,1)}, bf16[2,2048,384]{2,1,0:T(8,128)(2,1)}, u32[]{:S(2)}, u32[]{:S(2)}) collective-permute-start(bf16[2,2048,384]{2,1,0:T(8,128)(2,1)} %get-tuple-element.83), channel_id=1, source_target_pairs={{4,0},{8,4},{12,8},{16,12},{20,16},{24,20},{28,24},{5,1},{9,5},{13... | collective-permute-start | bytes 9437192 | tf_op jit(solution)/shard_map/ppermute | solution.py:28
  546.5 5.9 copy-start.30
  547.8 6.3 copy-start.28
  547.8 41.4 %copy-start.3 = (f32[2048,384]{1,0:T(8,128)S(1)}, f32[2048,384]{1,0:T(8,128)}, u32[]{:S(2)}) copy-start(f32[2048,384]{1,0:T(8,128)} %get-tuple-element.82) | copy-start | bytes 9437188
  591.6 2.8 copy-start.13
  591.6 3.3 copy-start.14
  596.1 16.4 %slice-start = ((s8[6291456]{0:T(1024)(128)(4,1)}), s8[4194304]{0:T(1024)(128)(4,1)S(1)}, s32[]{:S(2)}) async-start(s8[6291456]{0:T(1024)(128)(4,1)} %bitcast.146), calls=%async_computation.4 | async-start | bytes 8388608
  596.9 15.6 %copy-start.29 = (pred[1664]{0:T(1024)(128)(4,1)S(1)}, pred[1664]{0:T(1024)(128)(4,1)}, u32[]{:S(2)}) copy-start(pred[1664]{0:T(1024)(128)(4,1)} %iota_compare_fusion.1) | copy-start | bytes 4996
  596.9 15.6 %slice-start.1 = ((s8[6291456]{0:T(1024)(128)(4,1)}), s8[2097152]{0:T(1024)(128)(4,1)S(1)}, s32[]{:S(2)}) async-start(s8[6291456]{0:T(1024)(128)(4,1)} %bitcast.146), calls=%async_computation.5 | async-start | bytes 4194304
  751.0 5.2 copy-start.18
  752.2 4.9 copy-start.19
  753.0 4.2 copy-start.20
  753.1 4.3 copy-start.21
  753.1 4.5 copy-start.17
  759.2 3.1 copy-start.8
  759.4 2.9 copy-start.1
  759.5 4.5 copy-start.9
  (13 other events, 20.2 us)
Sparse Core Ops, SparseCore 0:
  200.0 139.6 all-gather.1
  414.9 228.8 reduce-scatter.1

commit v4 on v3

--- a/solution.py
+++ b/solution.py
@@ -884,21 +884,42 @@
     ]
 
 
-def exchange_kernel(local, extras, summed, *refs):
+def exchange_kernel(local, extras, summed, weights, *refs):
     part_ref, extra_refs = refs[0], refs[1 : 1 + extras]
-    out_ref, all_ref, payload = refs[1 + extras : 4 + extras]
-    sems = refs[4 + extras :]
+    refs = refs[1 + extras :]
+    if weights:
+        mine_ref, refs = refs[0], refs[1:]
+    out_ref, all_ref, refs = refs[0], refs[1], refs[2:]
+    if weights:
+        weight_ref, refs = refs[0], refs[1:]
+    payload, sems = refs[0], refs[1:]
     size = out_ref.shape[0]
     span = size // PIECES
     _, near, far, _ = partners()
-    greet([on_head(near), on_head(far)])
+    if weights:
+        kinds = mine_ref.shape[0]
+        line = Line(lambda kind, blk: weight_ref.at[blk, kind], kinds, sems[-7:-1])
+        own = pltpu.make_async_copy(mine_ref, weight_ref.at[lax.axis_index("blk")], sems[-1])
+        own.start()
+        line.greet([on_head(near), on_head(far)])
+    else:
+        greet([on_head(near), on_head(far)])
     slots = Slots(summed)
     if not summed:
-        shares = Sum(part_ref, sems[7:10], sems[10:], size, True)
+        shares = Sum(part_ref, sems[7:10], sems[10:14], size, True)
         shares.start()
+    if weights:
+        own.wait()
+        for kind in range(kinds):
+            line.launch(kind)
+    if not summed:
         shares.turn()
     sent = []
     for piece in range(PIECES):
+        if weights and piece != 2:
+            hop = {0: 1, 1: 2, 3: 3}[piece]
+            for t in range(hop, line.half if piece == 3 else min(hop + 1, line.half)):
+                line.step(t)
         here = slice(piece * span, (piece + 1) * span)
         total = part_ref[here, :] if summed else shares.total(piece)
         result, share = local(total, here, *extra_refs)
@@ -909,23 +930,37 @@
     hand_on(all_ref, size, sems[:7], sent, slots)()
     if not summed:
         shares.finish()
-
-
-def exchange(local, part, extras, summed, number, name):
+    if weights:
+        line.finish()
+
+
+def exchange(local, part, extras, summed, number, name, mine=None):
     rows, width = part.shape
     size = rows if summed else rows // 4
-    vmem = pl.BlockSpec(memory_space=pltpu.VMEM)
+    vmem, anywhere = pl.BlockSpec(memory_space=pltpu.VMEM), pl.BlockSpec(memory_space=pl.ANY)
+    weights = mine is not None
+    inputs = [part, *extras]
+    out_specs = [vmem, anywhere]
+    out_shape = [
+        jax.ShapeDtypeStruct((size, width), f32),
+        jax.ShapeDtypeStruct((4 * size, width), bf16),
+    ]
+    scratch = [pltpu.VMEM((size, width), bf16)] + gather_sems()
+    if not summed:
+        scratch += sum_buffers(size, width) + sum_sems()
+    if weights:
+        peers = lax.axis_size("blk")
+        inputs.append(mine)
+        out_specs.append(anywhere)
+        out_shape.append(jax.ShapeDtypeStruct((peers,) + mine.shape, bf16))
+        scratch += [pltpu.SemaphoreType.DMA((mine.shape[0], peers // 2)) for _ in range(6)]
+        scratch.append(pltpu.SemaphoreType.DMA)
     return pl.pallas_call(
-        functools.partial(exchange_kernel, local, len(extras), summed),
-        in_specs=[vmem] * (1 + len(extras)),
-        out_specs=[vmem, pl.BlockSpec(memory_space=pl.ANY)],
-        out_shape=[
-            jax.ShapeDtypeStruct((size, width), f32),
-            jax.ShapeDtypeStruct((4 * size, width), bf16),
-        ],
-        scratch_shapes=[pltpu.VMEM((size, width), bf16)]
-        + gather_sems()
-        + ([] if summed else sum_buffers(size, width) + sum_sems()),
+        functools.partial(exchange_kernel, local, len(extras), summed, weights),
+        in_specs=[vmem] * len(inputs),
+        out_specs=out_specs,
+        out_shape=out_shape,
+        scratch_shapes=scratch,
         compiler_params=pltpu.CompilerParams(collective_id=number, has_side_effects=True),
         cost_estimate=pl.CostEstimate(
             flops=40_000_000_000 if summed else 70_000_000_000,
@@ -933,7 +968,7 @@
             bytes_accessed=16_000_000,
         ),
         name=name,
-    )(part, *extras)
+    )(*inputs)
 
 
 def column_chunks(width):
@@ -1154,10 +1189,10 @@
 FEED_COLUMNS = 512
 
 
-def feed_kernel(input_ref, cotangent_ref, weight_ref, down_ref, grad_ref, total_ref, acts, turned0,
-                turned1, stage, near_buf, far_buf, near_send, near_recv, far_send, far_recv):
+def feed_kernel(input_ref, cotangent_ref, weight_ref, down_weight_ref, down_ref, grad_ref, total_ref,
+                acts, turned0, turned1, stage, near_buf, far_buf, near_send, near_recv, far_send, far_recv):
     step = pl.program_id(0)
-    hidden_width = weight_ref.shape[1] // 3
+    hidden_width = down_weight_ref.shape[1]
     size = total_ref.shape[0]
     per = size // FEED_TILE
     tiles = 4 * per
@@ -1193,7 +1228,7 @@
         )
         gate = dot(inputs, weight_ref[:, gate_at])
         up = dot(inputs, weight_ref[:, up_at])
-        grad_hidden = dot(cotangent, weight_ref[:, down_at])
+        grad_hidden = dot(cotangent, down_weight_ref[...])
         opening = jax.nn.sigmoid(gate)
         active = gate * opening
         hidden = (active * up).astype(bf16)
@@ -1202,7 +1237,7 @@
         acts[here, gate_at] = grad_gate
         acts[here, up_at] = grad_up
         acts[here, down_at] = hidden
-        down_ref[...] = dot(hidden, weight_ref[:, down_at], NT).astype(bf16)
+        down_ref[...] = dot(hidden, down_weight_ref[...], NT).astype(bf16)
         back = dot(grad_gate, weight_ref[:, gate_at], NT) + dot(
             grad_up, weight_ref[:, up_at], NT
         )
@@ -1249,9 +1284,9 @@
             to_far(piece).wait_send()
 
 
-def feed(inputs, cotangent, weight, number):
+def feed(inputs, cotangent, weight, down_weight, number):
     rows, width = inputs.shape
-    columns = weight.shape[1]
+    columns = weight.shape[1] + down_weight.shape[1]
     size = rows // 4
     tiles, per = rows // FEED_TILE, size // FEED_TILE
     tile = pl.BlockSpec((FEED_TILE, width), lambda n: (jnp.minimum(n, tiles - 1), 0))
@@ -1262,7 +1297,7 @@
     return pl.pallas_call(
         feed_kernel,
         grid=(tiles + columns // FEED_COLUMNS,),
-        in_specs=[tile, tile, whole((width, columns))],
+        in_specs=[tile, tile, whole(weight.shape), whole(down_weight.shape)],
         out_specs=[
             tile,
             pl.BlockSpec((width, FEED_COLUMNS), lambda n: (0, jnp.maximum(n - tiles, 0))),
@@ -1293,7 +1328,7 @@
             bytes_accessed=45_000_000,
         ),
         name="feed",
-    )(inputs, cotangent, weight)
+    )(inputs, cotangent, weight, down_weight)
 
 
 def over_tokens(operand, other_side):
@@ -1399,7 +1434,8 @@
     mine, earlier_kv, earlier_terms, so_far = lax.optimization_barrier(
         (mine, earlier_kv, earlier_terms, so_far)
     )
-    second = all_rows(mine)
+    second = all_rows(mine[:, : 2 * hidden_width])
+    mine_down = mine[:, 2 * hidden_width :].reshape(groups, share, hidden_width)
     attended, lse = attend(
         False, ranges, query, earlier_kv, terms, earlier_terms, begins, local_heads, so_far
     )
@@ -1407,10 +1443,11 @@
     attended_wide = attended.astype(f32)
     gated = (opened * attended_wide).astype(bf16)
     branch = dot(gated, output_weight, NT).astype(bf16)
-    middle, input2 = exchange(
-        after_attention, branch, [tokens, gain2], False, 1, "exchange_middle"
-    )
-    down, second_grad, grad_input2 = feed(input2, cotangent_all, second, 4)
+    middle, input2, down_weight = exchange(
+        after_attention, branch, [tokens, gain2], False, 1, "exchange_middle", mine_down
+    )
+    down_weight = down_weight.reshape(model_width, hidden_width)
+    down, second_grad, grad_input2 = feed(input2, cotangent_all, second, down_weight, 4)
     second_part = row_sums(second_grad)
     grad_middle, grad_branch = exchange(
         after_hidden, grad_input2, [cotangent, middle, gain2], True, 2, "exchange_hidden"

time: 775 us -> 767 us (0.990)
  waiting for transfers between devices: 97.9 us -> 56 us
  Pallas kernels: 524 us -> 554 us
    all_gather x1, waiting for transfers between devices: 34.1 us -> 0.02 us  [all_rows(): return lax.all_gather(mine, 'blk', axis=0, tiled=True)]
    pallas_call x2, Pallas kernels: 122 us -> 145 us  [exchange(): pl.pallas_call(functools.partial(exchange_kernel, local, len(extras), sum...]
    ppermute x5, waiting for transfers between devices: 46.3 us -> 37.2 us  [passed_along(): return lax.ppermute(array, axis, pairs)]
  transfers between devices with their start and end apart: 8 -> 8, of which waited for: 4 -> 3; matrix products, arithmetic and copies ran while one was open for 13% -> 13% of each run, Pallas kernels for 44% -> 49%
where the time goes in v4:
time: 767 us; the launch traced here: 763 us
  Pallas kernels  554 us (72%)
  matrix products  69.9 us (9%)
  waiting for transfers between devices  56 us (7%)
  other arithmetic  27.8 us (4%)
  starting transfers between devices  20.2 us (3%)
  local copies, waits for them, and re-layouts  20.2 us (3%)
  between operations  14.9 us (2%)
    pallas_call x2, Pallas kernels, exchange(): pl.pallas_call(functools.partial(exchange_kernel, local, len(extras), sum...  145 us
    pallas_call x1, Pallas kernels, finish_last(): pl.pallas_call(finish_last_kernel, in_specs=[vmem] * 9, out_specs=[vmem]...  107 us
    pallas_call x1, Pallas kernels, gather_first(): pl.pallas_call(gather_first_kernel, in_specs=[vmem] * 3, out_specs=[anywh...  84.4 us
    pallas_call x1, Pallas kernels, feed(): pl.pallas_call(feed_kernel, grid=(tiles + columns // FEED_COLUMNS,), in_s...  73.9 us
    pallas_call x2, Pallas kernels, attend_back(): pl.pallas_call(functools.partial(attend_back_kernel, local_heads, own), g...  72.7 us
    pallas_call x2, Pallas kernels, attend(): pl.pallas_call(functools.partial(attend_kernel, local_heads, own), grid_s...  49.7 us
    dot_general x5, matrix products, dot(): return lax.dot_general(a, b, dims, preferred_element_type=f32, **kw)  48.3 us
    ppermute x5, waiting for transfers between devices, passed_along(): return lax.ppermute(array, axis, pairs)  37.2 us
  transfers between devices with their start and end apart: 8, of which 3 were waited for; matrix products, arithmetic and copies ran while one was open for 13% of the time, Pallas kernels for 49%

profile of v4, /device:TPU:0, one launch (start us, length us, event | category | flops | bytes accessed | tf_op | source)
XLA Modules:
  0.0 762.6 jit_solution(15122456241115529423)
XLA Ops:
  7.9 4.8 collective-permute-start
  21.2 84.4 %gather_first.1 = (bf16[8,4,48,2048]{3,2,1,0:T(8,128)(2,1)}, bf16[2048,1536]{1,0:T(8,128)(2,1)}, bf16[2048,1536]{1,0:T(8,128)(2,1)}) custom-call(bf16[4,48,2048]{2,1,0:T(8,128)(2,1)} %bitcast.130, bf16[512,1536]{1,0:T(8,128)(2,1)} %tokens_ref.3, bf16[512,1536]{1,0:T(8,128)(2,1)} %refs_1_.3), custom_call_target="tpu_custom_call" | custom-call | flops 70000001024 | bytes 30000000 | tf_op jit(solution)/shard_map/gather_first/pallas_call | solution.py:789
  105.6 1.7 convert_reduce_fusion.2
  108.7 16.4 %project.1 = (bf16[2048,1536]{1,0:T(8,128)(2,1)}, bf16[2048,768]{1,0:T(8,128)(2,1)}, bf16[2048,128]{1,0:T(8,128)(2,1)}, bf16[32,2048]{1,0:T(8,128)(2,1)}, f32[2048,128]{1,0:T(8,128)}) custom-call(bf16[2048,1536]{1,0:T(8,128)(2,1)} %get-tuple-element.55.tokens_ref, f32[8,1536]{1,0:T(8,128)} %broadcast_in_dim.53.gain_ref, bf16[1536,2048]{1,0:T(8,128)(2,1)} %bitcast.140, ...), custom_call_target="tpu_custom_call" | custom-call | flops 5637144576 | bytes 20000000 | tf_op jit(solution)/shard_map/project/pallas_call | solution.py:102
  125.0 3.5 collective-permute-start.2
  128.5 5.1 collective-permute-start.1
  135.0 3.5 all-to-all-start
  138.8 7.7 %convolution_convert_fusion.3.q_ref = bf16[2048,384]{1,0:T(8,128)(2,1)} fusion(bf16[2048,1536]{1,0:T(8,128)(2,1)} %get-tuple-element.57, bf16[1536,2048]{1,0:T(8,128)(2,1)} %bitcast.141), kind=kOutput, calls=%fused_computation.18 | convolution fusion | flops 2416705536 | bytes 9043968 | tf_op jit(solution)/shard_map/dot_general | solution.py:22
  146.5 3.3 convert_reduce_fusion
  151.2 40.8 %attend_own.1 = (f32[384,2048]{1,0:T(8,128)}, f32[24,2048]{1,0:T(8,128)}) custom-call(s32[2,4]{1,0:T(2,128)} %pad_add_fusion.1.ranges_ref, bf16[2048,384]{1,0:T(8,128)(2,1)} %convolution_convert_fusion.3.q_ref, bf16[2048,768]{1,0:T(8,128)(2,1)} %get-tuple-element.58.k_ref.v_ref, bf16[2048,768]{1,0:T(8,128)(2,1)} %get-tuple-element.58.k_ref.v_ref, ...), custom_call_target="tpu_custom_call" | custom-call | flops 40000000000 | bytes 12000000 | tf_op jit(solution)/shard_map/attend_own/pallas_call | solution.py:326
  192.1 7.7 %collective-permute-done.1.k_ref.v_ref = bf16[2048,768]{1,0:T(8,128)(2,1)} collective-permute-done((bf16[2048,768]{1,0:T(8,128)(2,1)}, bf16[2048,768]{1,0:T(8,128)(2,1)}, u32[]{:S(2)}, u32[]{:S(2)}) %collective-permute-start.1) | collective-permute-done | bytes 3145760 | tf_op jit(solution)/shard_map/ppermute | solution.py:28
  202.9 8.4 %add_divide_fusion = f32[2048,384]{1,0:T(8,128)} fusion(bf16[2048,1536]{1,0:T(8,128)(2,1)} %get-tuple-element.57, bf16[1536,2048]{1,0:T(8,128)(2,1)} %bitcast.142), kind=kOutput, calls=%fused_computation.16 | convolution fusion | flops 2418278400 | bytes 10616832 | tf_op jit(solution)/shard_map/dot_general | solution.py:22
  212.2 8.9 %attend_prev.1 = (bf16[2048,384]{1,0:T(8,128)(2,1)}, f32[24,2048]{1,0:T(8,128)}) custom-call(s32[2,4]{1,0:T(2,128)} %pad_add_fusion.1.ranges_ref, bf16[2048,384]{1,0:T(8,128)(2,1)} %convolution_convert_fusion.3.q_ref, bf16[2048,768]{1,0:T(8,128)(2,1)} %collective-permute-done.1.k_ref.v_ref, bf16[2048,768]{1,0:T(8,128)(2,1)} %collective-permute-done.1.k_ref.v_ref, ...), custom_call_target="tpu_custom_call" | custom-call | flops 10000000000 | bytes 12000000 | tf_op jit(solution)/shard_map/attend_prev/pallas_call | solution.py:326
  221.0 7.9 %convolution_convert_fusion.refs_0_ = bf16[2048,1536]{1,0:T(8,128)(2,1)} fusion(bf16[1536,2048]{1,0:T(8,128)(2,1)} %bitcast.143, f32[2048,384]{1,0:T(8,128)S(1)} %copy-done.9, bf16[2048,384]{1,0:T(8,128)(2,1)} %get-tuple-element.70.o_ref), kind=kOutput, calls=%fused_computation.2 | convolution fusion | flops 2421424128 | bytes 12189696 | tf_op jit(solution)/shard_map/dot_general | solution.py:22
  229.6 100.6 %exchange_middle.1 = (f32[512,1536]{1,0:T(8,128)}, bf16[2048,1536]{1,0:T(8,128)(2,1)}, bf16[8,4,48,1024]{3,2,1,0:T(8,128)(2,1)}) custom-call(bf16[2048,1536]{1,0:T(8,128)(2,1)} %convolution_convert_fusion.refs_0_, bf16[512,1536]{1,0:T(8,128)(2,1)} %tokens_ref.3, f32[8,1536]{1,0:T(8,128)} %broadcast_in_dim.95.refs_2_.refs_3_, bf16[4,48,1024]{2,1,0:T(8,128)(2,1)} %bitcast.137), custom_call_target="tpu_custom_call" | custom-call | flops 70000001024 | bytes 16000000 | tf_op jit(solution)/shard_map/exchange_middle/pallas_call | solution.py:958
  330.2 73.9 %feed.1 = (bf16[2048,1536]{1,0:T(8,128)(2,1)}, bf16[1536,3072]{1,0:T(8,128)(2,1)}, f32[512,1536]{1,0:T(8,128)}) custom-call(bf16[2048,1536]{1,0:T(8,128)(2,1)} %get-tuple-element.72.input_ref, bf16[2048,1536]{1,0:T(8,128)(2,1)} %get-tuple-element.73.cotangent_ref, bf16[1536,2048]{1,0:T(8,128)(2,1)} %all-gather.2.cloned.1.call-done.weight_ref, ...), custom_call_target="tpu_custom_call" | custom-call | flops 57982058496 | bytes 45000000 | tf_op jit(solution)/shard_map/feed/pallas_call | solution.py:1297
  404.1 44.3 %exchange_hidden.1 = (f32[512,1536]{1,0:T(8,128)}, bf16[2048,1536]{1,0:T(8,128)(2,1)}) custom-call(f32[512,1536]{1,0:T(8,128)} %get-tuple-element.75.refs_0_, bf16[512,1536]{1,0:T(8,128)(2,1)} %refs_1_.3, f32[512,1536]{1,0:T(8,128)} %get-tuple-element.76.refs_2_.middle_ref, f32[8,1536]{1,0:T(8,128)} %broadcast_in_dim.95.refs_2_.refs_3_), custom_call_target="tpu_custom_call" | custom-call | flops 40000000000 | bytes 16000000 | tf_op jit(solution)/shard_map/exchange_hidden/pallas_call | solution.py:958
  448.5 8.8 %multiply_convert_fusion = (bf16[2048,384]{1,0:T(8,128)(2,1)}, f32[2048,384]{1,0:T(8,128)}) fusion(f32[2048,384]{1,0:T(8,128)S(1)} %copy-done.10, bf16[2048,1536]{1,0:T(8,128)(2,1)} %get-tuple-element.77, bf16[1536,2048]{1,0:T(8,128)(2,1)} %bitcast.144), kind=kOutput, calls=%fused_computation.15 | convolution fusion | flops 2417491968 | bytes 15335424 | tf_op jit(solution)/shard_map/dot_general | solution.py:22
  457.3 10.8 %attend_back_prev.1 = (f32[2048,384]{1,0:T(8,128)}, f32[2048,128]{1,0:T(8,128)}, bf16[2,2048,384]{2,1,0:T(8,128)(2,1)}, f32[2048,128]{1,0:T(8,128)}) custom-call(s32[2,4]{1,0:T(2,128)} %pad_add_fusion.1.ranges_ref, bf16[2048,384]{1,0:T(8,128)(2,1)} %convolution_convert_fusion.3.q_ref, bf16[2048,768]{1,0:T(8,128)(2,1)} %collective-permute-done.1.k_ref.v_ref, ...), custom_call_target="tpu_custom_call" | custom-call | flops 15000000512 | bytes 25000000 | tf_op jit(solution)/shard_map/attend_back_prev/pallas_call | solution.py:487
  468.1 1.5 copy.111
  472.2 61.9 %attend_back_own.1 = (bf16[2048,384]{1,0:T(8,128)(2,1)}, f32[2048,384]{1,0:T(8,128)}, f32[2048,384]{1,0:T(8,128)}, f32[2048,128]{1,0:T(8,128)}) custom-call(s32[2,4]{1,0:T(2,128)} %pad_add_fusion.1.ranges_ref, bf16[2048,384]{1,0:T(8,128)(2,1)} %convolution_convert_fusion.3.q_ref, bf16[2048,768]{1,0:T(8,128)(2,1)} %get-tuple-element.58.k_ref.v_ref, ...), custom_call_target="tpu_custom_call" | custom-call | flops 80000000000 | bytes 25000000 | tf_op jit(solution)/shard_map/attend_back_own/pallas_call | solution.py:487
  534.1 7.8 %convolution_convert_fusion.2 = bf16[1536,384]{1,0:T(8,128)(2,1)} fusion(bf16[2048,1536]{1,0:T(8,128)(2,1)} %get-tuple-element.77, f32[2048,384]{1,0:T(8,128)S(1)} %copy-done.10, bf16[2048,384]{1,0:T(8,128)(2,1)} %get-tuple-element.70.o_ref), kind=kOutput, calls=%fused_computation.17 | convolution fusion | flops 2418868224 | bytes 12189696 | tf_op jit(solution)/shard_map/dot_general | solution.py:1335
  543.4 4.5 decay_back.1
  547.8 1.9 convert_reduce_fusion.1
  550.2 29.4 %collective-permute-done.4 = bf16[2,2048,384]{2,1,0:T(8,128)(2,1)} collective-permute-done((bf16[2,2048,384]{2,1,0:T(8,128)(2,1)}, bf16[2,2048,384]{2,1,0:T(8,128)(2,1)}, u32[]{:S(2)}, u32[]{:S(2)}) %collective-permute-start.4) | collective-permute-done | bytes 3145760 | tf_op jit(solution)/shard_map/ppermute | solution.py:28
  579.6 1.9 fusion.7
  582.0 2.2 fusion.8
  587.2 15.5 %convolution_convert_fusion.1.first_ref = bf16[2048,1536]{1,0:T(8,128)(2,1)} fusion(bf16[2048,1664]{1,0:T(8,128)(2,1)S(1)} %fusion.9, bf16[1536,2048]{1,0:T(8,128)(2,1)} %bitcast.145), kind=kOutput, calls=%fused_computation.3 | convolution fusion | flops 10472128512 | bytes 18219008 | tf_op jit(solution)/shard_map/dot_general | solution.py:22
  602.8 13.8 %select_convert_fusion = bf16[1536,1664]{1,0:T(8,128)(2,1)} fusion(bf16[2048,1536]{1,0:T(8,128)(2,1)S(1)} %bitcast.152, bf16[2048,1664]{1,0:T(8,128)(2,1)S(1)} %fusion.9, bf16[1536]{0:T(1024)(128)(2,1)S(1)} %select_reduce_fusion, pred[1664]{0:T(1024)(128)(4,1)S(1)} %copy-done.28), kind=kOutput, calls=%fused_computation.1 | convolution fusion | flops 10471538688 | bytes 18223744 | tf_op jit(solution)/shard_map/dot_general | solution.py:1335
  616.6 18.7 %reduce-scatter.2.cloned.1.call-done = bf16[192,3072]{1,0:T(8,128)(2,1)} async-done(((bf16[1536,3072]{1,0:T(8,128)(2,1)}), bf16[192,3072]{1,0:T(8,128)(2,1)}) %reduce-scatter.2.cloned.1.call-update) | async-done | bytes 1179664 | tf_op jit(solution)/shard_map/reduce_scatter | solution.py:1353
  635.3 107.1 %finish_last.1 = (bf16[4,48,1664]{2,1,0:T(8,128)(2,1)}, bf16[4,48,384]{2,1,0:T(8,128)(2,1)}, bf16[4,48,3072]{2,1,0:T(8,128)(2,1)}, f32[512,1536]{1,0:T(8,128)}, bf16[512,1536]{1,0:T(8,128)(2,1)}) custom-call(bf16[8,4,48,1664]{3,2,1,0:T(8,128)(2,1)} %bitcast.148, bf16[8,4,48,384]{3,2,1,0:T(8,128)(2,1)} %bitcast.150, bf16[4,48,3072]{2,1,0:T(8,128)(2,1)} %bitcast.147, ...), custom_call_target="tpu_custom_call" | custom-call | flops 80000000000 | bytes 40000000 | tf_op jit(solution)/shard_map/finish_last/pallas_call | solution.py:1120
  753.8 1.7 copy.160
  (159 shorter events, 37.1 us)
Async XLA Ops:
  7.9 138.6 %collective-permute-start = (s32[2048]{0:T(1024)S(1)}, s32[2048]{0:T(1024)S(1)}, u32[]{:S(2)}, u32[]{:S(2)}) collective-permute-start(s32[2048]{0:T(1024)S(1)} %broadcast_add_fusion), channel_id=1, source_target_pairs={{0,4},{4,8},{8,12},{12,16},{16,20},{20,24},{24,28},{1,5},{5,9},{9,... | collective-permute-start | bytes 24584 | tf_op jit(solution)/shard_map/ppermute | solution.py:28
  21.2 86.2 %copy-start.33 = (f32[24]{0:T(128)S(1)}, f32[24]{0:T(128)}, u32[]{:S(2)}) copy-start(f32[24]{0:T(128)} %param.23) | copy-start | bytes 292
  108.7 24.9 %copy-start.25 = (f32[48,4096]{1,0:T(8,128)S(1)}, f32[48,4096]{1,0:T(8,128)}, u32[]{:S(2)}) copy-start(f32[48,4096]{1,0:T(8,128)} %param.28) | copy-start | bytes 2359300
  108.7 25.0 %copy-start.5 = (f32[48,4096]{1,0:T(8,128)S(1)}, f32[48,4096]{1,0:T(8,128)}, u32[]{:S(2)}) copy-start(f32[48,4096]{1,0:T(8,128)} %param.26) | copy-start | bytes 2359300
  108.7 25.0 %copy-start.3 = (f32[48,4096]{1,0:T(8,128)S(1)}, f32[48,4096]{1,0:T(8,128)}, u32[]{:S(2)}) copy-start(f32[48,4096]{1,0:T(8,128)} %param.27) | copy-start | bytes 2359300
  125.0 67.0 %collective-permute-start.2 = (bf16[32,2048]{1,0:T(8,128)(2,1)}, bf16[32,2048]{1,0:T(8,128)(2,1)S(1)}, u32[]{:S(2)}, u32[]{:S(2)}) collective-permute-start(bf16[32,2048]{1,0:T(8,128)(2,1)} %get-tuple-element.63), channel_id=1, source_target_pairs={{0,4},{4,8},{8,12},{12,16},{16,20},{20,24},{24,28},{1,5},{5,9},{9,... | collective-permute-start | bytes 393224 | tf_op jit(solution)/shard_map/ppermute | solution.py:28
  128.5 71.3 %collective-permute-start.1 = (bf16[2048,768]{1,0:T(8,128)(2,1)}, bf16[2048,768]{1,0:T(8,128)(2,1)}, u32[]{:S(2)}, u32[]{:S(2)}) collective-permute-start(bf16[2048,768]{1,0:T(8,128)(2,1)} %get-tuple-element.58.k_ref.v_ref), channel_id=1, source_target_pairs={{0,4},{4,8},{8,12},{12,16},{16,20},{20,24},{24,28},{1,5},{5,9},{9,... | collective-permute-start | bytes 9437192 | tf_op jit(solution)/shard_map/ppermute | solution.py:28
  135.0 57.0 %all-to-all-start = ((bf16[48,4,3072]{2,0,1:T(8,128)(2,1)}), bf16[48,4,3072]{2,0,1:T(8,128)(2,1)S(1)}, u32[]{:S(2)}, u32[]{:S(2)}) async-start(bf16[48,4,3072]{2,0,1:T(8,128)(2,1)} %pad_maximum_fusion), calls=%async_computation | async-start | bytes 2359296 | tf_op jit(solution)/shard_map/all_to_all | solution.py:1344
  138.6 191.6 %all-gather.2.cloned.1.call-start = ((), (), s32[]{:S(2)}) async-start(), calls=%async_computation.2 | async-start | bytes 7077888 | tf_op jit(solution)/shard_map/all_gather | solution.py:1349
  192.1 19.3 %copy-start.32 = (bf16[32,2048]{1,0:T(8,128)(2,1)}, bf16[32,2048]{1,0:T(8,128)(2,1)S(1)}, u32[]{:S(2)}) copy-start(bf16[32,2048]{1,0:T(8,128)(2,1)S(1)} %collective-permute-done.2.t_key_ref) | copy-start | bytes 393220
  200.8 434.6 %reduce-scatter.2.cloned.1.call-start = ((), (), s32[]{:S(2)}) async-start(), calls=%async_computation.3 | async-start | bytes 10616832 | tf_op jit(solution)/shard_map/reduce_scatter | solution.py:1353
  212.2 8.9 %copy-start.9 = (f32[2048,384]{1,0:T(8,128)S(1)}, f32[2048,384]{1,0:T(8,128)}, u32[]{:S(2)}) copy-start(f32[2048,384]{1,0:T(8,128)} %add_divide_fusion) | copy-start | bytes 9437188
  404.1 44.4 %copy-start.10 = (f32[2048,384]{1,0:T(8,128)S(1)}, f32[2048,384]{1,0:T(8,128)}, u32[]{:S(2)}) copy-start(f32[2048,384]{1,0:T(8,128)} %add_divide_fusion) | copy-start | bytes 9437188
  469.6 72.3 %collective-permute-start.3 = (f32[2048,8]{0,1:T(8,128)S(1)}, f32[2048,8]{0,1:T(8,128)S(1)}, u32[]{:S(2)}, u32[]{:S(2)}) collective-permute-start(f32[2048,8]{0,1:T(8,128)S(1)} %copy.111), channel_id=1, source_target_pairs={{4,0},{8,4},{12,8},{16,12},{20,16},{24,20},{28,24},{5,1},{9,5},{13... | collective-permute-start | bytes 196616 | tf_op jit(solution)/shard_map/ppermute | solution.py:28
  470.9 108.7 %collective-permute-start.4 = (bf16[2,2048,384]{2,1,0:T(8,128)(2,1)}, bf16[2,2048,384]{2,1,0:T(8,128)(2,1)}, u32[]{:S(2)}, u32[]{:S(2)}) collective-permute-start(bf16[2,2048,384]{2,1,0:T(8,128)(2,1)} %get-tuple-element.85), channel_id=1, source_target_pairs={{4,0},{8,4},{12,8},{16,12},{20,16},{24,20},{28,24},{5,1},{9,5},{13... | collective-permute-start | bytes 9437192 | tf_op jit(solution)/shard_map/ppermute | solution.py:28
  542.0 5.9 copy-start.29
  543.4 6.3 copy-start.27
  543.4 36.3 %copy-start.2 = (f32[2048,384]{1,0:T(8,128)S(1)}, f32[2048,384]{1,0:T(8,128)}, u32[]{:S(2)}) copy-start(f32[2048,384]{1,0:T(8,128)} %get-tuple-element.84) | copy-start | bytes 9437188
  579.6 2.4 copy-start.1
  582.0 2.8 copy-start.12
  582.0 3.3 copy-start.13
  586.5 16.3 %slice-start = ((s8[6291456]{0:T(1024)(128)(4,1)}), s8[4194304]{0:T(1024)(128)(4,1)S(1)}, s32[]{:S(2)}) async-start(s8[6291456]{0:T(1024)(128)(4,1)} %bitcast.151), calls=%async_computation.4 | async-start | bytes 8388608
  587.2 15.6 %copy-start.28 = (pred[1664]{0:T(1024)(128)(4,1)S(1)}, pred[1664]{0:T(1024)(128)(4,1)}, u32[]{:S(2)}) copy-start(pred[1664]{0:T(1024)(128)(4,1)} %iota_compare_fusion.1) | copy-start | bytes 4996
  587.2 15.6 %slice-start.1 = ((s8[6291456]{0:T(1024)(128)(4,1)}), s8[2097152]{0:T(1024)(128)(4,1)S(1)}, s32[]{:S(2)}) async-start(s8[6291456]{0:T(1024)(128)(4,1)} %bitcast.151), calls=%async_computation.5 | async-start | bytes 4194304
  742.5 5.2 copy-start.17
  743.7 4.9 copy-start.18
  744.5 4.2 copy-start.19
  744.6 4.3 copy-start.20
  744.6 4.5 copy-start.16
  750.7 3.1 copy-start.7
  750.9 2.9 copy-start
  751.0 4.5 copy-start.8
  (12 other events, 17.9 us)
Sparse Core Ops, SparseCore 0:
  200.9 123.5 all-gather.1
  404.2 231.0 reduce-scatter.1

commit v5 on v3

--- a/solution.py
+++ b/solution.py
@@ -884,21 +884,130 @@
     ]
 
 
+def column_chunks(width):
+    count = max(width // 512, 1)
+    first = width - 512 * (count - 1)
+    return [(0, first)] + [(first + 512 * n, 512) for n in range(count - 1)]
+
+
+class RowSums:
+    def __init__(self, arrays, sems):
+        self.pair_send, self.pair_recv, self.line_send, self.line_recv = sems
+        self.here, self.partner, self.after = blk_peers()
+        self.steps = len(self.after)
+        self.chunks = [
+            array + (pl.ds(start, wide),)
+            for array in arrays
+            for start, wide in column_chunks(array[0].shape[3])
+        ]
+        self.sent = []
+
+    def others(self):
+        return [on_blk(self.partner)] + [on_blk(peer) for peer in self.after[1:]]
+
+    def pair_wait(self, c, t):
+        _, pair_buf, _, _, at = self.chunks[c]
+        block = pair_buf.at[t, :, :, at]
+        remote(
+            block, block, self.pair_send.at[c, t], self.pair_recv.at[c, t], on_blk(self.partner)
+        ).wait_recv()
+
+    def start(self):
+        for c, (ref, pair_buf, _, _, at) in enumerate(self.chunks):
+            for t in list(range(1, self.steps)) + [0]:
+                copy = remote(
+                    ref.at[self.after[t] + self.partner - self.here, :, :, at],
+                    pair_buf.at[t, :, :, at],
+                    self.pair_send.at[c, t],
+                    self.pair_recv.at[c, t],
+                    on_blk(self.partner),
+                )
+                copy.start()
+                self.sent.append(copy)
+
+    def pass_on(self, c):
+        ref, pair_buf, line_buf, _, at = self.chunks[c]
+        for t in range(1, self.steps):
+            self.pair_wait(c, t)
+
+            def add(group, carry):
+                pair_buf[t, group, :, at] = (
+                    ref[self.after[t], group, :, at].astype(f32)
+                    + pair_buf[t, group, :, at].astype(f32)
+                ).astype(bf16)
+                return carry
+
+            lax.fori_loop(0, ref.shape[1], add, 0)
+            copy = remote(
+                pair_buf.at[t, :, :, at], line_buf.at[t, :, :, at], self.line_send.at[c, t],
+                self.line_recv.at[c, t], on_blk(self.after[t]),
+            )
+            copy.start()
+            self.sent.append(copy)
+
+    def add_up(self, c):
+        ref, pair_buf, line_buf, out_ref, at = self.chunks[c]
+        self.pair_wait(c, 0)
+        for t in range(1, self.steps):
+            block = line_buf.at[t, :, :, at]
+            remote(
+                block, block, self.line_send.at[c, t], self.line_recv.at[c, t],
+                on_blk(self.after[t]),
+            ).wait_recv()
+
+        def add_all(group, carry):
+            total = ref[self.here, group, :, at].astype(f32)
+            total = total + pair_buf[0, group, :, at].astype(f32)
+            for t in range(1, self.steps):
+                total = total + line_buf[t, group, :, at].astype(f32)
+            out_ref[group, :, at] = total.astype(bf16)
+            return carry
+
+        lax.fori_loop(0, ref.shape[1], add_all, 0)
+
+    def finish(self):
+        for copy in self.sent:
+            copy.wait_send()
+
+
+def row_sum_buffers(half, groups, share, columns):
+    return [pltpu.VMEM((half, groups, share, columns), bf16) for _ in range(2)]
+
+
+def row_sum_sems(chunks, half):
+    return [pltpu.SemaphoreType.DMA((chunks, half)) for _ in range(4)]
+
+
 def exchange_kernel(local, extras, summed, *refs):
-    part_ref, extra_refs = refs[0], refs[1 : 1 + extras]
-    out_ref, all_ref, payload = refs[1 + extras : 4 + extras]
-    sems = refs[4 + extras :]
+    part_ref, extra_refs, mine_ref = refs[0], refs[1 : 1 + extras], refs[1 + extras]
+    out_ref, all_ref, weight_ref, payload = refs[2 + extras : 6 + extras]
+    sems = refs[6 + extras :]
     size = out_ref.shape[0]
     span = size // PIECES
     _, near, far, _ = partners()
-    greet([on_head(near), on_head(far)])
     slots = Slots(summed)
-    if not summed:
-        shares = Sum(part_ref, sems[7:10], sems[10:], size, True)
+    if summed:
+        beside = RowSums([(mine_ref, sems[7], sems[8], weight_ref)], sems[9:13])
+        greet([on_head(near), on_head(far)] + beside.others())
+        beside.start()
+    else:
+        kinds = mine_ref.shape[0]
+        beside = Line(lambda kind, blk: weight_ref.at[blk, kind], kinds, sems[-7:-1])
+        own = pltpu.make_async_copy(mine_ref, weight_ref.at[lax.axis_index("blk")], sems[-1])
+        own.start()
+        beside.greet([on_head(near), on_head(far)])
+        shares = Sum(part_ref, sems[7:10], sems[10:14], size, True)
         shares.start()
+        own.wait()
+        for kind in range(kinds):
+            beside.launch(kind)
         shares.turn()
     sent = []
     for piece in range(PIECES):
+        if not summed and piece != 2:
+            hop = {0: 1, 1: 2, 3: 3}[piece]
+            for t in range(hop, beside.half if piece == 3 else min(hop + 1, beside.half)):
+                beside.step(t)
         here = slice(piece * span, (piece + 1) * span)
         total = part_ref[here, :] if summed else shares.total(piece)
         result, share = local(total, here, *extra_refs)
@@ -906,82 +1015,70 @@
         payload[here, :] = share.astype(bf16)
         source = payload.at[pl.ds(piece * span, span), :]
         sent.append(spread_piece(source, all_ref, size, sems[:7], piece, slots))
-    hand_on(all_ref, size, sems[:7], sent, slots)()
+    if summed:
+        for c in range(len(beside.chunks)):
+            beside.pass_on(c)
+    finish_rows = hand_on(all_ref, size, sems[:7], sent, slots)
+    if summed:
+        for c in range(len(beside.chunks)):
+            beside.add_up(c)
+    finish_rows()
     if not summed:
         shares.finish()
-
-
-def exchange(local, part, extras, summed, number, name):
+    beside.finish()
+
+
+def exchange(local, part, extras, summed, number, name, mine):
     rows, width = part.shape
     size = rows if summed else rows // 4
-    vmem = pl.BlockSpec(memory_space=pltpu.VMEM)
+    peers = lax.axis_size("blk")
+    vmem, anywhere = pl.BlockSpec(memory_space=pltpu.VMEM), pl.BlockSpec(memory_space=pl.ANY)
+    scratch = [pltpu.VMEM((size, width), bf16)] + gather_sems()
+    if summed:
+        beside = mine.shape[1:]
+        scratch += row_sum_buffers(peers // 2, *beside)
+        scratch += row_sum_sems(len(column_chunks(beside[2])), peers // 2)
+    else:
+        beside = (peers,) + mine.shape
+        scratch += sum_buffers(size, width) + sum_sems()
+        scratch += [pltpu.SemaphoreType.DMA((mine.shape[0], peers // 2)) for _ in range(6)]
+        scratch.append(pltpu.SemaphoreType.DMA)
     return pl.pallas_call(
         functools.partial(exchange_kernel, local, len(extras), summed),
-        in_specs=[vmem] * (1 + len(extras)),
-        out_specs=[vmem, pl.BlockSpec(memory_space=pl.ANY)],
+        in_specs=[vmem] * (2 + len(extras)),
+        out_specs=[vmem, anywhere, vmem if summed else anywhere],
         out_shape=[
             jax.ShapeDtypeStruct((size, width), f32),
             jax.ShapeDtypeStruct((4 * size, width), bf16),
+            jax.ShapeDtypeStruct(beside, bf16),
         ],
-        scratch_shapes=[pltpu.VMEM((size, width), bf16)]
-        + gather_sems()
-        + ([] if summed else sum_buffers(size, width) + sum_sems()),
+        scratch_shapes=scratch,
         compiler_params=pltpu.CompilerParams(collective_id=number, has_side_effects=True),
         cost_estimate=pl.CostEstimate(
-            flops=40_000_000_000 if summed else 70_000_000_000,
+            flops=60_000_000_000 if summed else 80_000_000_000,
             transcendentals=0,
             bytes_accessed=16_000_000,
         ),
         name=name,
-    )(part, *extras)
-
-
-def column_chunks(width):
-    count = max(width // 512, 1)
-    first = width - 512 * (count - 1)
-    return [(0, first)] + [(first + 512 * n, 512) for n in range(count - 1)]
-
-
-def finish_last_kernel(grad_ref, output_grad_ref, second_ref, first_ref, down_ref, grad_middle_ref,
-                       tokens_ref, gain_ref, middle_ref, weights_ref, output_ref, second_out_ref,
-                       tokens_grad_ref, result_ref, *refs):
-    buffers = (refs[0:3], refs[3:6])
-    first_buffers, down_buffers = refs[6:9], refs[9:12]
-    pair_send, pair_recv, line_send, line_recv, swap_send, swap_recv = refs[12:18]
-    first_sems, down_sems = refs[18:22], refs[22:26]
+    )(part, *extras, mine)
+
+
+def finish_last_kernel(grads_ref, first_ref, grad_ref, output_grad_ref, second_ref, second_down_ref,
+                       grad_middle_ref, tokens_ref, gain_ref, weights_ref, output_ref,
+                       second_out_ref, second_down_out_ref, tokens_grad_ref, part_buf, *refs):
+    pair0, line0, pair1, line1, row0, row1 = refs[:6]
+    swap_send, swap_recv = refs[10:12]
     me, near, far, cross = partners()
     others = (near, far, cross)
-    here, partner, after = blk_peers()
-    steps = len(after)
-    greet(
-        [on_head(other) for other in others]
-        + [on_blk(partner)]
-        + [on_blk(peer) for peer in after[1:]]
-    )
-    size = result_ref.shape[0]
-    first = Sum(first_ref, first_buffers, first_sems, size, True)
-    down = Sum(down_ref, down_buffers, down_sems, size, False)
-    chunks = []
-    for ref, out_ref, some in (
-        (grad_ref, weights_ref, buffers[0]), (output_grad_ref, output_ref, buffers[1])
-    ):
-        for start, wide in column_chunks(ref.shape[3]):
-            chunks.append((ref, out_ref, some, pl.ds(start, wide)))
-    groups = grad_ref.shape[1]
-    first.start()
+    sums = RowSums(
+        [(grad_ref, pair0, line0, row0), (output_grad_ref, pair1, line1, row1)], refs[6:10]
+    )
+    outs = {id(row0): weights_ref, id(row1): output_ref}
+    greet([on_head(other) for other in others] + sums.others())
+    size = tokens_grad_ref.shape[0]
+    first = Sum(part_buf, refs[12:15], refs[15:19], size, True)
+    sums.start()
     sent = []
-    for c, (ref, _, (pair_buf, _, _), at) in enumerate(chunks):
-        for t in list(range(1, steps)) + [0]:
-            copy = remote(
-                ref.at[after[t] + partner - here, :, :, at],
-                pair_buf.at[t, :, :, at],
-                pair_send.at[c, t],
-                pair_recv.at[c, t],
-                on_blk(partner),
-            )
-            copy.start()
-            sent.append(copy)
-    first.turn()
 
     def swap(source_ref, out_ref, c):
         for kind, other in enumerate(others):
@@ -992,70 +1089,48 @@
             copy.start()
             sent.append(copy)
 
-    swap(second_ref, second_out_ref, len(chunks))
-    down.start()
-    down.turn()
+    count = len(sums.chunks)
+    swap(second_ref, second_out_ref, count)
+    swap(second_down_ref, second_down_out_ref, count + 1)
+    columns = grads_ref.shape[1]
+    tiles = part_buf.shape[0] // 256
+
+    def multiply(n, carry):
+        here = tile_of(n, 256)
+        part_buf[here, :] = dot(grads_ref[here, :], first_ref[:, :columns], NT).astype(bf16)
+        return carry
+
+    lax.fori_loop(0, tiles // 4, multiply, 0)
+    sums.pass_on(0)
+    lax.fori_loop(tiles // 4, tiles, multiply, 0)
+    first.start()
 
     def add_up(c):
-        ref, out_ref, (pair_buf, line_buf, row_buf), at = chunks[c]
-        block = pair_buf.at[0, :, :, at]
-        remote(block, block, pair_send.at[c, 0], pair_recv.at[c, 0], on_blk(partner)).wait_recv()
-        for t in range(1, steps):
-            block = line_buf.at[t, :, :, at]
-            remote(
-                block, block, line_send.at[c, t], line_recv.at[c, t], on_blk(after[t])
-            ).wait_recv()
-
-        def add_all(group, carry):
-            total = ref[here, group, :, at].astype(f32) + pair_buf[0, group, :, at].astype(f32)
-            for t in range(1, steps):
-                total = total + line_buf[t, group, :, at].astype(f32)
-            row_buf[group, :, at] = total.astype(bf16)
-            return carry
-
-        lax.fori_loop(0, groups, add_all, 0)
-        out_ref[me, :, at] = row_buf[me, :, at]
-        swap(row_buf.at[:, :, at], out_ref.at[:, :, at], c)
-
-    def put(shares, local, out_ref, extra_refs):
-        for piece in range(PIECES):
-            rows = shares.piece(piece)
-            value, _ = local(shares.total(piece), rows, *extra_refs)
-            out_ref[rows, :] = value.astype(out_ref.dtype)
-
-    for c, (ref, _, (pair_buf, line_buf, _), at) in enumerate(chunks):
-        for t in range(1, steps):
-            block = pair_buf.at[t, :, :, at]
-            remote(
-                block, block, pair_send.at[c, t], pair_recv.at[c, t], on_blk(partner)
-            ).wait_recv()
-
-            def add(group, carry):
-                pair_buf[t, group, :, at] = (
-                    ref[after[t], group, :, at].astype(f32)
-                    + pair_buf[t, group, :, at].astype(f32)
-                ).astype(bf16)
-                return carry
-
-            lax.fori_loop(0, groups, add, 0)
-            copy = remote(
-                block, line_buf.at[t, :, :, at], line_send.at[c, t], line_recv.at[c, t],
-                on_blk(after[t]),
-            )
-            copy.start()
-            sent.append(copy)
-        if c > 0:
-            add_up(c - 1)
-    put(first, after_first, tokens_grad_ref, (grad_middle_ref, tokens_ref, gain_ref))
-    add_up(len(chunks) - 1)
-    put(down, after_down, result_ref, (middle_ref,))
+        sums.add_up(c)
+        _, _, _, row_ref, at = sums.chunks[c]
+        out_ref = outs[id(row_ref)]
+        out_ref[me, :, at] = row_ref[me, :, at]
+        swap(row_ref.at[:, :, at], out_ref.at[:, :, at], c)
+
+    for c in range(1, count):
+        sums.pass_on(c)
+        if c == 1:
+            first.turn()
+        add_up(c - 1)
+    for piece in range(PIECES):
+        rows = first.piece(piece)
+        tokens_grad_ref[rows, :], _ = after_first(
+            first.total(piece), rows, grad_middle_ref, tokens_ref, gain_ref
+        )
+    add_up(count - 1)
     second_out_ref[me] = second_ref[me]
-    for c in range(len(chunks) + 1):
-        if c < len(chunks):
-            _, out_ref, _, at = chunks[c]
-            out_ref = out_ref.at[:, :, at]
+    second_down_out_ref[me] = second_down_ref[me]
+    for c in range(count + 2):
+        if c < count:
+            _, _, _, row_ref, at = sums.chunks[c]
+            out_ref = outs[id(row_ref)].at[:, :, at]
         else:
-            out_ref = second_out_ref
+            out_ref = second_out_ref if c == count else second_down_out_ref
         for kind, other in enumerate(others):
             block = out_ref.at[other]
             remote(
@@ -1063,57 +1138,51 @@
             ).wait_recv()
     for copy in sent:
         copy.wait_send()
+    sums.finish()
     first.finish()
-    down.finish()
-
-
-def finish_last(grad, output_grad, second, groups, part_first, part_down, grad_middle, tokens, gain,
-                middle, number):
+
+
+def finish_last(grads, first, grad, output_grad, second, second_down, grad_middle, tokens, gain,
+                number):
     peers = lax.axis_size("blk")
-    share = grad.shape[0] // (peers * groups)
+    groups, share, down_columns = second_down.shape
     rows, width = tokens.shape
     vmem = pl.BlockSpec(memory_space=pltpu.VMEM)
     half = peers // 2
     widths = (grad.shape[1], output_grad.shape[1])
-    chunks = sum(len(column_chunks(width)) for width in widths)
-
-    def blocks(columns):
-        return [pltpu.VMEM((half, groups, share, columns), bf16) for _ in range(2)] + [
-            pltpu.VMEM((groups, share, columns), bf16)
-        ]
-
+    chunks = sum(len(column_chunks(columns)) for columns in widths)
     return pl.pallas_call(
         finish_last_kernel,
         in_specs=[vmem] * 9,
         out_specs=[vmem] * 5,
         out_shape=[
             jax.ShapeDtypeStruct((groups, share, columns), bf16)
-            for columns in widths + (second.shape[1],)
+            for columns in widths + (second.shape[1], down_columns)
         ]
-        + [
-            jax.ShapeDtypeStruct((rows, width), f32),
-            jax.ShapeDtypeStruct((rows, width), bf16),
-        ],
-        scratch_shapes=blocks(widths[0])
-        + blocks(widths[1])
+        + [jax.ShapeDtypeStruct((rows, width), f32)],
+        scratch_shapes=[pltpu.VMEM((4 * rows, width), bf16)]
+        + row_sum_buffers(half, groups, share, widths[0])
+        + row_sum_buffers(half, groups, share, widths[1])
+        + [pltpu.VMEM((groups, share, columns), bf16) for columns in widths]
+        + row_sum_sems(chunks, half)
+        + [pltpu.SemaphoreType.DMA((chunks + 2, 3)) for _ in range(2)]
         + sum_buffers(rows, width)
-        + sum_buffers(rows, width)
-        + [pltpu.SemaphoreType.DMA((chunks, half)) for _ in range(4)]
-        + [pltpu.SemaphoreType.DMA((chunks + 1, 3)) for _ in range(2)]
-        + sum_sems()
         + sum_sems(),
         compiler_params=pltpu.CompilerParams(
-            collective_id=number, has_side_effects=True, vmem_limit_bytes=60 << 20
+            collective_id=number, has_side_effects=True, vmem_limit_bytes=62 << 20
         ),
         cost_estimate=pl.CostEstimate(
-            flops=80_000_000_000, transcendentals=0, bytes_accessed=40_000_000
+            flops=90_000_000_000, transcendentals=0, bytes_accessed=40_000_000
         ),
         name="finish_last",
     )(
+        grads,
+        first,
         grad.reshape(peers, groups, share, widths[0]),
         output_grad.reshape(peers, groups, share, widths[1]),
         second.reshape(groups, share, second.shape[1]),
-        part_first, part_down, grad_middle, tokens, gain, middle,
+        second_down,
+        grad_middle, tokens, gain,
     )
 
 
@@ -1146,26 +1215,30 @@
     return grad, None
 
 
-def after_down(total, here, middle_ref):
-    return middle_ref[here, :] + total, None
-
-
 FEED_TILE = 256
 FEED_COLUMNS = 512
 
 
-def feed_kernel(input_ref, cotangent_ref, weight_ref, down_ref, grad_ref, total_ref, acts, turned0,
-                turned1, stage, near_buf, far_buf, near_send, near_recv, far_send, far_recv):
+def feed_kernel(input_ref, cotangent_ref, weight_ref, down_weight_ref, down_ref, grad_ref, grad_down_ref,
+                total_ref, acts, turned0, turned1, stage, near_buf, far_buf, down_stage, near_send,
+                near_recv, far_send, far_recv, down_sems):
     step = pl.program_id(0)
-    hidden_width = weight_ref.shape[1] // 3
+    hidden_width = down_weight_ref.shape[1]
     size = total_ref.shape[0]
     per = size // FEED_TILE
     tiles = 4 * per
-    _, near, far, _ = partners()
+    me, near, far, cross = partners()
 
     @pl.when(step == 0)
     def _():
         greet([on_head(near), on_head(far)])
+
+    def down_copy(at):
+        shard = sum(jnp.where(at // per == n, s, 0) for n, s in enumerate((cross, far, near, me)))
+        row = pl.multiple_of(shard * size + (at % per) * FEED_TILE, FEED_TILE)
+        return pltpu.make_async_copy(
+            down_stage.at[at % 2], down_ref.at[pl.ds(row, FEED_TILE), :], down_sems.at[at % 2]
+        )
 
     def to_near(which, piece):
         return remote(
@@ -1193,7 +1266,7 @@
         )
         gate = dot(inputs, weight_ref[:, gate_at])
         up = dot(inputs, weight_ref[:, up_at])
-        grad_hidden = dot(cotangent, weight_ref[:, down_at])
+        grad_hidden = dot(cotangent, down_weight_ref[...])
         opening = jax.nn.sigmoid(gate)
         active = gate * opening
         hidden = (active * up).astype(bf16)
@@ -1202,7 +1275,9 @@
         acts[here, gate_at] = grad_gate
         acts[here, up_at] = grad_up
         acts[here, down_at] = hidden
-        down_ref[...] = dot(hidden, weight_ref[:, down_at], NT).astype(bf16)
+        pl.when(step >= 2)(lambda: down_copy(step - 2).wait())
+        down_stage[step % 2] = dot(hidden, down_weight_ref[...], NT).astype(bf16)
+        down_copy(step).start()
         back = dot(grad_gate, weight_ref[:, gate_at], NT) + dot(
             grad_up, weight_ref[:, up_at], NT
         )
@@ -1235,10 +1310,12 @@
 
         @pl.when(jnp.logical_not(from_input))
         def _():
-            grad_ref[...] = dot(turned1[...], acts[:, at]).astype(bf16)
+            grad_down_ref[...] = dot(turned1[...], acts[:, at]).astype(bf16)
 
     @pl.when(step == pl.num_programs(0) - 1)
     def _():
+        down_copy(tiles - 2).wait()
+        down_copy(tiles - 1).wait()
         for piece in range(per):
             here = slice(piece * FEED_TILE, (piece + 1) * FEED_TILE)
             to_near(1, piece).wait_recv()
@@ -1249,11 +1326,12 @@
             to_far(piece).wait_send()
 
 
-def feed(inputs, cotangent, weight, number):
+def feed(inputs, cotangent, weight, down_weight, number):
     rows, width = inputs.shape
-    columns = weight.shape[1]
+    columns = weight.shape[1] + down_weight.shape[1]
     size = rows // 4
     tiles, per = rows // FEED_TILE, size // FEED_TILE
+    wide = weight.shape[1] // FEED_COLUMNS
     tile = pl.BlockSpec((FEED_TILE, width), lambda n: (jnp.minimum(n, tiles - 1), 0))
 
     def whole(shape):
@@ -1262,15 +1340,17 @@
     return pl.pallas_call(
         feed_kernel,
         grid=(tiles + columns // FEED_COLUMNS,),
-        in_specs=[tile, tile, whole((width, columns))],
+        in_specs=[tile, tile, whole(weight.shape), whole(down_weight.shape)],
         out_specs=[
-            tile,
-            pl.BlockSpec((width, FEED_COLUMNS), lambda n: (0, jnp.maximum(n - tiles, 0))),
+            pl.BlockSpec(memory_space=pl.ANY),
+            pl.BlockSpec((width, FEED_COLUMNS), lambda n: (0, jnp.clip(n - tiles, 0, wide - 1))),
+            pl.BlockSpec((width, FEED_COLUMNS), lambda n: (0, jnp.maximum(n - tiles - wide, 0))),
             whole((size, width)),
         ],
         out_shape=[
             jax.ShapeDtypeStruct((rows, width), bf16),
-            jax.ShapeDtypeStruct((width, columns), bf16),
+            jax.ShapeDtypeStruct((width, weight.shape[1]), bf16),
+            jax.ShapeDtypeStruct((width, down_weight.shape[1]), bf16),
             jax.ShapeDtypeStruct((size, width), f32),
         ],
         scratch_shapes=[
@@ -1280,10 +1360,12 @@
             pltpu.VMEM((2 * per, FEED_TILE, width), bf16),
             pltpu.VMEM((2, per, FEED_TILE, width), bf16),
             pltpu.VMEM((per, FEED_TILE, width), bf16),
+            pltpu.VMEM((2, FEED_TILE, width), bf16),
             pltpu.SemaphoreType.DMA((2, per)),
             pltpu.SemaphoreType.DMA((2, per)),
             pltpu.SemaphoreType.DMA((per,)),
             pltpu.SemaphoreType.DMA((per,)),
+            pltpu.SemaphoreType.DMA((2,)),
         ],
         compiler_params=pltpu.CompilerParams(
             collective_id=number, has_side_effects=True, vmem_limit_bytes=63 << 20
@@ -1293,7 +1375,7 @@
             bytes_accessed=45_000_000,
         ),
         name="feed",
-    )(inputs, cotangent, weight)
+    )(inputs, cotangent, weight, down_weight)
 
 
 def over_tokens(operand, other_side):
@@ -1399,7 +1481,8 @@
     mine, earlier_kv, earlier_terms, so_far = lax.optimization_barrier(
         (mine, earlier_kv, earlier_terms, so_far)
     )
-    second = all_rows(mine)
+    second = all_rows(mine[:, : 2 * hidden_width])
+    mine_down = mine[:, 2 * hidden_width :].reshape(groups, share, hidden_width)
     attended, lse = attend(
         False, ranges, query, earlier_kv, terms, earlier_terms, begins, local_heads, so_far
     )
@@ -1407,13 +1490,17 @@
     attended_wide = attended.astype(f32)
     gated = (opened * attended_wide).astype(bf16)
     branch = dot(gated, output_weight, NT).astype(bf16)
-    middle, input2 = exchange(
-        after_attention, branch, [tokens, gain2], False, 1, "exchange_middle"
-    )
-    down, second_grad, grad_input2 = feed(input2, cotangent_all, second, 4)
+    middle, input2, down_weight = exchange(
+        after_attention, branch, [tokens, gain2], False, 1, "exchange_middle", mine_down
+    )
+    down_weight = down_weight.reshape(model_width, hidden_width)
+    down, second_grad, down_grad, grad_input2 = feed(
+        input2, cotangent_all, second, down_weight, 4
+    )
     second_part = row_sums(second_grad)
-    grad_middle, grad_branch = exchange(
-        after_hidden, grad_input2, [cotangent, middle, gain2], True, 2, "exchange_hidden"
+    grad_middle, grad_branch, down_part = exchange(
+        after_hidden, grad_input2, [cotangent, middle, gain2], True, 2, "exchange_hidden",
+        down_grad.reshape(-1, groups, share, hidden_width),
     )
 
     grad_gated = dot(grad_branch, output_weight)
@@ -1448,13 +1535,15 @@
         column == 2 * local_width + local_heads, spread_bias, first_grad
     ).astype(bf16)
     output_grad = over_tokens(grad_branch, gated).astype(bf16)
-    grad_input1 = dot(grads, first[:, : kv_width + 2 * local_width], NT).astype(bf16)
-    first_sum, output_sum, second_sum, tokens_grad, result = finish_last(
-        first_grad, output_grad, second_part, groups, grad_input1, down, grad_middle, tokens,
-        gain1, middle, 3,
-    )
-    first_sum, output_sum, second_sum = (
-        jnp.swapaxes(array, 0, 1).astype(f32) for array in (first_sum, output_sum, second_sum)
+    down, second_part, first_grad = lax.optimization_barrier((down, second_part, first_grad))
+    first_sum, output_sum, second_sum, down_sum, tokens_grad = finish_last(
+        grads, first, first_grad, output_grad, second_part, down_part, grad_middle, tokens, gain1, 3
+    )
+    down = lax.psum_scatter(down, "head", scatter_dimension=0, tiled=True)
+    result = (middle + down.astype(f32)).astype(bf16)
+    first_sum, output_sum, second_sum, down_sum = (
+        jnp.swapaxes(array, 0, 1).astype(f32)
+        for array in (first_sum, output_sum, second_sum, down_sum)
     )
 
     def columns(array, start, width):
@@ -1467,9 +1556,10 @@
         columns(first_sum, kv_width + n * local_width, local_width) for n in range(2)
     )
     output_total = columns(output_sum, 0, local_width)
-    gate_sum, up_sum, down_sum = (
-        columns(second_sum, n * hidden_width, hidden_width) for n in range(3)
-    )
+    gate_sum, up_sum = (
+        columns(second_sum, n * hidden_width, hidden_width) for n in range(2)
+    )
+    down_sum = columns(down_sum, 0, hidden_width)
 
     def along(weight, grad):
         return jnp.sum(low(weight).astype(f32) * grad, axis=1)

time: 775 us -> 805 us (1.039)
  Pallas kernels: 524 us -> 613 us
  waiting for transfers between devices: 97.9 us -> 46.9 us
  matrix products: 67.8 us -> 56.2 us
    pallas_call x2, Pallas kernels: 122 us -> 187 us  [exchange(): pl.pallas_call(functools.partial(exchange_kernel, local, len(extras), sum...]
    all_gather x1, waiting for transfers between devices: 34.1 us -> 0.02 us  [all_rows(): return lax.all_gather(mine, 'blk', axis=0, tiled=True)]
    pallas_call x1, Pallas kernels: 107 us -> 131 us  [finish_last(): pl.pallas_call(finish_last_kernel, in_specs=[vmem] * 9, out_specs=[vmem]...]
    reduce_scatter x1, waiting for transfers between devices: 17.4 us -> 0.01 us  [row_sums(): return lax.psum_scatter(grad, 'blk', scatter_dimension=0, tiled=True)]
    dot_general x5 -> x4, matrix products: 46.3 us -> 32.8 us  [dot(): return lax.dot_general(a, b, dims, preferred_element_type=f32, **kw)]
  transfers between devices with their start and end apart: 8 -> 9, of which waited for: 4 -> 2; matrix products, arithmetic and copies ran while one was open for 13% -> 12% of each run, Pallas kernels for 44% -> 67%
where the time goes in v5:
time: 805 us; the launch traced here: 803 us
  Pallas kernels  613 us (76%)
  matrix products  56.2 us (7%)
  waiting for transfers between devices  46.9 us (6%)
  other arithmetic  30.3 us (4%)
  local copies, waits for them, and re-layouts  22.2 us (3%)
  starting transfers between devices  18.7 us (2%)
  between operations  14.9 us (2%)
    pallas_call x2, Pallas kernels, exchange(): pl.pallas_call(functools.partial(exchange_kernel, local, len(extras), sum...  187 us
    pallas_call x1, Pallas kernels, finish_last(): pl.pallas_call(finish_last_kernel, in_specs=[vmem] * 9, out_specs=[vmem]...  131 us
    pallas_call x1, Pallas kernels, gather_first(): pl.pallas_call(gather_first_kernel, in_specs=[vmem] * 3, out_specs=[anywh...  84.4 us
    pallas_call x1, Pallas kernels, feed(): pl.pallas_call(feed_kernel, grid=(tiles + columns // FEED_COLUMNS,), in_s...  76 us
    pallas_call x2, Pallas kernels, attend_back(): pl.pallas_call(functools.partial(attend_back_kernel, local_heads, own), g...  67.6 us
    ppermute x5, waiting for transfers between devices, passed_along(): return lax.ppermute(array, axis, pairs)  46.8 us
    pallas_call x2, Pallas kernels, attend(): pl.pallas_call(functools.partial(attend_kernel, local_heads, own), grid_s...  46 us
    dot_general x4, matrix products, dot(): return lax.dot_general(a, b, dims, preferred_element_type=f32, **kw)  32.8 us
  transfers between devices with their start and end apart: 9, of which 2 were waited for; matrix products, arithmetic and copies ran while one was open for 12% of the time, Pallas kernels for 67%

profile of v5, /device:TPU:0, one launch (start us, length us, event | category | flops | bytes accessed | tf_op | source)
XLA Modules:
  0.0 802.5 jit_solution(5700263410715053937)
XLA Ops:
  7.9 4.8 collective-permute-start
  21.2 84.4 %gather_first.1 = (bf16[8,4,48,2048]{3,2,1,0:T(8,128)(2,1)}, bf16[2048,1536]{1,0:T(8,128)(2,1)}, bf16[2048,1536]{1,0:T(8,128)(2,1)}) custom-call(bf16[4,48,2048]{2,1,0:T(8,128)(2,1)} %bitcast.131, bf16[512,1536]{1,0:T(8,128)(2,1)} %tokens_ref.3, bf16[512,1536]{1,0:T(8,128)(2,1)} %refs_1_.3), custom_call_target="tpu_custom_call" | custom-call | flops 70000001024 | bytes 30000000 | tf_op jit(solution)/shard_map/gather_first/pallas_call | solution.py:789
  105.6 1.8 convert_reduce_fusion.2
  108.7 16.3 %project.1 = (bf16[2048,1536]{1,0:T(8,128)(2,1)}, bf16[2048,768]{1,0:T(8,128)(2,1)}, bf16[2048,128]{1,0:T(8,128)(2,1)}, bf16[32,2048]{1,0:T(8,128)(2,1)}, f32[2048,128]{1,0:T(8,128)}) custom-call(bf16[2048,1536]{1,0:T(8,128)(2,1)} %get-tuple-element.60.tokens_ref, f32[8,1536]{1,0:T(8,128)} %broadcast_in_dim.51.gain_ref, bf16[1536,2048]{1,0:T(8,128)(2,1)} %bitcast.141, ...), custom_call_target="tpu_custom_call" | custom-call | flops 5637144576 | bytes 20000000 | tf_op jit(solution)/shard_map/project/pallas_call | solution.py:102
  125.0 5.2 collective-permute-start.1
  131.6 3.5 all-to-all-start
  135.2 1.9 collective-permute-start.2
  137.1 7.7 convolution_convert_fusion.2.q_ref
  144.8 3.3 convert_reduce_fusion
  149.5 37.0 %attend_own.1 = (f32[384,2048]{1,0:T(8,128)}, f32[24,2048]{1,0:T(8,128)}) custom-call(s32[2,4]{1,0:T(2,128)} %pad_add_fusion.1.ranges_ref, bf16[2048,384]{1,0:T(8,128)(2,1)} %convolution_convert_fusion.2.q_ref, bf16[2048,768]{1,0:T(8,128)(2,1)} %get-tuple-element.63.k_ref.v_ref, bf16[2048,768]{1,0:T(8,128)(2,1)} %get-tuple-element.63.k_ref.v_ref, ...), custom_call_target="tpu_custom_call" | custom-call | flops 40000000000 | bytes 12000000 | tf_op jit(solution)/shard_map/attend_own/pallas_call | solution.py:326
  186.5 12.8 %collective-permute-done.2.t_key_ref = bf16[32,2048]{1,0:T(8,128)(2,1)S(1)} collective-permute-done((bf16[32,2048]{1,0:T(8,128)(2,1)S(1)}, bf16[32,2048]{1,0:T(8,128)(2,1)S(1)}, u32[]{:S(2)}, u32[]{:S(2)}) %collective-permute-start.2) | collective-permute-done | bytes 131104 | tf_op jit(solution)/shard_map/ppermute | solution.py:28
  202.3 8.6 %add_divide_fusion = f32[2048,384]{1,0:T(8,128)} fusion(bf16[2048,1536]{1,0:T(8,128)(2,1)} %get-tuple-element.62, bf16[1536,2048]{1,0:T(8,128)(2,1)} %bitcast.143), kind=kOutput, calls=%fused_computation.15 | convolution fusion | flops 2418278400 | bytes 10616832 | tf_op jit(solution)/shard_map/dot_general | solution.py:22
  211.7 8.9 %attend_prev.1 = (bf16[2048,384]{1,0:T(8,128)(2,1)}, f32[24,2048]{1,0:T(8,128)}) custom-call(s32[2,4]{1,0:T(2,128)} %pad_add_fusion.1.ranges_ref, bf16[2048,384]{1,0:T(8,128)(2,1)} %convolution_convert_fusion.2.q_ref, bf16[2048,768]{1,0:T(8,128)(2,1)} %collective-permute-done.1.k_ref.v_ref, bf16[2048,768]{1,0:T(8,128)(2,1)} %collective-permute-done.1.k_ref.v_ref, ...), custom_call_target="tpu_custom_call" | custom-call | flops 10000000000 | bytes 12000000 | tf_op jit(solution)/shard_map/attend_prev/pallas_call | solution.py:326
  220.7 7.9 convolution_convert_fusion.refs_0_
  229.2 99.9 %exchange_middle.1 = (f32[512,1536]{1,0:T(8,128)}, bf16[2048,1536]{1,0:T(8,128)(2,1)}, bf16[8,4,48,1024]{3,2,1,0:T(8,128)(2,1)}) custom-call(bf16[2048,1536]{1,0:T(8,128)(2,1)} %convolution_convert_fusion.refs_0_, bf16[512,1536]{1,0:T(8,128)(2,1)} %tokens_ref.3, f32[8,1536]{1,0:T(8,128)} %broadcast_in_dim.54.refs_2_.refs_3_, bf16[4,48,1024]{2,1,0:T(8,128)(2,1)} %bitcast.138), custom_call_target="tpu_custom_call" | custom-call | flops 80000000000 | bytes 16000000 | tf_op jit(solution)/shard_map/exchange_middle/pallas_call | solution.py:1046
  329.1 76.0 %feed.1 = (bf16[2048,1536]{1,0:T(8,128)(2,1)}, bf16[1536,2048]{1,0:T(8,128)(2,1)}, bf16[1536,1024]{1,0:T(8,128)(2,1)}, f32[512,1536]{1,0:T(8,128)}) custom-call(bf16[2048,1536]{1,0:T(8,128)(2,1)} %get-tuple-element.78.input_ref, bf16[2048,1536]{1,0:T(8,128)(2,1)} %get-tuple-element.79.cotangent_ref, ...), custom_call_target="tpu_custom_call" | custom-call | flops 57982058496 | bytes 45000000 | tf_op jit(solution)/shard_map/feed/pallas_call | solution.py:1340
  405.3 87.3 %exchange_hidden.1 = (f32[512,1536]{1,0:T(8,128)}, bf16[2048,1536]{1,0:T(8,128)(2,1)}, bf16[4,48,1024]{2,1,0:T(8,128)(2,1)}) custom-call(f32[512,1536]{1,0:T(8,128)} %get-tuple-element.83.refs_0_, bf16[512,1536]{1,0:T(8,128)(2,1)} %refs_1_.3, f32[512,1536]{1,0:T(8,128)} %get-tuple-element.77.refs_2_, f32[8,1536]{1,0:T(8,128)} %broadcast_in_dim.54.refs_2_.refs_3_, ...), custom_call_target="tpu_custom_call" | custom-call | flops 60000002048 | bytes 16000000 | tf_op jit(solution)/shard_map/exchange_hidden/pallas_call | solution.py:1046
  492.6 8.7 %multiply_convert_fusion = (bf16[2048,384]{1,0:T(8,128)(2,1)}, f32[2048,384]{1,0:T(8,128)}) fusion(f32[2048,384]{1,0:T(8,128)S(1)} %copy-done.11, bf16[2048,1536]{1,0:T(8,128)(2,1)} %get-tuple-element.85, bf16[1536,2048]{1,0:T(8,128)(2,1)} %bitcast.145), kind=kOutput, calls=%fused_computation.14 | convolution fusion | flops 2417491968 | bytes 15335424 | tf_op jit(solution)/shard_map/dot_general | solution.py:22
  501.3 10.9 %attend_back_prev.1 = (f32[2048,384]{1,0:T(8,128)}, f32[2048,128]{1,0:T(8,128)}, bf16[2,2048,384]{2,1,0:T(8,128)(2,1)}, f32[2048,128]{1,0:T(8,128)}) custom-call(s32[2,4]{1,0:T(2,128)} %pad_add_fusion.1.ranges_ref, bf16[2048,384]{1,0:T(8,128)(2,1)} %convolution_convert_fusion.2.q_ref, bf16[2048,768]{1,0:T(8,128)(2,1)} %collective-permute-done.1.k_ref.v_ref, ...), custom_call_target="tpu_custom_call" | custom-call | flops 15000000512 | bytes 25000000 | tf_op jit(solution)/shard_map/attend_back_prev/pallas_call | solution.py:487
  513.5 1.5 copy.111
  516.6 56.8 %attend_back_own.1 = (bf16[2048,384]{1,0:T(8,128)(2,1)}, f32[2048,384]{1,0:T(8,128)}, f32[2048,384]{1,0:T(8,128)}, f32[2048,128]{1,0:T(8,128)}) custom-call(s32[2,4]{1,0:T(2,128)} %pad_add_fusion.1.ranges_ref, bf16[2048,384]{1,0:T(8,128)(2,1)} %convolution_convert_fusion.2.q_ref, bf16[2048,768]{1,0:T(8,128)(2,1)} %get-tuple-element.63.k_ref.v_ref, ...), custom_call_target="tpu_custom_call" | custom-call | flops 80000000000 | bytes 25000000 | tf_op jit(solution)/shard_map/attend_back_own/pallas_call | solution.py:487
  573.3 34.0 %collective-permute-done.3 = f32[2048,8]{0,1:T(8,128)S(1)} collective-permute-done((f32[2048,8]{0,1:T(8,128)S(1)}, f32[2048,8]{0,1:T(8,128)S(1)}, u32[]{:S(2)}, u32[]{:S(2)}) %collective-permute-start.3) | collective-permute-done | bytes 65568 | tf_op jit(solution)/shard_map/ppermute | solution.py:28
  608.7 4.5 decay_back.1
  613.1 1.9 convert_reduce_fusion.1
  615.5 1.9 fusion.6
  617.9 2.2 fusion.7
  623.3 2.8 copy-done.27
  626.1 15.7 %select_convert_fusion = bf16[1536,1664]{1,0:T(8,128)(2,1)} fusion(bf16[2048,1536]{1,0:T(8,128)(2,1)} %get-tuple-element.62, bf16[2048,1664]{1,0:T(8,128)(2,1)S(1)} %fusion.8.grads_ref, bf16[1536]{0:T(1024)(128)(2,1)S(1)} %select_reduce_fusion, pred[1664]{0:T(1024)(128)(4,1)S(1)} %copy-done.32), kind=kOutput, calls=%fused_computation.1 | convolution fusion | flops 10471538688 | bytes 18223744 | tf_op jit(solution)/shard_map/dot_general | solution.py:1382
  641.9 7.7 convolution_convert_fusion.1
  649.6 131.3 %finish_last.1 = (bf16[4,48,1664]{2,1,0:T(8,128)(2,1)}, bf16[4,48,384]{2,1,0:T(8,128)(2,1)}, bf16[4,48,2048]{2,1,0:T(8,128)(2,1)}, bf16[4,48,1024]{2,1,0:T(8,128)(2,1)}, f32[512,1536]{1,0:T(8,128)}) custom-call(bf16[2048,1664]{1,0:T(8,128)(2,1)} %copy-done.27, bf16[1536,2048]{1,0:T(8,128)(2,1)} %bitcast.146, bf16[8,4,48,1664]{3,2,1,0:T(8,128)(2,1)} %bitcast.149, ...), custom_call_target="tpu_custom_call" | custom-call | flops 89999998976 | bytes 40000000 | tf_op jit(solution)/shard_map/finish_last/pallas_call | solution.py:1154
  790.7 3.2 add_convert_fusion
  793.8 1.7 copy.158
  (167 shorter events, 35.7 us)
Async XLA Ops:
  7.9 136.9 %collective-permute-start = (s32[2048]{0:T(1024)S(1)}, s32[2048]{0:T(1024)S(1)}, u32[]{:S(2)}, u32[]{:S(2)}) collective-permute-start(s32[2048]{0:T(1024)S(1)} %broadcast_add_fusion), channel_id=1, source_target_pairs={{0,4},{4,8},{8,12},{12,16},{16,20},{20,24},{24,28},{1,5},{5,9},{9,... | collective-permute-start | bytes 24584 | tf_op jit(solution)/shard_map/ppermute | solution.py:28
  21.2 86.2 %copy-start.38 = (f32[24]{0:T(128)S(1)}, f32[24]{0:T(128)}, u32[]{:S(2)}) copy-start(f32[24]{0:T(128)} %param.23) | copy-start | bytes 292
  108.7 21.5 %copy-start.4 = (f32[48,4096]{1,0:T(8,128)S(1)}, f32[48,4096]{1,0:T(8,128)}, u32[]{:S(2)}) copy-start(f32[48,4096]{1,0:T(8,128)} %param.26) | copy-start | bytes 2359300
  108.7 21.6 %copy-start.6 = (f32[48,4096]{1,0:T(8,128)S(1)}, f32[48,4096]{1,0:T(8,128)}, u32[]{:S(2)}) copy-start(f32[48,4096]{1,0:T(8,128)} %param.27) | copy-start | bytes 2359300
  108.7 21.6 %copy-start.24 = (f32[48,4096]{1,0:T(8,128)S(1)}, f32[48,4096]{1,0:T(8,128)}, u32[]{:S(2)}) copy-start(f32[48,4096]{1,0:T(8,128)} %param.28) | copy-start | bytes 2359300
  125.0 74.4 %collective-permute-start.1 = (bf16[2048,768]{1,0:T(8,128)(2,1)}, bf16[2048,768]{1,0:T(8,128)(2,1)}, u32[]{:S(2)}, u32[]{:S(2)}) collective-permute-start(bf16[2048,768]{1,0:T(8,128)(2,1)} %get-tuple-element.63.k_ref.v_ref), channel_id=1, source_target_pairs={{0,4},{4,8},{8,12},{12,16},{16,20},{20,24},{24,28},{1,5},{5,9},{9,... | collective-permute-start | bytes 9437192 | tf_op jit(solution)/shard_map/ppermute | solution.py:28
  130.4 4.8 copy-start.37
  131.6 67.8 %all-to-all-start = ((bf16[48,4,3072]{2,0,1:T(8,128)(2,1)}), bf16[48,4,3072]{2,0,1:T(8,128)(2,1)S(1)}, u32[]{:S(2)}, u32[]{:S(2)}) async-start(bf16[48,4,3072]{2,0,1:T(8,128)(2,1)} %pad_maximum_fusion), calls=%async_computation | async-start | bytes 2359296 | tf_op jit(solution)/shard_map/all_to_all | solution.py:1391
  135.2 194.0 %all-gather.2.cloned.1.call-start = ((), (), s32[]{:S(2)}) async-start(), calls=%async_computation.3 | async-start | bytes 7077888 | tf_op jit(solution)/shard_map/all_gather | solution.py:1396
  135.2 64.2 %collective-permute-start.2 = (bf16[32,2048]{1,0:T(8,128)(2,1)S(1)}, bf16[32,2048]{1,0:T(8,128)(2,1)S(1)}, u32[]{:S(2)}, u32[]{:S(2)}) collective-permute-start(bf16[32,2048]{1,0:T(8,128)(2,1)S(1)} %copy-done.37), channel_id=1, source_target_pairs={{0,4},{4,8},{8,12},{12,16},{16,20},{20,24},{24,28},{1,5},{5,9},{9,... | collective-permute-start | bytes 393224 | tf_op jit(solution)/shard_map/ppermute | solution.py:28
  199.4 11.5 %copy-start.36 = (bf16[32,2048]{1,0:T(8,128)(2,1)}, bf16[32,2048]{1,0:T(8,128)(2,1)S(1)}, u32[]{:S(2)}) copy-start(bf16[32,2048]{1,0:T(8,128)(2,1)S(1)} %collective-permute-done.2.t_key_ref) | copy-start | bytes 393220
  200.4 441.5 %reduce-scatter.3.cloned.1.call-start = ((), (), s32[]{:S(2)}) async-start(), calls=%async_computation.4 | async-start | bytes 7077888 | tf_op jit(solution)/shard_map/reduce_scatter | solution.py:1400
  211.7 9.0 %copy-start.10 = (f32[2048,384]{1,0:T(8,128)S(1)}, f32[2048,384]{1,0:T(8,128)}, u32[]{:S(2)}) copy-start(f32[2048,384]{1,0:T(8,128)} %add_divide_fusion) | copy-start | bytes 9437188
  405.1 385.5 %reduce-scatter.5.cloned.1.call-start = ((), (), s32[]{:S(2)}) async-start(), calls=%async_computation.5 | async-start | bytes 7864320 | tf_op jit(solution)/shard_map/reduce_scatter | solution.py:1542
  405.3 87.3 %copy-start.11 = (f32[2048,384]{1,0:T(8,128)S(1)}, f32[2048,384]{1,0:T(8,128)}, u32[]{:S(2)}) copy-start(f32[2048,384]{1,0:T(8,128)} %add_divide_fusion) | copy-start | bytes 9437188
  512.2 103.3 %collective-permute-start.4 = (bf16[2,2048,384]{2,1,0:T(8,128)(2,1)}, bf16[2,2048,384]{2,1,0:T(8,128)(2,1)}, u32[]{:S(2)}, u32[]{:S(2)}) collective-permute-start(bf16[2,2048,384]{2,1,0:T(8,128)(2,1)} %get-tuple-element.93), channel_id=1, source_target_pairs={{4,0},{8,4},{12,8},{16,12},{20,16},{24,20},{28,24},{5,1},{9,5},{13... | collective-permute-start | bytes 9437192 | tf_op jit(solution)/shard_map/ppermute | solution.py:28
  515.0 92.2 %collective-permute-start.3 = (f32[2048,8]{0,1:T(8,128)S(1)}, f32[2048,8]{0,1:T(8,128)S(1)}, u32[]{:S(2)}, u32[]{:S(2)}) collective-permute-start(f32[2048,8]{0,1:T(8,128)S(1)} %copy.111), channel_id=1, source_target_pairs={{4,0},{8,4},{12,8},{16,12},{20,16},{24,20},{28,24},{5,1},{9,5},{13... | collective-permute-start | bytes 196616 | tf_op jit(solution)/shard_map/ppermute | solution.py:28
  573.3 39.8 %copy-start.33 = (pred[128]{0:T(512)(128)(4,1)S(1)}, pred[128]{0:T(512)(128)(4,1)}, u32[]{:S(2)}) copy-start(pred[128]{0:T(512)(128)(4,1)} %iota_compare_fusion.2) | copy-start | bytes 388
  608.7 6.3 copy-start.31
  608.7 6.9 copy-start.3
  617.9 2.8 copy-start.13
  617.9 3.3 copy-start.14
  622.4 3.8 copy-start.32
  623.3 2.9 copy-start.27
  780.9 4.5 copy-start.28
  782.1 4.0 copy-start.25
  782.2 6.1 copy-start.29
  782.4 6.0 copy-start.20
  786.6 2.4 copy-start.8
  786.7 2.5 copy-start.5
  786.8 2.6 copy-start.9
  790.7 3.2 copy-start.1
  (16 other events, 31.9 us)
Sparse Core Ops, SparseCore 0:
  200.5 124.2 all-gather.1
  405.2 169.4 reduce-scatter.2
  642.0 105.6 reduce-scatter.4

commit v6 on v5

--- a/solution.py
+++ b/solution.py
@@ -979,17 +979,17 @@
 
 
 def exchange_kernel(local, extras, summed, *refs):
-    part_ref, extra_refs, mine_ref = refs[0], refs[1 : 1 + extras], refs[1 + extras]
-    out_ref, all_ref, weight_ref, payload = refs[2 + extras : 6 + extras]
-    sems = refs[6 + extras :]
+    part_ref, extra_refs, refs = refs[0], refs[1 : 1 + extras], refs[1 + extras :]
+    if summed:
+        out_ref, all_ref, payload, *sems = refs
+    else:
+        mine_ref, out_ref, all_ref, weight_ref, payload, *sems = refs
     size = out_ref.shape[0]
     span = size // PIECES
     _, near, far, _ = partners()
     slots = Slots(summed)
     if summed:
-        beside = RowSums([(mine_ref, sems[7], sems[8], weight_ref)], sems[9:13])
-        greet([on_head(near), on_head(far)] + beside.others())
-        beside.start()
+        greet([on_head(near), on_head(far)])
     else:
         kinds = mine_ref.shape[0]
         beside = Line(lambda kind, blk: weight_ref.at[blk, kind], kinds, sems[-7:-1])
@@ -1015,68 +1015,63 @@
         payload[here, :] = share.astype(bf16)
         source = payload.at[pl.ds(piece * span, span), :]
         sent.append(spread_piece(source, all_ref, size, sems[:7], piece, slots))
-    if summed:
-        for c in range(len(beside.chunks)):
-            beside.pass_on(c)
-    finish_rows = hand_on(all_ref, size, sems[:7], sent, slots)
-    if summed:
-        for c in range(len(beside.chunks)):
-            beside.add_up(c)
-    finish_rows()
+    hand_on(all_ref, size, sems[:7], sent, slots)()
     if not summed:
         shares.finish()
-    beside.finish()
-
-
-def exchange(local, part, extras, summed, number, name, mine):
+        beside.finish()
+
+
+def exchange(local, part, extras, summed, number, name, mine=None):
     rows, width = part.shape
     size = rows if summed else rows // 4
     peers = lax.axis_size("blk")
     vmem, anywhere = pl.BlockSpec(memory_space=pltpu.VMEM), pl.BlockSpec(memory_space=pl.ANY)
+    inputs = [part, *extras]
+    out_specs = [vmem, anywhere]
+    out_shape = [
+        jax.ShapeDtypeStruct((size, width), f32),
+        jax.ShapeDtypeStruct((4 * size, width), bf16),
+    ]
     scratch = [pltpu.VMEM((size, width), bf16)] + gather_sems()
-    if summed:
-        beside = mine.shape[1:]
-        scratch += row_sum_buffers(peers // 2, *beside)
-        scratch += row_sum_sems(len(column_chunks(beside[2])), peers // 2)
-    else:
-        beside = (peers,) + mine.shape
+    if not summed:
+        inputs.append(mine)
+        out_specs.append(anywhere)
+        out_shape.append(jax.ShapeDtypeStruct((peers,) + mine.shape, bf16))
         scratch += sum_buffers(size, width) + sum_sems()
         scratch += [pltpu.SemaphoreType.DMA((mine.shape[0], peers // 2)) for _ in range(6)]
         scratch.append(pltpu.SemaphoreType.DMA)
     return pl.pallas_call(
         functools.partial(exchange_kernel, local, len(extras), summed),
-        in_specs=[vmem] * (2 + len(extras)),
-        out_specs=[vmem, anywhere, vmem if summed else anywhere],
-        out_shape=[
-            jax.ShapeDtypeStruct((size, width), f32),
-            jax.ShapeDtypeStruct((4 * size, width), bf16),
-            jax.ShapeDtypeStruct(beside, bf16),
-        ],
+        in_specs=[vmem] * len(inputs),
+        out_specs=out_specs,
+        out_shape=out_shape,
         scratch_shapes=scratch,
         compiler_params=pltpu.CompilerParams(collective_id=number, has_side_effects=True),
         cost_estimate=pl.CostEstimate(
-            flops=60_000_000_000 if summed else 80_000_000_000,
+            flops=40_000_000_000 if summed else 80_000_000_000,
             transcendentals=0,
             bytes_accessed=16_000_000,
         ),
         name=name,
-    )(part, *extras, mine)
-
-
-def finish_last_kernel(grads_ref, first_ref, grad_ref, output_grad_ref, second_ref, second_down_ref,
-                       grad_middle_ref, tokens_ref, gain_ref, weights_ref, output_ref,
-                       second_out_ref, second_down_out_ref, tokens_grad_ref, part_buf, *refs):
-    pair0, line0, pair1, line1, row0, row1 = refs[:6]
-    swap_send, swap_recv = refs[10:12]
+    )(*inputs)
+
+
+def finish_last_kernel(grads_ref, first_ref, grad_ref, output_grad_ref, down_grad_ref, second_ref,
+                       grad_middle_ref, tokens_ref, gain_ref, weights_ref, output_ref, down_ref,
+                       second_out_ref, tokens_grad_ref, part_buf, *refs):
+    swap_send, swap_recv = refs[13:15]
     me, near, far, cross = partners()
     others = (near, far, cross)
-    sums = RowSums(
-        [(grad_ref, pair0, line0, row0), (output_grad_ref, pair1, line1, row1)], refs[6:10]
-    )
-    outs = {id(row0): weights_ref, id(row1): output_ref}
+    arrays = (down_grad_ref, grad_ref, output_grad_ref)
+    sums = RowSums([(array,) + refs[3 * n : 3 * n + 3] for n, array in enumerate(arrays)], refs[9:13])
+    outs = [
+        out_ref
+        for array, out_ref in zip(arrays, (down_ref, weights_ref, output_ref))
+        for _ in column_chunks(array.shape[3])
+    ]
     greet([on_head(other) for other in others] + sums.others())
     size = tokens_grad_ref.shape[0]
-    first = Sum(part_buf, refs[12:15], refs[15:19], size, True)
+    first = Sum(part_buf, refs[15:18], refs[18:22], size, True)
     sums.start()
     sent = []
 
@@ -1091,7 +1086,6 @@
 
     count = len(sums.chunks)
     swap(second_ref, second_out_ref, count)
-    swap(second_down_ref, second_down_out_ref, count + 1)
     columns = grads_ref.shape[1]
     tiles = part_buf.shape[0] // 256
 
@@ -1100,18 +1094,16 @@
         part_buf[here, :] = dot(grads_ref[here, :], first_ref[:, :columns], NT).astype(bf16)
         return carry
 
-    lax.fori_loop(0, tiles // 4, multiply, 0)
-    sums.pass_on(0)
-    lax.fori_loop(tiles // 4, tiles, multiply, 0)
-    first.start()
-
     def add_up(c):
         sums.add_up(c)
         _, _, _, row_ref, at = sums.chunks[c]
-        out_ref = outs[id(row_ref)]
-        out_ref[me, :, at] = row_ref[me, :, at]
-        swap(row_ref.at[:, :, at], out_ref.at[:, :, at], c)
-
+        outs[c][me, :, at] = row_ref[me, :, at]
+        swap(row_ref.at[:, :, at], outs[c].at[:, :, at], c)
+
+    lax.fori_loop(0, tiles // 2, multiply, 0)
+    sums.pass_on(0)
+    lax.fori_loop(tiles // 2, tiles, multiply, 0)
+    first.start()
     for c in range(1, count):
         sums.pass_on(c)
         if c == 1:
@@ -1124,13 +1116,11 @@
         )
     add_up(count - 1)
     second_out_ref[me] = second_ref[me]
-    second_down_out_ref[me] = second_down_ref[me]
-    for c in range(count + 2):
+    for c in range(count + 1):
         if c < count:
-            _, _, _, row_ref, at = sums.chunks[c]
-            out_ref = outs[id(row_ref)].at[:, :, at]
+            out_ref = outs[c].at[:, :, sums.chunks[c][4]]
         else:
-            out_ref = second_out_ref if c == count else second_down_out_ref
+            out_ref = second_out_ref
         for kind, other in enumerate(others):
             block = out_ref.at[other]
             remote(
@@ -1142,47 +1132,50 @@
     first.finish()
 
 
-def finish_last(grads, first, grad, output_grad, second, second_down, grad_middle, tokens, gain,
-                number):
+def finish_last(grads, first, grad, output_grad, down_grad, second, groups, grad_middle, tokens,
+                gain, number):
     peers = lax.axis_size("blk")
-    groups, share, down_columns = second_down.shape
+    share = grad.shape[0] // (peers * groups)
     rows, width = tokens.shape
     vmem = pl.BlockSpec(memory_space=pltpu.VMEM)
     half = peers // 2
-    widths = (grad.shape[1], output_grad.shape[1])
-    chunks = sum(len(column_chunks(columns)) for columns in widths)
+    arrays = (down_grad, grad, output_grad)
+    chunks = sum(len(column_chunks(array.shape[1])) for array in arrays)
+
+    def blocks(array):
+        return array.reshape(peers, groups, share, array.shape[1])
+
+    def parts(array):
+        return jax.ShapeDtypeStruct((groups, share, array.shape[1]), bf16)
+
+    row_sum_scratch = []
+    for array in arrays:
+        row_sum_scratch += row_sum_buffers(half, groups, share, array.shape[1])
+        row_sum_scratch.append(pltpu.VMEM((groups, share, array.shape[1]), bf16))
     return pl.pallas_call(
         finish_last_kernel,
         in_specs=[vmem] * 9,
         out_specs=[vmem] * 5,
         out_shape=[
-            jax.ShapeDtypeStruct((groups, share, columns), bf16)
-            for columns in widths + (second.shape[1], down_columns)
-        ]
-        + [jax.ShapeDtypeStruct((rows, width), f32)],
+            parts(grad), parts(output_grad), parts(down_grad), parts(second),
+            jax.ShapeDtypeStruct((rows, width), f32),
+        ],
         scratch_shapes=[pltpu.VMEM((4 * rows, width), bf16)]
-        + row_sum_buffers(half, groups, share, widths[0])
-        + row_sum_buffers(half, groups, share, widths[1])
-        + [pltpu.VMEM((groups, share, columns), bf16) for columns in widths]
+        + row_sum_scratch
         + row_sum_sems(chunks, half)
-        + [pltpu.SemaphoreType.DMA((chunks + 2, 3)) for _ in range(2)]
+        + [pltpu.SemaphoreType.DMA((chunks + 1, 3)) for _ in range(2)]
         + sum_buffers(rows, width)
         + sum_sems(),
         compiler_params=pltpu.CompilerParams(
-            collective_id=number, has_side_effects=True, vmem_limit_bytes=62 << 20
+            collective_id=number, has_side_effects=True, vmem_limit_bytes=63 << 20
         ),
         cost_estimate=pl.CostEstimate(
-            flops=90_000_000_000, transcendentals=0, bytes_accessed=40_000_000
+            flops=110_000_000_000, transcendentals=0, bytes_accessed=40_000_000
         ),
         name="finish_last",
     )(
-        grads,
-        first,
-        grad.reshape(peers, groups, share, widths[0]),
-        output_grad.reshape(peers, groups, share, widths[1]),
-        second.reshape(groups, share, second.shape[1]),
-        second_down,
-        grad_middle, tokens, gain,
+        grads, first, blocks(grad), blocks(output_grad), blocks(down_grad),
+        second.reshape(groups, share, second.shape[1]), grad_middle, tokens, gain,
     )
 
 
@@ -1498,9 +1491,8 @@
         input2, cotangent_all, second, down_weight, 4
     )
     second_part = row_sums(second_grad)
-    grad_middle, grad_branch, down_part = exchange(
-        after_hidden, grad_input2, [cotangent, middle, gain2], True, 2, "exchange_hidden",
-        down_grad.reshape(-1, groups, share, hidden_width),
+    grad_middle, grad_branch = exchange(
+        after_hidden, grad_input2, [cotangent, middle, gain2], True, 2, "exchange_hidden"
     )
 
     grad_gated = dot(grad_branch, output_weight)
@@ -1535,9 +1527,10 @@
         column == 2 * local_width + local_heads, spread_bias, first_grad
     ).astype(bf16)
     output_grad = over_tokens(grad_branch, gated).astype(bf16)
-    down, second_part, first_grad = lax.optimization_barrier((down, second_part, first_grad))
-    first_sum, output_sum, second_sum, down_sum, tokens_grad = finish_last(
-        grads, first, first_grad, output_grad, second_part, down_part, grad_middle, tokens, gain1, 3
+    down, second_part = lax.optimization_barrier((down, second_part))
+    first_sum, output_sum, down_sum, second_sum, tokens_grad = finish_last(
+        grads, first, first_grad, output_grad, down_grad, second_part, groups, grad_middle, tokens,
+        gain1, 3,
     )
     down = lax.psum_scatter(down, "head", scatter_dimension=0, tiled=True)
     result = (middle + down.astype(f32)).astype(bf16)

time: 805 us -> 782 us (0.971)
  waiting for transfers between devices: 46.9 us -> 24.4 us
    pallas_call x2, Pallas kernels: 187 us -> 142 us  [exchange(): pl.pallas_call(functools.partial(exchange_kernel, local, len(extras), sum...]
    pallas_call x1, Pallas kernels: 131 us -> 155 us  [finish_last(): pl.pallas_call(finish_last_kernel, in_specs=[vmem] * 9, out_specs=[vmem]...]
    ppermute x5, waiting for transfers between devices: 46.8 us -> 24.3 us  [passed_along(): return lax.ppermute(array, axis, pairs)]
    pallas_call x2, Pallas kernels: 67.6 us -> 80.5 us  [attend_back(): pl.pallas_call(functools.partial(attend_back_kernel, local_heads, own), g...]
    pallas_call x2, Pallas kernels: 46 us -> 56.6 us  [attend(): pl.pallas_call(functools.partial(attend_kernel, local_heads, own), grid_s...]
  transfers between devices with their start and end apart: 9 -> 9, of which waited for: 2 -> 2; matrix products, arithmetic and copies ran while one was open for 12% -> 12% of each run, Pallas kernels for 67% -> 69%
where the time goes in v6:
time: 782 us
  Pallas kernels  615 us (79%)
  matrix products  56.4 us (7%)
  other arithmetic  30.1 us (4%)
  waiting for transfers between devices  24.4 us (3%)
  local copies, waits for them, and re-layouts  22.2 us (3%)
  starting transfers between devices  19 us (2%)
  between operations  14.7 us (2%)
    pallas_call x1, Pallas kernels, finish_last(): pl.pallas_call(finish_last_kernel, in_specs=[vmem] * 9, out_specs=[vmem]...  155 us
    pallas_call x2, Pallas kernels, exchange(): pl.pallas_call(functools.partial(exchange_kernel, local, len(extras), sum...  142 us
    pallas_call x1, Pallas kernels, gather_first(): pl.pallas_call(gather_first_kernel, in_specs=[vmem] * 3, out_specs=[anywh...  84.4 us
    pallas_call x2, Pallas kernels, attend_back(): pl.pallas_call(functools.partial(attend_back_kernel, local_heads, own), g...  80.5 us
    pallas_call x1, Pallas kernels, feed(): pl.pallas_call(feed_kernel, grid=(tiles + columns // FEED_COLUMNS,), in_s...  76.6 us
    pallas_call x2, Pallas kernels, attend(): pl.pallas_call(functools.partial(attend_kernel, local_heads, own), grid_s...  56.6 us
    dot_general x4, matrix products, dot(): return lax.dot_general(a, b, dims, preferred_element_type=f32, **kw)  32.9 us
    ppermute x5, waiting for transfers between devices, passed_along(): return lax.ppermute(array, axis, pairs)  24.3 us
  transfers between devices with their start and end apart: 9, of which 2 were waited for; matrix products, arithmetic and copies ran while one was open for 12% of the time, Pallas kernels for 69%

profile of v6, /device:TPU:0, one launch (start us, length us, event | category | flops | bytes accessed | tf_op | source)
XLA Modules:
  0.0 781.9 jit_solution(9925896475289864306)
XLA Ops:
  7.9 4.8 collective-permute-start
  21.2 84.4 %gather_first.1 = (bf16[8,4,48,2048]{3,2,1,0:T(8,128)(2,1)}, bf16[2048,1536]{1,0:T(8,128)(2,1)}, bf16[2048,1536]{1,0:T(8,128)(2,1)}) custom-call(bf16[4,48,2048]{2,1,0:T(8,128)(2,1)} %bitcast.131, bf16[512,1536]{1,0:T(8,128)(2,1)} %tokens_ref.3, bf16[512,1536]{1,0:T(8,128)(2,1)} %refs_1_.3), custom_call_target="tpu_custom_call" | custom-call | flops 70000001024 | bytes 30000000 | tf_op jit(solution)/shard_map/gather_first/pallas_call | solution.py:789
  105.6 1.8 convert_reduce_fusion.2
  108.7 16.3 %project.1 = (bf16[2048,1536]{1,0:T(8,128)(2,1)}, bf16[2048,768]{1,0:T(8,128)(2,1)}, bf16[2048,128]{1,0:T(8,128)(2,1)}, bf16[32,2048]{1,0:T(8,128)(2,1)}, f32[2048,128]{1,0:T(8,128)}) custom-call(bf16[2048,1536]{1,0:T(8,128)(2,1)} %get-tuple-element.58.tokens_ref, f32[8,1536]{1,0:T(8,128)} %broadcast_in_dim.51.gain_ref, bf16[1536,2048]{1,0:T(8,128)(2,1)} %bitcast.141, ...), custom_call_target="tpu_custom_call" | custom-call | flops 5637144576 | bytes 20000000 | tf_op jit(solution)/shard_map/project/pallas_call | solution.py:102
  125.1 5.1 collective-permute-start.1
  131.6 3.5 all-to-all-start
  135.2 2.0 collective-permute-start.2
  137.1 7.7 convolution_convert_fusion.2.q_ref
  144.8 3.3 convert_reduce_fusion
  149.5 47.7 %attend_own.1 = (f32[384,2048]{1,0:T(8,128)}, f32[24,2048]{1,0:T(8,128)}) custom-call(s32[2,4]{1,0:T(2,128)} %pad_add_fusion.1.ranges_ref, bf16[2048,384]{1,0:T(8,128)(2,1)} %convolution_convert_fusion.2.q_ref, bf16[2048,768]{1,0:T(8,128)(2,1)} %get-tuple-element.61.k_ref.v_ref, bf16[2048,768]{1,0:T(8,128)(2,1)} %get-tuple-element.61.k_ref.v_ref, ...), custom_call_target="tpu_custom_call" | custom-call | flops 40000000000 | bytes 12000000 | tf_op jit(solution)/shard_map/attend_own/pallas_call | solution.py:326
  197.2 2.2 collective-permute-done.2.t_key_ref
  202.5 8.5 %add_divide_fusion = f32[2048,384]{1,0:T(8,128)} fusion(bf16[2048,1536]{1,0:T(8,128)(2,1)} %get-tuple-element.60, bf16[1536,2048]{1,0:T(8,128)(2,1)} %bitcast.143), kind=kOutput, calls=%fused_computation.15 | convolution fusion | flops 2418278400 | bytes 10616832 | tf_op jit(solution)/shard_map/dot_general | solution.py:22
  211.8 8.9 %attend_prev.1 = (bf16[2048,384]{1,0:T(8,128)(2,1)}, f32[24,2048]{1,0:T(8,128)}) custom-call(s32[2,4]{1,0:T(2,128)} %pad_add_fusion.1.ranges_ref, bf16[2048,384]{1,0:T(8,128)(2,1)} %convolution_convert_fusion.2.q_ref, bf16[2048,768]{1,0:T(8,128)(2,1)} %collective-permute-done.1.k_ref.v_ref, bf16[2048,768]{1,0:T(8,128)(2,1)} %collective-permute-done.1.k_ref.v_ref, ...), custom_call_target="tpu_custom_call" | custom-call | flops 10000000000 | bytes 12000000 | tf_op jit(solution)/shard_map/attend_prev/pallas_call | solution.py:326
  220.7 7.8 %convolution_convert_fusion.refs_0_ = bf16[2048,1536]{1,0:T(8,128)(2,1)} fusion(bf16[1536,2048]{1,0:T(8,128)(2,1)} %bitcast.144, f32[2048,384]{1,0:T(8,128)S(1)} %copy-done.10, bf16[2048,384]{1,0:T(8,128)(2,1)} %get-tuple-element.73.o_ref), kind=kOutput, calls=%fused_computation.2 | convolution fusion | flops 2421424128 | bytes 12189696 | tf_op jit(solution)/shard_map/dot_general | solution.py:22
  229.2 97.9 %exchange_middle.1 = (f32[512,1536]{1,0:T(8,128)}, bf16[2048,1536]{1,0:T(8,128)(2,1)}, bf16[8,4,48,1024]{3,2,1,0:T(8,128)(2,1)}) custom-call(bf16[2048,1536]{1,0:T(8,128)(2,1)} %convolution_convert_fusion.refs_0_, bf16[512,1536]{1,0:T(8,128)(2,1)} %tokens_ref.3, f32[8,1536]{1,0:T(8,128)} %broadcast_in_dim.54.refs_2_.refs_3_, bf16[4,48,1024]{2,1,0:T(8,128)(2,1)} %bitcast.138), custom_call_target="tpu_custom_call" | custom-call | flops 80000000000 | bytes 16000000 | tf_op jit(solution)/shard_map/exchange_middle/pallas_call | solution.py:1043
  327.1 76.6 %feed.1 = (bf16[2048,1536]{1,0:T(8,128)(2,1)}, bf16[1536,2048]{1,0:T(8,128)(2,1)}, bf16[1536,1024]{1,0:T(8,128)(2,1)}, f32[512,1536]{1,0:T(8,128)}) custom-call(bf16[2048,1536]{1,0:T(8,128)(2,1)} %get-tuple-element.76.input_ref, bf16[2048,1536]{1,0:T(8,128)(2,1)} %get-tuple-element.77.cotangent_ref, ...), custom_call_target="tpu_custom_call" | custom-call | flops 57982058496 | bytes 45000000 | tf_op jit(solution)/shard_map/feed/pallas_call | solution.py:1333
  404.2 43.9 %exchange_hidden.1 = (f32[512,1536]{1,0:T(8,128)}, bf16[2048,1536]{1,0:T(8,128)(2,1)}) custom-call(f32[512,1536]{1,0:T(8,128)} %get-tuple-element.82.refs_0_, bf16[512,1536]{1,0:T(8,128)(2,1)} %refs_1_.3, f32[512,1536]{1,0:T(8,128)} %get-tuple-element.75.refs_2_, f32[8,1536]{1,0:T(8,128)} %broadcast_in_dim.54.refs_2_.refs_3_), custom_call_target="tpu_custom_call" | custom-call | flops 40000000000 | bytes 16000000 | tf_op jit(solution)/shard_map/exchange_hidden/pallas_call | solution.py:1043
  448.1 9.0 %multiply_convert_fusion = (bf16[2048,384]{1,0:T(8,128)(2,1)}, f32[2048,384]{1,0:T(8,128)}) fusion(f32[2048,384]{1,0:T(8,128)S(1)} %copy-done.11, bf16[2048,1536]{1,0:T(8,128)(2,1)} %get-tuple-element.83, bf16[1536,2048]{1,0:T(8,128)(2,1)} %bitcast.145), kind=kOutput, calls=%fused_computation.13 | convolution fusion | flops 2417491968 | bytes 15335424 | tf_op jit(solution)/shard_map/dot_general | solution.py:22
  457.1 10.9 %attend_back_prev.1 = (f32[2048,384]{1,0:T(8,128)}, f32[2048,128]{1,0:T(8,128)}, bf16[2,2048,384]{2,1,0:T(8,128)(2,1)}, f32[2048,128]{1,0:T(8,128)}) custom-call(s32[2,4]{1,0:T(2,128)} %pad_add_fusion.1.ranges_ref, bf16[2048,384]{1,0:T(8,128)(2,1)} %convolution_convert_fusion.2.q_ref, bf16[2048,768]{1,0:T(8,128)(2,1)} %collective-permute-done.1.k_ref.v_ref, ...), custom_call_target="tpu_custom_call" | custom-call | flops 15000000512 | bytes 25000000 | tf_op jit(solution)/shard_map/attend_back_prev/pallas_call | solution.py:487
  469.3 1.5 copy.111
  472.1 69.6 %attend_back_own.1 = (bf16[2048,384]{1,0:T(8,128)(2,1)}, f32[2048,384]{1,0:T(8,128)}, f32[2048,384]{1,0:T(8,128)}, f32[2048,128]{1,0:T(8,128)}) custom-call(s32[2,4]{1,0:T(2,128)} %pad_add_fusion.1.ranges_ref, bf16[2048,384]{1,0:T(8,128)(2,1)} %convolution_convert_fusion.2.q_ref, bf16[2048,768]{1,0:T(8,128)(2,1)} %get-tuple-element.61.k_ref.v_ref, ...), custom_call_target="tpu_custom_call" | custom-call | flops 80000000000 | bytes 25000000 | tf_op jit(solution)/shard_map/attend_back_own/pallas_call | solution.py:487
  541.7 7.7 convolution_convert_fusion.1
  549.5 22.1 %collective-permute-done.4 = f32[2048,8]{0,1:T(8,128)S(1)} collective-permute-done((f32[2048,8]{0,1:T(8,128)S(1)}, f32[2048,8]{0,1:T(8,128)S(1)}, u32[]{:S(2)}, u32[]{:S(2)}) %collective-permute-start.4) | collective-permute-done | bytes 65568 | tf_op jit(solution)/shard_map/ppermute | solution.py:28
  572.9 4.5 decay_back.1
  577.4 1.9 convert_reduce_fusion.1
  579.8 1.9 fusion.6
  582.2 2.2 fusion.7
  587.4 2.9 copy-done.27
  590.3 15.7 %select_convert_fusion = bf16[1536,1664]{1,0:T(8,128)(2,1)} fusion(bf16[2048,1536]{1,0:T(8,128)(2,1)} %get-tuple-element.60, bf16[2048,1664]{1,0:T(8,128)(2,1)S(1)} %fusion.8.grads_ref, bf16[1536]{0:T(1024)(128)(2,1)S(1)} %select_reduce_fusion, pred[1664]{0:T(1024)(128)(4,1)S(1)} %copy-done.32), kind=kOutput, calls=%fused_computation.1 | convolution fusion | flops 10471538688 | bytes 18223744 | tf_op jit(solution)/shard_map/dot_general | solution.py:1375
  606.0 154.6 %finish_last.1 = (bf16[4,48,1664]{2,1,0:T(8,128)(2,1)}, bf16[4,48,384]{2,1,0:T(8,128)(2,1)}, bf16[4,48,1024]{2,1,0:T(8,128)(2,1)}, bf16[4,48,2048]{2,1,0:T(8,128)(2,1)}, f32[512,1536]{1,0:T(8,128)}) custom-call(bf16[2048,1664]{1,0:T(8,128)(2,1)} %copy-done.27, bf16[1536,2048]{1,0:T(8,128)(2,1)} %bitcast.146, bf16[8,4,48,1664]{3,2,1,0:T(8,128)(2,1)} %bitcast.149, ...), custom_call_target="tpu_custom_call" | custom-call | flops 109999996928 | bytes 40000000 | tf_op jit(solution)/shard_map/finish_last/pallas_call | solution.py:1155
  770.4 3.2 add_convert_fusion
  773.5 1.7 copy.158
  (167 shorter events, 35.8 us)
Async XLA Ops:
  7.9 136.9 %collective-permute-start = (s32[2048]{0:T(1024)S(1)}, s32[2048]{0:T(1024)S(1)}, u32[]{:S(2)}, u32[]{:S(2)}) collective-permute-start(s32[2048]{0:T(1024)S(1)} %broadcast_add_fusion), channel_id=1, source_target_pairs={{0,4},{4,8},{8,12},{12,16},{16,20},{20,24},{24,28},{1,5},{5,9},{9,... | collective-permute-start | bytes 24584 | tf_op jit(solution)/shard_map/ppermute | solution.py:28
  21.2 86.2 %copy-start.38 = (f32[24]{0:T(128)S(1)}, f32[24]{0:T(128)}, u32[]{:S(2)}) copy-start(f32[24]{0:T(128)} %param.23) | copy-start | bytes 292
  108.7 21.5 %copy-start.4 = (f32[48,4096]{1,0:T(8,128)S(1)}, f32[48,4096]{1,0:T(8,128)}, u32[]{:S(2)}) copy-start(f32[48,4096]{1,0:T(8,128)} %param.26) | copy-start | bytes 2359300
  108.7 21.5 %copy-start.6 = (f32[48,4096]{1,0:T(8,128)S(1)}, f32[48,4096]{1,0:T(8,128)}, u32[]{:S(2)}) copy-start(f32[48,4096]{1,0:T(8,128)} %param.27) | copy-start | bytes 2359300
  108.7 21.6 %copy-start.24 = (f32[48,4096]{1,0:T(8,128)S(1)}, f32[48,4096]{1,0:T(8,128)}, u32[]{:S(2)}) copy-start(f32[48,4096]{1,0:T(8,128)} %param.28) | copy-start | bytes 2359300
  125.1 74.4 %collective-permute-start.1 = (bf16[2048,768]{1,0:T(8,128)(2,1)}, bf16[2048,768]{1,0:T(8,128)(2,1)}, u32[]{:S(2)}, u32[]{:S(2)}) collective-permute-start(bf16[2048,768]{1,0:T(8,128)(2,1)} %get-tuple-element.61.k_ref.v_ref), channel_id=1, source_target_pairs={{0,4},{4,8},{8,12},{12,16},{16,20},{20,24},{24,28},{1,5},{5,9},{9,... | collective-permute-start | bytes 9437192 | tf_op jit(solution)/shard_map/ppermute | solution.py:28
  130.4 4.8 copy-start.37
  131.6 67.8 %all-to-all-start = ((bf16[48,4,3072]{2,0,1:T(8,128)(2,1)}), bf16[48,4,3072]{2,0,1:T(8,128)(2,1)S(1)}, u32[]{:S(2)}, u32[]{:S(2)}) async-start(bf16[48,4,3072]{2,0,1:T(8,128)(2,1)} %pad_maximum_fusion), calls=%async_computation | async-start | bytes 2359296 | tf_op jit(solution)/shard_map/all_to_all | solution.py:1384
  135.1 192.0 %all-gather.2.cloned.1.call-start = ((), (), s32[]{:S(2)}) async-start(), calls=%async_computation.3 | async-start | bytes 7077888 | tf_op jit(solution)/shard_map/all_gather | solution.py:1389
  135.2 64.2 %collective-permute-start.2 = (bf16[32,2048]{1,0:T(8,128)(2,1)S(1)}, bf16[32,2048]{1,0:T(8,128)(2,1)S(1)}, u32[]{:S(2)}, u32[]{:S(2)}) collective-permute-start(bf16[32,2048]{1,0:T(8,128)(2,1)S(1)} %copy-done.37), channel_id=1, source_target_pairs={{0,4},{4,8},{8,12},{12,16},{16,20},{20,24},{24,28},{1,5},{5,9},{9,... | collective-permute-start | bytes 393224 | tf_op jit(solution)/shard_map/ppermute | solution.py:28
  199.4 11.6 %copy-start.36 = (bf16[32,2048]{1,0:T(8,128)(2,1)}, bf16[32,2048]{1,0:T(8,128)(2,1)S(1)}, u32[]{:S(2)}) copy-start(bf16[32,2048]{1,0:T(8,128)(2,1)S(1)} %collective-permute-done.2.t_key_ref) | copy-start | bytes 393220
  200.4 405.6 %reduce-scatter.3.cloned.1.call-start = ((), (), s32[]{:S(2)}) async-start(), calls=%async_computation.4 | async-start | bytes 7077888 | tf_op jit(solution)/shard_map/reduce_scatter | solution.py:1393
  211.8 8.9 %copy-start.10 = (f32[2048,384]{1,0:T(8,128)S(1)}, f32[2048,384]{1,0:T(8,128)}, u32[]{:S(2)}) copy-start(f32[2048,384]{1,0:T(8,128)} %add_divide_fusion) | copy-start | bytes 9437188
  403.7 366.6 %reduce-scatter.5.cloned.1.call-start = ((), (), s32[]{:S(2)}) async-start(), calls=%async_computation.5 | async-start | bytes 7864320 | tf_op jit(solution)/shard_map/reduce_scatter | solution.py:1535
  404.2 43.9 %copy-start.11 = (f32[2048,384]{1,0:T(8,128)S(1)}, f32[2048,384]{1,0:T(8,128)}, u32[]{:S(2)}) copy-start(f32[2048,384]{1,0:T(8,128)} %add_divide_fusion) | copy-start | bytes 9437188
  468.0 111.8 %collective-permute-start.3 = (bf16[2,2048,384]{2,1,0:T(8,128)(2,1)}, bf16[2,2048,384]{2,1,0:T(8,128)(2,1)}, u32[]{:S(2)}, u32[]{:S(2)}) collective-permute-start(bf16[2,2048,384]{2,1,0:T(8,128)(2,1)} %get-tuple-element.88), channel_id=1, source_target_pairs={{4,0},{8,4},{12,8},{16,12},{20,16},{24,20},{28,24},{5,1},{9,5},{13... | collective-permute-start | bytes 9437192 | tf_op jit(solution)/shard_map/ppermute | solution.py:28
  470.8 100.7 %collective-permute-start.4 = (f32[2048,8]{0,1:T(8,128)S(1)}, f32[2048,8]{0,1:T(8,128)S(1)}, u32[]{:S(2)}, u32[]{:S(2)}) collective-permute-start(f32[2048,8]{0,1:T(8,128)S(1)} %copy.111), channel_id=1, source_target_pairs={{4,0},{8,4},{12,8},{16,12},{20,16},{24,20},{28,24},{5,1},{9,5},{13... | collective-permute-start | bytes 196616 | tf_op jit(solution)/shard_map/ppermute | solution.py:28
  549.5 27.9 %copy-start.33 = (pred[128]{0:T(512)(128)(4,1)S(1)}, pred[128]{0:T(512)(128)(4,1)}, u32[]{:S(2)}) copy-start(pred[128]{0:T(512)(128)(4,1)} %iota_compare_fusion.2) | copy-start | bytes 388
  572.9 6.3 copy-start.31
  572.9 6.8 copy-start.3
  582.2 2.8 copy-start.13
  582.2 3.3 copy-start.14
  586.6 3.6 copy-start.32
  587.4 2.9 copy-start.27
  760.6 4.5 copy-start.28
  761.8 4.0 copy-start.25
  761.9 6.1 copy-start.29
  762.0 6.1 copy-start.20
  766.3 2.4 copy-start.8
  766.4 2.5 copy-start.5
  766.5 2.6 copy-start.9
  770.4 3.2 copy-start.1
  (16 other events, 31.9 us)
Sparse Core Ops, SparseCore 0:
  200.5 121.8 all-gather.1
  403.9 139.1 reduce-scatter.2
  606.1 93.4 reduce-scatter.4

commit v7 on v4

--- a/solution.py
+++ b/solution.py
@@ -516,7 +516,7 @@
         ),
         out_shape=out_shape,
         cost_estimate=pl.CostEstimate(
-            flops=80_000_000_000 if own else 15_000_000_000,
+            flops=20_000_000_000 if own else 10_000_000_000,
             transcendentals=20_000_000,
             bytes_accessed=25_000_000,
         ),
@@ -727,8 +727,24 @@
             lax.fori_loop(0, self.half, wait, 0)
 
 
-def gather_first_kernel(pack_ref, tokens_ref, cotangent_ref, pack_all, tokens_all, cotangent_all,
-                        *sems):
+def gather_first_kernel(before, after, *refs):
+    small_ref, weight_refs = refs[0], refs[1 : 1 + before + after]
+    tokens_ref, cotangent_ref, pack_all, tokens_all, cotangent_all, pack_ref = refs[
+        1 + before + after : 7 + before + after
+    ]
+    sems = refs[7 + before + after :]
+    groups = pack_ref.shape[0]
+    start = 0
+    for n, ref in enumerate(weight_refs):
+        if n == before:
+            pack_ref[:, :, start : start + LANES] = small_ref[...]
+            start += LANES
+        wide = ref.shape[1] // groups
+        for group in range(groups):
+            pack_ref[group, :, start : start + wide] = ref[
+                :, group * wide : (group + 1) * wide
+            ].astype(bf16)
+        start += wide
     swap_send, swap_recv, swap_own = sems[:3]
     token_sems, cotangent_sems = sems[9:16], sems[16:23]
     me, near, far, cross = partners()
@@ -780,18 +796,21 @@
     finish_cotangent()
 
 
-def gather_first(pack, tokens, cotangent, number):
-    groups, share, columns = pack.shape
+def gather_first(before, small, after, tokens, cotangent, number):
+    groups, share, _ = small.shape
+    weights = [*before, *after]
+    columns = LANES + sum(weight.shape[1] // groups for weight in weights)
     peers = lax.axis_size("blk")
     rows, width = tokens.shape
     whole = jax.ShapeDtypeStruct((groups * rows, width), bf16)
     vmem, anywhere = pl.BlockSpec(memory_space=pltpu.VMEM), pl.BlockSpec(memory_space=pl.ANY)
     all_pack, all_tokens, all_cotangent = pl.pallas_call(
-        gather_first_kernel,
-        in_specs=[vmem] * 3,
+        functools.partial(gather_first_kernel, len(before), len(after)),
+        in_specs=[vmem] * (3 + len(weights)),
         out_specs=[anywhere] * 3,
         out_shape=[jax.ShapeDtypeStruct((peers, groups, share, columns), bf16), whole, whole],
         scratch_shapes=[
+            pltpu.VMEM((groups, share, columns), bf16),
             pltpu.SemaphoreType.DMA((3,)),
             pltpu.SemaphoreType.DMA((3,)),
             pltpu.SemaphoreType.DMA,
@@ -804,7 +823,7 @@
             flops=70_000_000_000, transcendentals=0, bytes_accessed=30_000_000
         ),
         name="gather_first",
-    )(pack, tokens, cotangent)
+    )(small, *weights, tokens, cotangent)
     return all_pack.reshape(peers * groups * share, columns), all_tokens, all_cotangent
 
 
@@ -963,7 +982,7 @@
         scratch_shapes=scratch,
         compiler_params=pltpu.CompilerParams(collective_id=number, has_side_effects=True),
         cost_estimate=pl.CostEstimate(
-            flops=40_000_000_000 if summed else 70_000_000_000,
+            flops=10_000_000_000 if summed else 70_000_000_000,
             transcendentals=0,
             bytes_accessed=16_000_000,
         ),
@@ -977,13 +996,12 @@
     return [(0, first)] + [(first + 512 * n, 512) for n in range(count - 1)]
 
 
-def finish_last_kernel(grad_ref, output_grad_ref, second_ref, first_ref, down_ref, grad_middle_ref,
-                       tokens_ref, gain_ref, middle_ref, weights_ref, output_ref, second_out_ref,
-                       tokens_grad_ref, result_ref, *refs):
+def finish_last_kernel(grad_ref, output_grad_ref, second_ref, first_ref, grad_middle_ref, tokens_ref,
+                       gain_ref, weights_ref, output_ref, second_out_ref, tokens_grad_ref, *refs):
     buffers = (refs[0:3], refs[3:6])
-    first_buffers, down_buffers = refs[6:9], refs[9:12]
-    pair_send, pair_recv, line_send, line_recv, swap_send, swap_recv = refs[12:18]
-    first_sems, down_sems = refs[18:22], refs[22:26]
+    first_buffers = refs[6:9]
+    pair_send, pair_recv, line_send, line_recv, swap_send, swap_recv = refs[9:15]
+    first_sems = refs[15:19]
     me, near, far, cross = partners()
     others = (near, far, cross)
     here, partner, after = blk_peers()
@@ -993,9 +1011,8 @@
         + [on_blk(partner)]
         + [on_blk(peer) for peer in after[1:]]
     )
-    size = result_ref.shape[0]
+    size = tokens_grad_ref.shape[0]
     first = Sum(first_ref, first_buffers, first_sems, size, True)
-    down = Sum(down_ref, down_buffers, down_sems, size, False)
     chunks = []
     for ref, out_ref, some in (
         (grad_ref, weights_ref, buffers[0]), (output_grad_ref, output_ref, buffers[1])
@@ -1028,8 +1045,6 @@
             sent.append(copy)
 
     swap(second_ref, second_out_ref, len(chunks))
-    down.start()
-    down.turn()
 
     def add_up(c):
         ref, out_ref, (pair_buf, line_buf, row_buf), at = chunks[c]
@@ -1052,12 +1067,6 @@
         out_ref[me, :, at] = row_buf[me, :, at]
         swap(row_buf.at[:, :, at], out_ref.at[:, :, at], c)
 
-    def put(shares, local, out_ref, extra_refs):
-        for piece in range(PIECES):
-            rows = shares.piece(piece)
-            value, _ = local(shares.total(piece), rows, *extra_refs)
-            out_ref[rows, :] = value.astype(out_ref.dtype)
-
     for c, (ref, _, (pair_buf, line_buf, _), at) in enumerate(chunks):
         for t in range(1, steps):
             block = pair_buf.at[t, :, :, at]
@@ -1081,9 +1090,12 @@
             sent.append(copy)
         if c > 0:
             add_up(c - 1)
-    put(first, after_first, tokens_grad_ref, (grad_middle_ref, tokens_ref, gain_ref))
+    for piece in range(PIECES):
+        rows = first.piece(piece)
+        tokens_grad_ref[rows, :], _ = after_first(
+            first.total(piece), rows, grad_middle_ref, tokens_ref, gain_ref
+        )
     add_up(len(chunks) - 1)
-    put(down, after_down, result_ref, (middle_ref,))
     second_out_ref[me] = second_ref[me]
     for c in range(len(chunks) + 1):
         if c < len(chunks):
@@ -1099,11 +1111,9 @@
     for copy in sent:
         copy.wait_send()
     first.finish()
-    down.finish()
-
-
-def finish_last(grad, output_grad, second, groups, part_first, part_down, grad_middle, tokens, gain,
-                middle, number):
+
+
+def finish_last(grad, output_grad, second, groups, part_first, grad_middle, tokens, gain, number):
     peers = lax.axis_size("blk")
     share = grad.shape[0] // (peers * groups)
     rows, width = tokens.shape
@@ -1119,23 +1129,18 @@
 
     return pl.pallas_call(
         finish_last_kernel,
-        in_specs=[vmem] * 9,
-        out_specs=[vmem] * 5,
+        in_specs=[vmem] * 7,
+        out_specs=[vmem] * 4,
         out_shape=[
             jax.ShapeDtypeStruct((groups, share, columns), bf16)
             for columns in widths + (second.shape[1],)
         ]
-        + [
-            jax.ShapeDtypeStruct((rows, width), f32),
-            jax.ShapeDtypeStruct((rows, width), bf16),
-        ],
+        + [jax.ShapeDtypeStruct((rows, width), f32)],
         scratch_shapes=blocks(widths[0])
         + blocks(widths[1])
         + sum_buffers(rows, width)
-        + sum_buffers(rows, width)
         + [pltpu.SemaphoreType.DMA((chunks, half)) for _ in range(4)]
         + [pltpu.SemaphoreType.DMA((chunks + 1, 3)) for _ in range(2)]
-        + sum_sems()
         + sum_sems(),
         compiler_params=pltpu.CompilerParams(
             collective_id=number, has_side_effects=True, vmem_limit_bytes=60 << 20
@@ -1148,7 +1153,7 @@
         grad.reshape(peers, groups, share, widths[0]),
         output_grad.reshape(peers, groups, share, widths[1]),
         second.reshape(groups, share, second.shape[1]),
-        part_first, part_down, grad_middle, tokens, gain, middle,
+        part_first, grad_middle, tokens, gain,
     )
 
 
@@ -1179,10 +1184,6 @@
         total * gain_ref[0:1, :], tokens_ref[here, :].astype(f32)
     )
     return grad, None
-
-
-def after_down(total, here, middle_ref):
-    return middle_ref[here, :] + total, None
 
 
 FEED_TILE = 256
@@ -1353,6 +1354,20 @@
     return lax.psum_scatter(grad, "blk", scatter_dimension=0, tiled=True)
 
 
+def crossing_sum(part):
+    cross, far, near, own = (piece.astype(f32) for piece in jnp.split(part, 4))
+    members = range(lax.axis_size("head"))
+    got = lax.ppermute(
+        jnp.concatenate([cross, near]).astype(bf16), "head",
+        [(n, n + 1 - 2 * (n % 2)) for n in members],
+    )
+    of_far, of_own = jnp.split(got.astype(f32), 2)
+    back = lax.ppermute(
+        (far + of_far).astype(bf16), "head", [(n, (n + 2) % 4) for n in members]
+    )
+    return own + of_own + back.astype(f32)
+
+
 def body(
     tokens,
     segment,
@@ -1388,28 +1403,12 @@
         [forget_low, spread(norm1_gain), spread(norm2_gain), jnp.zeros((share, groups, rest), bf16)],
         axis=2,
     )
-    pack = jnp.concatenate(
-        [
-            low(piece).reshape(share, groups, -1)
-            for piece in (w_key, w_value, small, w_query, w_gate_out, w_output)
-        ],
-        axis=2,
-    )
     first, tokens_all, cotangent_all = gather_first(
-        jnp.swapaxes(pack, 0, 1), tokens, cotangent, 0
+        (w_key, w_value), jnp.swapaxes(small, 0, 1), (w_query, w_gate_out, w_output), tokens,
+        cotangent, 0,
     )
     kv_width = 2 * local_width + LANES
     output_weight = first[:, kv_width + 2 * local_width :]
-
-    segment_plus = segment + 1
-    earlier_segment = passed_along(segment_plus, "blk", 1)
-    window = jnp.concatenate([earlier_segment, segment_plus])
-    begins = jnp.sum(
-        (window[:, None] < segment_plus[None, :]).astype(jnp.int32), axis=0
-    )
-    tiles = begins.reshape(rows // Q_TILE, Q_TILE)
-    ranges = jnp.stack([tiles[:, 0] // K_TILE, (tiles[:, -1] + K_TILE - 1) // K_TILE])
-    begins = jnp.broadcast_to(begins[None, :], (8, rows))
 
     def gain_rows(column):
         gain = first[:, 2 * local_width + local_heads + column].astype(f32)
@@ -1428,9 +1427,19 @@
         input1, first[:, kv_width + local_width : kv_width + 2 * local_width]
     )
 
+    segment_plus, _ = lax.optimization_barrier((segment + 1, key_value))
+    earlier_segment = passed_along(segment_plus, "blk", 1)
+    window = jnp.concatenate([earlier_segment, segment_plus])
+    begins = jnp.sum(
+        (window[:, None] < segment_plus[None, :]).astype(jnp.int32), axis=0
+    )
+    tiles = begins.reshape(rows // Q_TILE, Q_TILE)
+    ranges = jnp.stack([tiles[:, 0] // K_TILE, (tiles[:, -1] + K_TILE - 1) // K_TILE])
+    begins = jnp.broadcast_to(begins[None, :], (8, rows))
+
     so_far = attend(True, ranges, query, key_value, terms, terms, begins, local_heads)
-    later = lax.optimization_barrier((low(w_gate), low(w_up), low(w_down), key_value))
-    mine = sent_columns(later[:3], groups)
+    later = lax.optimization_barrier((w_gate, w_up, w_down, key_value))
+    mine = sent_columns([low(weight) for weight in later[:3]], groups)
     mine, earlier_kv, earlier_terms, so_far = lax.optimization_barrier(
         (mine, earlier_kv, earlier_terms, so_far)
     )
@@ -1453,6 +1462,8 @@
         after_hidden, grad_input2, [cotangent, middle, gain2], True, 2, "exchange_hidden"
     )
 
+    down, grad_branch = lax.optimization_barrier((down, grad_branch))
+    result = (middle + crossing_sum(down)).astype(bf16)
     grad_gated = dot(grad_branch, output_weight)
     grad_attended = (grad_gated * opened).astype(bf16)
     grad_gate_pre = (grad_gated * attended_wide * opened * (1.0 - opened)).astype(bf16)
@@ -1486,9 +1497,8 @@
     ).astype(bf16)
     output_grad = over_tokens(grad_branch, gated).astype(bf16)
     grad_input1 = dot(grads, first[:, : kv_width + 2 * local_width], NT).astype(bf16)
-    first_sum, output_sum, second_sum, tokens_grad, result = finish_last(
-        first_grad, output_grad, second_part, groups, grad_input1, down, grad_middle, tokens,
-        gain1, middle, 3,
+    first_sum, output_sum, second_sum, tokens_grad = finish_last(
+        first_grad, output_grad, second_part, groups, grad_input1, grad_middle, tokens, gain1, 3
     )
     first_sum, output_sum, second_sum = (
         jnp.swapaxes(array, 0, 1).astype(f32) for array in (first_sum, output_sum, second_sum)

time: 767 us -> 802 us (1.046)
  waiting for transfers between devices: 56 us -> 85.7 us
    ppermute x5, waiting for transfers between devices: 37.2 us -> 75.9 us  [passed_along(): return lax.ppermute(array, axis, pairs)]
    reduce_scatter x1, waiting for transfers between devices: 18.7 us -> 6.99 us  [row_sums(): return lax.psum_scatter(grad, 'blk', scatter_dimension=0, tiled=True)]
    pallas_call x2, Pallas kernels: 192 us -> 183 us  [the longest x1 96.3 us: finish_last(): pl.pallas_call(finish_last_kernel, in_specs=[vmem] * 7, out_specs=[vmem]...]
  transfers between devices with their start and end apart: 8 -> 10, of which waited for: 3 -> 4; matrix products, arithmetic and copies ran while one was open for 13% -> 13% of each run, Pallas kernels for 49% -> 35%
where the time goes in v7:
time: 802 us; the launch traced here: 795 us
  Pallas kernels  549 us (68%)
  waiting for transfers between devices  85.7 us (11%)
  matrix products  73.1 us (9%)
  other arithmetic  33 us (4%)
  local copies, waits for them, and re-layouts  20.1 us (3%)
  starting transfers between devices  19.1 us (2%)
  between operations  15.2 us (2%)
    pallas_call x2, Pallas kernels, exchange(): pl.pallas_call(functools.partial(exchange_kernel, local, len(extras), sum...  149 us
    pallas_call x1, Pallas kernels, finish_last(): pl.pallas_call(finish_last_kernel, in_specs=[vmem] * 7, out_specs=[vmem]...  96.3 us
    pallas_call x1, Pallas kernels, gather_first(): pl.pallas_call(functools.partial(gather_first_kernel, len(before), len(af...  86.5 us
    ppermute x5, waiting for transfers between devices, passed_along(): return lax.ppermute(array, axis, pairs)  75.9 us
    pallas_call x1, Pallas kernels, feed(): pl.pallas_call(feed_kernel, grid=(tiles + columns // FEED_COLUMNS,), in_s...  74.6 us
    pallas_call x2, Pallas kernels, attend_back(): pl.pallas_call(functools.partial(attend_back_kernel, local_heads, own), g...  72 us
    pallas_call x2, Pallas kernels, attend(): pl.pallas_call(functools.partial(attend_kernel, local_heads, own), grid_s...  49.5 us
    dot_general x5, matrix products, dot(): return lax.dot_general(a, b, dims, preferred_element_type=f32, **kw)  47.4 us
  transfers between devices with their start and end apart: 10, of which 4 were waited for; matrix products, arithmetic and copies ran while one was open for 13% of the time, Pallas kernels for 35%

profile of v7, /device:TPU:0, one launch (start us, length us, event | category | flops | bytes accessed | tf_op | source)
XLA Modules:
  0.0 794.7 jit_solution(16874300883797467692)
XLA Ops:
  10.3 86.5 %gather_first.1 = (bf16[8,4,48,2048]{3,2,1,0:T(8,128)(2,1)}, bf16[2048,1536]{1,0:T(8,128)(2,1)}, bf16[2048,1536]{1,0:T(8,128)(2,1)}) custom-call(bf16[4,48,128]{2,1,0:T(8,128)(2,1)} %maximum_bitcast_fusion.refs_0_, f32[48,1536]{1,0:T(8,128)} %refs_1_.3, f32[48,1536]{1,0:T(8,128)} %refs_2_.1, f32[48,1536]{1,0:T(8,128)} %refs_3_.1, f32[48,1536]{1,0:T(8,128)} %refs_4_.1, ...), custom_call_target="tpu_custom_call" | custom-call | flops 70000001024 | bytes 30000000 | tf_op jit(solution)/shard_map/gather_first/pallas_call | solution.py:807
  99.9 16.4 %project.1 = (bf16[2048,1536]{1,0:T(8,128)(2,1)}, bf16[2048,768]{1,0:T(8,128)(2,1)}, bf16[2048,128]{1,0:T(8,128)(2,1)}, bf16[32,2048]{1,0:T(8,128)(2,1)}, f32[2048,128]{1,0:T(8,128)}) custom-call(bf16[2048,1536]{1,0:T(8,128)(2,1)} %get-tuple-element.57.tokens_ref, f32[8,1536]{1,0:T(8,128)} %broadcast_in_dim.51.gain_ref, bf16[1536,2048]{1,0:T(8,128)(2,1)} %bitcast.116, ...), custom_call_target="tpu_custom_call" | custom-call | flops 5637144576 | bytes 20000000 | tf_op jit(solution)/shard_map/project/pallas_call | solution.py:102
  116.2 5.1 collective-permute-start.1
  124.5 3.5 all-to-all-start
  128.1 3.6 collective-permute-start.2
  131.7 7.7 convolution_convert_fusion.3.q_ref
  139.4 49.1 %collective-permute-done = s32[2048]{0:T(1024)S(1)} collective-permute-done((s32[2048]{0:T(1024)S(1)}, s32[2048]{0:T(1024)S(1)}, u32[]{:S(2)}, u32[]{:S(2)}) %collective-permute-start) | collective-permute-done | bytes 8224 | tf_op jit(solution)/shard_map/ppermute | solution.py:28
  188.4 3.3 convert_reduce_fusion
  193.2 40.5 %attend_own.1 = (f32[384,2048]{1,0:T(8,128)}, f32[24,2048]{1,0:T(8,128)}) custom-call(s32[2,4]{1,0:T(2,128)} %pad_add_fusion.1.ranges_ref, bf16[2048,384]{1,0:T(8,128)(2,1)} %convolution_convert_fusion.3.q_ref, bf16[2048,768]{1,0:T(8,128)(2,1)} %get-tuple-element.60.k_ref.v_ref, bf16[2048,768]{1,0:T(8,128)(2,1)} %get-tuple-element.60.k_ref.v_ref, ...), custom_call_target="tpu_custom_call" | custom-call | flops 40000000000 | bytes 12000000 | tf_op jit(solution)/shard_map/attend_own/pallas_call | solution.py:326
  235.0 8.5 %add_divide_fusion = f32[2048,384]{1,0:T(8,128)} fusion(bf16[2048,1536]{1,0:T(8,128)(2,1)} %get-tuple-element.59, bf16[1536,2048]{1,0:T(8,128)(2,1)} %bitcast.118), kind=kOutput, calls=%fused_computation.23 | convolution fusion | flops 2418278400 | bytes 10616832 | tf_op jit(solution)/shard_map/dot_general | solution.py:22
  244.3 9.0 %attend_prev.1 = (bf16[2048,384]{1,0:T(8,128)(2,1)}, f32[24,2048]{1,0:T(8,128)}) custom-call(s32[2,4]{1,0:T(2,128)} %pad_add_fusion.1.ranges_ref, bf16[2048,384]{1,0:T(8,128)(2,1)} %convolution_convert_fusion.3.q_ref, bf16[2048,768]{1,0:T(8,128)(2,1)} %collective-permute-done.1.k_ref.v_ref, bf16[2048,768]{1,0:T(8,128)(2,1)} %collective-permute-done.1.k_ref.v_ref, ...), custom_call_target="tpu_custom_call" | custom-call | flops 10000000000 | bytes 12000000 | tf_op jit(solution)/shard_map/attend_prev/pallas_call | solution.py:326
  253.2 7.9 convolution_convert_fusion.refs_0_
  261.8 105.9 %exchange_middle.1 = (f32[512,1536]{1,0:T(8,128)}, bf16[2048,1536]{1,0:T(8,128)(2,1)}, bf16[8,4,48,1024]{3,2,1,0:T(8,128)(2,1)}) custom-call(bf16[2048,1536]{1,0:T(8,128)(2,1)} %convolution_convert_fusion.refs_0_, bf16[512,1536]{1,0:T(8,128)(2,1)} %tokens_ref.1, f32[8,1536]{1,0:T(8,128)} %broadcast_in_dim.54.refs_2_.refs_3_, bf16[4,48,1024]{2,1,0:T(8,128)(2,1)} %bitcast.113), custom_call_target="tpu_custom_call" | custom-call | flops 70000001024 | bytes 16000000 | tf_op jit(solution)/shard_map/exchange_middle/pallas_call | solution.py:977
  367.7 2.7 all-gather.2.cloned.1.call-done.weight_ref
  370.4 74.6 %feed.1 = (bf16[2048,1536]{1,0:T(8,128)(2,1)}, bf16[1536,3072]{1,0:T(8,128)(2,1)}, f32[512,1536]{1,0:T(8,128)}) custom-call(bf16[2048,1536]{1,0:T(8,128)(2,1)} %get-tuple-element.76.input_ref, bf16[2048,1536]{1,0:T(8,128)(2,1)} %get-tuple-element.77.cotangent_ref, bf16[1536,2048]{1,0:T(8,128)(2,1)} %all-gather.2.cloned.1.call-done.weight_ref, ...), custom_call_target="tpu_custom_call" | custom-call | flops 57982058496 | bytes 45000000 | tf_op jit(solution)/shard_map/feed/pallas_call | solution.py:1298
  445.1 43.0 %exchange_hidden.1 = (f32[512,1536]{1,0:T(8,128)}, bf16[2048,1536]{1,0:T(8,128)(2,1)}) custom-call(f32[512,1536]{1,0:T(8,128)} %get-tuple-element.80.refs_0_, bf16[512,1536]{1,0:T(8,128)(2,1)} %refs_1_.5, f32[512,1536]{1,0:T(8,128)} %get-tuple-element.75.refs_2_, f32[8,1536]{1,0:T(8,128)} %broadcast_in_dim.54.refs_2_.refs_3_), custom_call_target="tpu_custom_call" | custom-call | flops 10000000000 | bytes 16000000 | tf_op jit(solution)/shard_map/exchange_hidden/pallas_call | solution.py:977
  488.1 2.2 fusion.25
  494.6 6.3 multiply_convert_fusion
  500.9 10.8 %attend_back_prev.1 = (f32[2048,384]{1,0:T(8,128)}, f32[2048,128]{1,0:T(8,128)}, bf16[2,2048,384]{2,1,0:T(8,128)(2,1)}, f32[2048,128]{1,0:T(8,128)}) custom-call(s32[2,4]{1,0:T(2,128)} %pad_add_fusion.1.ranges_ref, bf16[2048,384]{1,0:T(8,128)(2,1)} %convolution_convert_fusion.3.q_ref, bf16[2048,768]{1,0:T(8,128)(2,1)} %collective-permute-done.1.k_ref.v_ref, ...), custom_call_target="tpu_custom_call" | custom-call | flops 10000000000 | bytes 25000000 | tf_op jit(solution)/shard_map/attend_back_prev/pallas_call | solution.py:487
  515.9 61.2 %attend_back_own.1 = (bf16[2048,384]{1,0:T(8,128)(2,1)}, f32[2048,384]{1,0:T(8,128)}, f32[2048,384]{1,0:T(8,128)}, f32[2048,128]{1,0:T(8,128)}) custom-call(s32[2,4]{1,0:T(2,128)} %pad_add_fusion.1.ranges_ref, bf16[2048,384]{1,0:T(8,128)(2,1)} %convolution_convert_fusion.3.q_ref, bf16[2048,768]{1,0:T(8,128)(2,1)} %get-tuple-element.60.k_ref.v_ref, ...), custom_call_target="tpu_custom_call" | custom-call | flops 20000000000 | bytes 25000000 | tf_op jit(solution)/shard_map/attend_back_own/pallas_call | solution.py:487
  577.0 7.7 convolution_convert_fusion.2
  584.8 26.8 %collective-permute-done.5 = f32[2048,8]{0,1:T(8,128)S(1)} collective-permute-done((f32[2048,8]{0,1:T(8,128)S(1)}, f32[2048,8]{0,1:T(8,128)S(1)}, u32[]{:S(2)}, u32[]{:S(2)}) %collective-permute-start.5) | collective-permute-done | bytes 65568 | tf_op jit(solution)/shard_map/ppermute | solution.py:28
  613.0 4.3 decay_back.1
  619.5 2.9 convert_element_type.197
  624.5 3.3 fusion.11
  627.8 3.1 fusion.12
  633.4 1.9 fusion.13
  635.3 18.0 %select_convert_fusion = bf16[1536,1664]{1,0:T(8,128)(2,1)} fusion(bf16[2048,1536]{1,0:T(8,128)(2,1)} %get-tuple-element.59, bf16[2048,1664]{1,0:T(8,128)(2,1)} %fusion.13, bf16[1536]{0:T(1024)(128)(2,1)S(1)} %select_reduce_fusion, pred[1664]{0:T(1024)(128)(4,1)S(1)} %iota_compare_fusion.1), kind=kOutput, calls=%fused_computation.1 | convolution fusion | flops 10471538688 | bytes 18223744 | tf_op jit(solution)/shard_map/dot_general | solution.py:1336
  653.2 17.1 %convolution_convert_fusion.1.first_ref = bf16[2048,1536]{1,0:T(8,128)(2,1)} fusion(bf16[2048,1664]{1,0:T(8,128)(2,1)} %fusion.13, bf16[1536,2048]{1,0:T(8,128)(2,1)} %bitcast.121), kind=kOutput, calls=%fused_computation.3 | convolution fusion | flops 10472128512 | bytes 18219008 | tf_op jit(solution)/shard_map/dot_general | solution.py:22
  670.3 2.1 fusion.8
  672.5 7.0 reduce-scatter.2.cloned.1.call-done
  679.5 96.3 %finish_last.1 = (bf16[4,48,1664]{2,1,0:T(8,128)(2,1)}, bf16[4,48,384]{2,1,0:T(8,128)(2,1)}, bf16[4,48,3072]{2,1,0:T(8,128)(2,1)}, f32[512,1536]{1,0:T(8,128)}) custom-call(bf16[8,4,48,1664]{3,2,1,0:T(8,128)(2,1)} %bitcast.124, bf16[8,4,48,384]{3,2,1,0:T(8,128)(2,1)} %bitcast.126, bf16[4,48,3072]{2,1,0:T(8,128)(2,1)} %bitcast.123, ...), custom_call_target="tpu_custom_call" | custom-call | flops 80000000000 | bytes 40000000 | tf_op jit(solution)/shard_map/finish_last/pallas_call | solution.py:1130
  (167 shorter events, 41.1 us)
Async XLA Ops:
  10.3 88.2 %copy-start.36 = (f32[24]{0:T(128)S(1)}, f32[24]{0:T(128)}, u32[]{:S(2)}) copy-start(f32[24]{0:T(128)} %param.23) | copy-start | bytes 292
  99.8 21.5 %copy-start.29 = (s32[2048]{0:T(1024)S(1)}, s32[2048]{0:T(1024)}, u32[]{:S(2)}) copy-start(s32[2048]{0:T(1024)} %param.16) | copy-start | bytes 24580
  99.8 23.3 %copy-start.22 = (f32[48,4096]{1,0:T(8,128)S(1)}, f32[48,4096]{1,0:T(8,128)}, u32[]{:S(2)}) copy-start(f32[48,4096]{1,0:T(8,128)} %param.28) | copy-start | bytes 2359300
  99.8 23.3 %copy-start.5 = (f32[48,4096]{1,0:T(8,128)S(1)}, f32[48,4096]{1,0:T(8,128)}, u32[]{:S(2)}) copy-start(f32[48,4096]{1,0:T(8,128)} %param.27) | copy-start | bytes 2359300
  99.8 23.4 %copy-start.3 = (f32[48,4096]{1,0:T(8,128)S(1)}, f32[48,4096]{1,0:T(8,128)}, u32[]{:S(2)}) copy-start(f32[48,4096]{1,0:T(8,128)} %param.26) | copy-start | bytes 2359300
  116.2 117.5 %collective-permute-start.1 = (bf16[2048,768]{1,0:T(8,128)(2,1)}, bf16[2048,768]{1,0:T(8,128)(2,1)}, u32[]{:S(2)}, u32[]{:S(2)}) collective-permute-start(bf16[2048,768]{1,0:T(8,128)(2,1)} %get-tuple-element.60.k_ref.v_ref), channel_id=1, source_target_pairs={{0,4},{4,8},{8,12},{12,16},{16,20},{20,24},{24,28},{1,5},{5,9},{9,... | collective-permute-start | bytes 9437192 | tf_op jit(solution)/shard_map/ppermute | solution.py:28
  121.3 67.1 %collective-permute-start = (s32[2048]{0:T(1024)S(1)}, s32[2048]{0:T(1024)S(1)}, u32[]{:S(2)}, u32[]{:S(2)}) collective-permute-start(s32[2048]{0:T(1024)S(1)} %broadcast_add_fusion), channel_id=1, source_target_pairs={{0,4},{4,8},{8,12},{12,16},{16,20},{20,24},{24,28},{1,5},{5,9},{9,... | collective-permute-start | bytes 24584 | tf_op jit(solution)/shard_map/ppermute | solution.py:28
  123.3 4.8 copy-start.35
  124.5 109.2 %all-to-all-start = ((bf16[48,4,3072]{2,0,1:T(8,128)(2,1)}), bf16[48,4,3072]{2,0,1:T(8,128)(2,1)S(1)}, u32[]{:S(2)}, u32[]{:S(2)}) async-start(bf16[48,4,3072]{2,0,1:T(8,128)(2,1)} %pad_maximum_fusion.1), calls=%async_computation | async-start | bytes 2359296 | tf_op jit(solution)/shard_map/all_to_all | solution.py:1345
  128.0 242.4 %all-gather.2.cloned.1.call-start = ((), (), s32[]{:S(2)}) async-start(), calls=%async_computation.2 | async-start | bytes 7077888 | tf_op jit(solution)/shard_map/all_gather | solution.py:1350
  128.1 105.6 %collective-permute-start.2 = (bf16[32,2048]{1,0:T(8,128)(2,1)S(1)}, bf16[32,2048]{1,0:T(8,128)(2,1)S(1)}, u32[]{:S(2)}, u32[]{:S(2)}) collective-permute-start(bf16[32,2048]{1,0:T(8,128)(2,1)S(1)} %copy-done.35), channel_id=1, source_target_pairs={{0,4},{4,8},{8,12},{12,16},{16,20},{20,24},{24,28},{1,5},{5,9},{9,... | collective-permute-start | bytes 393224 | tf_op jit(solution)/shard_map/ppermute | solution.py:28
  233.7 9.8 %copy-start.34 = (bf16[32,2048]{1,0:T(8,128)(2,1)}, bf16[32,2048]{1,0:T(8,128)(2,1)S(1)}, u32[]{:S(2)}) copy-start(bf16[32,2048]{1,0:T(8,128)(2,1)S(1)} %collective-permute-done.2.t_key_ref) | copy-start | bytes 393220
  234.7 444.7 %reduce-scatter.2.cloned.1.call-start = ((), (), s32[]{:S(2)}) async-start(), calls=%async_computation.3 | async-start | bytes 10616832 | tf_op jit(solution)/shard_map/reduce_scatter | solution.py:1354
  244.2 9.0 %copy-start.10 = (f32[2048,384]{1,0:T(8,128)S(1)}, f32[2048,384]{1,0:T(8,128)}, u32[]{:S(2)}) copy-start(f32[2048,384]{1,0:T(8,128)} %add_divide_fusion) | copy-start | bytes 9437188
  488.1 5.1 copy-start.37
  490.4 4.2 copy-start.11
  492.2 127.3 %collective-permute-start.3 = (bf16[1024,1536]{1,0:T(8,128)(2,1)}, bf16[1024,1536]{1,0:T(8,128)(2,1)}, u32[]{:S(2)}, u32[]{:S(2)}) collective-permute-start(bf16[1024,1536]{1,0:T(8,128)(2,1)} %pad_maximum_fusion), channel_id=1, source_target_pairs={{0,1},{1,0},{2,3},{3,2},{4,5},{5,4},{6,7},{7,6},{8,9},{9,8},{10,11... | collective-permute-start | bytes 9437192 | tf_op jit(solution)/shard_map/ppermute | solution.py:1360
  511.7 112.8 %collective-permute-start.6 = (bf16[2,2048,384]{2,1,0:T(8,128)(2,1)}, bf16[2,2048,384]{2,1,0:T(8,128)(2,1)}, u32[]{:S(2)}, u32[]{:S(2)}) collective-permute-start(bf16[2,2048,384]{2,1,0:T(8,128)(2,1)} %get-tuple-element.91), channel_id=1, source_target_pairs={{4,0},{8,4},{12,8},{16,12},{20,16},{24,20},{28,24},{5,1},{9,5},{13... | collective-permute-start | bytes 9437192 | tf_op jit(solution)/shard_map/ppermute | solution.py:28
  514.6 97.0 %collective-permute-start.5 = (f32[2048,8]{0,1:T(8,128)S(1)}, f32[2048,8]{0,1:T(8,128)S(1)}, u32[]{:S(2)}, u32[]{:S(2)}) collective-permute-start(f32[2048,8]{0,1:T(8,128)S(1)} %copy.91), channel_id=1, source_target_pairs={{4,0},{8,4},{12,8},{16,12},{20,16},{24,20},{28,24},{5,1},{9,5},{13... | collective-permute-start | bytes 196616 | tf_op jit(solution)/shard_map/ppermute | solution.py:28
  584.8 32.5 %copy-start.21 = (f32[2048,128]{1,0:T(8,128)S(1)}, f32[2048,128]{1,0:T(8,128)}, u32[]{:S(2)}) copy-start(f32[2048,128]{1,0:T(8,128)} %get-tuple-element.89) | copy-start | bytes 3145732
  617.3 5.1 slice-start
  622.9 47.4 %collective-permute-start.4 = (bf16[512,1536]{1,0:T(8,128)(2,1)S(1)}, bf16[512,1536]{1,0:T(8,128)(2,1)S(1)}, u32[]{:S(2)}, u32[]{:S(2)}) collective-permute-start(bf16[512,1536]{1,0:T(8,128)(2,1)S(1)} %fusion.5), channel_id=1, source_target_pairs={{0,2},{1,3},{2,0},{3,1},{4,6},{5,7},{6,4},{7,5},{8,10},{9,11},{10,... | collective-permute-start | bytes 4718600 | tf_op jit(solution)/shard_map/ppermute | solution.py:1365
  624.5 3.3 copy-start.1
  627.8 4.0 copy-start.15
  627.8 5.5 copy-start.13
  627.8 5.5 copy-start.14
  653.2 17.1 %copy-start.9 = (f32[512,1536]{1,0:T(8,128)S(1)}, f32[512,1536]{1,0:T(8,128)}, u32[]{:S(2)}) copy-start(f32[512,1536]{1,0:T(8,128)} %get-tuple-element.75.refs_2_) | copy-start | bytes 9437188
  777.1 4.3 copy-start.16
  777.4 4.3 copy-start.27
  778.0 3.8 copy-start.17
  778.7 3.1 copy-start.18
  783.2 4.2 copy-start.8
  (18 other events, 40.4 us)
Sparse Core Ops, SparseCore 0:
  234.8 135.5 all-gather.1
  445.2 234.2 reduce-scatter.1

commit v8 on v7

--- a/solution.py
+++ b/solution.py
@@ -1427,7 +1427,7 @@
         input1, first[:, kv_width + local_width : kv_width + 2 * local_width]
     )
 
-    segment_plus, _ = lax.optimization_barrier((segment + 1, key_value))
+    segment_plus = segment + 1
     earlier_segment = passed_along(segment_plus, "blk", 1)
     window = jnp.concatenate([earlier_segment, segment_plus])
     begins = jnp.sum(

time: 802 us -> 750 us (0.935)
  waiting for transfers between devices: 85.7 us -> 24.8 us
  Pallas kernels: 549 us -> 558 us
    ppermute x5, waiting for transfers between devices: 75.9 us -> 12.4 us  [passed_along(): return lax.ppermute(array, axis, pairs)]
    pallas_call x2, Pallas kernels: 72 us -> 81.9 us  [attend_back(): pl.pallas_call(functools.partial(attend_back_kernel, local_heads, own), g...]
    pallas_call x2, Pallas kernels: 49.5 us -> 57.6 us  [attend(): pl.pallas_call(functools.partial(attend_kernel, local_heads, own), grid_s...]
  transfers between devices with their start and end apart: 10 -> 10, of which waited for: 4 -> 4; matrix products, arithmetic and copies ran while one was open for 13% -> 15% of each run, Pallas kernels for 35% -> 52%
where the time goes in v8:
time: 750 us; the launch traced here: 745 us
  Pallas kernels  558 us (74%)
  matrix products  72.2 us (10%)
  other arithmetic  33.8 us (5%)
  waiting for transfers between devices  24.8 us (3%)
  starting transfers between devices  20.5 us (3%)
  local copies, waits for them, and re-layouts  20.3 us (3%)
  between operations  15.1 us (2%)
    pallas_call x2, Pallas kernels, exchange(): pl.pallas_call(functools.partial(exchange_kernel, local, len(extras), sum...  142 us
    pallas_call x1, Pallas kernels, finish_last(): pl.pallas_call(finish_last_kernel, in_specs=[vmem] * 7, out_specs=[vmem]...  96.1 us
    pallas_call x1, Pallas kernels, gather_first(): pl.pallas_call(functools.partial(gather_first_kernel, len(before), len(af...  84.8 us
    pallas_call x2, Pallas kernels, attend_back(): pl.pallas_call(functools.partial(attend_back_kernel, local_heads, own), g...  81.9 us
    pallas_call x1, Pallas kernels, feed(): pl.pallas_call(feed_kernel, grid=(tiles + columns // FEED_COLUMNS,), in_s...  74.8 us
    pallas_call x2, Pallas kernels, attend(): pl.pallas_call(functools.partial(attend_kernel, local_heads, own), grid_s...  57.6 us
    dot_general x5, matrix products, dot(): return lax.dot_general(a, b, dims, preferred_element_type=f32, **kw)  47.4 us
    dot_general x2, matrix products, over_tokens(): lax.dot_general(operand, other_side, (((0,), (0,)), ((), ())), preferred_...  24.8 us
  transfers between devices with their start and end apart: 10, of which 4 were waited for; matrix products, arithmetic and copies ran while one was open for 15% of the time, Pallas kernels for 52%

profile of v8, /device:TPU:0, one launch (start us, length us, event | category | flops | bytes accessed | tf_op | source)
XLA Modules:
  0.0 744.8 jit_solution(8519947804341849903)
XLA Ops:
  7.9 4.8 collective-permute-start
  15.9 84.8 %gather_first.1 = (bf16[8,4,48,2048]{3,2,1,0:T(8,128)(2,1)}, bf16[2048,1536]{1,0:T(8,128)(2,1)}, bf16[2048,1536]{1,0:T(8,128)(2,1)}) custom-call(bf16[4,48,128]{2,1,0:T(8,128)(2,1)} %maximum_bitcast_fusion.refs_0_, f32[48,1536]{1,0:T(8,128)} %refs_1_.3, f32[48,1536]{1,0:T(8,128)} %refs_2_.1, f32[48,1536]{1,0:T(8,128)} %refs_3_.1, f32[48,1536]{1,0:T(8,128)} %refs_4_.1, ...), custom_call_target="tpu_custom_call" | custom-call | flops 70000001024 | bytes 30000000 | tf_op jit(solution)/shard_map/gather_first/pallas_call | solution.py:807
  103.7 16.3 %project.1 = (bf16[2048,1536]{1,0:T(8,128)(2,1)}, bf16[2048,768]{1,0:T(8,128)(2,1)}, bf16[2048,128]{1,0:T(8,128)(2,1)}, bf16[32,2048]{1,0:T(8,128)(2,1)}, f32[2048,128]{1,0:T(8,128)}) custom-call(bf16[2048,1536]{1,0:T(8,128)(2,1)} %get-tuple-element.56.tokens_ref, f32[8,1536]{1,0:T(8,128)} %broadcast_in_dim.51.gain_ref, bf16[1536,2048]{1,0:T(8,128)(2,1)} %bitcast.116, ...), custom_call_target="tpu_custom_call" | custom-call | flops 5637144576 | bytes 20000000 | tf_op jit(solution)/shard_map/project/pallas_call | solution.py:102
  120.1 5.2 collective-permute-start.1
  126.6 3.5 all-to-all-start
  130.2 1.9 collective-permute-start.2
  132.1 7.7 %convolution_convert_fusion.3.q_ref = bf16[2048,384]{1,0:T(8,128)(2,1)} fusion(bf16[2048,1536]{1,0:T(8,128)(2,1)} %get-tuple-element.58, bf16[1536,2048]{1,0:T(8,128)(2,1)} %bitcast.117), kind=kOutput, calls=%fused_computation.25 | convolution fusion | flops 2416705536 | bytes 9043968 | tf_op jit(solution)/shard_map/dot_general | solution.py:22
  139.8 3.3 convert_reduce_fusion
  144.6 48.3 %attend_own.1 = (f32[384,2048]{1,0:T(8,128)}, f32[24,2048]{1,0:T(8,128)}) custom-call(s32[2,4]{1,0:T(2,128)} %pad_add_fusion.1.ranges_ref, bf16[2048,384]{1,0:T(8,128)(2,1)} %convolution_convert_fusion.3.q_ref, bf16[2048,768]{1,0:T(8,128)(2,1)} %get-tuple-element.59.k_ref.v_ref, bf16[2048,768]{1,0:T(8,128)(2,1)} %get-tuple-element.59.k_ref.v_ref, ...), custom_call_target="tpu_custom_call" | custom-call | flops 40000000000 | bytes 12000000 | tf_op jit(solution)/shard_map/attend_own/pallas_call | solution.py:326
  195.7 8.4 %add_divide_fusion = f32[2048,384]{1,0:T(8,128)} fusion(bf16[2048,1536]{1,0:T(8,128)(2,1)} %get-tuple-element.58, bf16[1536,2048]{1,0:T(8,128)(2,1)} %bitcast.118), kind=kOutput, calls=%fused_computation.23 | convolution fusion | flops 2418278400 | bytes 10616832 | tf_op jit(solution)/shard_map/dot_general | solution.py:22
  204.9 9.3 %attend_prev.1 = (bf16[2048,384]{1,0:T(8,128)(2,1)}, f32[24,2048]{1,0:T(8,128)}) custom-call(s32[2,4]{1,0:T(2,128)} %pad_add_fusion.1.ranges_ref, bf16[2048,384]{1,0:T(8,128)(2,1)} %convolution_convert_fusion.3.q_ref, bf16[2048,768]{1,0:T(8,128)(2,1)} %collective-permute-done.1.k_ref.v_ref, bf16[2048,768]{1,0:T(8,128)(2,1)} %collective-permute-done.1.k_ref.v_ref, ...), custom_call_target="tpu_custom_call" | custom-call | flops 10000000000 | bytes 12000000 | tf_op jit(solution)/shard_map/attend_prev/pallas_call | solution.py:326
  214.2 7.9 %convolution_convert_fusion.refs_0_ = bf16[2048,1536]{1,0:T(8,128)(2,1)} fusion(bf16[1536,2048]{1,0:T(8,128)(2,1)} %bitcast.119, f32[2048,384]{1,0:T(8,128)S(1)} %copy-done.10, bf16[2048,384]{1,0:T(8,128)(2,1)} %get-tuple-element.71.o_ref), kind=kOutput, calls=%fused_computation.2 | convolution fusion | flops 2421424128 | bytes 12189696 | tf_op jit(solution)/shard_map/dot_general | solution.py:22
  222.7 99.1 %exchange_middle.1 = (f32[512,1536]{1,0:T(8,128)}, bf16[2048,1536]{1,0:T(8,128)(2,1)}, bf16[8,4,48,1024]{3,2,1,0:T(8,128)(2,1)}) custom-call(bf16[2048,1536]{1,0:T(8,128)(2,1)} %convolution_convert_fusion.refs_0_, bf16[512,1536]{1,0:T(8,128)(2,1)} %tokens_ref.1, f32[8,1536]{1,0:T(8,128)} %broadcast_in_dim.54.refs_2_.refs_3_, bf16[4,48,1024]{2,1,0:T(8,128)(2,1)} %bitcast.113), custom_call_target="tpu_custom_call" | custom-call | flops 70000001024 | bytes 16000000 | tf_op jit(solution)/shard_map/exchange_middle/pallas_call | solution.py:977
  322.3 74.8 %feed.1 = (bf16[2048,1536]{1,0:T(8,128)(2,1)}, bf16[1536,3072]{1,0:T(8,128)(2,1)}, f32[512,1536]{1,0:T(8,128)}) custom-call(bf16[2048,1536]{1,0:T(8,128)(2,1)} %get-tuple-element.74.input_ref, bf16[2048,1536]{1,0:T(8,128)(2,1)} %get-tuple-element.75.cotangent_ref, bf16[1536,2048]{1,0:T(8,128)(2,1)} %all-gather.2.cloned.1.call-done.weight_ref, ...), custom_call_target="tpu_custom_call" | custom-call | flops 57982058496 | bytes 45000000 | tf_op jit(solution)/shard_map/feed/pallas_call | solution.py:1298
  397.1 43.1 %exchange_hidden.1 = (f32[512,1536]{1,0:T(8,128)}, bf16[2048,1536]{1,0:T(8,128)(2,1)}) custom-call(f32[512,1536]{1,0:T(8,128)} %get-tuple-element.78.refs_0_, bf16[512,1536]{1,0:T(8,128)(2,1)} %refs_1_.5, f32[512,1536]{1,0:T(8,128)} %get-tuple-element.73.refs_2_, f32[8,1536]{1,0:T(8,128)} %broadcast_in_dim.54.refs_2_.refs_3_), custom_call_target="tpu_custom_call" | custom-call | flops 10000000000 | bytes 16000000 | tf_op jit(solution)/shard_map/exchange_hidden/pallas_call | solution.py:977
  440.3 2.3 fusion.25
  442.6 1.8 pad_maximum_fusion
  446.8 6.3 multiply_convert_fusion
  453.1 10.9 %attend_back_prev.1 = (f32[2048,384]{1,0:T(8,128)}, f32[2048,128]{1,0:T(8,128)}, bf16[2,2048,384]{2,1,0:T(8,128)(2,1)}, f32[2048,128]{1,0:T(8,128)}) custom-call(s32[2,4]{1,0:T(2,128)} %pad_add_fusion.1.ranges_ref, bf16[2048,384]{1,0:T(8,128)(2,1)} %convolution_convert_fusion.3.q_ref, bf16[2048,768]{1,0:T(8,128)(2,1)} %collective-permute-done.1.k_ref.v_ref, ...), custom_call_target="tpu_custom_call" | custom-call | flops 10000000000 | bytes 25000000 | tf_op jit(solution)/shard_map/attend_back_prev/pallas_call | solution.py:487
  468.2 70.9 %attend_back_own.1 = (bf16[2048,384]{1,0:T(8,128)(2,1)}, f32[2048,384]{1,0:T(8,128)}, f32[2048,384]{1,0:T(8,128)}, f32[2048,128]{1,0:T(8,128)}) custom-call(s32[2,4]{1,0:T(2,128)} %pad_add_fusion.1.ranges_ref, bf16[2048,384]{1,0:T(8,128)(2,1)} %convolution_convert_fusion.3.q_ref, bf16[2048,768]{1,0:T(8,128)(2,1)} %get-tuple-element.59.k_ref.v_ref, ...), custom_call_target="tpu_custom_call" | custom-call | flops 20000000000 | bytes 25000000 | tf_op jit(solution)/shard_map/attend_back_own/pallas_call | solution.py:487
  539.1 7.7 %convolution_convert_fusion.2 = bf16[1536,384]{1,0:T(8,128)(2,1)} fusion(bf16[2048,1536]{1,0:T(8,128)(2,1)} %get-tuple-element.81, f32[2048,384]{1,0:T(8,128)S(1)} %copy-done.11, bf16[2048,384]{1,0:T(8,128)(2,1)} %get-tuple-element.71.o_ref), kind=kOutput, calls=%fused_computation.24 | convolution fusion | flops 2418868224 | bytes 12189696 | tf_op jit(solution)/shard_map/dot_general | solution.py:1336
  546.8 10.8 %collective-permute-done.5 = f32[2048,8]{0,1:T(8,128)S(1)} collective-permute-done((f32[2048,8]{0,1:T(8,128)S(1)}, f32[2048,8]{0,1:T(8,128)S(1)}, u32[]{:S(2)}, u32[]{:S(2)}) %collective-permute-start.5) | collective-permute-done | bytes 65568 | tf_op jit(solution)/shard_map/ppermute | solution.py:28
  559.1 4.3 decay_back.1
  565.6 2.9 convert_element_type.197
  570.6 3.2 fusion.11
  573.8 3.2 fusion.12
  579.6 1.9 fusion.13
  581.5 17.1 %select_convert_fusion = bf16[1536,1664]{1,0:T(8,128)(2,1)} fusion(bf16[2048,1536]{1,0:T(8,128)(2,1)} %get-tuple-element.58, bf16[2048,1664]{1,0:T(8,128)(2,1)} %fusion.13, bf16[1536]{0:T(1024)(128)(2,1)S(1)} %select_reduce_fusion, pred[1664]{0:T(1024)(128)(4,1)S(1)} %iota_compare_fusion.1), kind=kOutput, calls=%fused_computation.1 | convolution fusion | flops 10471538688 | bytes 18223744 | tf_op jit(solution)/shard_map/dot_general | solution.py:1336
  598.6 17.1 %convolution_convert_fusion.1.first_ref = bf16[2048,1536]{1,0:T(8,128)(2,1)} fusion(bf16[2048,1664]{1,0:T(8,128)(2,1)} %fusion.13, bf16[1536,2048]{1,0:T(8,128)(2,1)} %bitcast.121), kind=kOutput, calls=%fused_computation.3 | convolution fusion | flops 10472128512 | bytes 18219008 | tf_op jit(solution)/shard_map/dot_general | solution.py:22
  615.7 2.1 fusion.8
  617.9 11.9 %reduce-scatter.2.cloned.1.call-done = bf16[192,3072]{1,0:T(8,128)(2,1)} async-done(((bf16[1536,3072]{1,0:T(8,128)(2,1)}), bf16[192,3072]{1,0:T(8,128)(2,1)}) %reduce-scatter.2.cloned.1.call-update) | async-done | bytes 1179664 | tf_op jit(solution)/shard_map/reduce_scatter | solution.py:1354
  629.7 96.1 %finish_last.1 = (bf16[4,48,1664]{2,1,0:T(8,128)(2,1)}, bf16[4,48,384]{2,1,0:T(8,128)(2,1)}, bf16[4,48,3072]{2,1,0:T(8,128)(2,1)}, f32[512,1536]{1,0:T(8,128)}) custom-call(bf16[8,4,48,1664]{3,2,1,0:T(8,128)(2,1)} %bitcast.124, bf16[8,4,48,384]{3,2,1,0:T(8,128)(2,1)} %bitcast.126, bf16[4,48,3072]{2,1,0:T(8,128)(2,1)} %bitcast.123, ...), custom_call_target="tpu_custom_call" | custom-call | flops 80000000000 | bytes 40000000 | tf_op jit(solution)/shard_map/finish_last/pallas_call | solution.py:1130
  (165 shorter events, 40.4 us)
Async XLA Ops:
  7.9 131.9 %collective-permute-start = (s32[2048]{0:T(1024)S(1)}, s32[2048]{0:T(1024)S(1)}, u32[]{:S(2)}, u32[]{:S(2)}) collective-permute-start(s32[2048]{0:T(1024)S(1)} %broadcast_add_fusion), channel_id=1, source_target_pairs={{0,4},{4,8},{8,12},{12,16},{16,20},{20,24},{24,28},{1,5},{5,9},{9,... | collective-permute-start | bytes 24584 | tf_op jit(solution)/shard_map/ppermute | solution.py:28
  15.9 86.6 %copy-start.35 = (f32[24]{0:T(128)S(1)}, f32[24]{0:T(128)}, u32[]{:S(2)}) copy-start(f32[24]{0:T(128)} %param.23) | copy-start | bytes 292
  103.7 21.5 %copy-start.22 = (f32[48,4096]{1,0:T(8,128)S(1)}, f32[48,4096]{1,0:T(8,128)}, u32[]{:S(2)}) copy-start(f32[48,4096]{1,0:T(8,128)} %param.28) | copy-start | bytes 2359300
  103.7 21.5 %copy-start.5 = (f32[48,4096]{1,0:T(8,128)S(1)}, f32[48,4096]{1,0:T(8,128)}, u32[]{:S(2)}) copy-start(f32[48,4096]{1,0:T(8,128)} %param.27) | copy-start | bytes 2359300
  103.7 21.6 %copy-start.3 = (f32[48,4096]{1,0:T(8,128)S(1)}, f32[48,4096]{1,0:T(8,128)}, u32[]{:S(2)}) copy-start(f32[48,4096]{1,0:T(8,128)} %param.26) | copy-start | bytes 2359300
  120.1 74.4 %collective-permute-start.1 = (bf16[2048,768]{1,0:T(8,128)(2,1)}, bf16[2048,768]{1,0:T(8,128)(2,1)}, u32[]{:S(2)}, u32[]{:S(2)}) collective-permute-start(bf16[2048,768]{1,0:T(8,128)(2,1)} %get-tuple-element.59.k_ref.v_ref), channel_id=1, source_target_pairs={{0,4},{4,8},{8,12},{12,16},{16,20},{20,24},{24,28},{1,5},{5,9},{9,... | collective-permute-start | bytes 9437192 | tf_op jit(solution)/shard_map/ppermute | solution.py:28
  125.4 4.8 copy-start.34
  126.6 67.8 %all-to-all-start = ((bf16[48,4,3072]{2,0,1:T(8,128)(2,1)}), bf16[48,4,3072]{2,0,1:T(8,128)(2,1)S(1)}, u32[]{:S(2)}, u32[]{:S(2)}) async-start(bf16[48,4,3072]{2,0,1:T(8,128)(2,1)} %pad_maximum_fusion.1), calls=%async_computation | async-start | bytes 2359296 | tf_op jit(solution)/shard_map/all_to_all | solution.py:1345
  130.1 192.1 %all-gather.2.cloned.1.call-start = ((), (), s32[]{:S(2)}) async-start(), calls=%async_computation.2 | async-start | bytes 7077888 | tf_op jit(solution)/shard_map/all_gather | solution.py:1350
  130.2 64.2 %collective-permute-start.2 = (bf16[32,2048]{1,0:T(8,128)(2,1)S(1)}, bf16[32,2048]{1,0:T(8,128)(2,1)S(1)}, u32[]{:S(2)}, u32[]{:S(2)}) collective-permute-start(bf16[32,2048]{1,0:T(8,128)(2,1)S(1)} %copy-done.34), channel_id=1, source_target_pairs={{0,4},{4,8},{8,12},{12,16},{16,20},{20,24},{24,28},{1,5},{5,9},{9,... | collective-permute-start | bytes 393224 | tf_op jit(solution)/shard_map/ppermute | solution.py:28
  194.4 9.7 %copy-start.33 = (bf16[32,2048]{1,0:T(8,128)(2,1)}, bf16[32,2048]{1,0:T(8,128)(2,1)S(1)}, u32[]{:S(2)}) copy-start(bf16[32,2048]{1,0:T(8,128)(2,1)S(1)} %collective-permute-done.2.t_key_ref) | copy-start | bytes 393220
  195.4 434.3 %reduce-scatter.2.cloned.1.call-start = ((), (), s32[]{:S(2)}) async-start(), calls=%async_computation.3 | async-start | bytes 10616832 | tf_op jit(solution)/shard_map/reduce_scatter | solution.py:1354
  204.9 9.3 %copy-start.10 = (f32[2048,384]{1,0:T(8,128)S(1)}, f32[2048,384]{1,0:T(8,128)}, u32[]{:S(2)}) copy-start(f32[2048,384]{1,0:T(8,128)} %add_divide_fusion) | copy-start | bytes 9437188
  440.3 5.1 copy-start.36
  442.6 4.2 copy-start.11
  444.5 121.1 %collective-permute-start.3 = (bf16[1024,1536]{1,0:T(8,128)(2,1)}, bf16[1024,1536]{1,0:T(8,128)(2,1)}, u32[]{:S(2)}, u32[]{:S(2)}) collective-permute-start(bf16[1024,1536]{1,0:T(8,128)(2,1)} %pad_maximum_fusion), channel_id=1, source_target_pairs={{0,1},{1,0},{2,3},{3,2},{4,5},{5,4},{6,7},{7,6},{8,9},{9,8},{10,11... | collective-permute-start | bytes 9437192 | tf_op jit(solution)/shard_map/ppermute | solution.py:1360
  464.1 106.6 %collective-permute-start.6 = (bf16[2,2048,384]{2,1,0:T(8,128)(2,1)}, bf16[2,2048,384]{2,1,0:T(8,128)(2,1)}, u32[]{:S(2)}, u32[]{:S(2)}) collective-permute-start(bf16[2,2048,384]{2,1,0:T(8,128)(2,1)} %get-tuple-element.89), channel_id=1, source_target_pairs={{4,0},{8,4},{12,8},{16,12},{20,16},{24,20},{28,24},{5,1},{9,5},{13... | collective-permute-start | bytes 9437192 | tf_op jit(solution)/shard_map/ppermute | solution.py:28
  466.9 90.8 %collective-permute-start.5 = (f32[2048,8]{0,1:T(8,128)S(1)}, f32[2048,8]{0,1:T(8,128)S(1)}, u32[]{:S(2)}, u32[]{:S(2)}) collective-permute-start(f32[2048,8]{0,1:T(8,128)S(1)} %copy.91), channel_id=1, source_target_pairs={{4,0},{8,4},{12,8},{16,12},{20,16},{24,20},{28,24},{5,1},{9,5},{13... | collective-permute-start | bytes 196616 | tf_op jit(solution)/shard_map/ppermute | solution.py:28
  546.8 16.6 %copy-start.21 = (f32[2048,128]{1,0:T(8,128)S(1)}, f32[2048,128]{1,0:T(8,128)}, u32[]{:S(2)}) copy-start(f32[2048,128]{1,0:T(8,128)} %get-tuple-element.87) | copy-start | bytes 3145732
  563.4 5.1 slice-start
  569.0 46.7 %collective-permute-start.4 = (bf16[512,1536]{1,0:T(8,128)(2,1)S(1)}, bf16[512,1536]{1,0:T(8,128)(2,1)S(1)}, u32[]{:S(2)}, u32[]{:S(2)}) collective-permute-start(bf16[512,1536]{1,0:T(8,128)(2,1)S(1)} %fusion.5), channel_id=1, source_target_pairs={{0,2},{1,3},{2,0},{3,1},{4,6},{5,7},{6,4},{7,5},{8,10},{9,11},{10,... | collective-permute-start | bytes 4718600 | tf_op jit(solution)/shard_map/ppermute | solution.py:1365
  570.6 3.2 copy-start.1
  573.8 4.1 copy-start.15
  573.8 5.5 copy-start.13
  573.8 5.5 copy-start.14
  598.6 17.1 %copy-start.9 = (f32[512,1536]{1,0:T(8,128)S(1)}, f32[512,1536]{1,0:T(8,128)}, u32[]{:S(2)}) copy-start(f32[512,1536]{1,0:T(8,128)} %get-tuple-element.73.refs_2_) | copy-start | bytes 9437188
  727.2 4.3 copy-start.16
  727.5 4.3 copy-start.27
  728.1 3.8 copy-start.17
  728.8 3.1 copy-start.18
  729.2 3.0 copy-start.20
  733.3 4.2 copy-start.8
  (17 other events, 37.5 us)
Sparse Core Ops, SparseCore 0:
  195.5 126.7 all-gather.1
  397.2 232.4 reduce-scatter.1

commit v9 on v8

--- a/solution.py
+++ b/solution.py
@@ -996,8 +996,9 @@
     return [(0, first)] + [(first + 512 * n, 512) for n in range(count - 1)]
 
 
-def finish_last_kernel(grad_ref, output_grad_ref, second_ref, first_ref, grad_middle_ref, tokens_ref,
-                       gain_ref, weights_ref, output_ref, second_out_ref, tokens_grad_ref, *refs):
+def finish_last_kernel(grads_ref, weight_ref, grad_ref, output_grad_ref, second_ref,
+                       grad_middle_ref, tokens_ref, gain_ref, weights_ref, output_ref,
+                       second_out_ref, tokens_grad_ref, first_ref, *refs):
     buffers = (refs[0:3], refs[3:6])
     first_buffers = refs[6:9]
     pair_send, pair_recv, line_send, line_recv, swap_send, swap_recv = refs[9:15]
@@ -1020,7 +1021,6 @@
         for start, wide in column_chunks(ref.shape[3]):
             chunks.append((ref, out_ref, some, pl.ds(start, wide)))
     groups = grad_ref.shape[1]
-    first.start()
     sent = []
     for c, (ref, _, (pair_buf, _, _), at) in enumerate(chunks):
         for t in list(range(1, steps)) + [0]:
@@ -1033,7 +1033,6 @@
             )
             copy.start()
             sent.append(copy)
-    first.turn()
 
     def swap(source_ref, out_ref, c):
         for kind, other in enumerate(others):
@@ -1067,6 +1066,15 @@
         out_ref[me, :, at] = row_buf[me, :, at]
         swap(row_buf.at[:, :, at], out_ref.at[:, :, at], c)
 
+    across = grads_ref.shape[1]
+    tiles = first_ref.shape[0] // 256
+
+    def multiply(n, carry):
+        rows = tile_of(n, 256)
+        first_ref[rows, :] = dot(grads_ref[rows, :], weight_ref[:, :across], NT).astype(bf16)
+        return carry
+
+    lax.fori_loop(0, tiles // 2, multiply, 0)
     for c, (ref, _, (pair_buf, line_buf, _), at) in enumerate(chunks):
         for t in range(1, steps):
             block = pair_buf.at[t, :, :, at]
@@ -1088,7 +1096,12 @@
             )
             copy.start()
             sent.append(copy)
-        if c > 0:
+        if c == 0:
+            lax.fori_loop(tiles // 2, tiles, multiply, 0)
+            first.start()
+        else:
+            if c == 1:
+                first.turn()
             add_up(c - 1)
     for piece in range(PIECES):
         rows = first.piece(piece)
@@ -1113,7 +1126,7 @@
     first.finish()
 
 
-def finish_last(grad, output_grad, second, groups, part_first, grad_middle, tokens, gain, number):
+def finish_last(grads, first, grad, output_grad, second, groups, grad_middle, tokens, gain, number):
     peers = lax.axis_size("blk")
     share = grad.shape[0] // (peers * groups)
     rows, width = tokens.shape
@@ -1129,14 +1142,15 @@
 
     return pl.pallas_call(
         finish_last_kernel,
-        in_specs=[vmem] * 7,
+        in_specs=[vmem] * 8,
         out_specs=[vmem] * 4,
         out_shape=[
             jax.ShapeDtypeStruct((groups, share, columns), bf16)
             for columns in widths + (second.shape[1],)
         ]
         + [jax.ShapeDtypeStruct((rows, width), f32)],
-        scratch_shapes=blocks(widths[0])
+        scratch_shapes=[pltpu.VMEM((4 * rows, width), bf16)]
+        + blocks(widths[0])
         + blocks(widths[1])
         + sum_buffers(rows, width)
         + [pltpu.SemaphoreType.DMA((chunks, half)) for _ in range(4)]
@@ -1150,10 +1164,12 @@
         ),
         name="finish_last",
     )(
+        grads,
+        first,
         grad.reshape(peers, groups, share, widths[0]),
         output_grad.reshape(peers, groups, share, widths[1]),
         second.reshape(groups, share, second.shape[1]),
-        part_first, grad_middle, tokens, gain,
+        grad_middle, tokens, gain,
     )
 
 
@@ -1440,8 +1456,8 @@
     so_far = attend(True, ranges, query, key_value, terms, terms, begins, local_heads)
     later = lax.optimization_barrier((w_gate, w_up, w_down, key_value))
     mine = sent_columns([low(weight) for weight in later[:3]], groups)
-    mine, earlier_kv, earlier_terms, so_far = lax.optimization_barrier(
-        (mine, earlier_kv, earlier_terms, so_far)
+    mine, earlier_kv, earlier_terms, so_far, gate_raw = lax.optimization_barrier(
+        (mine, earlier_kv, earlier_terms, so_far, gate_raw)
     )
     second = all_rows(mine[:, : 2 * hidden_width])
     mine_down = mine[:, 2 * hidden_width :].reshape(groups, share, hidden_width)
@@ -1496,9 +1512,8 @@
         column == 2 * local_width + local_heads, spread_bias, first_grad
     ).astype(bf16)
     output_grad = over_tokens(grad_branch, gated).astype(bf16)
-    grad_input1 = dot(grads, first[:, : kv_width + 2 * local_width], NT).astype(bf16)
     first_sum, output_sum, second_sum, tokens_grad = finish_last(
-        first_grad, output_grad, second_part, groups, grad_input1, grad_middle, tokens, gain1, 3
+        grads, first, first_grad, output_grad, second_part, groups, grad_middle, tokens, gain1, 3
     )
     first_sum, output_sum, second_sum = (
         jnp.swapaxes(array, 0, 1).astype(f32) for array in (first_sum, output_sum, second_sum)

time: 750 us -> 753 us (level)
  waiting for transfers between devices: 24.8 us -> 63.3 us
  Pallas kernels: 558 us -> 540 us
  matrix products: 72.2 us -> 56.2 us
    ppermute x5, waiting for transfers between devices: 12.4 us -> 35.3 us  [passed_along(): return lax.ppermute(array, axis, pairs)]
    dot_general x5 -> x4, matrix products: 47.4 us -> 30.1 us  [dot(): return lax.dot_general(a, b, dims, preferred_element_type=f32, **kw)]
    all_gather x1, waiting for transfers between devices: 0.46 us -> 15.6 us  [all_rows(): return lax.all_gather(mine, 'blk', axis=0, tiled=True)]
    pallas_call x2, Pallas kernels: 81.9 us -> 72 us  [attend_back(): pl.pallas_call(functools.partial(attend_back_kernel, local_heads, own), g...]
    pallas_call x2, Pallas kernels: 57.6 us -> 49.4 us  [attend(): pl.pallas_call(functools.partial(attend_kernel, local_heads, own), grid_s...]
    ppermute x1, waiting for transfers between devices: 0.01 us -> 8.13 us  [crossing_sum(): lax.ppermute((far + of_far).astype(bf16), 'head', [(n, (n + 2) % 4) for n...]
    reduce_scatter x1, waiting for transfers between devices: 11.9 us -> 4.21 us  [row_sums(): return lax.psum_scatter(grad, 'blk', scatter_dimension=0, tiled=True)]
  transfers between devices with their start and end apart: 10 -> 10, of which waited for: 4 -> 5; matrix products, arithmetic and copies ran while one was open for 15% -> 12% of each run, Pallas kernels for 52% -> 50%
where the time goes in v9:
time: 753 us; the launch traced here: 745 us
  Pallas kernels  540 us (72%)
  waiting for transfers between devices  63.3 us (8%)
  matrix products  56.2 us (7%)
  other arithmetic  30.3 us (4%)
  local copies, waits for them, and re-layouts  20.7 us (3%)
  starting transfers between devices  20.3 us (3%)
  between operations  14.9 us (2%)
    pallas_call x2, Pallas kernels, exchange(): pl.pallas_call(functools.partial(exchange_kernel, local, len(extras), sum...  146 us
    pallas_call x1, Pallas kernels, finish_last(): pl.pallas_call(finish_last_kernel, in_specs=[vmem] * 8, out_specs=[vmem]...  92.2 us
    pallas_call x1, Pallas kernels, gather_first(): pl.pallas_call(functools.partial(gather_first_kernel, len(before), len(af...  84.8 us
    pallas_call x1, Pallas kernels, feed(): pl.pallas_call(feed_kernel, grid=(tiles + columns // FEED_COLUMNS,), in_s...  74.7 us
    pallas_call x2, Pallas kernels, attend_back(): pl.pallas_call(functools.partial(attend_back_kernel, local_heads, own), g...  72 us
    pallas_call x2, Pallas kernels, attend(): pl.pallas_call(functools.partial(attend_kernel, local_heads, own), grid_s...  49.4 us
    ppermute x5, waiting for transfers between devices, passed_along(): return lax.ppermute(array, axis, pairs)  35.3 us
    dot_general x4, matrix products, dot(): return lax.dot_general(a, b, dims, preferred_element_type=f32, **kw)  30.1 us
  transfers between devices with their start and end apart: 10, of which 5 were waited for; matrix products, arithmetic and copies ran while one was open for 12% of the time, Pallas kernels for 50%

profile of v9, /device:TPU:0, one launch (start us, length us, event | category | flops | bytes accessed | tf_op | source)
XLA Modules:
  0.0 745.2 jit_solution(10699984592020150371)
XLA Ops:
  7.9 4.8 collective-permute-start.2
  15.9 84.8 %gather_first.1 = (bf16[8,4,48,2048]{3,2,1,0:T(8,128)(2,1)}, bf16[2048,1536]{1,0:T(8,128)(2,1)}, bf16[2048,1536]{1,0:T(8,128)(2,1)}) custom-call(bf16[4,48,128]{2,1,0:T(8,128)(2,1)} %maximum_bitcast_fusion.refs_0_, f32[48,1536]{1,0:T(8,128)} %refs_1_.3, f32[48,1536]{1,0:T(8,128)} %refs_2_.1, f32[48,1536]{1,0:T(8,128)} %refs_3_.1, f32[48,1536]{1,0:T(8,128)} %refs_4_.1, ...), custom_call_target="tpu_custom_call" | custom-call | flops 70000001024 | bytes 30000000 | tf_op jit(solution)/shard_map/gather_first/pallas_call | solution.py:807
  103.7 16.3 %project.1 = (bf16[2048,1536]{1,0:T(8,128)(2,1)}, bf16[2048,768]{1,0:T(8,128)(2,1)}, bf16[2048,128]{1,0:T(8,128)(2,1)}, bf16[32,2048]{1,0:T(8,128)(2,1)}, f32[2048,128]{1,0:T(8,128)}) custom-call(bf16[2048,1536]{1,0:T(8,128)(2,1)} %get-tuple-element.57.tokens_ref, f32[8,1536]{1,0:T(8,128)} %broadcast_in_dim.51.gain_ref, bf16[1536,2048]{1,0:T(8,128)(2,1)} %bitcast.115, ...), custom_call_target="tpu_custom_call" | custom-call | flops 5637144576 | bytes 20000000 | tf_op jit(solution)/shard_map/project/pallas_call | solution.py:102
  120.1 5.1 collective-permute-start
  126.6 3.5 all-to-all-start
  130.2 2.0 collective-permute-start.1
  132.2 7.7 %convolution_convert_fusion.2.q_ref = bf16[2048,384]{1,0:T(8,128)(2,1)} fusion(bf16[2048,1536]{1,0:T(8,128)(2,1)} %get-tuple-element.64, bf16[1536,2048]{1,0:T(8,128)(2,1)} %bitcast.116), kind=kOutput, calls=%fused_computation.23 | convolution fusion | flops 2416705536 | bytes 9043968 | tf_op jit(solution)/shard_map/dot_general | solution.py:22
  139.9 8.2 %fusion.13 = f32[2048,384]{1,0:T(8,128)} fusion(bf16[2048,1536]{1,0:T(8,128)(2,1)} %get-tuple-element.64, bf16[1536,2048]{1,0:T(8,128)(2,1)} %bitcast.117), kind=kOutput, calls=%fused_computation.31 | convolution fusion | flops 2415919104 | bytes 10616832 | tf_op jit(solution)/shard_map/dot_general | solution.py:22
  148.0 3.3 convert_reduce_fusion
  152.8 40.5 %attend_own.1 = (f32[384,2048]{1,0:T(8,128)}, f32[24,2048]{1,0:T(8,128)}) custom-call(s32[2,4]{1,0:T(2,128)} %pad_add_fusion.1.ranges_ref, bf16[2048,384]{1,0:T(8,128)(2,1)} %convolution_convert_fusion.2.q_ref, bf16[2048,768]{1,0:T(8,128)(2,1)} %get-tuple-element.59.k_ref.v_ref, bf16[2048,768]{1,0:T(8,128)(2,1)} %get-tuple-element.59.k_ref.v_ref, ...), custom_call_target="tpu_custom_call" | custom-call | flops 40000000000 | bytes 12000000 | tf_op jit(solution)/shard_map/attend_own/pallas_call | solution.py:326
  196.5 8.9 %attend_prev.1 = (bf16[2048,384]{1,0:T(8,128)(2,1)}, f32[24,2048]{1,0:T(8,128)}) custom-call(s32[2,4]{1,0:T(2,128)} %pad_add_fusion.1.ranges_ref, bf16[2048,384]{1,0:T(8,128)(2,1)} %convolution_convert_fusion.2.q_ref, bf16[2048,768]{1,0:T(8,128)(2,1)} %collective-permute-done.k_ref.v_ref, bf16[2048,768]{1,0:T(8,128)(2,1)} %collective-permute-done.k_ref.v_ref, ...), custom_call_target="tpu_custom_call" | custom-call | flops 10000000000 | bytes 12000000 | tf_op jit(solution)/shard_map/attend_prev/pallas_call | solution.py:326
  205.4 7.8 %convolution_convert_fusion.refs_0_ = bf16[2048,1536]{1,0:T(8,128)(2,1)} fusion(bf16[1536,2048]{1,0:T(8,128)(2,1)} %bitcast.118, bf16[2048,384]{1,0:T(8,128)(2,1)} %get-tuple-element.73.o_ref, f32[2048,384]{1,0:T(8,128)S(1)} %copy-done.9), kind=kOutput, calls=%fused_computation.2 | convolution fusion | flops 2423783424 | bytes 12189696 | tf_op jit(solution)/shard_map/dot_general | solution.py:22
  213.8 102.6 %exchange_middle.1 = (f32[512,1536]{1,0:T(8,128)}, bf16[2048,1536]{1,0:T(8,128)(2,1)}, bf16[8,4,48,1024]{3,2,1,0:T(8,128)(2,1)}) custom-call(bf16[2048,1536]{1,0:T(8,128)(2,1)} %convolution_convert_fusion.refs_0_, bf16[512,1536]{1,0:T(8,128)(2,1)} %tokens_ref.1, f32[8,1536]{1,0:T(8,128)} %broadcast_in_dim.54.refs_2_.refs_3_, bf16[4,48,1024]{2,1,0:T(8,128)(2,1)} %bitcast.112), custom_call_target="tpu_custom_call" | custom-call | flops 70000001024 | bytes 16000000 | tf_op jit(solution)/shard_map/exchange_middle/pallas_call | solution.py:977
  316.4 15.6 %all-gather.2.cloned.1.call-done.weight_ref = bf16[1536,2048]{1,0:T(8,128)(2,1)} async-done(((bf16[192,2048]{1,0:T(8,128)(2,1)}), bf16[1536,2048]{1,0:T(8,128)(2,1)}) %all-gather.2.cloned.1.call-update) | async-done | bytes 6291472 | tf_op jit(solution)/shard_map/all_gather | solution.py:1366
  332.0 74.7 %feed.1 = (bf16[2048,1536]{1,0:T(8,128)(2,1)}, bf16[1536,3072]{1,0:T(8,128)(2,1)}, f32[512,1536]{1,0:T(8,128)}) custom-call(bf16[2048,1536]{1,0:T(8,128)(2,1)} %get-tuple-element.76.input_ref, bf16[2048,1536]{1,0:T(8,128)(2,1)} %get-tuple-element.77.cotangent_ref, bf16[1536,2048]{1,0:T(8,128)(2,1)} %all-gather.2.cloned.1.call-done.weight_ref, ...), custom_call_target="tpu_custom_call" | custom-call | flops 57982058496 | bytes 45000000 | tf_op jit(solution)/shard_map/feed/pallas_call | solution.py:1314
  406.8 43.2 %exchange_hidden.1 = (f32[512,1536]{1,0:T(8,128)}, bf16[2048,1536]{1,0:T(8,128)(2,1)}) custom-call(f32[512,1536]{1,0:T(8,128)} %get-tuple-element.80.refs_0_, bf16[512,1536]{1,0:T(8,128)(2,1)} %refs_1_.5, f32[512,1536]{1,0:T(8,128)} %get-tuple-element.75.refs_2_, f32[8,1536]{1,0:T(8,128)} %broadcast_in_dim.54.refs_2_.refs_3_), custom_call_target="tpu_custom_call" | custom-call | flops 10000000000 | bytes 16000000 | tf_op jit(solution)/shard_map/exchange_hidden/pallas_call | solution.py:977
  450.0 2.2 fusion.25
  452.3 1.9 pad_maximum_fusion
  456.2 6.5 multiply_convert_fusion
  462.7 10.8 %attend_back_prev.1 = (f32[2048,384]{1,0:T(8,128)}, f32[2048,128]{1,0:T(8,128)}, bf16[2,2048,384]{2,1,0:T(8,128)(2,1)}, f32[2048,128]{1,0:T(8,128)}) custom-call(s32[2,4]{1,0:T(2,128)} %pad_add_fusion.1.ranges_ref, bf16[2048,384]{1,0:T(8,128)(2,1)} %convolution_convert_fusion.2.q_ref, bf16[2048,768]{1,0:T(8,128)(2,1)} %collective-permute-done.k_ref.v_ref, ...), custom_call_target="tpu_custom_call" | custom-call | flops 10000000000 | bytes 25000000 | tf_op jit(solution)/shard_map/attend_back_prev/pallas_call | solution.py:487
  477.7 61.2 %attend_back_own.1 = (bf16[2048,384]{1,0:T(8,128)(2,1)}, f32[2048,384]{1,0:T(8,128)}, f32[2048,384]{1,0:T(8,128)}, f32[2048,128]{1,0:T(8,128)}) custom-call(s32[2,4]{1,0:T(2,128)} %pad_add_fusion.1.ranges_ref, bf16[2048,384]{1,0:T(8,128)(2,1)} %convolution_convert_fusion.2.q_ref, bf16[2048,768]{1,0:T(8,128)(2,1)} %get-tuple-element.59.k_ref.v_ref, ...), custom_call_target="tpu_custom_call" | custom-call | flops 20000000000 | bytes 25000000 | tf_op jit(solution)/shard_map/attend_back_own/pallas_call | solution.py:487
  538.9 7.8 %convolution_convert_fusion.1 = bf16[1536,384]{1,0:T(8,128)(2,1)} fusion(bf16[2048,1536]{1,0:T(8,128)(2,1)} %get-tuple-element.83, bf16[2048,384]{1,0:T(8,128)(2,1)} %get-tuple-element.73.o_ref, f32[2048,384]{1,0:T(8,128)S(1)} %copy-done.10), kind=kOutput, calls=%fused_computation.22 | convolution fusion | flops 2421227520 | bytes 12189696 | tf_op jit(solution)/shard_map/dot_general | solution.py:1352
  546.6 34.2 %collective-permute-done.6 = f32[2048,8]{0,1:T(8,128)S(1)} collective-permute-done((f32[2048,8]{0,1:T(8,128)S(1)}, f32[2048,8]{0,1:T(8,128)S(1)}, u32[]{:S(2)}, u32[]{:S(2)}) %collective-permute-start.6) | collective-permute-done | bytes 65568 | tf_op jit(solution)/shard_map/ppermute | solution.py:28
  582.2 4.3 decay_back.1
  588.8 2.9 convert_element_type.194
  594.1 2.0 fusion.10
  596.5 2.2 fusion.11
  602.2 18.3 %select_convert_fusion = bf16[1536,1664]{1,0:T(8,128)(2,1)} fusion(bf16[2048,1536]{1,0:T(8,128)(2,1)} %get-tuple-element.64, bf16[2048,1664]{1,0:T(8,128)(2,1)S(1)} %fusion.12.grads_ref, bf16[1536]{0:T(1024)(128)(2,1)S(1)} %select_reduce_fusion, pred[1664]{0:T(1024)(128)(4,1)S(1)} %iota_compare_fusion.1), kind=kOutput, calls=%fused_computation.1 | convolution fusion | flops 10471538688 | bytes 18223744 | tf_op jit(solution)/shard_map/dot_general | solution.py:1352
  620.5 8.1 %collective-permute-done.4 = bf16[512,1536]{1,0:T(8,128)(2,1)S(1)} collective-permute-done((bf16[512,1536]{1,0:T(8,128)(2,1)S(1)}, bf16[512,1536]{1,0:T(8,128)(2,1)S(1)}, u32[]{:S(2)}, u32[]{:S(2)}) %collective-permute-start.4) | collective-permute-done | bytes 1572896 | tf_op jit(solution)/shard_map/ppermute | solution.py:1381
  628.6 2.1 fusion.7
  630.7 4.2 reduce-scatter.2.cloned.1.call-done
  634.9 92.2 %finish_last.1 = (bf16[4,48,1664]{2,1,0:T(8,128)(2,1)}, bf16[4,48,384]{2,1,0:T(8,128)(2,1)}, bf16[4,48,3072]{2,1,0:T(8,128)(2,1)}, f32[512,1536]{1,0:T(8,128)}) custom-call(bf16[2048,1664]{1,0:T(8,128)(2,1)} %copy-done.23, bf16[1536,2048]{1,0:T(8,128)(2,1)} %bitcast.120, bf16[8,4,48,1664]{3,2,1,0:T(8,128)(2,1)} %bitcast.123, ...), custom_call_target="tpu_custom_call" | custom-call | flops 80000000000 | bytes 40000000 | tf_op jit(solution)/shard_map/finish_last/pallas_call | solution.py:1143
  (164 shorter events, 40.4 us)
Async XLA Ops:
  7.9 140.2 %collective-permute-start.2 = (s32[2048]{0:T(1024)S(1)}, s32[2048]{0:T(1024)S(1)}, u32[]{:S(2)}, u32[]{:S(2)}) collective-permute-start(s32[2048]{0:T(1024)S(1)} %broadcast_add_fusion), channel_id=1, source_target_pairs={{0,4},{4,8},{8,12},{12,16},{16,20},{20,24},{24,28},{1,5},{5,9},{9,... | collective-permute-start | bytes 24584 | tf_op jit(solution)/shard_map/ppermute | solution.py:28
  15.9 86.6 %copy-start.35 = (f32[24]{0:T(128)S(1)}, f32[24]{0:T(128)}, u32[]{:S(2)}) copy-start(f32[24]{0:T(128)} %param.23) | copy-start | bytes 292
  103.7 21.5 %copy-start.22 = (f32[48,4096]{1,0:T(8,128)S(1)}, f32[48,4096]{1,0:T(8,128)}, u32[]{:S(2)}) copy-start(f32[48,4096]{1,0:T(8,128)} %param.28) | copy-start | bytes 2359300
  103.7 21.5 %copy-start.5 = (f32[48,4096]{1,0:T(8,128)S(1)}, f32[48,4096]{1,0:T(8,128)}, u32[]{:S(2)}) copy-start(f32[48,4096]{1,0:T(8,128)} %param.27) | copy-start | bytes 2359300
  103.7 21.6 %copy-start.3 = (f32[48,4096]{1,0:T(8,128)S(1)}, f32[48,4096]{1,0:T(8,128)}, u32[]{:S(2)}) copy-start(f32[48,4096]{1,0:T(8,128)} %param.26) | copy-start | bytes 2359300
  120.1 74.4 %collective-permute-start = (bf16[2048,768]{1,0:T(8,128)(2,1)}, bf16[2048,768]{1,0:T(8,128)(2,1)}, u32[]{:S(2)}, u32[]{:S(2)}) collective-permute-start(bf16[2048,768]{1,0:T(8,128)(2,1)} %get-tuple-element.59.k_ref.v_ref), channel_id=1, source_target_pairs={{0,4},{4,8},{8,12},{12,16},{16,20},{20,24},{24,28},{1,5},{5,9},{9,... | collective-permute-start | bytes 9437192 | tf_op jit(solution)/shard_map/ppermute | solution.py:28
  125.4 4.8 copy-start.34
  126.6 67.8 %all-to-all-start = ((bf16[48,4,3072]{2,0,1:T(8,128)(2,1)}), bf16[48,4,3072]{2,0,1:T(8,128)(2,1)S(1)}, u32[]{:S(2)}, u32[]{:S(2)}) async-start(bf16[48,4,3072]{2,0,1:T(8,128)(2,1)} %pad_maximum_fusion.1), calls=%async_computation | async-start | bytes 2359296 | tf_op jit(solution)/shard_map/all_to_all | solution.py:1361
  130.1 201.9 %all-gather.2.cloned.1.call-start = ((), (), s32[]{:S(2)}) async-start(), calls=%async_computation.2 | async-start | bytes 7077888 | tf_op jit(solution)/shard_map/all_gather | solution.py:1366
  130.2 64.2 %collective-permute-start.1 = (bf16[32,2048]{1,0:T(8,128)(2,1)S(1)}, bf16[32,2048]{1,0:T(8,128)(2,1)S(1)}, u32[]{:S(2)}, u32[]{:S(2)}) collective-permute-start(bf16[32,2048]{1,0:T(8,128)(2,1)S(1)} %copy-done.34), channel_id=1, source_target_pairs={{0,4},{4,8},{8,12},{12,16},{16,20},{20,24},{24,28},{1,5},{5,9},{9,... | collective-permute-start | bytes 393224 | tf_op jit(solution)/shard_map/ppermute | solution.py:28
  195.4 439.5 %reduce-scatter.2.cloned.1.call-start = ((), (), s32[]{:S(2)}) async-start(), calls=%async_computation.3 | async-start | bytes 10616832 | tf_op jit(solution)/shard_map/reduce_scatter | solution.py:1370
  196.5 8.9 %copy-start.9 = (f32[2048,384]{1,0:T(8,128)S(1)}, f32[2048,384]{1,0:T(8,128)}, u32[]{:S(2)}) copy-start(f32[2048,384]{1,0:T(8,128)} %fusion.13) | copy-start | bytes 9437188
  450.0 4.7 copy-start.36
  452.3 3.9 copy-start.10
  454.2 134.6 %collective-permute-start.3 = (bf16[1024,1536]{1,0:T(8,128)(2,1)}, bf16[1024,1536]{1,0:T(8,128)(2,1)}, u32[]{:S(2)}, u32[]{:S(2)}) collective-permute-start(bf16[1024,1536]{1,0:T(8,128)(2,1)} %pad_maximum_fusion), channel_id=1, source_target_pairs={{0,1},{1,0},{2,3},{3,2},{4,5},{5,4},{6,7},{7,6},{8,9},{9,8},{10,11... | collective-permute-start | bytes 9437192 | tf_op jit(solution)/shard_map/ppermute | solution.py:1376
  473.5 120.2 %collective-permute-start.5 = (bf16[2,2048,384]{2,1,0:T(8,128)(2,1)}, bf16[2,2048,384]{2,1,0:T(8,128)(2,1)}, u32[]{:S(2)}, u32[]{:S(2)}) collective-permute-start(bf16[2,2048,384]{2,1,0:T(8,128)(2,1)} %get-tuple-element.88), channel_id=1, source_target_pairs={{4,0},{8,4},{12,8},{16,12},{20,16},{24,20},{28,24},{5,1},{9,5},{13... | collective-permute-start | bytes 9437192 | tf_op jit(solution)/shard_map/ppermute | solution.py:28
  476.4 104.4 %collective-permute-start.6 = (f32[2048,8]{0,1:T(8,128)S(1)}, f32[2048,8]{0,1:T(8,128)S(1)}, u32[]{:S(2)}, u32[]{:S(2)}) collective-permute-start(f32[2048,8]{0,1:T(8,128)S(1)} %copy.86), channel_id=1, source_target_pairs={{4,0},{8,4},{12,8},{16,12},{20,16},{24,20},{28,24},{5,1},{9,5},{13... | collective-permute-start | bytes 196616 | tf_op jit(solution)/shard_map/ppermute | solution.py:28
  546.6 39.9 %copy-start.21 = (f32[2048,128]{1,0:T(8,128)S(1)}, f32[2048,128]{1,0:T(8,128)}, u32[]{:S(2)}) copy-start(f32[2048,128]{1,0:T(8,128)} %get-tuple-element.92) | copy-start | bytes 3145732
  586.6 5.1 slice-start
  588.7 2.9 slice-start.1
  592.2 36.4 %collective-permute-start.4 = (bf16[512,1536]{1,0:T(8,128)(2,1)S(1)}, bf16[512,1536]{1,0:T(8,128)(2,1)S(1)}, u32[]{:S(2)}, u32[]{:S(2)}) collective-permute-start(bf16[512,1536]{1,0:T(8,128)(2,1)S(1)} %fusion.4), channel_id=1, source_target_pairs={{0,2},{1,3},{2,0},{3,1},{4,6},{5,7},{6,4},{7,5},{8,10},{9,11},{10,... | collective-permute-start | bytes 4718600 | tf_op jit(solution)/shard_map/ppermute | solution.py:1381
  596.5 2.8 copy-start.13
  596.5 3.3 copy-start.14
  602.1 18.3 %copy-start.23 = (bf16[2048,1664]{1,0:T(8,128)(2,1)}, bf16[2048,1664]{1,0:T(8,128)(2,1)S(1)}, u32[]{:S(2)}) copy-start(bf16[2048,1664]{1,0:T(8,128)(2,1)S(1)} %fusion.12.grads_ref) | copy-start | bytes 20447236
  602.1 26.4 %copy-start.12 = (f32[512,1536]{1,0:T(8,128)S(1)}, f32[512,1536]{1,0:T(8,128)}, u32[]{:S(2)}) copy-start(f32[512,1536]{1,0:T(8,128)} %get-tuple-element.75.refs_2_) | copy-start | bytes 9437188
  728.5 3.8 copy-start.16
  728.8 3.8 copy-start.28
  729.3 3.3 copy-start.17
  729.5 3.1 copy-start.18
  729.7 2.9 copy-start.19
  729.9 3.0 copy-start.20
  734.1 4.2 copy-start.8
  (17 other events, 34.7 us)
Sparse Core Ops, SparseCore 0:
  195.5 136.4 all-gather.1
  406.9 227.9 reduce-scatter.1

commit v10 on v9

--- a/solution.py
+++ b/solution.py
@@ -787,7 +787,8 @@
     cotangent_sent = spread_all(cotangent_ref, cotangent_all, cotangent_sems, crossing)
     for t in range(1, line.half):
         line.step(t)
-    finish_tokens = hand_on(tokens_all, size, token_sems, tokens_sent, by_device)
+        if t == min(2, line.half - 1):
+            finish_tokens = hand_on(tokens_all, size, token_sems, tokens_sent, by_device)
     finish_cotangent = hand_on(cotangent_all, size, cotangent_sems, cotangent_sent, crossing)
     for swap in swaps[1:]:
         swap.wait_send()
@@ -1459,8 +1460,8 @@
     mine, earlier_kv, earlier_terms, so_far, gate_raw = lax.optimization_barrier(
         (mine, earlier_kv, earlier_terms, so_far, gate_raw)
     )
-    second = all_rows(mine[:, : 2 * hidden_width])
-    mine_down = mine[:, 2 * hidden_width :].reshape(groups, share, hidden_width)
+    down_weight = all_rows(mine[:, 2 * hidden_width :])
+    mine_second = mine[:, : 2 * hidden_width].reshape(groups, share, 2 * hidden_width)
     attended, lse = attend(
         False, ranges, query, earlier_kv, terms, earlier_terms, begins, local_heads, so_far
     )
@@ -1468,10 +1469,10 @@
     attended_wide = attended.astype(f32)
     gated = (opened * attended_wide).astype(bf16)
     branch = dot(gated, output_weight, NT).astype(bf16)
-    middle, input2, down_weight = exchange(
-        after_attention, branch, [tokens, gain2], False, 1, "exchange_middle", mine_down
-    )
-    down_weight = down_weight.reshape(model_width, hidden_width)
+    middle, input2, second = exchange(
+        after_attention, branch, [tokens, gain2], False, 1, "exchange_middle", mine_second
+    )
+    second = second.reshape(model_width, 2 * hidden_width)
     down, second_grad, grad_input2 = feed(input2, cotangent_all, second, down_weight, 4)
     second_part = row_sums(second_grad)
     grad_middle, grad_branch = exchange(

time: 753 us -> 745 us (0.989)
  waiting for transfers between devices: 63.3 us -> 53.1 us
    reduce_scatter x1, waiting for transfers between devices: 4.21 us -> 21.9 us  [row_sums(): return lax.psum_scatter(grad, 'blk', scatter_dimension=0, tiled=True)]
    all_gather x1, waiting for transfers between devices: 15.6 us -> 0.02 us  [all_rows(): return lax.all_gather(mine, 'blk', axis=0, tiled=True)]
    ppermute x5, waiting for transfers between devices: 35.3 us -> 22.7 us  [passed_along(): return lax.ppermute(array, axis, pairs)]
    pallas_call x2, Pallas kernels: 146 us -> 155 us  [exchange(): pl.pallas_call(functools.partial(exchange_kernel, local, len(extras), sum...]
  transfers between devices with their start and end apart: 10 -> 10, of which waited for: 5 -> 4; matrix products, arithmetic and copies ran while one was open for 12% -> 12% of each run, Pallas kernels for 50% -> 51%
where the time goes in v10:
time: 745 us; the launch traced here: 743 us
  Pallas kernels  547 us (73%)
  matrix products  56.2 us (8%)
  waiting for transfers between devices  53.1 us (7%)
  other arithmetic  30.3 us (4%)
  local copies, waits for them, and re-layouts  20.4 us (3%)
  starting transfers between devices  20.3 us (3%)
  between operations  14.9 us (2%)
    pallas_call x2, Pallas kernels, exchange(): pl.pallas_call(functools.partial(exchange_kernel, local, len(extras), sum...  155 us
    pallas_call x1, Pallas kernels, finish_last(): pl.pallas_call(finish_last_kernel, in_specs=[vmem] * 8, out_specs=[vmem]...  92.2 us
    pallas_call x1, Pallas kernels, gather_first(): pl.pallas_call(functools.partial(gather_first_kernel, len(before), len(af...  84.8 us
    pallas_call x1, Pallas kernels, feed(): pl.pallas_call(feed_kernel, grid=(tiles + columns // FEED_COLUMNS,), in_s...  73.8 us
    pallas_call x2, Pallas kernels, attend_back(): pl.pallas_call(functools.partial(attend_back_kernel, local_heads, own), g...  72 us
    pallas_call x2, Pallas kernels, attend(): pl.pallas_call(functools.partial(attend_kernel, local_heads, own), grid_s...  49.3 us
    dot_general x4, matrix products, dot(): return lax.dot_general(a, b, dims, preferred_element_type=f32, **kw)  30.1 us
    dot_general x2, matrix products, over_tokens(): lax.dot_general(operand, other_side, (((0,), (0,)), ((), ())), preferred_...  26 us
  transfers between devices with their start and end apart: 10, of which 4 were waited for; matrix products, arithmetic and copies ran while one was open for 12% of the time, Pallas kernels for 51%

profile of v10, /device:TPU:0, one launch (start us, length us, event | category | flops | bytes accessed | tf_op | source)
XLA Modules:
  0.0 742.6 jit_solution(5752449858360837849)
XLA Ops:
  7.9 4.8 collective-permute-start.2
  15.9 84.8 %gather_first.1 = (bf16[8,4,48,2048]{3,2,1,0:T(8,128)(2,1)}, bf16[2048,1536]{1,0:T(8,128)(2,1)}, bf16[2048,1536]{1,0:T(8,128)(2,1)}) custom-call(bf16[4,48,128]{2,1,0:T(8,128)(2,1)} %maximum_bitcast_fusion.refs_0_, f32[48,1536]{1,0:T(8,128)} %refs_1_.3, f32[48,1536]{1,0:T(8,128)} %refs_2_.1, f32[48,1536]{1,0:T(8,128)} %refs_3_.1, f32[48,1536]{1,0:T(8,128)} %refs_4_.1, ...), custom_call_target="tpu_custom_call" | custom-call | flops 70000001024 | bytes 30000000 | tf_op jit(solution)/shard_map/gather_first/pallas_call | solution.py:808
  100.7 1.8 convert_reduce_fusion.2
  103.7 16.3 %project.1 = (bf16[2048,1536]{1,0:T(8,128)(2,1)}, bf16[2048,768]{1,0:T(8,128)(2,1)}, bf16[2048,128]{1,0:T(8,128)(2,1)}, bf16[32,2048]{1,0:T(8,128)(2,1)}, f32[2048,128]{1,0:T(8,128)}) custom-call(bf16[2048,1536]{1,0:T(8,128)(2,1)} %get-tuple-element.57.tokens_ref, f32[8,1536]{1,0:T(8,128)} %broadcast_in_dim.51.gain_ref, bf16[1536,2048]{1,0:T(8,128)(2,1)} %bitcast.115, ...), custom_call_target="tpu_custom_call" | custom-call | flops 5637144576 | bytes 20000000 | tf_op jit(solution)/shard_map/project/pallas_call | solution.py:102
  120.1 5.1 collective-permute-start
  126.6 3.5 all-to-all-start
  130.2 2.0 collective-permute-start.1
  132.2 7.7 %convolution_convert_fusion.2.q_ref = bf16[2048,384]{1,0:T(8,128)(2,1)} fusion(bf16[2048,1536]{1,0:T(8,128)(2,1)} %get-tuple-element.64, bf16[1536,2048]{1,0:T(8,128)(2,1)} %bitcast.116), kind=kOutput, calls=%fused_computation.23 | convolution fusion | flops 2416705536 | bytes 9043968 | tf_op jit(solution)/shard_map/dot_general | solution.py:22
  139.9 8.2 %fusion.13 = f32[2048,384]{1,0:T(8,128)} fusion(bf16[2048,1536]{1,0:T(8,128)(2,1)} %get-tuple-element.64, bf16[1536,2048]{1,0:T(8,128)(2,1)} %bitcast.117), kind=kOutput, calls=%fused_computation.31 | convolution fusion | flops 2415919104 | bytes 10616832 | tf_op jit(solution)/shard_map/dot_general | solution.py:22
  148.0 3.3 convert_reduce_fusion
  152.8 40.5 %attend_own.1 = (f32[384,2048]{1,0:T(8,128)}, f32[24,2048]{1,0:T(8,128)}) custom-call(s32[2,4]{1,0:T(2,128)} %pad_add_fusion.1.ranges_ref, bf16[2048,384]{1,0:T(8,128)(2,1)} %convolution_convert_fusion.2.q_ref, bf16[2048,768]{1,0:T(8,128)(2,1)} %get-tuple-element.59.k_ref.v_ref, bf16[2048,768]{1,0:T(8,128)(2,1)} %get-tuple-element.59.k_ref.v_ref, ...), custom_call_target="tpu_custom_call" | custom-call | flops 40000000000 | bytes 12000000 | tf_op jit(solution)/shard_map/attend_own/pallas_call | solution.py:326
  196.5 8.8 %attend_prev.1 = (bf16[2048,384]{1,0:T(8,128)(2,1)}, f32[24,2048]{1,0:T(8,128)}) custom-call(s32[2,4]{1,0:T(2,128)} %pad_add_fusion.1.ranges_ref, bf16[2048,384]{1,0:T(8,128)(2,1)} %convolution_convert_fusion.2.q_ref, bf16[2048,768]{1,0:T(8,128)(2,1)} %collective-permute-done.k_ref.v_ref, bf16[2048,768]{1,0:T(8,128)(2,1)} %collective-permute-done.k_ref.v_ref, ...), custom_call_target="tpu_custom_call" | custom-call | flops 10000000000 | bytes 12000000 | tf_op jit(solution)/shard_map/attend_prev/pallas_call | solution.py:326
  205.3 7.8 %convolution_convert_fusion.refs_0_ = bf16[2048,1536]{1,0:T(8,128)(2,1)} fusion(bf16[1536,2048]{1,0:T(8,128)(2,1)} %bitcast.118, bf16[2048,384]{1,0:T(8,128)(2,1)} %get-tuple-element.73.o_ref, f32[2048,384]{1,0:T(8,128)S(1)} %copy-done.9), kind=kOutput, calls=%fused_computation.2 | convolution fusion | flops 2423783424 | bytes 12189696 | tf_op jit(solution)/shard_map/dot_general | solution.py:22
  213.8 110.8 %exchange_middle.1 = (f32[512,1536]{1,0:T(8,128)}, bf16[2048,1536]{1,0:T(8,128)(2,1)}, bf16[8,4,48,2048]{3,2,1,0:T(8,128)(2,1)}) custom-call(bf16[2048,1536]{1,0:T(8,128)(2,1)} %convolution_convert_fusion.refs_0_, bf16[512,1536]{1,0:T(8,128)(2,1)} %tokens_ref.1, f32[8,1536]{1,0:T(8,128)} %broadcast_in_dim.54.refs_2_.refs_3_, bf16[4,48,2048]{2,1,0:T(8,128)(2,1)} %bitcast.112), custom_call_target="tpu_custom_call" | custom-call | flops 70000001024 | bytes 16000000 | tf_op jit(solution)/shard_map/exchange_middle/pallas_call | solution.py:978
  324.6 73.8 %feed.1 = (bf16[2048,1536]{1,0:T(8,128)(2,1)}, bf16[1536,3072]{1,0:T(8,128)(2,1)}, f32[512,1536]{1,0:T(8,128)}) custom-call(bf16[2048,1536]{1,0:T(8,128)(2,1)} %get-tuple-element.76.input_ref, bf16[2048,1536]{1,0:T(8,128)(2,1)} %get-tuple-element.77.cotangent_ref, bf16[1536,2048]{1,0:T(8,128)(2,1)} %bitcast.123, ...), custom_call_target="tpu_custom_call" | custom-call | flops 57982058496 | bytes 45000000 | tf_op jit(solution)/shard_map/feed/pallas_call | solution.py:1315
  398.4 43.9 %exchange_hidden.1 = (f32[512,1536]{1,0:T(8,128)}, bf16[2048,1536]{1,0:T(8,128)(2,1)}) custom-call(f32[512,1536]{1,0:T(8,128)} %get-tuple-element.80.refs_0_, bf16[512,1536]{1,0:T(8,128)(2,1)} %refs_1_.5, f32[512,1536]{1,0:T(8,128)} %get-tuple-element.75.refs_2_, f32[8,1536]{1,0:T(8,128)} %broadcast_in_dim.54.refs_2_.refs_3_), custom_call_target="tpu_custom_call" | custom-call | flops 10000000000 | bytes 16000000 | tf_op jit(solution)/shard_map/exchange_hidden/pallas_call | solution.py:978
  442.4 2.3 fusion.25
  444.6 1.9 pad_maximum_fusion
  448.5 6.5 multiply_convert_fusion
  455.0 10.8 %attend_back_prev.1 = (f32[2048,384]{1,0:T(8,128)}, f32[2048,128]{1,0:T(8,128)}, bf16[2,2048,384]{2,1,0:T(8,128)(2,1)}, f32[2048,128]{1,0:T(8,128)}) custom-call(s32[2,4]{1,0:T(2,128)} %pad_add_fusion.1.ranges_ref, bf16[2048,384]{1,0:T(8,128)(2,1)} %convolution_convert_fusion.2.q_ref, bf16[2048,768]{1,0:T(8,128)(2,1)} %collective-permute-done.k_ref.v_ref, ...), custom_call_target="tpu_custom_call" | custom-call | flops 10000000000 | bytes 25000000 | tf_op jit(solution)/shard_map/attend_back_prev/pallas_call | solution.py:487
  470.0 61.2 %attend_back_own.1 = (bf16[2048,384]{1,0:T(8,128)(2,1)}, f32[2048,384]{1,0:T(8,128)}, f32[2048,384]{1,0:T(8,128)}, f32[2048,128]{1,0:T(8,128)}) custom-call(s32[2,4]{1,0:T(2,128)} %pad_add_fusion.1.ranges_ref, bf16[2048,384]{1,0:T(8,128)(2,1)} %convolution_convert_fusion.2.q_ref, bf16[2048,768]{1,0:T(8,128)(2,1)} %get-tuple-element.59.k_ref.v_ref, ...), custom_call_target="tpu_custom_call" | custom-call | flops 20000000000 | bytes 25000000 | tf_op jit(solution)/shard_map/attend_back_own/pallas_call | solution.py:487
  531.2 7.8 %convolution_convert_fusion.1 = bf16[1536,384]{1,0:T(8,128)(2,1)} fusion(bf16[2048,1536]{1,0:T(8,128)(2,1)} %get-tuple-element.83, bf16[2048,384]{1,0:T(8,128)(2,1)} %get-tuple-element.73.o_ref, f32[2048,384]{1,0:T(8,128)S(1)} %copy-done.10), kind=kOutput, calls=%fused_computation.22 | convolution fusion | flops 2421227520 | bytes 12189696 | tf_op jit(solution)/shard_map/dot_general | solution.py:1353
  539.0 21.6 %collective-permute-done.6 = f32[2048,8]{0,1:T(8,128)S(1)} collective-permute-done((f32[2048,8]{0,1:T(8,128)S(1)}, f32[2048,8]{0,1:T(8,128)S(1)}, u32[]{:S(2)}, u32[]{:S(2)}) %collective-permute-start.6) | collective-permute-done | bytes 65568 | tf_op jit(solution)/shard_map/ppermute | solution.py:28
  562.0 4.3 decay_back.1
  568.5 2.9 convert_element_type.194
  573.5 2.0 fusion.10
  575.8 2.2 fusion.11
  581.5 18.3 %select_convert_fusion = bf16[1536,1664]{1,0:T(8,128)(2,1)} fusion(bf16[2048,1536]{1,0:T(8,128)(2,1)} %get-tuple-element.64, bf16[2048,1664]{1,0:T(8,128)(2,1)S(1)} %fusion.12.grads_ref, bf16[1536]{0:T(1024)(128)(2,1)S(1)} %select_reduce_fusion, pred[1664]{0:T(1024)(128)(4,1)S(1)} %iota_compare_fusion.1), kind=kOutput, calls=%fused_computation.1 | convolution fusion | flops 10471538688 | bytes 18223744 | tf_op jit(solution)/shard_map/dot_general | solution.py:1353
  599.8 8.4 %collective-permute-done.4 = bf16[512,1536]{1,0:T(8,128)(2,1)S(1)} collective-permute-done((bf16[512,1536]{1,0:T(8,128)(2,1)S(1)}, bf16[512,1536]{1,0:T(8,128)(2,1)S(1)}, u32[]{:S(2)}, u32[]{:S(2)}) %collective-permute-start.4) | collective-permute-done | bytes 1572896 | tf_op jit(solution)/shard_map/ppermute | solution.py:1382
  608.3 2.1 fusion.7
  610.4 21.9 %reduce-scatter.2.cloned.1.call-done = bf16[192,3072]{1,0:T(8,128)(2,1)} async-done(((bf16[1536,3072]{1,0:T(8,128)(2,1)}), bf16[192,3072]{1,0:T(8,128)(2,1)}) %reduce-scatter.2.cloned.1.call-update) | async-done | bytes 1179664 | tf_op jit(solution)/shard_map/reduce_scatter | solution.py:1371
  632.3 92.2 %finish_last.1 = (bf16[4,48,1664]{2,1,0:T(8,128)(2,1)}, bf16[4,48,384]{2,1,0:T(8,128)(2,1)}, bf16[4,48,3072]{2,1,0:T(8,128)(2,1)}, f32[512,1536]{1,0:T(8,128)}) custom-call(bf16[2048,1664]{1,0:T(8,128)(2,1)} %copy-done.23, bf16[1536,2048]{1,0:T(8,128)(2,1)} %bitcast.120, bf16[8,4,48,1664]{3,2,1,0:T(8,128)(2,1)} %bitcast.124, ...), custom_call_target="tpu_custom_call" | custom-call | flops 80000000000 | bytes 40000000 | tf_op jit(solution)/shard_map/finish_last/pallas_call | solution.py:1144
  (164 shorter events, 38.4 us)
Async XLA Ops:
  7.9 140.2 %collective-permute-start.2 = (s32[2048]{0:T(1024)S(1)}, s32[2048]{0:T(1024)S(1)}, u32[]{:S(2)}, u32[]{:S(2)}) collective-permute-start(s32[2048]{0:T(1024)S(1)} %broadcast_add_fusion), channel_id=1, source_target_pairs={{0,4},{4,8},{8,12},{12,16},{16,20},{20,24},{24,28},{1,5},{5,9},{9,... | collective-permute-start | bytes 24584 | tf_op jit(solution)/shard_map/ppermute | solution.py:28
  15.9 86.6 %copy-start.35 = (f32[24]{0:T(128)S(1)}, f32[24]{0:T(128)}, u32[]{:S(2)}) copy-start(f32[24]{0:T(128)} %param.23) | copy-start | bytes 292
  103.7 21.5 %copy-start.22 = (f32[48,4096]{1,0:T(8,128)S(1)}, f32[48,4096]{1,0:T(8,128)}, u32[]{:S(2)}) copy-start(f32[48,4096]{1,0:T(8,128)} %param.28) | copy-start | bytes 2359300
  103.7 21.5 %copy-start.5 = (f32[48,4096]{1,0:T(8,128)S(1)}, f32[48,4096]{1,0:T(8,128)}, u32[]{:S(2)}) copy-start(f32[48,4096]{1,0:T(8,128)} %param.27) | copy-start | bytes 2359300
  103.7 21.6 %copy-start.3 = (f32[48,4096]{1,0:T(8,128)S(1)}, f32[48,4096]{1,0:T(8,128)}, u32[]{:S(2)}) copy-start(f32[48,4096]{1,0:T(8,128)} %param.26) | copy-start | bytes 2359300
  120.1 74.4 %collective-permute-start = (bf16[2048,768]{1,0:T(8,128)(2,1)}, bf16[2048,768]{1,0:T(8,128)(2,1)}, u32[]{:S(2)}, u32[]{:S(2)}) collective-permute-start(bf16[2048,768]{1,0:T(8,128)(2,1)} %get-tuple-element.59.k_ref.v_ref), channel_id=1, source_target_pairs={{0,4},{4,8},{8,12},{12,16},{16,20},{20,24},{24,28},{1,5},{5,9},{9,... | collective-permute-start | bytes 9437192 | tf_op jit(solution)/shard_map/ppermute | solution.py:28
  125.4 4.8 copy-start.34
  126.6 67.8 %all-to-all-start = ((bf16[48,4,3072]{2,0,1:T(8,128)(2,1)}), bf16[48,4,3072]{2,0,1:T(8,128)(2,1)S(1)}, u32[]{:S(2)}, u32[]{:S(2)}) async-start(bf16[48,4,3072]{2,0,1:T(8,128)(2,1)} %pad_maximum_fusion.1), calls=%async_computation | async-start | bytes 2359296 | tf_op jit(solution)/shard_map/all_to_all | solution.py:1362
  130.1 194.4 %all-gather.2.cloned.1.call-start = ((), (), s32[]{:S(2)}) async-start(), calls=%async_computation.2 | async-start | bytes 3538944 | tf_op jit(solution)/shard_map/all_gather | solution.py:1367
  130.2 64.2 %collective-permute-start.1 = (bf16[32,2048]{1,0:T(8,128)(2,1)S(1)}, bf16[32,2048]{1,0:T(8,128)(2,1)S(1)}, u32[]{:S(2)}, u32[]{:S(2)}) collective-permute-start(bf16[32,2048]{1,0:T(8,128)(2,1)S(1)} %copy-done.34), channel_id=1, source_target_pairs={{0,4},{4,8},{8,12},{12,16},{16,20},{20,24},{24,28},{1,5},{5,9},{9,... | collective-permute-start | bytes 393224 | tf_op jit(solution)/shard_map/ppermute | solution.py:28
  196.2 9.2 %copy-start.9 = (f32[2048,384]{1,0:T(8,128)S(1)}, f32[2048,384]{1,0:T(8,128)}, u32[]{:S(2)}) copy-start(f32[2048,384]{1,0:T(8,128)} %fusion.13) | copy-start | bytes 9437188
  196.2 436.1 %reduce-scatter.2.cloned.1.call-start = ((), (), s32[]{:S(2)}) async-start(), calls=%async_computation.3 | async-start | bytes 10616832 | tf_op jit(solution)/shard_map/reduce_scatter | solution.py:1371
  442.3 4.7 copy-start.36
  444.6 3.9 copy-start.10
  446.5 122.0 %collective-permute-start.3 = (bf16[1024,1536]{1,0:T(8,128)(2,1)}, bf16[1024,1536]{1,0:T(8,128)(2,1)}, u32[]{:S(2)}, u32[]{:S(2)}) collective-permute-start(bf16[1024,1536]{1,0:T(8,128)(2,1)} %pad_maximum_fusion), channel_id=1, source_target_pairs={{0,1},{1,0},{2,3},{3,2},{4,5},{5,4},{6,7},{7,6},{8,9},{9,8},{10,11... | collective-permute-start | bytes 9437192 | tf_op jit(solution)/shard_map/ppermute | solution.py:1377
  465.9 107.6 %collective-permute-start.5 = (bf16[2,2048,384]{2,1,0:T(8,128)(2,1)}, bf16[2,2048,384]{2,1,0:T(8,128)(2,1)}, u32[]{:S(2)}, u32[]{:S(2)}) collective-permute-start(bf16[2,2048,384]{2,1,0:T(8,128)(2,1)} %get-tuple-element.88), channel_id=1, source_target_pairs={{4,0},{8,4},{12,8},{16,12},{20,16},{24,20},{28,24},{5,1},{9,5},{13... | collective-permute-start | bytes 9437192 | tf_op jit(solution)/shard_map/ppermute | solution.py:28
  468.7 91.9 %collective-permute-start.6 = (f32[2048,8]{0,1:T(8,128)S(1)}, f32[2048,8]{0,1:T(8,128)S(1)}, u32[]{:S(2)}, u32[]{:S(2)}) collective-permute-start(f32[2048,8]{0,1:T(8,128)S(1)} %copy.86), channel_id=1, source_target_pairs={{4,0},{8,4},{12,8},{16,12},{20,16},{24,20},{28,24},{5,1},{9,5},{13... | collective-permute-start | bytes 196616 | tf_op jit(solution)/shard_map/ppermute | solution.py:28
  539.0 27.3 %copy-start.21 = (f32[2048,128]{1,0:T(8,128)S(1)}, f32[2048,128]{1,0:T(8,128)}, u32[]{:S(2)}) copy-start(f32[2048,128]{1,0:T(8,128)} %get-tuple-element.92) | copy-start | bytes 3145732
  566.3 5.1 slice-start
  568.5 2.9 slice-start.1
  571.9 36.3 %collective-permute-start.4 = (bf16[512,1536]{1,0:T(8,128)(2,1)S(1)}, bf16[512,1536]{1,0:T(8,128)(2,1)S(1)}, u32[]{:S(2)}, u32[]{:S(2)}) collective-permute-start(bf16[512,1536]{1,0:T(8,128)(2,1)S(1)} %fusion.4), channel_id=1, source_target_pairs={{0,2},{1,3},{2,0},{3,1},{4,6},{5,7},{6,4},{7,5},{8,10},{9,11},{10,... | collective-permute-start | bytes 4718600 | tf_op jit(solution)/shard_map/ppermute | solution.py:1382
  575.8 2.8 copy-start.13
  575.8 3.3 copy-start.14
  581.5 18.3 %copy-start.23 = (bf16[2048,1664]{1,0:T(8,128)(2,1)}, bf16[2048,1664]{1,0:T(8,128)(2,1)S(1)}, u32[]{:S(2)}) copy-start(bf16[2048,1664]{1,0:T(8,128)(2,1)S(1)} %fusion.12.grads_ref) | copy-start | bytes 20447236
  581.5 26.7 %copy-start.12 = (f32[512,1536]{1,0:T(8,128)S(1)}, f32[512,1536]{1,0:T(8,128)}, u32[]{:S(2)}) copy-start(f32[512,1536]{1,0:T(8,128)} %get-tuple-element.75.refs_2_) | copy-start | bytes 9437188
  725.9 3.8 copy-start.16
  726.1 3.8 copy-start.28
  726.7 3.3 copy-start.17
  726.9 3.1 copy-start.18
  727.1 2.9 copy-start.19
  727.3 3.0 copy-start.20
  731.4 4.2 copy-start.8
  (17 other events, 34.3 us)
Sparse Core Ops, SparseCore 0:
  196.3 80.1 all-gather.1
  398.5 233.7 reduce-scatter.1

commit v11 on v10

--- a/solution.py
+++ b/solution.py
@@ -51,7 +51,7 @@
     return outs, carry
 
 
-PROJECT_TILE = 256
+PROJECT_TILE = 512
 TERM_ROWS = 32
 
 
@@ -1204,7 +1204,7 @@
 
 
 FEED_TILE = 256
-FEED_COLUMNS = 512
+FEED_COLUMNS = 1024
 
 
 def feed_kernel(input_ref, cotangent_ref, weight_ref, down_weight_ref, down_ref, grad_ref, total_ref,
@@ -1247,7 +1247,7 @@
         gate = dot(inputs, weight_ref[:, gate_at])
         up = dot(inputs, weight_ref[:, up_at])
         grad_hidden = dot(cotangent, down_weight_ref[...])
-        opening = jax.nn.sigmoid(gate)
+        opening = 0.5 * jnp.tanh(0.5 * gate) + 0.5
         active = gate * opening
         hidden = (active * up).astype(bf16)
         grad_gate = (grad_hidden * up * opening * (1.0 + gate * (1.0 - opening))).astype(bf16)

time: 745 us -> 746 us (level)
    ppermute x5, waiting for transfers between devices: 22.7 us -> 47.6 us  [passed_along(): return lax.ppermute(array, axis, pairs)]
    reduce_scatter x1, waiting for transfers between devices: 21.9 us -> 2.92 us  [row_sums(): return lax.psum_scatter(grad, 'blk', scatter_dimension=0, tiled=True)]
  transfers between devices with their start and end apart: 10 -> 10, of which waited for: 4 -> 4; matrix products, arithmetic and copies ran while one was open for 12% -> 12% of each run, Pallas kernels for 51% -> 50%
where the time goes in v11:
time: 746 us; the launch traced here: 744 us
  Pallas kernels  542 us (73%)
  waiting for transfers between devices  59.3 us (8%)
  matrix products  55.9 us (7%)
  other arithmetic  30.3 us (4%)
  local copies, waits for them, and re-layouts  20.6 us (3%)
  starting transfers between devices  20.2 us (3%)
  between operations  15 us (2%)
    pallas_call x2, Pallas kernels, exchange(): pl.pallas_call(functools.partial(exchange_kernel, local, len(extras), sum...  155 us
    pallas_call x1, Pallas kernels, finish_last(): pl.pallas_call(finish_last_kernel, in_specs=[vmem] * 8, out_specs=[vmem]...  95.9 us
    pallas_call x1, Pallas kernels, gather_first(): pl.pallas_call(functools.partial(gather_first_kernel, len(before), len(af...  84.8 us
    pallas_call x1, Pallas kernels, feed(): pl.pallas_call(feed_kernel, grid=(tiles + columns // FEED_COLUMNS,), in_s...  73.3 us
    pallas_call x2, Pallas kernels, attend_back(): pl.pallas_call(functools.partial(attend_back_kernel, local_heads, own), g...  67.8 us
    ppermute x5, waiting for transfers between devices, passed_along(): return lax.ppermute(array, axis, pairs)  47.6 us
    pallas_call x2, Pallas kernels, attend(): pl.pallas_call(functools.partial(attend_kernel, local_heads, own), grid_s...  45.7 us
    dot_general x4, matrix products, dot(): return lax.dot_general(a, b, dims, preferred_element_type=f32, **kw)  30.2 us
  transfers between devices with their start and end apart: 10, of which 4 were waited for; matrix products, arithmetic and copies ran while one was open for 12% of the time, Pallas kernels for 50%

profile of v11, /device:TPU:0, one launch (start us, length us, event | category | flops | bytes accessed | tf_op | source)
XLA Modules:
  0.0 743.5 jit_solution(3007227606062527228)
XLA Ops:
  7.9 4.8 collective-permute-start.2
  15.9 84.8 %gather_first.1 = (bf16[8,4,48,2048]{3,2,1,0:T(8,128)(2,1)}, bf16[2048,1536]{1,0:T(8,128)(2,1)}, bf16[2048,1536]{1,0:T(8,128)(2,1)}) custom-call(bf16[4,48,128]{2,1,0:T(8,128)(2,1)} %maximum_bitcast_fusion.refs_0_, f32[48,1536]{1,0:T(8,128)} %refs_1_.3, f32[48,1536]{1,0:T(8,128)} %refs_2_.1, f32[48,1536]{1,0:T(8,128)} %refs_3_.1, f32[48,1536]{1,0:T(8,128)} %refs_4_.1, ...), custom_call_target="tpu_custom_call" | custom-call | flops 70000001024 | bytes 30000000 | tf_op jit(solution)/shard_map/gather_first/pallas_call | solution.py:808
  103.7 15.1 %project.1 = (bf16[2048,1536]{1,0:T(8,128)(2,1)}, bf16[2048,768]{1,0:T(8,128)(2,1)}, bf16[2048,128]{1,0:T(8,128)(2,1)}, bf16[32,2048]{1,0:T(8,128)(2,1)}, f32[2048,128]{1,0:T(8,128)}) custom-call(bf16[2048,1536]{1,0:T(8,128)(2,1)} %get-tuple-element.57.tokens_ref, f32[8,1536]{1,0:T(8,128)} %broadcast_in_dim.51.gain_ref, bf16[1536,2048]{1,0:T(8,128)(2,1)} %bitcast.115, ...), custom_call_target="tpu_custom_call" | custom-call | flops 5637144576 | bytes 20000000 | tf_op jit(solution)/shard_map/project/pallas_call | solution.py:102
  118.8 5.1 collective-permute-start
  125.4 3.5 all-to-all-start
  129.0 2.0 collective-permute-start.1
  131.0 7.7 %convolution_convert_fusion.2.q_ref = bf16[2048,384]{1,0:T(8,128)(2,1)} fusion(bf16[2048,1536]{1,0:T(8,128)(2,1)} %get-tuple-element.64, bf16[1536,2048]{1,0:T(8,128)(2,1)} %bitcast.116), kind=kOutput, calls=%fused_computation.23 | convolution fusion | flops 2416705536 | bytes 9043968 | tf_op jit(solution)/shard_map/dot_general | solution.py:22
  138.6 8.2 %fusion.13 = f32[2048,384]{1,0:T(8,128)} fusion(bf16[2048,1536]{1,0:T(8,128)(2,1)} %get-tuple-element.64, bf16[1536,2048]{1,0:T(8,128)(2,1)} %bitcast.117), kind=kOutput, calls=%fused_computation.31 | convolution fusion | flops 2415919104 | bytes 10616832 | tf_op jit(solution)/shard_map/dot_general | solution.py:22
  146.8 3.3 convert_reduce_fusion
  151.6 36.9 %attend_own.1 = (f32[384,2048]{1,0:T(8,128)}, f32[24,2048]{1,0:T(8,128)}) custom-call(s32[2,4]{1,0:T(2,128)} %pad_add_fusion.1.ranges_ref, bf16[2048,384]{1,0:T(8,128)(2,1)} %convolution_convert_fusion.2.q_ref, bf16[2048,768]{1,0:T(8,128)(2,1)} %get-tuple-element.59.k_ref.v_ref, bf16[2048,768]{1,0:T(8,128)(2,1)} %get-tuple-element.59.k_ref.v_ref, ...), custom_call_target="tpu_custom_call" | custom-call | flops 40000000000 | bytes 12000000 | tf_op jit(solution)/shard_map/attend_own/pallas_call | solution.py:326
  188.5 4.7 collective-permute-done.1.t_key_ref
  195.5 8.8 %attend_prev.1 = (bf16[2048,384]{1,0:T(8,128)(2,1)}, f32[24,2048]{1,0:T(8,128)}) custom-call(s32[2,4]{1,0:T(2,128)} %pad_add_fusion.1.ranges_ref, bf16[2048,384]{1,0:T(8,128)(2,1)} %convolution_convert_fusion.2.q_ref, bf16[2048,768]{1,0:T(8,128)(2,1)} %collective-permute-done.k_ref.v_ref, bf16[2048,768]{1,0:T(8,128)(2,1)} %collective-permute-done.k_ref.v_ref, ...), custom_call_target="tpu_custom_call" | custom-call | flops 10000000000 | bytes 12000000 | tf_op jit(solution)/shard_map/attend_prev/pallas_call | solution.py:326
  204.3 7.8 %convolution_convert_fusion.refs_0_ = bf16[2048,1536]{1,0:T(8,128)(2,1)} fusion(bf16[1536,2048]{1,0:T(8,128)(2,1)} %bitcast.118, bf16[2048,384]{1,0:T(8,128)(2,1)} %get-tuple-element.73.o_ref, f32[2048,384]{1,0:T(8,128)S(1)} %copy-done.9), kind=kOutput, calls=%fused_computation.2 | convolution fusion | flops 2423783424 | bytes 12189696 | tf_op jit(solution)/shard_map/dot_general | solution.py:22
  212.7 111.3 %exchange_middle.1 = (f32[512,1536]{1,0:T(8,128)}, bf16[2048,1536]{1,0:T(8,128)(2,1)}, bf16[8,4,48,2048]{3,2,1,0:T(8,128)(2,1)}) custom-call(bf16[2048,1536]{1,0:T(8,128)(2,1)} %convolution_convert_fusion.refs_0_, bf16[512,1536]{1,0:T(8,128)(2,1)} %tokens_ref.1, f32[8,1536]{1,0:T(8,128)} %broadcast_in_dim.54.refs_2_.refs_3_, bf16[4,48,2048]{2,1,0:T(8,128)(2,1)} %bitcast.112), custom_call_target="tpu_custom_call" | custom-call | flops 70000001024 | bytes 16000000 | tf_op jit(solution)/shard_map/exchange_middle/pallas_call | solution.py:978
  324.0 73.3 %feed.1 = (bf16[2048,1536]{1,0:T(8,128)(2,1)}, bf16[1536,3072]{1,0:T(8,128)(2,1)}, f32[512,1536]{1,0:T(8,128)}) custom-call(bf16[2048,1536]{1,0:T(8,128)(2,1)} %get-tuple-element.76.input_ref, bf16[2048,1536]{1,0:T(8,128)(2,1)} %get-tuple-element.77.cotangent_ref, bf16[1536,2048]{1,0:T(8,128)(2,1)} %bitcast.123, ...), custom_call_target="tpu_custom_call" | custom-call | flops 57982058496 | bytes 45000000 | tf_op jit(solution)/shard_map/feed/pallas_call | solution.py:1315
  397.4 44.0 %exchange_hidden.1 = (f32[512,1536]{1,0:T(8,128)}, bf16[2048,1536]{1,0:T(8,128)(2,1)}) custom-call(f32[512,1536]{1,0:T(8,128)} %get-tuple-element.80.refs_0_, bf16[512,1536]{1,0:T(8,128)(2,1)} %refs_1_.5, f32[512,1536]{1,0:T(8,128)} %get-tuple-element.75.refs_2_, f32[8,1536]{1,0:T(8,128)} %broadcast_in_dim.54.refs_2_.refs_3_), custom_call_target="tpu_custom_call" | custom-call | flops 10000000000 | bytes 16000000 | tf_op jit(solution)/shard_map/exchange_hidden/pallas_call | solution.py:978
  441.5 2.3 fusion.25
  443.8 1.9 pad_maximum_fusion
  447.6 6.5 multiply_convert_fusion
  454.1 10.8 %attend_back_prev.1 = (f32[2048,384]{1,0:T(8,128)}, f32[2048,128]{1,0:T(8,128)}, bf16[2,2048,384]{2,1,0:T(8,128)(2,1)}, f32[2048,128]{1,0:T(8,128)}) custom-call(s32[2,4]{1,0:T(2,128)} %pad_add_fusion.1.ranges_ref, bf16[2048,384]{1,0:T(8,128)(2,1)} %convolution_convert_fusion.2.q_ref, bf16[2048,768]{1,0:T(8,128)(2,1)} %collective-permute-done.k_ref.v_ref, ...), custom_call_target="tpu_custom_call" | custom-call | flops 10000000000 | bytes 25000000 | tf_op jit(solution)/shard_map/attend_back_prev/pallas_call | solution.py:487
  469.2 56.9 %attend_back_own.1 = (bf16[2048,384]{1,0:T(8,128)(2,1)}, f32[2048,384]{1,0:T(8,128)}, f32[2048,384]{1,0:T(8,128)}, f32[2048,128]{1,0:T(8,128)}) custom-call(s32[2,4]{1,0:T(2,128)} %pad_add_fusion.1.ranges_ref, bf16[2048,384]{1,0:T(8,128)(2,1)} %convolution_convert_fusion.2.q_ref, bf16[2048,768]{1,0:T(8,128)(2,1)} %get-tuple-element.59.k_ref.v_ref, ...), custom_call_target="tpu_custom_call" | custom-call | flops 20000000000 | bytes 25000000 | tf_op jit(solution)/shard_map/attend_back_own/pallas_call | solution.py:487
  526.1 7.8 %convolution_convert_fusion.1 = bf16[1536,384]{1,0:T(8,128)(2,1)} fusion(bf16[2048,1536]{1,0:T(8,128)(2,1)} %get-tuple-element.83, bf16[2048,384]{1,0:T(8,128)(2,1)} %get-tuple-element.73.o_ref, f32[2048,384]{1,0:T(8,128)S(1)} %copy-done.10), kind=kOutput, calls=%fused_computation.22 | convolution fusion | flops 2421227520 | bytes 12189696 | tf_op jit(solution)/shard_map/dot_general | solution.py:1353
  533.8 42.9 %collective-permute-done.6 = f32[2048,8]{0,1:T(8,128)S(1)} collective-permute-done((f32[2048,8]{0,1:T(8,128)S(1)}, f32[2048,8]{0,1:T(8,128)S(1)}, u32[]{:S(2)}, u32[]{:S(2)}) %collective-permute-start.6) | collective-permute-done | bytes 65568 | tf_op jit(solution)/shard_map/ppermute | solution.py:28
  578.1 4.3 decay_back.1
  584.7 2.9 convert_element_type.194
  589.6 2.0 fusion.10
  592.0 2.2 fusion.11
  597.6 18.0 %select_convert_fusion = bf16[1536,1664]{1,0:T(8,128)(2,1)} fusion(bf16[2048,1536]{1,0:T(8,128)(2,1)} %get-tuple-element.64, bf16[2048,1664]{1,0:T(8,128)(2,1)S(1)} %fusion.12.grads_ref, bf16[1536]{0:T(1024)(128)(2,1)S(1)} %select_reduce_fusion, pred[1664]{0:T(1024)(128)(4,1)S(1)} %iota_compare_fusion.1), kind=kOutput, calls=%fused_computation.1 | convolution fusion | flops 10471538688 | bytes 18223744 | tf_op jit(solution)/shard_map/dot_general | solution.py:1353
  615.7 8.7 %collective-permute-done.4 = bf16[512,1536]{1,0:T(8,128)(2,1)S(1)} collective-permute-done((bf16[512,1536]{1,0:T(8,128)(2,1)S(1)}, bf16[512,1536]{1,0:T(8,128)(2,1)S(1)}, u32[]{:S(2)}, u32[]{:S(2)}) %collective-permute-start.4) | collective-permute-done | bytes 1572896 | tf_op jit(solution)/shard_map/ppermute | solution.py:1382
  624.4 2.1 fusion.7
  626.5 2.9 reduce-scatter.2.cloned.1.call-done
  629.4 95.9 %finish_last.1 = (bf16[4,48,1664]{2,1,0:T(8,128)(2,1)}, bf16[4,48,384]{2,1,0:T(8,128)(2,1)}, bf16[4,48,3072]{2,1,0:T(8,128)(2,1)}, f32[512,1536]{1,0:T(8,128)}) custom-call(bf16[2048,1664]{1,0:T(8,128)(2,1)} %copy-done.23, bf16[1536,2048]{1,0:T(8,128)(2,1)} %bitcast.120, bf16[8,4,48,1664]{3,2,1,0:T(8,128)(2,1)} %bitcast.124, ...), custom_call_target="tpu_custom_call" | custom-call | flops 80000000000 | bytes 40000000 | tf_op jit(solution)/shard_map/finish_last/pallas_call | solution.py:1144
  (164 shorter events, 39.1 us)
Async XLA Ops:
  7.9 138.9 %collective-permute-start.2 = (s32[2048]{0:T(1024)S(1)}, s32[2048]{0:T(1024)S(1)}, u32[]{:S(2)}, u32[]{:S(2)}) collective-permute-start(s32[2048]{0:T(1024)S(1)} %broadcast_add_fusion), channel_id=1, source_target_pairs={{0,4},{4,8},{8,12},{12,16},{16,20},{20,24},{24,28},{1,5},{5,9},{9,... | collective-permute-start | bytes 24584 | tf_op jit(solution)/shard_map/ppermute | solution.py:28
  15.9 86.6 %copy-start.35 = (f32[24]{0:T(128)S(1)}, f32[24]{0:T(128)}, u32[]{:S(2)}) copy-start(f32[24]{0:T(128)} %param.23) | copy-start | bytes 292
  103.7 20.2 %copy-start.22 = (f32[48,4096]{1,0:T(8,128)S(1)}, f32[48,4096]{1,0:T(8,128)}, u32[]{:S(2)}) copy-start(f32[48,4096]{1,0:T(8,128)} %param.28) | copy-start | bytes 2359300
  103.7 20.3 %copy-start.5 = (f32[48,4096]{1,0:T(8,128)S(1)}, f32[48,4096]{1,0:T(8,128)}, u32[]{:S(2)}) copy-start(f32[48,4096]{1,0:T(8,128)} %param.27) | copy-start | bytes 2359300
  103.7 20.3 %copy-start.3 = (f32[48,4096]{1,0:T(8,128)S(1)}, f32[48,4096]{1,0:T(8,128)}, u32[]{:S(2)}) copy-start(f32[48,4096]{1,0:T(8,128)} %param.26) | copy-start | bytes 2359300
  118.8 74.4 %collective-permute-start = (bf16[2048,768]{1,0:T(8,128)(2,1)}, bf16[2048,768]{1,0:T(8,128)(2,1)}, u32[]{:S(2)}, u32[]{:S(2)}) collective-permute-start(bf16[2048,768]{1,0:T(8,128)(2,1)} %get-tuple-element.59.k_ref.v_ref), channel_id=1, source_target_pairs={{0,4},{4,8},{8,12},{12,16},{16,20},{20,24},{24,28},{1,5},{5,9},{9,... | collective-permute-start | bytes 9437192 | tf_op jit(solution)/shard_map/ppermute | solution.py:28
  124.2 4.8 copy-start.34
  125.4 67.8 %all-to-all-start = ((bf16[48,4,3072]{2,0,1:T(8,128)(2,1)}), bf16[48,4,3072]{2,0,1:T(8,128)(2,1)S(1)}, u32[]{:S(2)}, u32[]{:S(2)}) async-start(bf16[48,4,3072]{2,0,1:T(8,128)(2,1)} %pad_maximum_fusion.1), calls=%async_computation | async-start | bytes 2359296 | tf_op jit(solution)/shard_map/all_to_all | solution.py:1362
  128.9 195.1 %all-gather.2.cloned.1.call-start = ((), (), s32[]{:S(2)}) async-start(), calls=%async_computation.2 | async-start | bytes 3538944 | tf_op jit(solution)/shard_map/all_gather | solution.py:1367
  129.0 64.2 %collective-permute-start.1 = (bf16[32,2048]{1,0:T(8,128)(2,1)S(1)}, bf16[32,2048]{1,0:T(8,128)(2,1)S(1)}, u32[]{:S(2)}, u32[]{:S(2)}) collective-permute-start(bf16[32,2048]{1,0:T(8,128)(2,1)S(1)} %copy-done.34), channel_id=1, source_target_pairs={{0,4},{4,8},{8,12},{12,16},{16,20},{20,24},{24,28},{1,5},{5,9},{9,... | collective-permute-start | bytes 393224 | tf_op jit(solution)/shard_map/ppermute | solution.py:28
  194.9 9.3 %copy-start.9 = (f32[2048,384]{1,0:T(8,128)S(1)}, f32[2048,384]{1,0:T(8,128)}, u32[]{:S(2)}) copy-start(f32[2048,384]{1,0:T(8,128)} %fusion.13) | copy-start | bytes 9437188
  194.9 434.5 %reduce-scatter.2.cloned.1.call-start = ((), (), s32[]{:S(2)}) async-start(), calls=%async_computation.3 | async-start | bytes 10616832 | tf_op jit(solution)/shard_map/reduce_scatter | solution.py:1371
  441.5 4.7 copy-start.36
  443.7 3.9 copy-start.10
  445.6 139.0 %collective-permute-start.3 = (bf16[1024,1536]{1,0:T(8,128)(2,1)}, bf16[1024,1536]{1,0:T(8,128)(2,1)}, u32[]{:S(2)}, u32[]{:S(2)}) collective-permute-start(bf16[1024,1536]{1,0:T(8,128)(2,1)} %pad_maximum_fusion), channel_id=1, source_target_pairs={{0,1},{1,0},{2,3},{3,2},{4,5},{5,4},{6,7},{7,6},{8,9},{9,8},{10,11... | collective-permute-start | bytes 9437192 | tf_op jit(solution)/shard_map/ppermute | solution.py:1377
  465.0 124.5 %collective-permute-start.5 = (bf16[2,2048,384]{2,1,0:T(8,128)(2,1)}, bf16[2,2048,384]{2,1,0:T(8,128)(2,1)}, u32[]{:S(2)}, u32[]{:S(2)}) collective-permute-start(bf16[2,2048,384]{2,1,0:T(8,128)(2,1)} %get-tuple-element.88), channel_id=1, source_target_pairs={{4,0},{8,4},{12,8},{16,12},{20,16},{24,20},{28,24},{5,1},{9,5},{13... | collective-permute-start | bytes 9437192 | tf_op jit(solution)/shard_map/ppermute | solution.py:28
  467.9 108.9 %collective-permute-start.6 = (f32[2048,8]{0,1:T(8,128)S(1)}, f32[2048,8]{0,1:T(8,128)S(1)}, u32[]{:S(2)}, u32[]{:S(2)}) collective-permute-start(f32[2048,8]{0,1:T(8,128)S(1)} %copy.86), channel_id=1, source_target_pairs={{4,0},{8,4},{12,8},{16,12},{20,16},{24,20},{28,24},{5,1},{9,5},{13... | collective-permute-start | bytes 196616 | tf_op jit(solution)/shard_map/ppermute | solution.py:28
  533.8 48.6 %copy-start.21 = (f32[2048,128]{1,0:T(8,128)S(1)}, f32[2048,128]{1,0:T(8,128)}, u32[]{:S(2)}) copy-start(f32[2048,128]{1,0:T(8,128)} %get-tuple-element.92) | copy-start | bytes 3145732
  582.4 5.2 slice-start
  584.6 3.1 slice-start.1
  588.2 36.2 %collective-permute-start.4 = (bf16[512,1536]{1,0:T(8,128)(2,1)S(1)}, bf16[512,1536]{1,0:T(8,128)(2,1)S(1)}, u32[]{:S(2)}, u32[]{:S(2)}) collective-permute-start(bf16[512,1536]{1,0:T(8,128)(2,1)S(1)} %fusion.4), channel_id=1, source_target_pairs={{0,2},{1,3},{2,0},{3,1},{4,6},{5,7},{6,4},{7,5},{8,10},{9,11},{10,... | collective-permute-start | bytes 4718600 | tf_op jit(solution)/shard_map/ppermute | solution.py:1382
  592.0 2.8 copy-start.13
  592.0 3.3 copy-start.14
  597.6 18.0 %copy-start.23 = (bf16[2048,1664]{1,0:T(8,128)(2,1)}, bf16[2048,1664]{1,0:T(8,128)(2,1)S(1)}, u32[]{:S(2)}) copy-start(bf16[2048,1664]{1,0:T(8,128)(2,1)S(1)} %fusion.12.grads_ref) | copy-start | bytes 20447236
  597.6 26.7 %copy-start.12 = (f32[512,1536]{1,0:T(8,128)S(1)}, f32[512,1536]{1,0:T(8,128)}, u32[]{:S(2)}) copy-start(f32[512,1536]{1,0:T(8,128)} %get-tuple-element.75.refs_2_) | copy-start | bytes 9437188
  726.7 3.8 copy-start.16
  727.0 3.8 copy-start.28
  727.5 3.3 copy-start.17
  727.7 3.1 copy-start.18
  727.9 2.9 copy-start.19
  728.1 3.0 copy-start.20
  732.3 4.2 copy-start.8
  (17 other events, 34.4 us)
Sparse Core Ops, SparseCore 0:
  195.0 78.7 all-gather.1
  397.5 231.8 reduce-scatter.1

commit v12 on v11

--- a/solution.py
+++ b/solution.py
@@ -1439,10 +1439,10 @@
     )
     earlier_kv = passed_along(key_value, "blk", 1)
     earlier_terms = passed_along(turned_terms, "blk", 1)
-    query = dot(input1, first[:, kv_width : kv_width + local_width]).astype(bf16)
-    gate_raw = dot(
-        input1, first[:, kv_width + local_width : kv_width + 2 * local_width]
-    )
+    query_gate = lax.optimization_barrier(
+        dot(input1, first[:, kv_width : kv_width + 2 * local_width])
+    )
+    query, gate_raw = query_gate[:, :local_width].astype(bf16), query_gate[:, local_width:]
 
     segment_plus = segment + 1
     earlier_segment = passed_along(segment_plus, "blk", 1)

time: 746 us -> 754 us (1.011)
  Pallas kernels: 542 us -> 577 us
  waiting for transfers between devices: 59.3 us -> 38.4 us
  matrix products: 55.9 us -> 48.1 us
    ppermute x5, waiting for transfers between devices: 47.6 us -> 25.1 us  [passed_along(): return lax.ppermute(array, axis, pairs)]
    pallas_call x2, Pallas kernels: 67.8 us -> 80.4 us  [attend_back(): pl.pallas_call(functools.partial(attend_back_kernel, local_heads, own), g...]
    pallas_call x1, Pallas kernels: 73.3 us -> 84 us  [feed(): pl.pallas_call(feed_kernel, grid=(tiles + columns // FEED_COLUMNS,), in_s...]
    pallas_call x2, Pallas kernels: 45.7 us -> 56.3 us  [attend(): pl.pallas_call(functools.partial(attend_kernel, local_heads, own), grid_s...]
    dot_general x4 -> x3, matrix products: 30.2 us -> 22.3 us  [dot(): return lax.dot_general(a, b, dims, preferred_element_type=f32, **kw)]
  transfers between devices with their start and end apart: 10 -> 10, of which waited for: 4 -> 3; matrix products, arithmetic and copies ran while one was open for 12% -> 11% of each run, Pallas kernels for 50% -> 52%
where the time goes in v12:
time: 754 us; the launch traced here: 757 us
  Pallas kernels  577 us (77%)
  matrix products  48.1 us (6%)
  waiting for transfers between devices  38.4 us (5%)
  other arithmetic  31 us (4%)
  local copies, waits for them, and re-layouts  26.5 us (4%)
  starting transfers between devices  21.2 us (3%)
  between operations  15.1 us (2%)
    pallas_call x2, Pallas kernels, exchange(): pl.pallas_call(functools.partial(exchange_kernel, local, len(extras), sum...  152 us
    pallas_call x1, Pallas kernels, finish_last(): pl.pallas_call(finish_last_kernel, in_specs=[vmem] * 8, out_specs=[vmem]...  100 us
    pallas_call x1, Pallas kernels, gather_first(): pl.pallas_call(functools.partial(gather_first_kernel, len(before), len(af...  84.8 us
    pallas_call x1, Pallas kernels, feed(): pl.pallas_call(feed_kernel, grid=(tiles + columns // FEED_COLUMNS,), in_s...  84 us
    pallas_call x2, Pallas kernels, attend_back(): pl.pallas_call(functools.partial(attend_back_kernel, local_heads, own), g...  80.4 us
    pallas_call x2, Pallas kernels, attend(): pl.pallas_call(functools.partial(attend_kernel, local_heads, own), grid_s...  56.3 us
    dot_general x2, matrix products, over_tokens(): lax.dot_general(operand, other_side, (((0,), (0,)), ((), ())), preferred_...  25.8 us
    ppermute x5, waiting for transfers between devices, passed_along(): return lax.ppermute(array, axis, pairs)  25.1 us
  transfers between devices with their start and end apart: 10, of which 3 were waited for; matrix products, arithmetic and copies ran while one was open for 11% of the time, Pallas kernels for 52%

profile of v12, /device:TPU:0, one launch (start us, length us, event | category | flops | bytes accessed | tf_op | source)
XLA Modules:
  0.0 756.9 jit_solution(4557097067491619545)
XLA Ops:
  7.9 4.8 collective-permute-start.2
  15.9 84.8 %gather_first.1 = (bf16[8,4,48,2048]{3,2,1,0:T(8,128)(2,1)}, bf16[2048,1536]{1,0:T(8,128)(2,1)}, bf16[2048,1536]{1,0:T(8,128)(2,1)}) custom-call(bf16[4,48,128]{2,1,0:T(8,128)(2,1)} %maximum_bitcast_fusion.refs_0_, f32[48,1536]{1,0:T(8,128)} %refs_1_.3, f32[48,1536]{1,0:T(8,128)} %refs_2_.1, f32[48,1536]{1,0:T(8,128)} %refs_3_.1, f32[48,1536]{1,0:T(8,128)} %refs_4_.1, ...), custom_call_target="tpu_custom_call" | custom-call | flops 70000001024 | bytes 30000000 | tf_op jit(solution)/shard_map/gather_first/pallas_call | solution.py:808
  103.7 15.1 %project.1 = (bf16[2048,1536]{1,0:T(8,128)(2,1)}, bf16[2048,768]{1,0:T(8,128)(2,1)}, bf16[2048,128]{1,0:T(8,128)(2,1)}, bf16[32,2048]{1,0:T(8,128)(2,1)}, f32[2048,128]{1,0:T(8,128)}) custom-call(bf16[2048,1536]{1,0:T(8,128)(2,1)} %get-tuple-element.57.tokens_ref, f32[8,1536]{1,0:T(8,128)} %broadcast_in_dim.51.gain_ref, bf16[1536,2048]{1,0:T(8,128)(2,1)} %bitcast.112, ...), custom_call_target="tpu_custom_call" | custom-call | flops 5637144576 | bytes 20000000 | tf_op jit(solution)/shard_map/project/pallas_call | solution.py:102
  118.8 5.1 collective-permute-start
  125.3 4.3 all-to-all-start
  129.6 2.1 collective-permute-start.1
  131.7 7.9 %fusion.10 = f32[2048,768]{1,0:T(8,128)S(1)} fusion(bf16[2048,1536]{1,0:T(8,128)(2,1)} %get-tuple-element.64, bf16[1536,2048]{1,0:T(8,128)(2,1)} %bitcast.113), kind=kOutput, calls=%fused_computation.24 | convolution fusion | flops 4831838208 | bytes 14942208 | tf_op jit(solution)/shard_map/dot_general | solution.py:22
  141.1 3.3 convert_reduce_fusion
  145.8 47.7 %attend_own.1 = (f32[384,2048]{1,0:T(8,128)}, f32[24,2048]{1,0:T(8,128)}) custom-call(s32[2,4]{1,0:T(2,128)} %pad_add_fusion.1.ranges_ref, bf16[2048,384]{1,0:T(8,128)(2,1)} %slice.135.q_ref, bf16[2048,768]{1,0:T(8,128)(2,1)} %get-tuple-element.59.k_ref.v_ref, bf16[2048,768]{1,0:T(8,128)(2,1)} %get-tuple-element.59.k_ref.v_ref, ...), custom_call_target="tpu_custom_call" | custom-call | flops 40000000000 | bytes 12000000 | tf_op jit(solution)/shard_map/attend_own/pallas_call | solution.py:326
  193.5 2.1 slice.75
  197.9 8.7 %attend_prev.1 = (bf16[2048,384]{1,0:T(8,128)(2,1)}, f32[24,2048]{1,0:T(8,128)}) custom-call(s32[2,4]{1,0:T(2,128)} %pad_add_fusion.1.ranges_ref, bf16[2048,384]{1,0:T(8,128)(2,1)} %slice.135.q_ref, bf16[2048,768]{1,0:T(8,128)(2,1)} %collective-permute-done.k_ref.v_ref, bf16[2048,768]{1,0:T(8,128)(2,1)} %collective-permute-done.k_ref.v_ref, ...), custom_call_target="tpu_custom_call" | custom-call | flops 10000000000 | bytes 12000000 | tf_op jit(solution)/shard_map/attend_prev/pallas_call | solution.py:326
  206.5 8.1 %convolution_convert_fusion.refs_0_ = bf16[2048,1536]{1,0:T(8,128)(2,1)} fusion(bf16[1536,2048]{1,0:T(8,128)(2,1)} %bitcast.114, bf16[2048,384]{1,0:T(8,128)(2,1)} %get-tuple-element.73.o_ref, f32[2048,384]{1,0:T(8,128)S(1)} %slice.94), kind=kOutput, calls=%fused_computation.2 | convolution fusion | flops 2423783424 | bytes 12189696 | tf_op jit(solution)/shard_map/dot_general | solution.py:22
  215.2 107.7 %exchange_middle.1 = (f32[512,1536]{1,0:T(8,128)}, bf16[2048,1536]{1,0:T(8,128)(2,1)}, bf16[8,4,48,2048]{3,2,1,0:T(8,128)(2,1)}) custom-call(bf16[2048,1536]{1,0:T(8,128)(2,1)} %convolution_convert_fusion.refs_0_, bf16[512,1536]{1,0:T(8,128)(2,1)} %tokens_ref.1, f32[8,1536]{1,0:T(8,128)} %broadcast_in_dim.54.refs_2_.refs_3_, bf16[4,48,2048]{2,1,0:T(8,128)(2,1)} %bitcast.109), custom_call_target="tpu_custom_call" | custom-call | flops 70000001024 | bytes 16000000 | tf_op jit(solution)/shard_map/exchange_middle/pallas_call | solution.py:978
  323.0 84.0 %feed.1 = (bf16[2048,1536]{1,0:T(8,128)(2,1)}, bf16[1536,3072]{1,0:T(8,128)(2,1)}, f32[512,1536]{1,0:T(8,128)}) custom-call(bf16[2048,1536]{1,0:T(8,128)(2,1)} %get-tuple-element.76.input_ref, bf16[2048,1536]{1,0:T(8,128)(2,1)} %get-tuple-element.77.cotangent_ref, bf16[1536,2048]{1,0:T(8,128)(2,1)} %bitcast.119, ...), custom_call_target="tpu_custom_call" | custom-call | flops 57982058496 | bytes 45000000 | tf_op jit(solution)/shard_map/feed/pallas_call | solution.py:1315
  407.0 44.1 %exchange_hidden.1 = (f32[512,1536]{1,0:T(8,128)}, bf16[2048,1536]{1,0:T(8,128)(2,1)}) custom-call(f32[512,1536]{1,0:T(8,128)} %get-tuple-element.80.refs_0_, bf16[512,1536]{1,0:T(8,128)(2,1)} %refs_1_.5, f32[512,1536]{1,0:T(8,128)} %get-tuple-element.75.refs_2_, f32[8,1536]{1,0:T(8,128)} %broadcast_in_dim.54.refs_2_.refs_3_), custom_call_target="tpu_custom_call" | custom-call | flops 10000000000 | bytes 16000000 | tf_op jit(solution)/shard_map/exchange_hidden/pallas_call | solution.py:978
  451.1 2.2 fusion.24
  457.4 6.4 multiply_convert_fusion
  463.8 10.8 %attend_back_prev.1 = (f32[2048,384]{1,0:T(8,128)}, f32[2048,128]{1,0:T(8,128)}, bf16[2,2048,384]{2,1,0:T(8,128)(2,1)}, f32[2048,128]{1,0:T(8,128)}) custom-call(s32[2,4]{1,0:T(2,128)} %pad_add_fusion.1.ranges_ref, bf16[2048,384]{1,0:T(8,128)(2,1)} %slice.135.q_ref, bf16[2048,768]{1,0:T(8,128)(2,1)} %collective-permute-done.k_ref.v_ref, ...), custom_call_target="tpu_custom_call" | custom-call | flops 10000000000 | bytes 25000000 | tf_op jit(solution)/shard_map/attend_back_prev/pallas_call | solution.py:487
  478.8 69.6 %attend_back_own.1 = (bf16[2048,384]{1,0:T(8,128)(2,1)}, f32[2048,384]{1,0:T(8,128)}, f32[2048,384]{1,0:T(8,128)}, f32[2048,128]{1,0:T(8,128)}) custom-call(s32[2,4]{1,0:T(2,128)} %pad_add_fusion.1.ranges_ref, bf16[2048,384]{1,0:T(8,128)(2,1)} %slice.135.q_ref, bf16[2048,768]{1,0:T(8,128)(2,1)} %get-tuple-element.59.k_ref.v_ref, ...), custom_call_target="tpu_custom_call" | custom-call | flops 20000000000 | bytes 25000000 | tf_op jit(solution)/shard_map/attend_back_own/pallas_call | solution.py:487
  548.4 7.8 %convolution_convert_fusion.1 = bf16[1536,384]{1,0:T(8,128)(2,1)} fusion(bf16[2048,1536]{1,0:T(8,128)(2,1)} %get-tuple-element.83, bf16[2048,384]{1,0:T(8,128)(2,1)} %get-tuple-element.73.o_ref, f32[2048,384]{1,0:T(8,128)S(1)} %copy-done.1), kind=kOutput, calls=%fused_computation.23 | convolution fusion | flops 2421227520 | bytes 12189696 | tf_op jit(solution)/shard_map/dot_general | solution.py:1353
  556.1 25.1 %collective-permute-done.6 = f32[2048,8]{0,1:T(8,128)S(1)} collective-permute-done((f32[2048,8]{0,1:T(8,128)S(1)}, f32[2048,8]{0,1:T(8,128)S(1)}, u32[]{:S(2)}, u32[]{:S(2)}) %collective-permute-start.6) | collective-permute-done | bytes 65568 | tf_op jit(solution)/shard_map/ppermute | solution.py:28
  582.6 2.3 pad.9.halo_ref
  584.8 4.3 decay_back.1
  589.2 2.0 convert_reduce_fusion.1
  591.7 2.9 convert_element_type.191
  597.3 2.0 fusion.12
  599.7 2.0 fusion.13
  604.9 18.0 %select_convert_fusion = bf16[1536,1664]{1,0:T(8,128)(2,1)} fusion(bf16[2048,1536]{1,0:T(8,128)(2,1)} %get-tuple-element.64, bf16[2048,1664]{1,0:T(8,128)(2,1)S(1)} %fusion.14.grads_ref, bf16[1536]{0:T(1024)(128)(2,1)S(1)} %select_reduce_fusion, pred[1664]{0:T(1024)(128)(4,1)S(1)} %iota_compare_fusion.1), kind=kOutput, calls=%fused_computation.1 | convolution fusion | flops 10471538688 | bytes 18223744 | tf_op jit(solution)/shard_map/dot_general | solution.py:1353
  622.9 8.5 %collective-permute-done.4 = bf16[512,1536]{1,0:T(8,128)(2,1)S(1)} collective-permute-done((bf16[512,1536]{1,0:T(8,128)(2,1)S(1)}, bf16[512,1536]{1,0:T(8,128)(2,1)S(1)}, u32[]{:S(2)}, u32[]{:S(2)}) %collective-permute-start.4) | collective-permute-done | bytes 1572896 | tf_op jit(solution)/shard_map/ppermute | solution.py:1382
  631.4 2.1 fusion.7
  633.5 4.7 reduce-scatter.2.cloned.1.call-done
  638.2 100.0 %finish_last.1 = (bf16[4,48,1664]{2,1,0:T(8,128)(2,1)}, bf16[4,48,384]{2,1,0:T(8,128)(2,1)}, bf16[4,48,3072]{2,1,0:T(8,128)(2,1)}, f32[512,1536]{1,0:T(8,128)}) custom-call(bf16[2048,1664]{1,0:T(8,128)(2,1)} %copy-done.21, bf16[1536,2048]{1,0:T(8,128)(2,1)} %bitcast.116, bf16[8,4,48,1664]{3,2,1,0:T(8,128)(2,1)} %bitcast.120, ...), custom_call_target="tpu_custom_call" | custom-call | flops 80000000000 | bytes 40000000 | tf_op jit(solution)/shard_map/finish_last/pallas_call | solution.py:1144
  (163 shorter events, 41.5 us)
Async XLA Ops:
  7.9 133.2 %collective-permute-start.2 = (s32[2048]{0:T(1024)S(1)}, s32[2048]{0:T(1024)S(1)}, u32[]{:S(2)}, u32[]{:S(2)}) collective-permute-start(s32[2048]{0:T(1024)S(1)} %broadcast_add_fusion), channel_id=1, source_target_pairs={{0,4},{4,8},{8,12},{12,16},{16,20},{20,24},{24,28},{1,5},{5,9},{9,... | collective-permute-start | bytes 24584 | tf_op jit(solution)/shard_map/ppermute | solution.py:28
  15.9 86.5 %copy-start.34 = (f32[24]{0:T(128)S(1)}, f32[24]{0:T(128)}, u32[]{:S(2)}) copy-start(f32[24]{0:T(128)} %param.23) | copy-start | bytes 292
  103.7 20.2 %copy-start.20 = (f32[48,4096]{1,0:T(8,128)S(1)}, f32[48,4096]{1,0:T(8,128)}, u32[]{:S(2)}) copy-start(f32[48,4096]{1,0:T(8,128)} %param.28) | copy-start | bytes 2359300
  103.7 20.3 %copy-start.7 = (f32[48,4096]{1,0:T(8,128)S(1)}, f32[48,4096]{1,0:T(8,128)}, u32[]{:S(2)}) copy-start(f32[48,4096]{1,0:T(8,128)} %param.27) | copy-start | bytes 2359300
  103.7 20.3 %copy-start.5 = (f32[48,4096]{1,0:T(8,128)S(1)}, f32[48,4096]{1,0:T(8,128)}, u32[]{:S(2)}) copy-start(f32[48,4096]{1,0:T(8,128)} %param.26) | copy-start | bytes 2359300
  118.8 74.7 %collective-permute-start = (bf16[2048,768]{1,0:T(8,128)(2,1)}, bf16[2048,768]{1,0:T(8,128)(2,1)}, u32[]{:S(2)}, u32[]{:S(2)}) collective-permute-start(bf16[2048,768]{1,0:T(8,128)(2,1)} %get-tuple-element.59.k_ref.v_ref), channel_id=1, source_target_pairs={{0,4},{4,8},{8,12},{12,16},{16,20},{20,24},{24,28},{1,5},{5,9},{9,... | collective-permute-start | bytes 9437192 | tf_op jit(solution)/shard_map/ppermute | solution.py:28
  124.1 5.5 copy-start.33
  125.3 68.2 %all-to-all-start = ((bf16[48,4,3072]{2,0,1:T(8,128)(2,1)}), bf16[48,4,3072]{2,0,1:T(8,128)(2,1)}, u32[]{:S(2)}, u32[]{:S(2)}) async-start(bf16[48,4,3072]{2,0,1:T(8,128)(2,1)} %pad_maximum_fusion.1), calls=%async_computation | async-start | bytes 2359296 | tf_op jit(solution)/shard_map/all_to_all | solution.py:1362
  129.5 193.4 %all-gather.2.cloned.1.call-start = ((), (), s32[]{:S(2)}) async-start(), calls=%async_computation.2 | async-start | bytes 3538944 | tf_op jit(solution)/shard_map/all_gather | solution.py:1367
  129.6 63.9 %collective-permute-start.1 = (bf16[32,2048]{1,0:T(8,128)(2,1)S(1)}, bf16[32,2048]{1,0:T(8,128)(2,1)S(1)}, u32[]{:S(2)}, u32[]{:S(2)}) collective-permute-start(bf16[32,2048]{1,0:T(8,128)(2,1)S(1)} %copy-done.33), channel_id=1, source_target_pairs={{0,4},{4,8},{8,12},{12,16},{16,20},{20,24},{24,28},{1,5},{5,9},{9,... | collective-permute-start | bytes 393224 | tf_op jit(solution)/shard_map/ppermute | solution.py:28
  141.0 65.5 %copy-start = (f32[2048,384]{1,0:T(8,128)}, f32[2048,384]{1,0:T(8,128)S(1)}, u32[]{:S(2)}) copy-start(f32[2048,384]{1,0:T(8,128)S(1)} %slice.94) | copy-start | bytes 9437188
  193.5 4.4 copy-start.32
  197.4 440.8 %reduce-scatter.2.cloned.1.call-start = ((), (), s32[]{:S(2)}) async-start(), calls=%async_computation.3 | async-start | bytes 10616832 | tf_op jit(solution)/shard_map/reduce_scatter | solution.py:1371
  451.1 5.1 copy-start.35
  453.4 4.0 copy-start.1
  455.3 136.4 %collective-permute-start.3 = (bf16[1024,1536]{1,0:T(8,128)(2,1)}, bf16[1024,1536]{1,0:T(8,128)(2,1)}, u32[]{:S(2)}, u32[]{:S(2)}) collective-permute-start(bf16[1024,1536]{1,0:T(8,128)(2,1)} %pad_maximum_fusion), channel_id=1, source_target_pairs={{0,1},{1,0},{2,3},{3,2},{4,5},{5,4},{6,7},{7,6},{8,9},{9,8},{10,11... | collective-permute-start | bytes 9437192 | tf_op jit(solution)/shard_map/ppermute | solution.py:1377
  474.7 121.9 %collective-permute-start.5 = (bf16[2,2048,384]{2,1,0:T(8,128)(2,1)}, bf16[2,2048,384]{2,1,0:T(8,128)(2,1)}, u32[]{:S(2)}, u32[]{:S(2)}) collective-permute-start(bf16[2,2048,384]{2,1,0:T(8,128)(2,1)} %get-tuple-element.88), channel_id=1, source_target_pairs={{4,0},{8,4},{12,8},{16,12},{20,16},{24,20},{28,24},{5,1},{9,5},{13... | collective-permute-start | bytes 9437192 | tf_op jit(solution)/shard_map/ppermute | solution.py:28
  477.5 103.7 %collective-permute-start.6 = (f32[2048,8]{0,1:T(8,128)S(1)}, f32[2048,8]{0,1:T(8,128)S(1)}, u32[]{:S(2)}, u32[]{:S(2)}) collective-permute-start(f32[2048,8]{0,1:T(8,128)S(1)} %copy.86), channel_id=1, source_target_pairs={{4,0},{8,4},{12,8},{16,12},{20,16},{24,20},{28,24},{5,1},{9,5},{13... | collective-permute-start | bytes 196616 | tf_op jit(solution)/shard_map/ppermute | solution.py:28
  589.2 5.4 slice-start
  591.7 2.9 slice-start.1
  595.1 36.3 %collective-permute-start.4 = (bf16[512,1536]{1,0:T(8,128)(2,1)S(1)}, bf16[512,1536]{1,0:T(8,128)(2,1)S(1)}, u32[]{:S(2)}, u32[]{:S(2)}) collective-permute-start(bf16[512,1536]{1,0:T(8,128)(2,1)S(1)} %fusion.4), channel_id=1, source_target_pairs={{0,2},{1,3},{2,0},{3,1},{4,6},{5,7},{6,4},{7,5},{8,10},{9,11},{10,... | collective-permute-start | bytes 4718600 | tf_op jit(solution)/shard_map/ppermute | solution.py:1382
  604.9 18.0 %copy-start.21 = (bf16[2048,1664]{1,0:T(8,128)(2,1)}, bf16[2048,1664]{1,0:T(8,128)(2,1)S(1)}, u32[]{:S(2)}) copy-start(bf16[2048,1664]{1,0:T(8,128)(2,1)S(1)} %fusion.14.grads_ref) | copy-start | bytes 20447236
  604.9 26.5 %copy-start.11 = (f32[512,1536]{1,0:T(8,128)S(1)}, f32[512,1536]{1,0:T(8,128)}, u32[]{:S(2)}) copy-start(f32[512,1536]{1,0:T(8,128)} %get-tuple-element.75.refs_2_) | copy-start | bytes 9437188
  738.2 2.9 copy-start.23
  739.6 4.3 copy-start.15
  739.9 4.3 copy-start.26
  740.4 3.8 copy-start.16
  741.1 3.1 copy-start.17
  741.3 2.9 copy-start.18
  741.5 3.0 copy-start.19
  745.4 2.8 copy-start.2
  745.7 4.2 copy-start.10
  (16 other events, 32.9 us)
Sparse Core Ops, SparseCore 0:
  197.5 71.4 all-gather.1
  407.1 231.0 reduce-scatter.1
